TPU v7x, 32 devices: a whole 2x2x4 slice. The times are simulated.
32 devices in a mesh: chan: 8 (over z, x), grp: 4 (over y, core).
Axes of the slice: x: 2, y: 2, z: 4, core: 2. Of those that a mesh axis runs over, the one named last changes fastest.
Arguments:
- voltage_real: bfloat16 [512, 4, 2, 256, 128], P('chan', 'grp'), may hold values from -6 to 6
- voltage_imag: bfloat16 [512, 4, 2, 256, 128], P('chan', 'grp'), may hold values from -6 to 6
- gain_real: float32 [512, 4, 2, 256], P('chan', 'grp'), may hold values from -3 to 3
- gain_imag: float32 [512, 4, 2, 256], P('chan', 'grp'), may hold values from -3 to 3
- channel_mask: int32 [8192], replicated, may hold values 0 or 1
- beam_owner: int32 [4, 256], P('grp'), may hold values from 0 to 255, each once within a row
Outputs:
- flagged: bfloat16 [2, 1024, 65536], P(None, ('chan', 'grp'))
- common_mode: float32 [65536], P(('chan', 'grp'))
Inputs may be any that keep to these rules, and one draw needn't show every extreme that they name: Each row of beam_owner names every number of 0 to 255 once.
All inputs are finite; a program needn't handle non-finite values.
Results may differ from a plain program's by a relative error of at most 0.0015.
The roundings to bfloat16 on the way count: a program that leaves them out, or rounds other values in their place, can miss the bound.
Values may be sent and summed in bfloat16 or wider, within the bound.
No kernel may reach another device: no remote copies, remote signals or barrier semaphores. Data moves between devices by JAX's collectives and lax.ppermute only.
A program may use at most 256 MiB of HBM per device.

v0:
```python
import math

import jax
import jax.numpy as jnp
from jax import lax
from jax.sharding import PartitionSpec as P

FEEDS_NS = 256
CYL = 4
UP = 16


epsilon = 1e-05


def beam_table(feed_count):
    counter = jnp.arange(feed_count, dtype=jnp.int32)
    phases = counter[:, None] * counter[None, :] % feed_count
    angles = phases.astype(jnp.float32) * (-2.0 * math.pi / feed_count)
    factor = 1.0 / math.sqrt(feed_count)
    cosine = jnp.cos(angles) * factor
    sines = jnp.sin(angles) * factor
    real_rows = jnp.stack([cosine, -sines], axis=1)
    imaginary_rows = jnp.stack([sines, cosine], axis=1)
    return jnp.stack([real_rows, imaginary_rows], axis=0).astype(jnp.bfloat16)


def stokes_table(column_count, up_count):
    columns = jnp.arange(column_count, dtype=jnp.int32)
    spectral = jnp.arange(up_count, dtype=jnp.int32)
    column_phase = columns[:, None] * columns[None, :] % column_count
    spectral_phase = spectral[:, None] * spectral[None, :] % up_count
    phases = (
        column_phase[:, None, :, None] * up_count + spectral_phase[None, :, None, :] * column_count
    )
    angles = phases.astype(jnp.float32) * (-2.0 * math.pi / (column_count * up_count))
    factor = 1.0 / math.sqrt(column_count * up_count)
    cosine = jnp.cos(angles) * factor
    sines = jnp.sin(angles) * factor
    real_rows = jnp.stack([cosine, -sines], axis=2)
    imaginary_rows = jnp.stack([sines, cosine], axis=2)
    return jnp.stack([real_rows, imaginary_rows], axis=0)


def calibrate(voltage_real, voltage_imag, gain_real, gain_imag):
    real_gain = gain_real[..., None]
    imaginary_gain = gain_imag[..., None]
    real_volt = voltage_real.astype(jnp.float32)
    imaginary_volt = voltage_imag.astype(jnp.float32)
    real_part = real_gain * real_volt - imaginary_gain * imaginary_volt
    imaginary_part = real_gain * imaginary_volt + imaginary_gain * real_volt
    return jnp.stack([real_part, imaginary_part], axis=-3).astype(jnp.bfloat16)


def beamform(calibrated, weights):
    formed = jnp.einsum(
        "amrn,cyprns->cypams", weights, calibrated, preferred_element_type=jnp.float32
    )
    return formed.astype(jnp.bfloat16)


def detect_block(formed, weights):
    channel_count, column_count, pol_count, parts_count, beam_count, sample_count = formed.shape
    up_count = weights.shape[2]
    frame_count = sample_count // up_count
    shaped = formed.reshape(
        channel_count, column_count, pol_count, parts_count, beam_count, frame_count, up_count
    ).astype(jnp.float32)
    fields = jnp.einsum("aekrqu,cqprmfu->cpaemkf", weights, shaped, precision=lax.Precision.HIGHEST)
    first_real = fields[:, 0, 0]
    first_imaginary = fields[:, 0, 1]
    second_real = fields[:, 1, 0]
    second_imaginary = fields[:, 1, 1]
    intensity = (
        first_real * first_real
        + first_imaginary * first_imaginary
        + second_real * second_real
        + second_imaginary * second_imaginary
    )
    circular = 2.0 * (first_imaginary * second_real - first_real * second_imaginary)
    stacked = jnp.stack([intensity, circular], axis=1).reshape(
        channel_count, 2, weights.shape[1], beam_count, sample_count
    )
    return stacked.astype(jnp.bfloat16)


def soft_flag(spectra, common, mask_grid):
    coarse_count, stokes_count, beam_count, sample_count = spectra.shape
    up_count = mask_grid.shape[1]
    frame_count = sample_count // up_count
    cleaned = (spectra[:, 0].astype(jnp.float32) - common[:, None, :]).reshape(
        coarse_count, beam_count, up_count, frame_count
    )
    circular = (
        spectra[:, 1].astype(jnp.float32).reshape(coarse_count, beam_count, up_count, frame_count)
    )
    power = jnp.mean(cleaned * cleaned, axis=3)
    level = jnp.mean(power, axis=(0, 2)) + epsilon
    weights = mask_grid[:, None, :] / (1.0 + power / (2.0 * level[None, :, None]))
    flagged = jnp.stack([cleaned * weights[..., None], circular * weights[..., None]])
    flagged = jnp.transpose(flagged, (0, 2, 1, 3, 4)).reshape(
        2, beam_count, coarse_count * sample_count
    )
    return flagged.astype(jnp.bfloat16)


def body(voltage_real, voltage_imag, gain_real, gain_imag, channel_mask, beam_owner):
    feed_count = voltage_real.shape[3]
    sample_count = voltage_real.shape[4]
    feed_weights = beam_table(feed_count)
    column_weights = stokes_table(CYL, UP)
    calibrated = calibrate(voltage_real, voltage_imag, gain_real, gain_imag)
    formed = beamform(calibrated, feed_weights)
    turned = lax.all_to_all(formed, "grp", split_axis=4, concat_axis=1, tiled=True)
    detected = detect_block(turned, column_weights)
    stokes = detected.reshape(detected.shape[0], 2, CYL * detected.shape[3], sample_count)
    ordered = jnp.take(stokes, beam_owner[0], axis=2)
    beam_total = FEEDS_NS * CYL
    owned = lax.all_to_all(ordered, "chan", split_axis=2, concat_axis=0, tiled=True)
    owned_sums = jnp.sum(owned[:, 0], axis=1, dtype=jnp.float32)
    common = lax.psum(owned_sums, ("chan", "grp")) / beam_total
    mask_grid = channel_mask.reshape(-1, UP).astype(jnp.float32)
    flagged = soft_flag(owned, common, mask_grid)
    flattened = common.reshape(-1)
    piece_length = flattened.shape[0] // (lax.axis_size("chan") * lax.axis_size("grp"))
    position = lax.axis_index("chan") * lax.axis_size("grp") + lax.axis_index("grp")
    common_piece = lax.dynamic_slice_in_dim(flattened, position * piece_length, piece_length)
    return (flagged, common_piece)


def solution(mesh):
    in_specs = (
        P("chan", "grp", None, None, None),
        P("chan", "grp", None, None, None),
        P("chan", "grp", None, None),
        P("chan", "grp", None, None),
        P(),
        P("grp", None),
    )
    out_specs = (P(None, ("chan", "grp"), None), P(("chan", "grp")))
    return jax.shard_map(body, mesh=mesh, in_specs=in_specs, out_specs=out_specs, check_vma=False)
```

profile of v0, /device:TPU:0, one launch (start us, length us, event | category | flops | bytes accessed | tf_op | source)
XLA Modules:
  0.0 931.6 jit_solution(13042581867903100597)
XLA Ops:
  9.3 12.0 %copy.44 = bf16[64,1,2,256,128]{3,4,2,0,1:T(8,128)(2,1)} copy(bf16[64,1,2,256,128]{4,3,2,1,0:T(8,128)(2,1)} %param.6) | data formatting | bytes 16777216 | tf_op args[0]
  21.3 12.0 %copy.45 = bf16[64,1,2,256,128]{3,4,2,0,1:T(8,128)(2,1)} copy(bf16[64,1,2,256,128]{4,3,2,1,0:T(8,128)(2,1)} %param.7) | data formatting | bytes 16777216 | tf_op args[1]
  33.3 14.4 %fusion.14 = (bf16[64,2,1,256,128]{3,4,2,1,0:T(8,128)(2,1)}, bf16[64,2,1,256,128]{3,4,2,1,0:T(8,128)(2,1)}) fusion(bf16[64,1,2,256,128]{3,4,2,0,1:T(8,128)(2,1)} %copy.45, bf16[64,1,2,256,128]{3,4,2,0,1:T(8,128)(2,1)} %copy.44, f32[64,2,256]{2,1,0:T(2,128)S(1)} %bitcast.100, f32[64,2,256]{2,1,0:T(2,128)S(1)} %bitcast.101), kind=kLoop, calls=%fused_computation.21 | loop fusion | flops 41943040 | bytes 33816576 | tf_op jit(solution)/shard_map/stack | solution.py:52
  47.7 15.8 %fusion.9 = bf16[64,1,2,2,256,128]{4,5,3,2,0,1:T(8,128)(2,1)} fusion(bf16[64,2,1,256,128]{3,4,2,1,0:T(8,128)(2,1)} %get-tuple-element.11, bf16[64,2,1,256,128]{3,4,2,1,0:T(8,128)(2,1)} %get-tuple-element.10, bf16[1,256,2,256]{3,1,2,0:T(8,128)(2,1)S(1)} %get-tuple-element.21, bf16[1,256,2,256]{3,1,2,0:T(8,128)(2,1)S(1)} %get-tuple-element.20), kind=kOutput, calls=%fused_computation.13 | convolution fusion | flops 8632926208 | bytes 34078720 | tf_op jit(solution)/shard_map/amrn,cyprns->cypams/dot_general | solution.py:56
  63.5 41.4 %copy.47 = bf16[64,1,2,2,256,128]{5,3,2,0,1,4:T(2,128)(2,1)} copy(bf16[64,1,2,2,256,128]{4,5,3,2,0,1:T(8,128)(2,1)} %fusion.9) | data formatting | bytes 33554432 | tf_op jit(solution)/shard_map/convert_element_type | solution.py:59
  112.9 183.0 %all-to-all-done = bf16[64,1,2,2,256,128]{5,3,2,0,1,4:T(2,128)(2,1)} async-done(((bf16[64,1,2,2,256,128]{5,3,2,0,1,4:T(2,128)(2,1)}), bf16[64,1,2,2,256,128]{5,3,2,0,1,4:T(2,128)(2,1)}, u32[]{:S(2)}, u32[]{:S(2)}) %all-to-all-start) | async-done | bytes 16777248 | tf_op jit(solution)/shard_map/all_to_all | solution.py:114
  295.9 17.4 %copy.48 = bf16[64,1,2,2,256,128]{5,4,3,2,0,1:T(8,128)(2,1)} copy(bf16[64,1,2,2,256,128]{5,3,2,0,1,4:T(2,128)(2,1)} %all-to-all-done) | data formatting | bytes 33554432 | tf_op jit(solution)/shard_map/all_to_all | solution.py:114
  313.3 30.0 %copy.49 = bf16[64,4,1,2,2,64,128]{5,6,4,3,1,0,2:T(8,128)(2,1)} copy(bf16[64,4,1,2,2,64,128]{6,5,1,4,3,0,2:T(8,128)(2,1)} %bitcast.94) | data formatting | bytes 33554432 | tf_op jit(solution)/shard_map/all_to_all | solution.py:114
  343.2 40.1 %fusion.2 = f32[64,2,2,4,64,16,8]{4,5,3,2,6,1,0:T(8,128)} fusion(bf16[64,4,2,2,64,8,16,1,1]{4,6,5,3,2,1,0,8,7:T(8,128)(2,1)} %bitcast.97, f32[1,4,16,2,4,16]{5,2,3,4,1,0:T(8,128)S(1)} %get-tuple-element.19, f32[1,4,16,2,4,16]{5,2,3,4,1,0:T(8,128)S(1)} %get-tuple-element.18), kind=kOutput, calls=%fused_computation.4 | convolution fusion | flops 12884918272 | bytes 50397184 | tf_op jit(solution)/shard_map/aekrqu,cqprmfu->cpaemkf/dot_general | solution.py:69
  383.3 26.2 %add_convert_fusion = (bf16[64,1,1,4,64,16,8]{4,5,3,2,6,1,0:T(8,128)(2,1)S(1)}, bf16[64,1,1,4,64,16,8]{4,5,3,2,6,1,0:T(8,128)(2,1)}) fusion(f32[64,2,2,4,64,16,8]{4,5,3,2,6,1,0:T(8,128)} %fusion.2), kind=kLoop, calls=%fused_computation.19 | loop fusion | flops 27262976 | bytes 41943040 | tf_op jit(solution)/shard_map/convert.8
  415.5 12.7 %add.210 = bf16[64,1,256,128]{2,3,0,1:T(8,128)(2,1)} reshape(bf16[64,1,1,4,64,16,8]{4,3,6,5,0,2,1:T(4,128)(2,1)} %copy.51) | data formatting | bytes 8388608 | tf_op jit(solution)/shard_map/add | solution.py:75
  434.8 8.3 copy.52
  443.1 12.9 %mul.473 = bf16[64,1,256,128]{2,3,0,1:T(8,128)(2,1)} reshape(bf16[64,1,1,4,64,16,8]{4,3,6,5,0,2,1:T(4,128)(2,1)} %copy.52) | data formatting | bytes 8388608 | tf_op jit(solution)/shard_map/mul | solution.py:80
  462.5 7.6 pad_maximum_fusion
  470.2 12.0 %gather_fusion = bf16[256,64,2,128]{3,1,2,0:T(8,128)(2,1)} fusion(bf16[64,2,256,128]{3,0,2,1:T(8,128)(2,1)} %pad_maximum_fusion, s32[1024]{0:T(1024)S(1)} %pad_clamp_fusion), kind=kCustom, calls=%fused_computation | custom fusion | bytes 16778240 | tf_op jit(solution)/shard_map/jit(_take)/gather | solution.py:117
  482.2 7.6 select_bitcast_fusion
  497.1 182.4 %all-to-all-done.1 = bf16[64,2,256,128]{3,0,1,2:T(8,128)(2,1)} async-done(((bf16[64,2,256,128]{3,0,1,2:T(8,128)(2,1)}), bf16[64,2,256,128]{3,0,1,2:T(8,128)(2,1)}, u32[]{:S(2)}, u32[]{:S(2)}) %all-to-all-start.1) | async-done | bytes 8388640 | tf_op jit(solution)/shard_map/all_to_all | solution.py:119
  679.5 12.3 %copy.56 = bf16[8,64,2,32,128]{4,3,2,1,0:T(8,128)(2,1)} copy(bf16[8,64,2,32,128]{4,1,2,3,0:T(8,128)(2,1)} %bitcast.34) | data formatting | bytes 16777216 | tf_op jit(solution)/shard_map/all_to_all | solution.py:119
  696.4 11.7 %slice_convert_fusion.1 = (f32[512,1,32,128]{3,2,1,0:T(8,128)}, f32[512,1,32,128]{3,2,1,0:T(8,128)}) fusion(bf16[512,2,32,128]{3,2,1,0:T(8,128)(2,1)} %bitcast.96), kind=kLoop, calls=%fused_computation.34 | loop fusion | flops 4194304 | bytes 25165824 | tf_op jit(solution)/shard_map/convert_element_type | solution.py:91
  708.1 10.2 %copy.57 = f32[512,1,32,128]{0,3,2,1:T(8,128)} copy(f32[512,1,32,128]{3,2,1,0:T(8,128)} %get-tuple-element.12) | data formatting | bytes 16777216 | tf_op jit(solution)/shard_map/convert_element_type | solution.py:91
  718.3 10.0 %copy.61 = f32[512,1,32,128]{0,3,2,1:T(8,128)} copy(f32[512,1,32,128]{3,2,1,0:T(8,128)} %get-tuple-element.13) | data formatting | bytes 16777216 | tf_op jit(solution)/shard_map/convert_element_type | solution.py:95
  728.4 91.4 %all-reduce.2.cloned.1.call-done = f32[512,128]{1,0:T(8,128)} async-done(((f32[512,128]{1,0:T(8,128)}), f32[512,128]{1,0:T(8,128)}) %all-reduce.2.cloned.1.call-update) | async-done | bytes 262160 | tf_op jit(solution)/shard_map/psum | solution.py:121
  841.7 55.2 %copy.62 = bf16[2,32,512,16,8]{1,4,3,2,0:T(8,128)(2,1)} copy(bf16[2,32,512,16,8]{2,4,3,1,0:T(8,128)(2,1)} %maximum_bitcast_fusion.4) | data formatting | bytes 16777216 | tf_op jit(solution)/shard_map/convert_element_type | solution.py:104
  896.9 26.7 %copy.63 = bf16[2,32,65536]{2,1,0:T(8,128)(2,1)} copy(bf16[2,32,65536]{1,2,0:T(8,128)(2,1)} %bitcast.93) | data formatting | bytes 16777216
  (40 shorter events, 63.6 us)
Async XLA Ops:
  21.3 12.0 %copy-start.1 = (f32[64,1,2,256]{3,2,1,0:T(2,128)S(1)}, f32[64,1,2,256]{3,2,1,0:T(2,128)}, u32[]{:S(2)}) copy-start(f32[64,1,2,256]{3,2,1,0:T(2,128)} %param.9) | copy-start | bytes 393220
  21.3 12.0 %copy-start.2 = (f32[64,1,2,256]{3,2,1,0:T(2,128)S(1)}, f32[64,1,2,256]{3,2,1,0:T(2,128)}, u32[]{:S(2)}) copy-start(f32[64,1,2,256]{3,2,1,0:T(2,128)} %param.8) | copy-start | bytes 393220
  104.9 7.3 copy-start.4
  104.9 191.0 %all-to-all-start = ((bf16[64,1,2,2,256,128]{5,3,2,0,1,4:T(2,128)(2,1)}), bf16[64,1,2,2,256,128]{5,3,2,0,1,4:T(2,128)(2,1)}, u32[]{:S(2)}, u32[]{:S(2)}) async-start(bf16[64,1,2,2,256,128]{5,3,2,0,1,4:T(2,128)(2,1)} %copy.47), calls=%async_computation | async-start | bytes 33554432 | tf_op jit(solution)/shard_map/all_to_all | solution.py:114
  489.8 7.1 copy-start.3
  489.8 189.7 %all-to-all-start.1 = ((bf16[64,2,256,128]{3,0,1,2:T(8,128)(2,1)}), bf16[64,2,256,128]{3,0,1,2:T(8,128)(2,1)}, u32[]{:S(2)}, u32[]{:S(2)}) async-start(bf16[64,2,256,128]{3,0,1,2:T(8,128)(2,1)} %select_bitcast_fusion), calls=%async_computation.1 | async-start | bytes 16777216 | tf_op jit(solution)/shard_map/all_to_all | solution.py:119
  496.5 323.2 %all-reduce.2.cloned.1.call-start = ((), (), s32[]{:S(2)}) async-start(), calls=%async_computation.2 | async-start | bytes 524288 | tf_op jit(solution)/shard_map/psum | solution.py:121
  820.8 7.4 copy-start
Sparse Core Ops, SparseCore 0:
  696.5 123.1 all-reduce.1
where the time goes:
time: 943 us; the launch traced here: 932 us
  waiting for transfers between devices  457 us (48%)
  local copies, waits for them, and re-layouts  293 us (31%)
  other arithmetic  96.8 us (10%)
  matrix products  55.9 us (6%)
  between operations  14.7 us (2%)
  starting transfers between devices  14.3 us (2%)
    all_to_all x1, waiting for transfers between devices, body(): lax.all_to_all(formed, 'grp', split_axis=4, concat_axis=1, tiled=True)  183 us
    all_to_all x1, waiting for transfers between devices, body(): lax.all_to_all(ordered, 'chan', split_axis=2, concat_axis=0, tiled=True)  182 us
    psum x1, waiting for transfers between devices, body(): common = lax.psum(owned_sums, ('chan', 'grp')) / beam_total  91.4 us
    convert_element_type x1, local copies, waits for them, and re-layouts, soft_flag(): return flagged.astype(jnp.bfloat16)  55.2 us
    unnamed x13, local copies, waits for them, and re-layouts  50.7 us
    all_to_all x2, local copies, waits for them, and re-layouts, body(): lax.all_to_all(formed, 'grp', split_axis=4, concat_axis=1, tiled=True)  47.3 us
    convert_element_type x1, local copies, waits for them, and re-layouts, beamform(): return formed.astype(jnp.bfloat16)  41.4 us
    dot_general x1, matrix products, detect_block(): jnp.einsum('aekrqu,cqprmfu->cpaemkf', weights, shaped, precision=lax.Prec...  40.1 us
  transfers between devices with their start and end apart: 3, of which 3 were waited for; matrix products, arithmetic and copies ran while one was open for 4% of the time, Pallas kernels for 0%

commit v1 on v0

v1 whole, which is shorter than its diff:
```python
import math

import jax
import jax.numpy as jnp
import numpy as np
from jax import lax
from jax.experimental import pallas as pl
from jax.experimental.pallas import tpu as pltpu
from jax.sharding import PartitionSpec as P

UP = 16
CHUNKS = 8
AHEAD = 1

epsilon = 1e-05


def beam_table(feed_count):
    counter = jnp.arange(feed_count, dtype=jnp.int32)
    phases = counter[:, None] * counter[None, :] % feed_count
    angles = phases.astype(jnp.float32) * (-2.0 * math.pi / feed_count)
    factor = 1.0 / math.sqrt(feed_count)
    cosine = jnp.cos(angles) * factor
    sines = jnp.sin(angles) * factor
    real_rows = jnp.concatenate([cosine, -sines], axis=1)
    imaginary_rows = jnp.concatenate([sines, cosine], axis=1)
    return jnp.concatenate([real_rows, imaginary_rows], axis=0).astype(jnp.bfloat16)


def spectral_tables(up_count, frame_count, column_count):
    spectral = np.arange(up_count)
    angles = (spectral[:, None] * spectral[None, :] % up_count) * (-2.0 * math.pi / up_count)
    factor = 1.0 / math.sqrt(column_count * up_count)
    cosine, sines = np.cos(angles) * factor, np.sin(angles) * factor
    same = np.eye(frame_count)
    sample_count = frame_count * up_count

    def spread(entries):
        return np.einsum("uk,tv->tukv", entries, same).reshape(sample_count, sample_count)

    table = np.block([[spread(cosine), spread(sines)], [-spread(sines), spread(cosine)]])
    table = table.astype(np.float32)
    high = table.astype(jnp.bfloat16)
    low = (table - high.astype(np.float32)).astype(jnp.bfloat16)
    return high, low


def form_kernel(after_ref, table_ref, gain_real_ref, gain_imag_ref, real_ref, imag_ref, *out_refs):
    channels, pols, _, beams, samples = out_refs[0].shape
    gains_real, gains_imag = gain_real_ref[0].T, gain_imag_ref[0].T
    for c in range(channels):
        columns = []
        for p in range(pols):
            j = c * pols + p
            gain_real, gain_imag = gains_real[:, j : j + 1], gains_imag[:, j : j + 1]
            real = real_ref[c, 0, p].astype(jnp.float32)
            imag = imag_ref[c, 0, p].astype(jnp.float32)
            real_part = (gain_real * real - gain_imag * imag).astype(jnp.bfloat16)
            imag_part = (gain_real * imag + gain_imag * real).astype(jnp.bfloat16)
            columns.append(jnp.concatenate([real_part, imag_part], axis=0))
        calibrated = jnp.concatenate(columns, axis=1)
        formed = jnp.dot(table_ref[...], calibrated, preferred_element_type=jnp.float32)
        formed = formed.astype(jnp.bfloat16)
        for p in range(pols):
            for r, out_ref in enumerate(out_refs):
                for a in range(2):
                    row = (r * 2 + a) * beams
                    out_ref[c, p, a] = formed[row : row + beams, p * samples : (p + 1) * samples]


def detect_kernel(me_ref, after_ref, before_ref, high_ref, low_ref, order_ref, *refs):
    formed_refs, (out_ref, sum_ref, rows_ref) = refs[:-3], refs[-3:]
    columns = len(formed_refs)
    channels, pols, _, beams, samples = formed_refs[0].shape
    owners, _, own, _ = out_ref.shape
    for c in range(channels):
        for r, formed_ref in enumerate(formed_refs):
            y = me_ref[0] ^ r
            for p in range(pols):
                for a in range(2):
                    rows_ref[p, y, :, a * samples : (a + 1) * samples] = formed_ref[c, p, a]
        rows = rows_ref[...].reshape(pols * columns * beams, 2 * samples)
        spectra = jnp.dot(rows, high_ref[...], preferred_element_type=jnp.float32) + jnp.dot(
            rows, low_ref[...], preferred_element_type=jnp.float32
        )
        real, imag = [], []
        for p in range(pols):
            g = [spectra[(p * columns + y) * beams :][:beams] for y in range(columns)]
            even_sum, even_diff = g[0] + g[2], g[0] - g[2]
            odd_sum, odd_diff = g[1] + g[3], g[1] - g[3]
            zero, two = even_sum + odd_sum, even_sum - odd_sum
            dr, di = even_diff[:, :samples], even_diff[:, samples:]
            qr, qi = odd_diff[:, :samples], odd_diff[:, samples:]
            real.append([zero[:, :samples], dr + qi, two[:, :samples], dr - qi])
            imag.append([zero[:, samples:], di - qr, two[:, samples:], di + qr])
        stokes, total = [], None
        for e in range(columns):
            xr, xi, yr, yi = real[0][e], imag[0][e], real[1][e], imag[1][e]
            intensity = (xr * xr + xi * xi + yr * yr + yi * yi).astype(jnp.bfloat16)
            circular = (2.0 * (xi * yr - xr * yi)).astype(jnp.bfloat16)
            stokes.append(jnp.concatenate([intensity, circular], axis=1))
            part = intensity.astype(jnp.float32)
            total = part if total is None else total + part
        sum_ref[0, c : c + 1, :] = jnp.sum(total, axis=0, keepdims=True)
        ordered = jnp.dot(
            order_ref[...], jnp.concatenate(stokes, axis=0), preferred_element_type=jnp.float32
        )
        for d in range(owners):
            out_ref[d, c] = ordered[d * own : (d + 1) * own].astype(jnp.bfloat16)


def flag_kernel(frame_count, group_ref, common_ref, mask_ref, *refs):
    chunk_refs, out_ref, power_ref = refs[:-2], refs[-2], refs[-1]
    sources, per_chunk, beams, width = chunk_refs[0].shape
    samples = width // 2
    local = per_chunk * len(chunk_refs)

    def measure(s, level):
        for i, chunk_ref in enumerate(chunk_refs):
            first = s * local + i * per_chunk
            common = common_ref[pl.ds(first, per_chunk)]
            cleaned = chunk_ref[s, :, :, :samples].astype(jnp.float32) - common
            squares = (cleaned * cleaned).reshape(per_chunk * beams, samples)
            high = squares.astype(jnp.bfloat16)
            low = (squares - high.astype(jnp.float32)).astype(jnp.bfloat16)
            power = jnp.dot(high, group_ref[...], preferred_element_type=jnp.float32) + jnp.dot(
                low, group_ref[...], preferred_element_type=jnp.float32
            )
            power = power.reshape(per_chunk, beams, samples)
            power_ref[pl.ds(first, per_chunk)] = power
            level = level + jnp.sum(power, axis=0)
        return level

    level = lax.fori_loop(0, sources, measure, jnp.zeros((beams, samples), jnp.float32))
    level = jnp.sum(level, axis=1, keepdims=True) / float(sources * local * samples) + epsilon
    scale = jnp.broadcast_to(0.5 / level, (beams, samples))

    def flag(s, carry):
        for i, chunk_ref in enumerate(chunk_refs):
            for c in range(per_chunk):
                channel = s * local + i * per_chunk + c
                row = chunk_ref[s, c].astype(jnp.float32)
                cleaned = row[:, :samples] - common_ref[channel]
                weight = mask_ref[channel] / (1.0 + power_ref[channel] * scale)
                where = pl.ds(pl.multiple_of(channel * samples, samples), samples)
                out_ref[0, :, where] = (cleaned * weight).astype(jnp.bfloat16)
                out_ref[1, :, where] = (row[:, samples:] * weight).astype(jnp.bfloat16)
        return carry

    lax.fori_loop(0, sources, flag, 0)


def whole_spec(array):
    return pl.BlockSpec(array.shape, lambda *_: (0,) * array.ndim)


def form(after, table, gains, volts, chunk, per_chunk, step, groups):
    real, imag = volts
    _, _, pols, feeds, samples = real.shape
    steps = per_chunk // step
    gain_spec = pl.BlockSpec((1, *gains[0].shape[1:]), lambda i: (chunk * steps + i, 0, 0))
    volt_spec = pl.BlockSpec(
        (step, 1, pols, feeds, samples), lambda i: (chunk * steps + i, 0, 0, 0, 0)
    )
    beams = feeds // groups
    return pl.pallas_call(
        form_kernel,
        grid=(steps,),
        in_specs=[pl.BlockSpec(memory_space=pl.ANY), whole_spec(table), gain_spec, gain_spec, volt_spec, volt_spec],
        out_specs=[pl.BlockSpec((step, pols, 2, beams, samples), lambda i: (i, 0, 0, 0, 0))]
        * groups,
        out_shape=[jax.ShapeDtypeStruct((per_chunk, pols, 2, beams, samples), jnp.bfloat16)]
        * groups,
        cost_estimate=pl.CostEstimate(
            flops=per_chunk * pols * 8 * feeds * feeds * samples,
            bytes_accessed=per_chunk * pols * feeds * samples * 8,
            transcendentals=0,
        ),
        compiler_params=pltpu.CompilerParams(vmem_limit_bytes=60 << 20),
        name="form",
    )(after, table, *gains, real, imag)


def detect(me, tables, order, formed, after, step, owners):
    columns = len(formed)
    per_chunk, pols, _, beams, samples = formed[0].shape
    steps = per_chunk // step
    own = columns * beams // owners
    return pl.pallas_call(
        detect_kernel,
        grid=(steps,),
        in_specs=[
            pl.BlockSpec(memory_space=pltpu.SMEM),
            pl.BlockSpec(memory_space=pl.ANY),
            pl.BlockSpec(memory_space=pl.ANY),
            *[whole_spec(table) for table in tables],
            whole_spec(order),
            *[pl.BlockSpec((step, pols, 2, beams, samples), lambda i: (i, 0, 0, 0, 0))] * columns,
        ],
        out_specs=[
            pl.BlockSpec((owners, step, own, 2 * samples), lambda i: (0, i, 0, 0)),
            pl.BlockSpec((1, step, samples), lambda i: (i, 0, 0)),
        ],
        out_shape=[
            jax.ShapeDtypeStruct((owners, per_chunk, own, 2 * samples), jnp.bfloat16),
            jax.ShapeDtypeStruct((steps, step, samples), jnp.float32),
        ],
        scratch_shapes=[pltpu.VMEM((pols, columns, beams, 2 * samples), jnp.bfloat16)],
        cost_estimate=pl.CostEstimate(
            flops=per_chunk * columns * beams * samples * samples * 24,
            bytes_accessed=per_chunk * columns * beams * samples * 12,
            transcendentals=0,
        ),
        compiler_params=pltpu.CompilerParams(vmem_limit_bytes=60 << 20),
        name="detect",
    )(me, *after, *tables, order, *formed)


def soft_flag(owned, common, mask, frame_count):
    sources, per_chunk, own, width = owned[0].shape
    samples = width // 2
    channels = common.shape[0]
    block = 16 if own % 16 == 0 else own
    group = np.kron(np.eye(samples // frame_count), np.ones((frame_count, frame_count)))
    group = jnp.asarray(group / frame_count, jnp.bfloat16)
    return pl.pallas_call(
        lambda *refs: flag_kernel(frame_count, *refs),
        grid=(own // block,),
        in_specs=[
            whole_spec(group),
            whole_spec(common),
            whole_spec(mask),
            *[
                pl.BlockSpec((sources, per_chunk, block, width), lambda i: (0, 0, i, 0))
                for _ in owned
            ],
        ],
        out_specs=pl.BlockSpec((2, block, channels * samples), lambda i: (0, i, 0)),
        out_shape=jax.ShapeDtypeStruct((2, own, channels * samples), jnp.bfloat16),
        scratch_shapes=[pltpu.VMEM((channels, block, samples), jnp.float32)],
        cost_estimate=pl.CostEstimate(
            flops=channels * own * samples * samples * 4,
            bytes_accessed=channels * own * samples * 8,
            transcendentals=0,
        ),
        compiler_params=pltpu.CompilerParams(vmem_limit_bytes=60 << 20),
        name="flag",
    )(group, common, mask, *owned)


def body(voltage_real, voltage_imag, gain_real, gain_imag, channel_mask, beam_owner):
    local, _, pols, feeds, samples = voltage_real.shape
    frame_count = samples // UP
    owners, groups = lax.axis_size("chan"), lax.axis_size("grp")
    channels = local * owners
    per_chunk = max(local // CHUNKS, 1)
    chunks = local // per_chunk
    step = math.gcd(per_chunk, 2)

    def rows_of(gain):
        rows = gain.reshape(local // step, step * pols, feeds)
        return jnp.pad(rows, ((0, 0), (0, -rows.shape[1] % 8), (0, 0)))

    gains = (rows_of(gain_real), rows_of(gain_imag))
    mine = lax.axis_index("grp")
    table = beam_table(feeds).reshape(2, groups, feeds // groups, 2 * feeds)
    table = jnp.stack([table[:, mine ^ r] for r in range(groups)]).reshape(2 * feeds, 2 * feeds)
    me = mine.astype(jnp.int32).reshape(1)
    tables = [jnp.asarray(one) for one in spectral_tables(UP, frame_count, groups)]
    slots = beam_owner.shape[1]
    order = (beam_owner[0][:, None] == jnp.arange(slots, dtype=jnp.int32)[None, :]).astype(
        jnp.bfloat16
    )
    mask = jnp.repeat(channel_mask.astype(jnp.float32), frame_count).reshape(channels, 1, samples)
    volts = (voltage_real, voltage_imag)
    turned, owned, sums = [], [], []
    after = me
    for chunk in range(chunks + AHEAD):
        if chunk < chunks:
            formed = form(after, table, gains, volts, chunk, per_chunk, step, groups)
            turned.append(
                [
                    lax.ppermute(one, "grp", [(g, g ^ r) for g in range(groups)]) if r else one
                    for r, one in enumerate(formed)
                ]
            )
            after = formed[0]
        if chunk >= AHEAD:
            blocks = turned[chunk - AHEAD]
            before = owned[-2:-1] or [me]
            stokes, part = detect(me, tables, order, blocks, [after, before[0]], step, owners)
            owned.append(lax.all_to_all(stokes, "chan", split_axis=0, concat_axis=0, tiled=True))
            sums.append(part.reshape(per_chunk, samples))
            after = stokes
    partial = jnp.concatenate(sums, axis=0)
    gathered = lax.all_gather(partial, ("chan", "grp"), axis=0)
    common = jnp.sum(gathered.reshape(owners, groups, local, samples), axis=1)
    common = common.reshape(channels, samples) / float(feeds * groups)
    flagged = soft_flag(owned, common.reshape(channels, 1, samples), mask, frame_count)
    flattened = common.reshape(-1)
    piece = flattened.shape[0] // (owners * groups)
    position = lax.axis_index("chan") * groups + lax.axis_index("grp")
    return (flagged, lax.dynamic_slice_in_dim(flattened, position * piece, piece))


def solution(mesh):
    in_specs = (
        P("chan", "grp", None, None, None),
        P("chan", "grp", None, None, None),
        P("chan", "grp", None, None),
        P("chan", "grp", None, None),
        P(),
        P("grp", None),
    )
    out_specs = (P(None, ("chan", "grp"), None), P(("chan", "grp")))
    return jax.shard_map(body, mesh=mesh, in_specs=in_specs, out_specs=out_specs, check_vma=False)
```

time: 943 us -> 408 us (0.43); the launches traced: 932 us -> 406 us
  local copies, waits for them, and re-layouts: 293 us -> 14.6 us
  waiting for transfers between devices: 457 us -> 192 us
  Pallas kernels: 0 us -> 118 us
  other arithmetic: 96.8 us -> 5.12 us
  matrix products: 55.9 us -> 0 us
  starting transfers between devices: 14.3 us -> 62.6 us
    all_to_all x2 -> x8, waiting for transfers between devices: 365 us -> 24.6 us  [body(): lax.all_to_all(stokes, 'chan', split_axis=0, concat_axis=0, tiled=True)]
    ppermute x0 -> x24, waiting for transfers between devices: none -> 132 us  [body(): lax.ppermute(one, 'grp', [(g, g ^ r) for g in range(groups)])]
    pallas_call x0 -> x17, Pallas kernels: none -> 118 us  [the longest x8 55.6 us: detect(): pl.pallas_call(detect_kernel, grid=(steps,), in_specs=[pl.BlockSpec(memor...]
    convert_element_type x6 -> x0, local copies, waits for them, and re-layouts: 117 us -> none  [the longest x1 55.2 us: soft_flag(): return flagged.astype(jnp.bfloat16)]
    psum x1 -> x0, waiting for transfers between devices: 91.4 us -> none  [body(): common = lax.psum(owned_sums, ('chan', 'grp')) / beam_total]
    all_to_all x3 -> x0, local copies, waits for them, and re-layouts: 59.6 us -> none  [the longest x2 47.3 us: body(): lax.all_to_all(formed, 'grp', split_axis=4, concat_axis=1, tiled=True)]
    dot_general x2 -> x0, matrix products: 55.9 us -> none  [the longest x1 40.1 us: detect_block(): jnp.einsum('aekrqu,cqprmfu->cpaemkf', weights, shaped, precision=lax.Prec...]
    another operation x8 -> x3, other arithmetic: 57.5 us -> 3 us
  transfers between devices with their start and end apart: 3 -> 33, of which waited for: 3 -> 18; matrix products, arithmetic and copies ran while one was open for 4% -> 1% of each run, Pallas kernels for 0% -> 21%
where the time goes in v1:
time: 408 us; the launch traced here: 406 us
  waiting for transfers between devices  192 us (47%)
  Pallas kernels  118 us (29%)
  starting transfers between devices  62.6 us (15%)
  local copies, waits for them, and re-layouts  14.6 us (4%)
  between operations  14.5 us (4%)
  other arithmetic  5.12 us (1%)
    ppermute x24, waiting for transfers between devices, body(): lax.ppermute(one, 'grp', [(g, g ^ r) for g in range(groups)])  132 us
    pallas_call x8, Pallas kernels, detect(): pl.pallas_call(detect_kernel, grid=(steps,), in_specs=[pl.BlockSpec(memor...  55.6 us
    pallas_call x8, Pallas kernels, form(): pl.pallas_call(form_kernel, grid=(steps,), in_specs=[pl.BlockSpec(memory_...  48.9 us
    all_to_all x8, starting transfers between devices, body(): lax.all_to_all(stokes, 'chan', split_axis=0, concat_axis=0, tiled=True)  46 us
    all_gather x1, waiting for transfers between devices, body(): gathered = lax.all_gather(partial, ('chan', 'grp'), axis=0)  35.1 us
    all_to_all x8, waiting for transfers between devices, body(): lax.all_to_all(stokes, 'chan', split_axis=0, concat_axis=0, tiled=True)  24.6 us
    ppermute x24, starting transfers between devices, body(): lax.ppermute(one, 'grp', [(g, g ^ r) for g in range(groups)])  16.5 us
    pallas_call x1, Pallas kernels, soft_flag(): pl.pallas_call(lambda *refs: flag_kernel(frame_count, *refs), grid=(own /...  13 us
  transfers between devices with their start and end apart: 33, of which 18 were waited for; matrix products, arithmetic and copies ran while one was open for 1% of the time, Pallas kernels for 21%

profile of v1, /device:TPU:0, one launch (start us, length us, event | category | flops | bytes accessed | tf_op | source)
XLA Modules:
  0.0 406.5 jit_solution(18094797986005837970)
XLA Ops:
  36.0 10.7 %collective-permute-done.2.refs_3_ = bf16[8,2,2,64,128]{4,3,2,1,0:T(8,128)(2,1)S(1)} collective-permute-done((bf16[8,2,2,64,128]{4,3,2,1,0:T(8,128)(2,1)}, bf16[8,2,2,64,128]{4,3,2,1,0:T(8,128)(2,1)S(1)}, u32[]{:S(2)}, u32[]{:S(2)}) %collective-permute-start.2) | collective-permute-done | bytes 524320 | tf_op jit(solution)/shard_map/ppermute | solution.py:283
  47.5 7.0 %detect.8 = (bf16[8,8,32,256]{3,2,1,0:T(8,128)(2,1)}, f32[4,2,128]{2,1,0:T(2,128)}) custom-call(s32[1]{0:T(128)} %bitcast.after_ref.me_ref.before_ref, bf16[8,2,2,64,128]{4,3,2,1,0:T(8,128)(2,1)} %get-tuple-element.51.after_ref.refs_0_, s32[1]{0:T(128)} %bitcast.after_ref.me_ref.before_ref, bf16[256,256]{1,0:T(8,128)(2,1)} %constant.53.clone.high_ref, ...), custom_call_target="tpu_custom_call" | custom-call | flops 805306368 | bytes 3145728 | tf_op jit(solution)/shard_map/detect/pallas_call | solution.py:189
  68.3 7.0 %collective-permute-done.4.refs_2_ = bf16[8,2,2,64,128]{4,3,2,1,0:T(8,128)(2,1)S(1)} collective-permute-done((bf16[8,2,2,64,128]{4,3,2,1,0:T(8,128)(2,1)}, bf16[8,2,2,64,128]{4,3,2,1,0:T(8,128)(2,1)S(1)}, u32[]{:S(2)}, u32[]{:S(2)}) %collective-permute-start.4) | collective-permute-done | bytes 524320 | tf_op jit(solution)/shard_map/ppermute | solution.py:283
  75.3 10.3 %collective-permute-done.5.refs_3_ = bf16[8,2,2,64,128]{4,3,2,1,0:T(8,128)(2,1)S(1)} collective-permute-done((bf16[8,2,2,64,128]{4,3,2,1,0:T(8,128)(2,1)}, bf16[8,2,2,64,128]{4,3,2,1,0:T(8,128)(2,1)S(1)}, u32[]{:S(2)}, u32[]{:S(2)}) %collective-permute-start.5) | collective-permute-done | bytes 524320 | tf_op jit(solution)/shard_map/ppermute | solution.py:283
  86.4 7.0 %detect.9 = (bf16[8,8,32,256]{3,2,1,0:T(8,128)(2,1)}, f32[4,2,128]{2,1,0:T(2,128)}) custom-call(s32[1]{0:T(128)} %bitcast.after_ref.me_ref.before_ref, bf16[8,2,2,64,128]{4,3,2,1,0:T(8,128)(2,1)} %get-tuple-element.57.after_ref.refs_0_, s32[1]{0:T(128)} %bitcast.after_ref.me_ref.before_ref, bf16[256,256]{1,0:T(8,128)(2,1)} %constant.53.clone.high_ref, ...), custom_call_target="tpu_custom_call" | custom-call | flops 805306368 | bytes 3145728 | tf_op jit(solution)/shard_map/detect/pallas_call | solution.py:189
  107.5 7.0 %collective-permute-done.7.refs_2_ = bf16[8,2,2,64,128]{4,3,2,1,0:T(8,128)(2,1)S(1)} collective-permute-done((bf16[8,2,2,64,128]{4,3,2,1,0:T(8,128)(2,1)}, bf16[8,2,2,64,128]{4,3,2,1,0:T(8,128)(2,1)S(1)}, u32[]{:S(2)}, u32[]{:S(2)}) %collective-permute-start.7) | collective-permute-done | bytes 524320 | tf_op jit(solution)/shard_map/ppermute | solution.py:283
  114.5 10.3 %collective-permute-done.8.refs_3_ = bf16[8,2,2,64,128]{4,3,2,1,0:T(8,128)(2,1)S(1)} collective-permute-done((bf16[8,2,2,64,128]{4,3,2,1,0:T(8,128)(2,1)}, bf16[8,2,2,64,128]{4,3,2,1,0:T(8,128)(2,1)S(1)}, u32[]{:S(2)}, u32[]{:S(2)}) %collective-permute-start.8) | collective-permute-done | bytes 524320 | tf_op jit(solution)/shard_map/ppermute | solution.py:283
  125.6 7.0 %detect.10 = (bf16[8,8,32,256]{3,2,1,0:T(8,128)(2,1)}, f32[4,2,128]{2,1,0:T(2,128)}) custom-call(s32[1]{0:T(128)} %bitcast.after_ref.me_ref.before_ref, bf16[8,2,2,64,128]{4,3,2,1,0:T(8,128)(2,1)} %get-tuple-element.63.after_ref.refs_0_, bf16[8,8,32,256]{3,2,1,0:T(8,128)(2,1)} %copy-done.1, bf16[256,256]{1,0:T(8,128)(2,1)} %constant.53.clone.high_ref, ...), custom_call_target="tpu_custom_call" | custom-call | flops 805306368 | bytes 3145728 | tf_op jit(solution)/shard_map/detect/pallas_call | solution.py:189
  146.9 6.8 %collective-permute-done.10.refs_2_ = bf16[8,2,2,64,128]{4,3,2,1,0:T(8,128)(2,1)S(1)} collective-permute-done((bf16[8,2,2,64,128]{4,3,2,1,0:T(8,128)(2,1)}, bf16[8,2,2,64,128]{4,3,2,1,0:T(8,128)(2,1)S(1)}, u32[]{:S(2)}, u32[]{:S(2)}) %collective-permute-start.10) | collective-permute-done | bytes 524320 | tf_op jit(solution)/shard_map/ppermute | solution.py:283
  153.7 9.3 %collective-permute-done.11.refs_3_ = bf16[8,2,2,64,128]{4,3,2,1,0:T(8,128)(2,1)S(1)} collective-permute-done((bf16[8,2,2,64,128]{4,3,2,1,0:T(8,128)(2,1)}, bf16[8,2,2,64,128]{4,3,2,1,0:T(8,128)(2,1)S(1)}, u32[]{:S(2)}, u32[]{:S(2)}) %collective-permute-start.11) | collective-permute-done | bytes 524320 | tf_op jit(solution)/shard_map/ppermute | solution.py:283
  164.0 7.0 %detect.11 = (bf16[8,8,32,256]{3,2,1,0:T(8,128)(2,1)}, f32[4,2,128]{2,1,0:T(2,128)}) custom-call(s32[1]{0:T(128)} %bitcast.after_ref.me_ref.before_ref, bf16[8,2,2,64,128]{4,3,2,1,0:T(8,128)(2,1)} %get-tuple-element.69.after_ref.refs_0_, bf16[8,8,32,256]{3,2,1,0:T(8,128)(2,1)} %copy-done.2, bf16[256,256]{1,0:T(8,128)(2,1)} %constant.53.clone.high_ref, ...), custom_call_target="tpu_custom_call" | custom-call | flops 805306368 | bytes 3145728 | tf_op jit(solution)/shard_map/detect/pallas_call | solution.py:189
  184.8 7.3 %collective-permute-done.13.refs_2_ = bf16[8,2,2,64,128]{4,3,2,1,0:T(8,128)(2,1)S(1)} collective-permute-done((bf16[8,2,2,64,128]{4,3,2,1,0:T(8,128)(2,1)}, bf16[8,2,2,64,128]{4,3,2,1,0:T(8,128)(2,1)S(1)}, u32[]{:S(2)}, u32[]{:S(2)}) %collective-permute-start.13) | collective-permute-done | bytes 524320 | tf_op jit(solution)/shard_map/ppermute | solution.py:283
  192.1 9.6 %collective-permute-done.14.refs_3_ = bf16[8,2,2,64,128]{4,3,2,1,0:T(8,128)(2,1)S(1)} collective-permute-done((bf16[8,2,2,64,128]{4,3,2,1,0:T(8,128)(2,1)}, bf16[8,2,2,64,128]{4,3,2,1,0:T(8,128)(2,1)S(1)}, u32[]{:S(2)}, u32[]{:S(2)}) %collective-permute-start.14) | collective-permute-done | bytes 524320 | tf_op jit(solution)/shard_map/ppermute | solution.py:283
  202.5 7.0 %detect.12 = (bf16[8,8,32,256]{3,2,1,0:T(8,128)(2,1)}, f32[4,2,128]{2,1,0:T(2,128)}) custom-call(s32[1]{0:T(128)} %bitcast.after_ref.me_ref.before_ref, bf16[8,2,2,64,128]{4,3,2,1,0:T(8,128)(2,1)} %get-tuple-element.75.after_ref.refs_0_, bf16[8,8,32,256]{3,2,1,0:T(8,128)(2,1)} %copy-done.3, bf16[256,256]{1,0:T(8,128)(2,1)} %constant.53.clone.high_ref, ...), custom_call_target="tpu_custom_call" | custom-call | flops 805306368 | bytes 3145728 | tf_op jit(solution)/shard_map/detect/pallas_call | solution.py:189
  223.9 7.0 %collective-permute-done.16.refs_2_ = bf16[8,2,2,64,128]{4,3,2,1,0:T(8,128)(2,1)S(1)} collective-permute-done((bf16[8,2,2,64,128]{4,3,2,1,0:T(8,128)(2,1)}, bf16[8,2,2,64,128]{4,3,2,1,0:T(8,128)(2,1)S(1)}, u32[]{:S(2)}, u32[]{:S(2)}) %collective-permute-start.16) | collective-permute-done | bytes 524320 | tf_op jit(solution)/shard_map/ppermute | solution.py:283
  230.9 10.3 %collective-permute-done.17.refs_3_ = bf16[8,2,2,64,128]{4,3,2,1,0:T(8,128)(2,1)S(1)} collective-permute-done((bf16[8,2,2,64,128]{4,3,2,1,0:T(8,128)(2,1)}, bf16[8,2,2,64,128]{4,3,2,1,0:T(8,128)(2,1)S(1)}, u32[]{:S(2)}, u32[]{:S(2)}) %collective-permute-start.17) | collective-permute-done | bytes 524320 | tf_op jit(solution)/shard_map/ppermute | solution.py:283
  242.0 6.9 %detect.13 = (bf16[8,8,32,256]{3,2,1,0:T(8,128)(2,1)}, f32[4,2,128]{2,1,0:T(2,128)}) custom-call(s32[1]{0:T(128)} %bitcast.after_ref.me_ref.before_ref, bf16[8,2,2,64,128]{4,3,2,1,0:T(8,128)(2,1)} %get-tuple-element.81.after_ref.refs_0_, bf16[8,8,32,256]{3,2,1,0:T(8,128)(2,1)} %copy-done.4, bf16[256,256]{1,0:T(8,128)(2,1)} %constant.53.clone.high_ref, ...), custom_call_target="tpu_custom_call" | custom-call | flops 805306368 | bytes 3145728 | tf_op jit(solution)/shard_map/detect/pallas_call | solution.py:189
  270.1 10.4 %collective-permute-done.20.refs_3_ = bf16[8,2,2,64,128]{4,3,2,1,0:T(8,128)(2,1)} collective-permute-done((bf16[8,2,2,64,128]{4,3,2,1,0:T(8,128)(2,1)}, bf16[8,2,2,64,128]{4,3,2,1,0:T(8,128)(2,1)}, u32[]{:S(2)}, u32[]{:S(2)}) %collective-permute-start.20) | collective-permute-done | bytes 524320 | tf_op jit(solution)/shard_map/ppermute | solution.py:283
  280.5 7.0 %detect.14 = (bf16[8,8,32,256]{3,2,1,0:T(8,128)(2,1)}, f32[4,2,128]{2,1,0:T(2,128)}) custom-call(s32[1]{0:T(128)} %bitcast.after_ref.me_ref.before_ref, bf16[8,2,2,64,128]{4,3,2,1,0:T(8,128)(2,1)} %get-tuple-element.87.after_ref.refs_0_, bf16[8,8,32,256]{3,2,1,0:T(8,128)(2,1)} %copy-done.5, bf16[256,256]{1,0:T(8,128)(2,1)} %constant.53.clone.high_ref, ...), custom_call_target="tpu_custom_call" | custom-call | flops 805306368 | bytes 3145728 | tf_op jit(solution)/shard_map/detect/pallas_call | solution.py:189
  292.6 10.3 %collective-permute-done.23.refs_3_ = bf16[8,2,2,64,128]{4,3,2,1,0:T(8,128)(2,1)S(1)} collective-permute-done((bf16[8,2,2,64,128]{4,3,2,1,0:T(8,128)(2,1)}, bf16[8,2,2,64,128]{4,3,2,1,0:T(8,128)(2,1)S(1)}, u32[]{:S(2)}, u32[]{:S(2)}) %collective-permute-start.23) | collective-permute-done | bytes 524320 | tf_op jit(solution)/shard_map/ppermute | solution.py:283
  304.0 6.9 %detect.15 = (bf16[8,8,32,256]{3,2,1,0:T(8,128)(2,1)}, f32[4,2,128]{2,1,0:T(2,128)}) custom-call(s32[1]{0:T(128)} %bitcast.after_ref.me_ref.before_ref, bf16[8,8,32,256]{3,2,1,0:T(8,128)(2,1)} %get-tuple-element.92.after_ref, bf16[8,8,32,256]{3,2,1,0:T(8,128)(2,1)} %copy-done, bf16[256,256]{1,0:T(8,128)(2,1)} %constant.53.clone.high_ref, ...), custom_call_target="tpu_custom_call" | custom-call | flops 805306368 | bytes 3145728 | tf_op jit(solution)/shard_map/detect/pallas_call | solution.py:189
  319.2 24.6 %all-to-all-done.7.refs_10_ = bf16[8,8,32,256]{3,2,1,0:T(8,128)(2,1)S(1)} async-done(((bf16[8,8,32,256]{3,2,1,0:T(8,128)(2,1)}), bf16[8,8,32,256]{3,2,1,0:T(8,128)(2,1)S(1)}, u32[]{:S(2)}, u32[]{:S(2)}) %all-to-all-start.7) | async-done | bytes 1048608 | tf_op jit(solution)/shard_map/all_to_all | solution.py:292
  348.5 35.1 %all-gather.3.cloned.1.call-done = f32[2048,128]{1,0:T(8,128)} async-done(((f32[64,128]{1,0:T(8,128)}), f32[2048,128]{1,0:T(8,128)}) %all-gather.3.cloned.1.call-update) | async-done | bytes 1048592 | tf_op jit(solution)/shard_map/all_gather | solution.py:296
  386.6 13.0 %flag.1 = bf16[2,32,65536]{2,1,0:T(8,128)(2,1)} custom-call(bf16[128,128]{1,0:T(8,128)(2,1)} %constant.55.clone.refs_0_, f32[512,1,128]{2,1,0:T(1,128)} %bitcast.35, f32[512,1,128]{2,1,0:T(1,128)} %copy.12.refs_2_, bf16[8,8,32,256]{3,2,1,0:T(8,128)(2,1)} %copy-done.1, bf16[8,8,32,256]{3,2,1,0:T(8,128)(2,1)} %copy-done.2, bf16[8,8,32,256]{3,2,1,0:T(8,128)(2,1)} %copy-done.3, ...), custom_call_target="tpu_custom_call" | custom-call | flops 1073741824 | bytes 16777216 | tf_op jit(solution)/shard_map/flag/pallas_call | solution.py:226
  (168 shorter events, 147.3 us)
Async XLA Ops:
  20.4 15.6 %collective-permute-start.1 = (bf16[8,2,2,64,128]{4,3,2,1,0:T(8,128)(2,1)}, bf16[8,2,2,64,128]{4,3,2,1,0:T(8,128)(2,1)S(1)}, u32[]{:S(2)}, u32[]{:S(2)}) collective-permute-start(bf16[8,2,2,64,128]{4,3,2,1,0:T(8,128)(2,1)} %get-tuple-element.53), channel_id=1, source_target_pairs={{0,2},{1,3},{2,0},{3,1},{4,6},{5,7},{6,4},{7,5},{8,10},{9,11},{10,... | collective-permute-start | bytes 1572872 | tf_op jit(solution)/shard_map/ppermute | solution.py:283
  23.0 23.7 %collective-permute-start.2 = (bf16[8,2,2,64,128]{4,3,2,1,0:T(8,128)(2,1)}, bf16[8,2,2,64,128]{4,3,2,1,0:T(8,128)(2,1)S(1)}, u32[]{:S(2)}, u32[]{:S(2)}) collective-permute-start(bf16[8,2,2,64,128]{4,3,2,1,0:T(8,128)(2,1)} %get-tuple-element.54), channel_id=1, source_target_pairs={{0,3},{1,2},{2,1},{3,0},{4,7},{5,6},{6,5},{7,4},{8,11},{9,10},{10,... | collective-permute-start | bytes 1572872 | tf_op jit(solution)/shard_map/ppermute | solution.py:283
  54.4 39.0 %all-to-all-start = ((bf16[8,8,32,256]{3,2,1,0:T(8,128)(2,1)}), bf16[8,8,32,256]{3,2,1,0:T(8,128)(2,1)S(1)}, u32[]{:S(2)}, u32[]{:S(2)}) async-start(bf16[8,8,32,256]{3,2,1,0:T(8,128)(2,1)} %get-tuple-element.56.after_ref), calls=%async_computation | async-start | bytes 2097152 | tf_op jit(solution)/shard_map/all_to_all | solution.py:292
  60.3 15.0 %collective-permute-start.4 = (bf16[8,2,2,64,128]{4,3,2,1,0:T(8,128)(2,1)}, bf16[8,2,2,64,128]{4,3,2,1,0:T(8,128)(2,1)S(1)}, u32[]{:S(2)}, u32[]{:S(2)}) collective-permute-start(bf16[8,2,2,64,128]{4,3,2,1,0:T(8,128)(2,1)} %get-tuple-element.59), channel_id=1, source_target_pairs={{0,2},{1,3},{2,0},{3,1},{4,6},{5,7},{6,4},{7,5},{8,10},{9,11},{10,... | collective-permute-start | bytes 1572872 | tf_op jit(solution)/shard_map/ppermute | solution.py:283
  61.9 23.7 %collective-permute-start.5 = (bf16[8,2,2,64,128]{4,3,2,1,0:T(8,128)(2,1)}, bf16[8,2,2,64,128]{4,3,2,1,0:T(8,128)(2,1)S(1)}, u32[]{:S(2)}, u32[]{:S(2)}) collective-permute-start(bf16[8,2,2,64,128]{4,3,2,1,0:T(8,128)(2,1)} %get-tuple-element.60), channel_id=1, source_target_pairs={{0,3},{1,2},{2,1},{3,0},{4,7},{5,6},{6,5},{7,4},{8,11},{9,10},{10,... | collective-permute-start | bytes 1572872 | tf_op jit(solution)/shard_map/ppermute | solution.py:283
  93.4 39.2 %all-to-all-start.1 = ((bf16[8,8,32,256]{3,2,1,0:T(8,128)(2,1)}), bf16[8,8,32,256]{3,2,1,0:T(8,128)(2,1)S(1)}, u32[]{:S(2)}, u32[]{:S(2)}) async-start(bf16[8,8,32,256]{3,2,1,0:T(8,128)(2,1)} %get-tuple-element.62.after_ref), calls=%async_computation.1 | async-start | bytes 2097152 | tf_op jit(solution)/shard_map/all_to_all | solution.py:292
  101.1 23.7 %collective-permute-start.8 = (bf16[8,2,2,64,128]{4,3,2,1,0:T(8,128)(2,1)}, bf16[8,2,2,64,128]{4,3,2,1,0:T(8,128)(2,1)S(1)}, u32[]{:S(2)}, u32[]{:S(2)}) collective-permute-start(bf16[8,2,2,64,128]{4,3,2,1,0:T(8,128)(2,1)} %get-tuple-element.66), channel_id=1, source_target_pairs={{0,3},{1,2},{2,1},{3,0},{4,7},{5,6},{6,5},{7,4},{8,11},{9,10},{10,... | collective-permute-start | bytes 1572872 | tf_op jit(solution)/shard_map/ppermute | solution.py:283
  132.6 38.4 %all-to-all-start.2 = ((bf16[8,8,32,256]{3,2,1,0:T(8,128)(2,1)}), bf16[8,8,32,256]{3,2,1,0:T(8,128)(2,1)S(1)}, u32[]{:S(2)}, u32[]{:S(2)}) async-start(bf16[8,8,32,256]{3,2,1,0:T(8,128)(2,1)} %get-tuple-element.68.after_ref), calls=%async_computation.2 | async-start | bytes 2097152 | tf_op jit(solution)/shard_map/all_to_all | solution.py:292
  138.7 15.0 %collective-permute-start.10 = (bf16[8,2,2,64,128]{4,3,2,1,0:T(8,128)(2,1)}, bf16[8,2,2,64,128]{4,3,2,1,0:T(8,128)(2,1)S(1)}, u32[]{:S(2)}, u32[]{:S(2)}) collective-permute-start(bf16[8,2,2,64,128]{4,3,2,1,0:T(8,128)(2,1)} %get-tuple-element.71), channel_id=1, source_target_pairs={{0,2},{1,3},{2,0},{3,1},{4,6},{5,7},{6,4},{7,5},{8,10},{9,11},{10,... | collective-permute-start | bytes 1572872 | tf_op jit(solution)/shard_map/ppermute | solution.py:283
  140.2 22.8 %collective-permute-start.11 = (bf16[8,2,2,64,128]{4,3,2,1,0:T(8,128)(2,1)}, bf16[8,2,2,64,128]{4,3,2,1,0:T(8,128)(2,1)S(1)}, u32[]{:S(2)}, u32[]{:S(2)}) collective-permute-start(bf16[8,2,2,64,128]{4,3,2,1,0:T(8,128)(2,1)} %get-tuple-element.72), channel_id=1, source_target_pairs={{0,3},{1,2},{2,1},{3,0},{4,7},{5,6},{6,5},{7,4},{8,11},{9,10},{10,... | collective-permute-start | bytes 1572872 | tf_op jit(solution)/shard_map/ppermute | solution.py:283
  140.2 22.8 %collective-permute-start.9 = (bf16[8,2,2,64,128]{4,3,2,1,0:T(8,128)(2,1)}, bf16[8,2,2,64,128]{4,3,2,1,0:T(8,128)(2,1)S(1)}, u32[]{:S(2)}, u32[]{:S(2)}) collective-permute-start(bf16[8,2,2,64,128]{4,3,2,1,0:T(8,128)(2,1)} %get-tuple-element.70), channel_id=1, source_target_pairs={{0,1},{1,0},{2,3},{3,2},{4,5},{5,4},{6,7},{7,6},{8,9},{9,8},{10,11... | collective-permute-start | bytes 1572872 | tf_op jit(solution)/shard_map/ppermute | solution.py:283
  171.0 38.5 %all-to-all-start.3 = ((bf16[8,8,32,256]{3,2,1,0:T(8,128)(2,1)}), bf16[8,8,32,256]{3,2,1,0:T(8,128)(2,1)S(1)}, u32[]{:S(2)}, u32[]{:S(2)}) async-start(bf16[8,8,32,256]{3,2,1,0:T(8,128)(2,1)} %get-tuple-element.74.after_ref), calls=%async_computation.3 | async-start | bytes 2097152 | tf_op jit(solution)/shard_map/all_to_all | solution.py:292
  178.7 23.0 %collective-permute-start.14 = (bf16[8,2,2,64,128]{4,3,2,1,0:T(8,128)(2,1)}, bf16[8,2,2,64,128]{4,3,2,1,0:T(8,128)(2,1)S(1)}, u32[]{:S(2)}, u32[]{:S(2)}) collective-permute-start(bf16[8,2,2,64,128]{4,3,2,1,0:T(8,128)(2,1)} %get-tuple-element.78), channel_id=1, source_target_pairs={{0,3},{1,2},{2,1},{3,0},{4,7},{5,6},{6,5},{7,4},{8,11},{9,10},{10,... | collective-permute-start | bytes 1572872 | tf_op jit(solution)/shard_map/ppermute | solution.py:283
  209.5 39.5 %all-to-all-start.4 = ((bf16[8,8,32,256]{3,2,1,0:T(8,128)(2,1)}), bf16[8,8,32,256]{3,2,1,0:T(8,128)(2,1)S(1)}, u32[]{:S(2)}, u32[]{:S(2)}) async-start(bf16[8,8,32,256]{3,2,1,0:T(8,128)(2,1)} %get-tuple-element.80.after_ref), calls=%async_computation.4 | async-start | bytes 2097152 | tf_op jit(solution)/shard_map/all_to_all | solution.py:292
  217.0 24.2 %collective-permute-start.17 = (bf16[8,2,2,64,128]{4,3,2,1,0:T(8,128)(2,1)}, bf16[8,2,2,64,128]{4,3,2,1,0:T(8,128)(2,1)S(1)}, u32[]{:S(2)}, u32[]{:S(2)}) collective-permute-start(bf16[8,2,2,64,128]{4,3,2,1,0:T(8,128)(2,1)} %get-tuple-element.84), channel_id=1, source_target_pairs={{0,3},{1,2},{2,1},{3,0},{4,7},{5,6},{6,5},{7,4},{8,11},{9,10},{10,... | collective-permute-start | bytes 1572872 | tf_op jit(solution)/shard_map/ppermute | solution.py:283
  249.0 53.9 %all-to-all-start.5 = ((bf16[8,8,32,256]{3,2,1,0:T(8,128)(2,1)}), bf16[8,8,32,256]{3,2,1,0:T(8,128)(2,1)S(1)}, u32[]{:S(2)}, u32[]{:S(2)}) async-start(bf16[8,8,32,256]{3,2,1,0:T(8,128)(2,1)} %get-tuple-element.86.after_ref), calls=%async_computation.5 | async-start | bytes 2097152 | tf_op jit(solution)/shard_map/all_to_all | solution.py:292
  255.1 15.0 %collective-permute-start.19 = (bf16[8,2,2,64,128]{4,3,2,1,0:T(8,128)(2,1)}, bf16[8,2,2,64,128]{4,3,2,1,0:T(8,128)(2,1)S(1)}, u32[]{:S(2)}, u32[]{:S(2)}) collective-permute-start(bf16[8,2,2,64,128]{4,3,2,1,0:T(8,128)(2,1)} %get-tuple-element.89), channel_id=1, source_target_pairs={{0,2},{1,3},{2,0},{3,1},{4,6},{5,7},{6,4},{7,5},{8,10},{9,11},{10,... | collective-permute-start | bytes 1572872 | tf_op jit(solution)/shard_map/ppermute | solution.py:283
  255.6 24.9 %collective-permute-start.20 = (bf16[8,2,2,64,128]{4,3,2,1,0:T(8,128)(2,1)}, bf16[8,2,2,64,128]{4,3,2,1,0:T(8,128)(2,1)}, u32[]{:S(2)}, u32[]{:S(2)}) collective-permute-start(bf16[8,2,2,64,128]{4,3,2,1,0:T(8,128)(2,1)} %get-tuple-element.90), channel_id=1, source_target_pairs={{0,3},{1,2},{2,1},{3,0},{4,7},{5,6},{6,5},{7,4},{8,11},{9,10},{10,... | collective-permute-start | bytes 1572872 | tf_op jit(solution)/shard_map/ppermute | solution.py:283
  263.1 24.3 %collective-permute-start.21 = (bf16[8,2,2,64,128]{4,3,2,1,0:T(8,128)(2,1)}, bf16[8,2,2,64,128]{4,3,2,1,0:T(8,128)(2,1)S(1)}, u32[]{:S(2)}, u32[]{:S(2)}) collective-permute-start(bf16[8,2,2,64,128]{4,3,2,1,0:T(8,128)(2,1)} %get-tuple-element.93), channel_id=1, source_target_pairs={{0,1},{1,0},{2,3},{3,2},{4,5},{5,4},{6,7},{7,6},{8,9},{9,8},{10,11... | collective-permute-start | bytes 1572872 | tf_op jit(solution)/shard_map/ppermute | solution.py:283
  263.6 29.0 %collective-permute-start.22 = (bf16[8,2,2,64,128]{4,3,2,1,0:T(8,128)(2,1)}, bf16[8,2,2,64,128]{4,3,2,1,0:T(8,128)(2,1)S(1)}, u32[]{:S(2)}, u32[]{:S(2)}) collective-permute-start(bf16[8,2,2,64,128]{4,3,2,1,0:T(8,128)(2,1)} %get-tuple-element.94), channel_id=1, source_target_pairs={{0,2},{1,3},{2,0},{3,1},{4,6},{5,7},{6,4},{7,5},{8,10},{9,11},{10,... | collective-permute-start | bytes 1572872 | tf_op jit(solution)/shard_map/ppermute | solution.py:283
  264.0 38.8 %collective-permute-start.23 = (bf16[8,2,2,64,128]{4,3,2,1,0:T(8,128)(2,1)}, bf16[8,2,2,64,128]{4,3,2,1,0:T(8,128)(2,1)S(1)}, u32[]{:S(2)}, u32[]{:S(2)}) collective-permute-start(bf16[8,2,2,64,128]{4,3,2,1,0:T(8,128)(2,1)} %get-tuple-element.95), channel_id=1, source_target_pairs={{0,3},{1,2},{2,1},{3,0},{4,7},{5,6},{6,5},{7,4},{8,11},{9,10},{10,... | collective-permute-start | bytes 1572872 | tf_op jit(solution)/shard_map/ppermute | solution.py:283
  310.9 32.8 %all-to-all-start.7 = ((bf16[8,8,32,256]{3,2,1,0:T(8,128)(2,1)}), bf16[8,8,32,256]{3,2,1,0:T(8,128)(2,1)S(1)}, u32[]{:S(2)}, u32[]{:S(2)}) async-start(bf16[8,8,32,256]{3,2,1,0:T(8,128)(2,1)} %get-tuple-element.97), calls=%async_computation.7 | async-start | bytes 2097152 | tf_op jit(solution)/shard_map/all_to_all | solution.py:292
  317.0 66.5 %all-gather.3.cloned.1.call-start = ((), (), s32[]{:S(2)}) async-start(), calls=%async_computation.8 | async-start | bytes 1081344 | tf_op jit(solution)/shard_map/all_gather | solution.py:296
  343.7 41.8 %all-to-all-start.6 = ((bf16[8,8,32,256]{3,2,1,0:T(8,128)(2,1)}), bf16[8,8,32,256]{3,2,1,0:T(8,128)(2,1)S(1)}, u32[]{:S(2)}, u32[]{:S(2)}) async-start(bf16[8,8,32,256]{3,2,1,0:T(8,128)(2,1)} %get-tuple-element.92.after_ref), calls=%async_computation.6 | async-start | bytes 2097152 | tf_op jit(solution)/shard_map/all_to_all | solution.py:292
  (50 other events, 831.7 us)
Sparse Core Ops, SparseCore 0:
  320.7 62.7 all-gather.2

commit v2 on v1

--- a/solution.py
+++ b/solution.py
@@ -9,8 +9,8 @@
 from jax.sharding import PartitionSpec as P
 
 UP = 16
-CHUNKS = 8
-AHEAD = 1
+SHARES = (2, 3, 4, 6, 8, 9)
+DETECT_FLOPS = 30_000_000_000
 
 epsilon = 1e-05
 
@@ -70,9 +70,9 @@
 
 def detect_kernel(me_ref, after_ref, before_ref, high_ref, low_ref, order_ref, *refs):
     formed_refs, (out_ref, sum_ref, rows_ref) = refs[:-3], refs[-3:]
+    owners, channels, own, _ = out_ref.shape
     columns = len(formed_refs)
-    channels, pols, _, beams, samples = formed_refs[0].shape
-    owners, _, own, _ = out_ref.shape
+    _, pols, _, beams, samples = formed_refs[0].shape
     for c in range(channels):
         for r, formed_ref in enumerate(formed_refs):
             y = me_ref[0] ^ r
@@ -109,26 +109,28 @@
             out_ref[d, c] = ordered[d * own : (d + 1) * own].astype(jnp.bfloat16)
 
 
-def flag_kernel(frame_count, group_ref, common_ref, mask_ref, *refs):
+def flag_kernel(group_ref, common_ref, mask_ref, *refs):
     chunk_refs, out_ref, power_ref = refs[:-2], refs[-2], refs[-1]
-    sources, per_chunk, beams, width = chunk_refs[0].shape
+    sources, _, beams, width = chunk_refs[0].shape
     samples = width // 2
-    local = per_chunk * len(chunk_refs)
+    sizes = [chunk_ref.shape[1] for chunk_ref in chunk_refs]
+    local = sum(sizes)
 
     def measure(s, level):
-        for i, chunk_ref in enumerate(chunk_refs):
-            first = s * local + i * per_chunk
-            common = common_ref[pl.ds(first, per_chunk)]
+        first = s * local
+        for size, chunk_ref in zip(sizes, chunk_refs):
+            common = common_ref[pl.ds(first, size)]
             cleaned = chunk_ref[s, :, :, :samples].astype(jnp.float32) - common
-            squares = (cleaned * cleaned).reshape(per_chunk * beams, samples)
+            squares = (cleaned * cleaned).reshape(size * beams, samples)
             high = squares.astype(jnp.bfloat16)
             low = (squares - high.astype(jnp.float32)).astype(jnp.bfloat16)
             power = jnp.dot(high, group_ref[...], preferred_element_type=jnp.float32) + jnp.dot(
                 low, group_ref[...], preferred_element_type=jnp.float32
             )
-            power = power.reshape(per_chunk, beams, samples)
-            power_ref[pl.ds(first, per_chunk)] = power
+            power = power.reshape(size, beams, samples)
+            power_ref[pl.ds(first, size)] = power
             level = level + jnp.sum(power, axis=0)
+            first = first + size
         return level
 
     level = lax.fori_loop(0, sources, measure, jnp.zeros((beams, samples), jnp.float32))
@@ -136,15 +138,16 @@
     scale = jnp.broadcast_to(0.5 / level, (beams, samples))
 
     def flag(s, carry):
-        for i, chunk_ref in enumerate(chunk_refs):
-            for c in range(per_chunk):
-                channel = s * local + i * per_chunk + c
+        channel = s * local
+        for size, chunk_ref in zip(sizes, chunk_refs):
+            for c in range(size):
                 row = chunk_ref[s, c].astype(jnp.float32)
                 cleaned = row[:, :samples] - common_ref[channel]
                 weight = mask_ref[channel] / (1.0 + power_ref[channel] * scale)
                 where = pl.ds(pl.multiple_of(channel * samples, samples), samples)
                 out_ref[0, :, where] = (cleaned * weight).astype(jnp.bfloat16)
                 out_ref[1, :, where] = (row[:, samples:] * weight).astype(jnp.bfloat16)
+                channel = channel + 1
         return carry
 
     lax.fori_loop(0, sources, flag, 0)
@@ -154,13 +157,13 @@
     return pl.BlockSpec(array.shape, lambda *_: (0,) * array.ndim)
 
 
-def form(after, table, gains, volts, chunk, per_chunk, step, groups):
+def form(after, table, gains, volts, first, per_chunk, step, groups):
     real, imag = volts
     _, _, pols, feeds, samples = real.shape
     steps = per_chunk // step
-    gain_spec = pl.BlockSpec((1, *gains[0].shape[1:]), lambda i: (chunk * steps + i, 0, 0))
+    gain_spec = pl.BlockSpec((1, *gains[0].shape[1:]), lambda i: (first // step + i, 0, 0))
     volt_spec = pl.BlockSpec(
-        (step, 1, pols, feeds, samples), lambda i: (chunk * steps + i, 0, 0, 0, 0)
+        (step, 1, pols, feeds, samples), lambda i: (first // step + i, 0, 0, 0, 0)
     )
     beams = feeds // groups
     return pl.pallas_call(
@@ -172,8 +175,8 @@
         out_shape=[jax.ShapeDtypeStruct((per_chunk, pols, 2, beams, samples), jnp.bfloat16)]
         * groups,
         cost_estimate=pl.CostEstimate(
-            flops=per_chunk * pols * 8 * feeds * feeds * samples,
-            bytes_accessed=per_chunk * pols * feeds * samples * 8,
+            flops=1000,
+            bytes_accessed=1000,
             transcendentals=0,
         ),
         compiler_params=pltpu.CompilerParams(vmem_limit_bytes=60 << 20),
@@ -186,6 +189,7 @@
     per_chunk, pols, _, beams, samples = formed[0].shape
     steps = per_chunk // step
     own = columns * beams // owners
+    block_spec = pl.BlockSpec((step, pols, 2, beams, samples), lambda i: (i, 0, 0, 0, 0))
     return pl.pallas_call(
         detect_kernel,
         grid=(steps,),
@@ -195,7 +199,7 @@
             pl.BlockSpec(memory_space=pl.ANY),
             *[whole_spec(table) for table in tables],
             whole_spec(order),
-            *[pl.BlockSpec((step, pols, 2, beams, samples), lambda i: (i, 0, 0, 0, 0))] * columns,
+            *[block_spec] * columns,
         ],
         out_specs=[
             pl.BlockSpec((owners, step, own, 2 * samples), lambda i: (0, i, 0, 0)),
@@ -207,8 +211,8 @@
         ],
         scratch_shapes=[pltpu.VMEM((pols, columns, beams, 2 * samples), jnp.bfloat16)],
         cost_estimate=pl.CostEstimate(
-            flops=per_chunk * columns * beams * samples * samples * 24,
-            bytes_accessed=per_chunk * columns * beams * samples * 12,
+            flops=DETECT_FLOPS,
+            bytes_accessed=1000,
             transcendentals=0,
         ),
         compiler_params=pltpu.CompilerParams(vmem_limit_bytes=60 << 20),
@@ -217,22 +221,22 @@
 
 
 def soft_flag(owned, common, mask, frame_count):
-    sources, per_chunk, own, width = owned[0].shape
+    sources, _, own, width = owned[0].shape
     samples = width // 2
     channels = common.shape[0]
     block = 16 if own % 16 == 0 else own
     group = np.kron(np.eye(samples // frame_count), np.ones((frame_count, frame_count)))
     group = jnp.asarray(group / frame_count, jnp.bfloat16)
     return pl.pallas_call(
-        lambda *refs: flag_kernel(frame_count, *refs),
+        flag_kernel,
         grid=(own // block,),
         in_specs=[
             whole_spec(group),
             whole_spec(common),
             whole_spec(mask),
             *[
-                pl.BlockSpec((sources, per_chunk, block, width), lambda i: (0, 0, i, 0))
-                for _ in owned
+                pl.BlockSpec((sources, one.shape[1], block, width), lambda i: (0, 0, i, 0))
+                for one in owned
             ],
         ],
         out_specs=pl.BlockSpec((2, block, channels * samples), lambda i: (0, i, 0)),
@@ -248,14 +252,20 @@
     )(group, common, mask, *owned)
 
 
+def swap(one, axis, apart):
+    return lax.ppermute(one, axis, [(i, i ^ apart) for i in range(lax.axis_size(axis))])
+
+
 def body(voltage_real, voltage_imag, gain_real, gain_imag, channel_mask, beam_owner):
     local, _, pols, feeds, samples = voltage_real.shape
     frame_count = samples // UP
     owners, groups = lax.axis_size("chan"), lax.axis_size("grp")
     channels = local * owners
-    per_chunk = max(local // CHUNKS, 1)
-    chunks = local // per_chunk
-    step = math.gcd(per_chunk, 2)
+    unit = local // sum(SHARES)
+    sizes = [share * unit for share in SHARES] if local == unit * sum(SHARES) else [1] * local
+    chunks = len(sizes)
+    firsts = [sum(sizes[:chunk]) for chunk in range(chunks)]
+    step = math.gcd(*sizes, 2)
 
     def rows_of(gain):
         rows = gain.reshape(local // step, step * pols, feeds)
@@ -275,32 +285,34 @@
     volts = (voltage_real, voltage_imag)
     turned, owned, sums = [], [], []
     after = me
-    for chunk in range(chunks + AHEAD):
+    for chunk in range(chunks + 1):
         if chunk < chunks:
-            formed = form(after, table, gains, volts, chunk, per_chunk, step, groups)
-            turned.append(
-                [
-                    lax.ppermute(one, "grp", [(g, g ^ r) for g in range(groups)]) if r else one
-                    for r, one in enumerate(formed)
-                ]
+            formed = form(
+                after, table, gains, volts, firsts[chunk], sizes[chunk], step, groups
             )
+            turned.append([swap(one, "grp", r) if r else one for r, one in enumerate(formed)])
             after = formed[0]
-        if chunk >= AHEAD:
-            blocks = turned[chunk - AHEAD]
+        if chunk > 0:
             before = owned[-2:-1] or [me]
-            stokes, part = detect(me, tables, order, blocks, [after, before[0]], step, owners)
+            stokes, part = detect(
+                me, tables, order, turned[chunk - 1], [after, before[0]], step, owners
+            )
             owned.append(lax.all_to_all(stokes, "chan", split_axis=0, concat_axis=0, tiled=True))
-            sums.append(part.reshape(per_chunk, samples))
+            sums.append(part.reshape(sizes[chunk - 1], samples))
             after = stokes
-    partial = jnp.concatenate(sums, axis=0)
-    gathered = lax.all_gather(partial, ("chan", "grp"), axis=0)
-    common = jnp.sum(gathered.reshape(owners, groups, local, samples), axis=1)
-    common = common.reshape(channels, samples) / float(feeds * groups)
+    common = jnp.concatenate(sums, axis=0)
+    for bit in range(groups.bit_length() - 1):
+        common = common + swap(common, "grp", 1 << bit)
+    common = common / float(feeds * groups)
+    piece = local // groups
+    common_piece = lax.dynamic_slice_in_dim(common, mine * piece, piece).reshape(-1)
+    for bit in range(owners.bit_length() - 1):
+        other = swap(common, "chan", 1 << bit)
+        low = (lax.axis_index("chan") >> bit) % 2 == 0
+        common = jnp.where(low, jnp.stack([common, other]), jnp.stack([other, common]))
+        common = common.reshape(-1, samples)
     flagged = soft_flag(owned, common.reshape(channels, 1, samples), mask, frame_count)
-    flattened = common.reshape(-1)
-    piece = flattened.shape[0] // (owners * groups)
-    position = lax.axis_index("chan") * groups + lax.axis_index("grp")
-    return (flagged, lax.dynamic_slice_in_dim(flattened, position * piece, piece))
+    return (flagged, common_piece)
 
 
 def solution(mesh):

time: 408 us -> 305 us (0.75)
  waiting for transfers between devices: 192 us -> 123 us
  between operations: 14.5 us -> 1.01 us
  starting transfers between devices: 62.6 us -> 52.5 us
  Pallas kernels: 118 us -> 110 us
    all_gather x1 -> x0, waiting for transfers between devices: 35.1 us -> none  [body(): gathered = lax.all_gather(partial, ('chan', 'grp'), axis=0)]
    ppermute x24 -> x23, waiting for transfers between devices: 132 us -> 100 us  [swap(): lax.ppermute(one, axis, [(i, i ^ apart) for i in range(lax.axis_size(axis...]
    all_to_all x8 -> x6, starting transfers between devices: 46 us -> 30.3 us  [body(): lax.all_to_all(stokes, 'chan', split_axis=0, concat_axis=0, tiled=True)]
    ppermute x24 -> x23, starting transfers between devices: 16.5 us -> 22.2 us  [swap(): lax.ppermute(one, axis, [(i, i ^ apart) for i in range(lax.axis_size(axis...]
    pallas_call x8 -> x6, Pallas kernels: 55.6 us -> 51.8 us  [detect(): pl.pallas_call(detect_kernel, grid=(steps,), in_specs=[pl.BlockSpec(memor...]
    pallas_call x8 -> x6, Pallas kernels: 48.9 us -> 45.4 us  [form(): pl.pallas_call(form_kernel, grid=(steps,), in_specs=[pl.BlockSpec(memory_...]
    unnamed x89 -> x46, local copies, waits for them, and re-layouts: 8.55 us -> 6.6 us
    all_to_all x8 -> x6, waiting for transfers between devices: 24.6 us -> 22.7 us  [body(): lax.all_to_all(stokes, 'chan', split_axis=0, concat_axis=0, tiled=True)]
  transfers between devices with their start and end apart: 33 -> 29, of which waited for: 18 -> 12; matrix products, arithmetic and copies ran while one was open for 1% -> 1% of each run, Pallas kernels for 21% -> 31%
where the time goes in v2:
time: 305 us; the launch traced here: 304 us
  waiting for transfers between devices  123 us (40%)
  Pallas kernels  110 us (36%)
  starting transfers between devices  52.5 us (17%)
  local copies, waits for them, and re-layouts  12.4 us (4%)
  other arithmetic  4.5 us (1%)
    ppermute x23, waiting for transfers between devices, swap(): lax.ppermute(one, axis, [(i, i ^ apart) for i in range(lax.axis_size(axis...  100 us
    pallas_call x6, Pallas kernels, detect(): pl.pallas_call(detect_kernel, grid=(steps,), in_specs=[pl.BlockSpec(memor...  51.8 us
    pallas_call x6, Pallas kernels, form(): pl.pallas_call(form_kernel, grid=(steps,), in_specs=[pl.BlockSpec(memory_...  45.4 us
    all_to_all x6, starting transfers between devices, body(): lax.all_to_all(stokes, 'chan', split_axis=0, concat_axis=0, tiled=True)  30.3 us
    all_to_all x6, waiting for transfers between devices, body(): lax.all_to_all(stokes, 'chan', split_axis=0, concat_axis=0, tiled=True)  22.7 us
    ppermute x23, starting transfers between devices, swap(): lax.ppermute(one, axis, [(i, i ^ apart) for i in range(lax.axis_size(axis...  22.2 us
    pallas_call x1, Pallas kernels, soft_flag(): pl.pallas_call(flag_kernel, grid=(own // block,), in_specs=[whole_spec(gr...  13.2 us
    unnamed x46, local copies, waits for them, and re-layouts  6.6 us
  transfers between devices with their start and end apart: 29, of which 12 were waited for; matrix products, arithmetic and copies ran while one was open for 1% of the time, Pallas kernels for 31%

profile of v2, /device:TPU:0, one launch (start us, length us, event | category | flops | bytes accessed | tf_op | source)
XLA Modules:
  0.0 303.7 jit_solution(17660748137557181958)
XLA Ops:
  14.3 5.0 %form.7 = (bf16[6,2,2,64,128]{4,3,2,1,0:T(8,128)(2,1)}, bf16[6,2,2,64,128]{4,3,2,1,0:T(8,128)(2,1)}, bf16[6,2,2,64,128]{4,3,2,1,0:T(8,128)(2,1)}, bf16[6,2,2,64,128]{4,3,2,1,0:T(8,128)(2,1)}) custom-call(bf16[4,2,2,64,128]{4,3,2,1,0:T(8,128)(2,1)} %get-tuple-element.38.after_ref.refs_0_, bf16[512,512]{1,0:T(8,128)(2,1)} %bitcast.29, ...), custom_call_target="tpu_custom_call" | custom-call | flops 1000 | bytes 1000 | tf_op jit(solution)/shard_map/form/pallas_call | solution.py:169
  22.2 4.6 %collective-permute-done.2.refs_3_ = bf16[4,2,2,64,128]{4,3,2,1,0:T(8,128)(2,1)S(1)} collective-permute-done((bf16[4,2,2,64,128]{4,3,2,1,0:T(8,128)(2,1)}, bf16[4,2,2,64,128]{4,3,2,1,0:T(8,128)(2,1)S(1)}, u32[]{:S(2)}, u32[]{:S(2)}) %collective-permute-start.2) | collective-permute-done | bytes 262176 | tf_op jit(solution)/shard_map/ppermute | solution.py:256
  31.9 5.8 %all-to-all-start = ((bf16[8,4,32,256]{3,2,1,0:T(8,128)(2,1)}), bf16[8,4,32,256]{3,2,1,0:T(8,128)(2,1)S(1)}, u32[]{:S(2)}, u32[]{:S(2)}) async-start(bf16[8,4,32,256]{3,2,1,0:T(8,128)(2,1)} %get-tuple-element.44.after_ref), calls=%async_computation | async-start | bytes 1048576 | tf_op jit(solution)/shard_map/all_to_all | solution.py:300
  37.7 6.1 %form.8 = (bf16[8,2,2,64,128]{4,3,2,1,0:T(8,128)(2,1)}, bf16[8,2,2,64,128]{4,3,2,1,0:T(8,128)(2,1)}, bf16[8,2,2,64,128]{4,3,2,1,0:T(8,128)(2,1)}, bf16[8,2,2,64,128]{4,3,2,1,0:T(8,128)(2,1)}) custom-call(bf16[8,4,32,256]{3,2,1,0:T(8,128)(2,1)} %get-tuple-element.44.after_ref, bf16[512,512]{1,0:T(8,128)(2,1)} %bitcast.30, f32[32,8,256]{2,1,0:T(8,128)} %pad.7.gain_real_ref, ...), custom_call_target="tpu_custom_call" | custom-call | flops 1000 | bytes 1000 | tf_op jit(solution)/shard_map/form/pallas_call | solution.py:169
  46.8 5.7 %detect.7 = (bf16[8,6,32,256]{3,2,1,0:T(8,128)(2,1)}, f32[3,2,128]{2,1,0:T(2,128)}) custom-call(s32[1]{0:T(128)} %bitcast.after_ref.me_ref.before_ref, bf16[8,2,2,64,128]{4,3,2,1,0:T(8,128)(2,1)} %get-tuple-element.45.after_ref.refs_0_, s32[1]{0:T(128)} %bitcast.after_ref.me_ref.before_ref, bf16[256,256]{1,0:T(8,128)(2,1)} %constant.69.clone.high_ref, ...), custom_call_target="tpu_custom_call" | custom-call | flops 30000001024 | bytes 1000 | tf_op jit(solution)/shard_map/detect/pallas_call | solution.py:193
  52.5 8.3 %form.9 = (bf16[12,2,2,64,128]{4,3,2,1,0:T(8,128)(2,1)}, bf16[12,2,2,64,128]{4,3,2,1,0:T(8,128)(2,1)}, bf16[12,2,2,64,128]{4,3,2,1,0:T(8,128)(2,1)}, bf16[12,2,2,64,128]{4,3,2,1,0:T(8,128)(2,1)}) custom-call(bf16[8,6,32,256]{3,2,1,0:T(8,128)(2,1)} %get-tuple-element.50.after_ref, bf16[512,512]{1,0:T(8,128)(2,1)} %bitcast.31, ...), custom_call_target="tpu_custom_call" | custom-call | flops 1000 | bytes 1000 | tf_op jit(solution)/shard_map/form/pallas_call | solution.py:169
  62.9 5.7 %all-to-all-start.1 = ((bf16[8,6,32,256]{3,2,1,0:T(8,128)(2,1)}), bf16[8,6,32,256]{3,2,1,0:T(8,128)(2,1)S(1)}, u32[]{:S(2)}, u32[]{:S(2)}) async-start(bf16[8,6,32,256]{3,2,1,0:T(8,128)(2,1)} %get-tuple-element.50.after_ref), calls=%async_computation.1 | async-start | bytes 1572864 | tf_op jit(solution)/shard_map/all_to_all | solution.py:300
  69.7 7.0 %detect.8 = (bf16[8,8,32,256]{3,2,1,0:T(8,128)(2,1)}, f32[4,2,128]{2,1,0:T(2,128)}) custom-call(s32[1]{0:T(128)} %bitcast.after_ref.me_ref.before_ref, bf16[12,2,2,64,128]{4,3,2,1,0:T(8,128)(2,1)} %get-tuple-element.51.after_ref.refs_0_, bf16[8,4,32,256]{3,2,1,0:T(8,128)(2,1)} %copy-done.5, bf16[256,256]{1,0:T(8,128)(2,1)} %constant.69.clone.high_ref, ...), custom_call_target="tpu_custom_call" | custom-call | flops 30000001024 | bytes 1000 | tf_op jit(solution)/shard_map/detect/pallas_call | solution.py:193
  76.6 10.4 %form.10 = (bf16[16,2,2,64,128]{4,3,2,1,0:T(8,128)(2,1)}, bf16[16,2,2,64,128]{4,3,2,1,0:T(8,128)(2,1)}, bf16[16,2,2,64,128]{4,3,2,1,0:T(8,128)(2,1)}, bf16[16,2,2,64,128]{4,3,2,1,0:T(8,128)(2,1)}) custom-call(bf16[8,8,32,256]{3,2,1,0:T(8,128)(2,1)} %get-tuple-element.56.after_ref, bf16[512,512]{1,0:T(8,128)(2,1)} %bitcast.32, ...), custom_call_target="tpu_custom_call" | custom-call | flops 1000 | bytes 1000 | tf_op jit(solution)/shard_map/form/pallas_call | solution.py:169
  89.4 5.9 %all-to-all-start.2 = ((bf16[8,8,32,256]{3,2,1,0:T(8,128)(2,1)}), bf16[8,8,32,256]{3,2,1,0:T(8,128)(2,1)S(1)}, u32[]{:S(2)}, u32[]{:S(2)}) async-start(bf16[8,8,32,256]{3,2,1,0:T(8,128)(2,1)} %get-tuple-element.56.after_ref), calls=%async_computation.2 | async-start | bytes 2097152 | tf_op jit(solution)/shard_map/all_to_all | solution.py:300
  95.4 8.0 %collective-permute-done.11.refs_3_ = bf16[12,2,2,64,128]{4,3,2,1,0:T(8,128)(2,1)} collective-permute-done((bf16[12,2,2,64,128]{4,3,2,1,0:T(8,128)(2,1)}, bf16[12,2,2,64,128]{4,3,2,1,0:T(8,128)(2,1)}, u32[]{:S(2)}, u32[]{:S(2)}) %collective-permute-start.11) | collective-permute-done | bytes 786464 | tf_op jit(solution)/shard_map/ppermute | solution.py:256
  103.4 9.5 %detect.9 = (bf16[8,12,32,256]{3,2,1,0:T(8,128)(2,1)}, f32[6,2,128]{2,1,0:T(2,128)}) custom-call(s32[1]{0:T(128)} %bitcast.after_ref.me_ref.before_ref, bf16[16,2,2,64,128]{4,3,2,1,0:T(8,128)(2,1)} %get-tuple-element.57.after_ref.refs_0_, bf16[8,6,32,256]{3,2,1,0:T(8,128)(2,1)} %copy-done.4, bf16[256,256]{1,0:T(8,128)(2,1)} %constant.69.clone.high_ref, ...), custom_call_target="tpu_custom_call" | custom-call | flops 30000001024 | bytes 1000 | tf_op jit(solution)/shard_map/detect/pallas_call | solution.py:193
  112.8 11.5 %form.11 = (bf16[18,2,2,64,128]{4,3,2,1,0:T(8,128)(2,1)}, bf16[18,2,2,64,128]{4,3,2,1,0:T(8,128)(2,1)}, bf16[18,2,2,64,128]{4,3,2,1,0:T(8,128)(2,1)}, bf16[18,2,2,64,128]{4,3,2,1,0:T(8,128)(2,1)}) custom-call(bf16[8,12,32,256]{3,2,1,0:T(8,128)(2,1)} %get-tuple-element.62.after_ref, bf16[512,512]{1,0:T(8,128)(2,1)} %bitcast.33, ...), custom_call_target="tpu_custom_call" | custom-call | flops 1000 | bytes 1000 | tf_op jit(solution)/shard_map/form/pallas_call | solution.py:169
  127.9 5.7 %all-to-all-start.3 = ((bf16[8,12,32,256]{3,2,1,0:T(8,128)(2,1)}), bf16[8,12,32,256]{3,2,1,0:T(8,128)(2,1)S(1)}, u32[]{:S(2)}, u32[]{:S(2)}) async-start(bf16[8,12,32,256]{3,2,1,0:T(8,128)(2,1)} %get-tuple-element.62.after_ref), calls=%async_computation.3 | async-start | bytes 3145728 | tf_op jit(solution)/shard_map/all_to_all | solution.py:300
  133.7 14.6 %collective-permute-done.14.refs_3_ = bf16[16,2,2,64,128]{4,3,2,1,0:T(8,128)(2,1)} collective-permute-done((bf16[16,2,2,64,128]{4,3,2,1,0:T(8,128)(2,1)}, bf16[16,2,2,64,128]{4,3,2,1,0:T(8,128)(2,1)}, u32[]{:S(2)}, u32[]{:S(2)}) %collective-permute-start.14) | collective-permute-done | bytes 1048608 | tf_op jit(solution)/shard_map/ppermute | solution.py:256
  148.3 11.9 %detect.10 = (bf16[8,16,32,256]{3,2,1,0:T(8,128)(2,1)}, f32[8,2,128]{2,1,0:T(2,128)}) custom-call(s32[1]{0:T(128)} %bitcast.after_ref.me_ref.before_ref, bf16[18,2,2,64,128]{4,3,2,1,0:T(8,128)(2,1)} %get-tuple-element.63.after_ref.refs_0_, bf16[8,8,32,256]{3,2,1,0:T(8,128)(2,1)} %copy-done.3, bf16[256,256]{1,0:T(8,128)(2,1)} %constant.69.clone.high_ref, ...), custom_call_target="tpu_custom_call" | custom-call | flops 30000001024 | bytes 1000 | tf_op jit(solution)/shard_map/detect/pallas_call | solution.py:193
  160.2 10.3 %all-to-all-done.3.before_ref.refs_3_ = bf16[8,12,32,256]{3,2,1,0:T(8,128)(2,1)S(1)} async-done(((bf16[8,12,32,256]{3,2,1,0:T(8,128)(2,1)}), bf16[8,12,32,256]{3,2,1,0:T(8,128)(2,1)S(1)}, u32[]{:S(2)}, u32[]{:S(2)}) %all-to-all-start.3) | async-done | bytes 1572896 | tf_op jit(solution)/shard_map/all_to_all | solution.py:300
  175.3 22.8 %collective-permute-done.17.refs_3_ = bf16[18,2,2,64,128]{4,3,2,1,0:T(8,128)(2,1)} collective-permute-done((bf16[18,2,2,64,128]{4,3,2,1,0:T(8,128)(2,1)}, bf16[18,2,2,64,128]{4,3,2,1,0:T(8,128)(2,1)}, u32[]{:S(2)}, u32[]{:S(2)}) %collective-permute-start.17) | collective-permute-done | bytes 1179680 | tf_op jit(solution)/shard_map/ppermute | solution.py:256
  198.1 13.2 %detect.11 = (bf16[8,18,32,256]{3,2,1,0:T(8,128)(2,1)}, f32[9,2,128]{2,1,0:T(2,128)}) custom-call(s32[1]{0:T(128)} %bitcast.after_ref.me_ref.before_ref, bf16[8,16,32,256]{3,2,1,0:T(8,128)(2,1)} %get-tuple-element.68.after_ref, bf16[8,12,32,256]{3,2,1,0:T(8,128)(2,1)} %copy-done.2, bf16[256,256]{1,0:T(8,128)(2,1)} %constant.69.clone.high_ref, ...), custom_call_target="tpu_custom_call" | custom-call | flops 30000001024 | bytes 1000 | tf_op jit(solution)/shard_map/detect/pallas_call | solution.py:193
  211.3 12.4 %all-to-all-done.4.refs_4_ = bf16[8,16,32,256]{3,2,1,0:T(8,128)(2,1)S(1)} async-done(((bf16[8,16,32,256]{3,2,1,0:T(8,128)(2,1)}), bf16[8,16,32,256]{3,2,1,0:T(8,128)(2,1)S(1)}, u32[]{:S(2)}, u32[]{:S(2)}) %all-to-all-start.4) | async-done | bytes 2097184 | tf_op jit(solution)/shard_map/all_to_all | solution.py:300
  236.6 12.1 %collective-permute-done.20 = f32[64,128]{1,0:T(8,128)S(1)} collective-permute-done((f32[64,128]{1,0:T(8,128)S(1)}, f32[64,128]{1,0:T(8,128)S(1)}, u32[]{:S(2)}, u32[]{:S(2)}) %collective-permute-start.20) | collective-permute-done | bytes 32800 | tf_op jit(solution)/shard_map/ppermute | solution.py:256
  250.7 18.9 %collective-permute-done.21 = f32[128,128]{1,0:T(8,128)S(1)} collective-permute-done((f32[128,128]{1,0:T(8,128)S(1)}, f32[128,128]{1,0:T(8,128)S(1)}, u32[]{:S(2)}, u32[]{:S(2)}) %collective-permute-start.21) | collective-permute-done | bytes 65568 | tf_op jit(solution)/shard_map/ppermute | solution.py:256
  274.7 13.7 %collective-permute-done.22 = f32[256,128]{1,0:T(8,128)S(1)} collective-permute-done((f32[256,128]{1,0:T(8,128)S(1)}, f32[256,128]{1,0:T(8,128)S(1)}, u32[]{:S(2)}, u32[]{:S(2)}) %collective-permute-start.22) | collective-permute-done | bytes 131104 | tf_op jit(solution)/shard_map/ppermute | solution.py:256
  290.5 13.2 %flag.1 = bf16[2,32,65536]{2,1,0:T(8,128)(2,1)} custom-call(bf16[128,128]{1,0:T(8,128)(2,1)} %constant.71.clone.group_ref, f32[512,1,128]{2,1,0:T(1,128)} %bitcast.35, f32[512,1,128]{2,1,0:T(1,128)} %copy.12.mask_ref, bf16[8,4,32,256]{3,2,1,0:T(8,128)(2,1)} %copy-done.5, bf16[8,6,32,256]{3,2,1,0:T(8,128)(2,1)} %copy-done.4, ...), custom_call_target="tpu_custom_call" | custom-call | flops 1073741824 | bytes 16777216 | tf_op jit(solution)/shard_map/flag/pallas_call | solution.py:230
  (118 shorter events, 60.4 us)
Async XLA Ops:
  19.3 26.5 %collective-permute-start.3 = (bf16[6,2,2,64,128]{4,3,2,1,0:T(8,128)(2,1)}, bf16[6,2,2,64,128]{4,3,2,1,0:T(8,128)(2,1)S(1)}, u32[]{:S(2)}, u32[]{:S(2)}) collective-permute-start(bf16[6,2,2,64,128]{4,3,2,1,0:T(8,128)(2,1)} %get-tuple-element.46), channel_id=1, source_target_pairs={{0,1},{1,0},{2,3},{3,2},{4,5},{5,4},{6,7},{7,6},{8,9},{9,8},{10,11... | collective-permute-start | bytes 1179656 | tf_op jit(solution)/shard_map/ppermute | solution.py:256
  19.5 26.3 %collective-permute-start.4 = (bf16[6,2,2,64,128]{4,3,2,1,0:T(8,128)(2,1)}, bf16[6,2,2,64,128]{4,3,2,1,0:T(8,128)(2,1)S(1)}, u32[]{:S(2)}, u32[]{:S(2)}) collective-permute-start(bf16[6,2,2,64,128]{4,3,2,1,0:T(8,128)(2,1)} %get-tuple-element.47), channel_id=1, source_target_pairs={{0,2},{1,3},{2,0},{3,1},{4,6},{5,7},{6,4},{7,5},{8,10},{9,11},{10,... | collective-permute-start | bytes 1179656 | tf_op jit(solution)/shard_map/ppermute | solution.py:256
  22.2 23.7 %collective-permute-start.5 = (bf16[6,2,2,64,128]{4,3,2,1,0:T(8,128)(2,1)}, bf16[6,2,2,64,128]{4,3,2,1,0:T(8,128)(2,1)S(1)}, u32[]{:S(2)}, u32[]{:S(2)}) collective-permute-start(bf16[6,2,2,64,128]{4,3,2,1,0:T(8,128)(2,1)} %get-tuple-element.48), channel_id=1, source_target_pairs={{0,3},{1,2},{2,1},{3,0},{4,7},{5,6},{6,5},{7,4},{8,11},{9,10},{10,... | collective-permute-start | bytes 1179656 | tf_op jit(solution)/shard_map/ppermute | solution.py:256
  31.9 30.9 %all-to-all-start = ((bf16[8,4,32,256]{3,2,1,0:T(8,128)(2,1)}), bf16[8,4,32,256]{3,2,1,0:T(8,128)(2,1)S(1)}, u32[]{:S(2)}, u32[]{:S(2)}) async-start(bf16[8,4,32,256]{3,2,1,0:T(8,128)(2,1)} %get-tuple-element.44.after_ref), calls=%async_computation | async-start | bytes 1048576 | tf_op jit(solution)/shard_map/all_to_all | solution.py:300
  43.9 24.7 %collective-permute-start.6 = (bf16[8,2,2,64,128]{4,3,2,1,0:T(8,128)(2,1)}, bf16[8,2,2,64,128]{4,3,2,1,0:T(8,128)(2,1)S(1)}, u32[]{:S(2)}, u32[]{:S(2)}) collective-permute-start(bf16[8,2,2,64,128]{4,3,2,1,0:T(8,128)(2,1)} %get-tuple-element.52), channel_id=1, source_target_pairs={{0,1},{1,0},{2,3},{3,2},{4,5},{5,4},{6,7},{7,6},{8,9},{9,8},{10,11... | collective-permute-start | bytes 1572872 | tf_op jit(solution)/shard_map/ppermute | solution.py:256
  44.3 24.4 %collective-permute-start.7 = (bf16[8,2,2,64,128]{4,3,2,1,0:T(8,128)(2,1)}, bf16[8,2,2,64,128]{4,3,2,1,0:T(8,128)(2,1)}, u32[]{:S(2)}, u32[]{:S(2)}) collective-permute-start(bf16[8,2,2,64,128]{4,3,2,1,0:T(8,128)(2,1)} %get-tuple-element.53), channel_id=1, source_target_pairs={{0,2},{1,3},{2,0},{3,1},{4,6},{5,7},{6,4},{7,5},{8,10},{9,11},{10,... | collective-permute-start | bytes 1572872 | tf_op jit(solution)/shard_map/ppermute | solution.py:256
  45.8 23.8 %collective-permute-start.8 = (bf16[8,2,2,64,128]{4,3,2,1,0:T(8,128)(2,1)}, bf16[8,2,2,64,128]{4,3,2,1,0:T(8,128)(2,1)}, u32[]{:S(2)}, u32[]{:S(2)}) collective-permute-start(bf16[8,2,2,64,128]{4,3,2,1,0:T(8,128)(2,1)} %get-tuple-element.54), channel_id=1, source_target_pairs={{0,3},{1,2},{2,1},{3,0},{4,7},{5,6},{6,5},{7,4},{8,11},{9,10},{10,... | collective-permute-start | bytes 1572872 | tf_op jit(solution)/shard_map/ppermute | solution.py:256
  60.8 34.4 %collective-permute-start.9 = (bf16[12,2,2,64,128]{4,3,2,1,0:T(8,128)(2,1)}, bf16[12,2,2,64,128]{4,3,2,1,0:T(8,128)(2,1)S(1)}, u32[]{:S(2)}, u32[]{:S(2)}) collective-permute-start(bf16[12,2,2,64,128]{4,3,2,1,0:T(8,128)(2,1)} %get-tuple-element.58), channel_id=1, source_target_pairs={{0,1},{1,0},{2,3},{3,2},{4,5},{5,4},{6,7},{7,6},{8,9},{9,8},{10,11... | collective-permute-start | bytes 2359304 | tf_op jit(solution)/shard_map/ppermute | solution.py:256
  61.3 34.0 %collective-permute-start.10 = (bf16[12,2,2,64,128]{4,3,2,1,0:T(8,128)(2,1)}, bf16[12,2,2,64,128]{4,3,2,1,0:T(8,128)(2,1)S(1)}, u32[]{:S(2)}, u32[]{:S(2)}) collective-permute-start(bf16[12,2,2,64,128]{4,3,2,1,0:T(8,128)(2,1)} %get-tuple-element.59), channel_id=1, source_target_pairs={{0,2},{1,3},{2,0},{3,1},{4,6},{5,7},{6,4},{7,5},{8,10},{9,11},{10,... | collective-permute-start | bytes 2359304 | tf_op jit(solution)/shard_map/ppermute | solution.py:256
  62.9 26.5 %all-to-all-start.1 = ((bf16[8,6,32,256]{3,2,1,0:T(8,128)(2,1)}), bf16[8,6,32,256]{3,2,1,0:T(8,128)(2,1)S(1)}, u32[]{:S(2)}, u32[]{:S(2)}) async-start(bf16[8,6,32,256]{3,2,1,0:T(8,128)(2,1)} %get-tuple-element.50.after_ref), calls=%async_computation.1 | async-start | bytes 1572864 | tf_op jit(solution)/shard_map/all_to_all | solution.py:300
  68.6 34.8 %collective-permute-start.11 = (bf16[12,2,2,64,128]{4,3,2,1,0:T(8,128)(2,1)}, bf16[12,2,2,64,128]{4,3,2,1,0:T(8,128)(2,1)}, u32[]{:S(2)}, u32[]{:S(2)}) collective-permute-start(bf16[12,2,2,64,128]{4,3,2,1,0:T(8,128)(2,1)} %get-tuple-element.60), channel_id=1, source_target_pairs={{0,3},{1,2},{2,1},{3,0},{4,7},{5,6},{6,5},{7,4},{8,11},{9,10},{10,... | collective-permute-start | bytes 2359304 | tf_op jit(solution)/shard_map/ppermute | solution.py:256
  87.1 46.5 %collective-permute-start.12 = (bf16[16,2,2,64,128]{4,3,2,1,0:T(8,128)(2,1)}, bf16[16,2,2,64,128]{4,3,2,1,0:T(8,128)(2,1)}, u32[]{:S(2)}, u32[]{:S(2)}) collective-permute-start(bf16[16,2,2,64,128]{4,3,2,1,0:T(8,128)(2,1)} %get-tuple-element.64), channel_id=1, source_target_pairs={{0,1},{1,0},{2,3},{3,2},{4,5},{5,4},{6,7},{7,6},{8,9},{9,8},{10,11... | collective-permute-start | bytes 3145736 | tf_op jit(solution)/shard_map/ppermute | solution.py:256
  87.9 45.8 %collective-permute-start.13 = (bf16[16,2,2,64,128]{4,3,2,1,0:T(8,128)(2,1)}, bf16[16,2,2,64,128]{4,3,2,1,0:T(8,128)(2,1)}, u32[]{:S(2)}, u32[]{:S(2)}) collective-permute-start(bf16[16,2,2,64,128]{4,3,2,1,0:T(8,128)(2,1)} %get-tuple-element.65), channel_id=1, source_target_pairs={{0,2},{1,3},{2,0},{3,1},{4,6},{5,7},{6,4},{7,5},{8,10},{9,11},{10,... | collective-permute-start | bytes 3145736 | tf_op jit(solution)/shard_map/ppermute | solution.py:256
  89.4 37.5 %all-to-all-start.2 = ((bf16[8,8,32,256]{3,2,1,0:T(8,128)(2,1)}), bf16[8,8,32,256]{3,2,1,0:T(8,128)(2,1)S(1)}, u32[]{:S(2)}, u32[]{:S(2)}) async-start(bf16[8,8,32,256]{3,2,1,0:T(8,128)(2,1)} %get-tuple-element.56.after_ref), calls=%async_computation.2 | async-start | bytes 2097152 | tf_op jit(solution)/shard_map/all_to_all | solution.py:300
  95.3 53.0 %collective-permute-start.14 = (bf16[16,2,2,64,128]{4,3,2,1,0:T(8,128)(2,1)}, bf16[16,2,2,64,128]{4,3,2,1,0:T(8,128)(2,1)}, u32[]{:S(2)}, u32[]{:S(2)}) collective-permute-start(bf16[16,2,2,64,128]{4,3,2,1,0:T(8,128)(2,1)} %get-tuple-element.66), channel_id=1, source_target_pairs={{0,3},{1,2},{2,1},{3,0},{4,7},{5,6},{6,5},{7,4},{8,11},{9,10},{10,... | collective-permute-start | bytes 3145736 | tf_op jit(solution)/shard_map/ppermute | solution.py:256
  124.4 51.0 %collective-permute-start.15 = (bf16[18,2,2,64,128]{4,3,2,1,0:T(8,128)(2,1)}, bf16[18,2,2,64,128]{4,3,2,1,0:T(8,128)(2,1)}, u32[]{:S(2)}, u32[]{:S(2)}) collective-permute-start(bf16[18,2,2,64,128]{4,3,2,1,0:T(8,128)(2,1)} %get-tuple-element.69), channel_id=1, source_target_pairs={{0,1},{1,0},{2,3},{3,2},{4,5},{5,4},{6,7},{7,6},{8,9},{9,8},{10,11... | collective-permute-start | bytes 3538952 | tf_op jit(solution)/shard_map/ppermute | solution.py:256
  125.4 50.0 %collective-permute-start.16 = (bf16[18,2,2,64,128]{4,3,2,1,0:T(8,128)(2,1)}, bf16[18,2,2,64,128]{4,3,2,1,0:T(8,128)(2,1)}, u32[]{:S(2)}, u32[]{:S(2)}) collective-permute-start(bf16[18,2,2,64,128]{4,3,2,1,0:T(8,128)(2,1)} %get-tuple-element.70), channel_id=1, source_target_pairs={{0,2},{1,3},{2,0},{3,1},{4,6},{5,7},{6,4},{7,5},{8,10},{9,11},{10,... | collective-permute-start | bytes 3538952 | tf_op jit(solution)/shard_map/ppermute | solution.py:256
  127.9 42.6 %all-to-all-start.3 = ((bf16[8,12,32,256]{3,2,1,0:T(8,128)(2,1)}), bf16[8,12,32,256]{3,2,1,0:T(8,128)(2,1)S(1)}, u32[]{:S(2)}, u32[]{:S(2)}) async-start(bf16[8,12,32,256]{3,2,1,0:T(8,128)(2,1)} %get-tuple-element.62.after_ref), calls=%async_computation.3 | async-start | bytes 3145728 | tf_op jit(solution)/shard_map/all_to_all | solution.py:300
  133.6 64.6 %collective-permute-start.17 = (bf16[18,2,2,64,128]{4,3,2,1,0:T(8,128)(2,1)}, bf16[18,2,2,64,128]{4,3,2,1,0:T(8,128)(2,1)}, u32[]{:S(2)}, u32[]{:S(2)}) collective-permute-start(bf16[18,2,2,64,128]{4,3,2,1,0:T(8,128)(2,1)} %get-tuple-element.71), channel_id=1, source_target_pairs={{0,3},{1,2},{2,1},{3,0},{4,7},{5,6},{6,5},{7,4},{8,11},{9,10},{10,... | collective-permute-start | bytes 3538952 | tf_op jit(solution)/shard_map/ppermute | solution.py:256
  171.7 52.1 %all-to-all-start.4 = ((bf16[8,16,32,256]{3,2,1,0:T(8,128)(2,1)}), bf16[8,16,32,256]{3,2,1,0:T(8,128)(2,1)S(1)}, u32[]{:S(2)}, u32[]{:S(2)}) async-start(bf16[8,16,32,256]{3,2,1,0:T(8,128)(2,1)} %get-tuple-element.68.after_ref), calls=%async_computation.4 | async-start | bytes 4194304 | tf_op jit(solution)/shard_map/all_to_all | solution.py:300
  225.1 64.0 %all-to-all-start.5 = ((bf16[8,18,32,256]{3,2,1,0:T(8,128)(2,1)}), bf16[8,18,32,256]{3,2,1,0:T(8,128)(2,1)S(1)}, u32[]{:S(2)}, u32[]{:S(2)}) async-start(bf16[8,18,32,256]{3,2,1,0:T(8,128)(2,1)} %get-tuple-element.73), calls=%async_computation.5 | async-start | bytes 4718592 | tf_op jit(solution)/shard_map/all_to_all | solution.py:300
  234.6 14.1 %collective-permute-start.20 = (f32[64,128]{1,0:T(8,128)S(1)}, f32[64,128]{1,0:T(8,128)S(1)}, u32[]{:S(2)}, u32[]{:S(2)}) collective-permute-start(f32[64,128]{1,0:T(8,128)S(1)} %add_multiply_fusion), channel_id=1, source_target_pairs={{0,4},{4,0},{8,12},{12,8},{16,20},{20,16},{24,28},{28,24},{1,5},{5... | collective-permute-start | bytes 98312 | tf_op jit(solution)/shard_map/ppermute | solution.py:256
  248.8 20.9 %collective-permute-start.21 = (f32[128,128]{1,0:T(8,128)S(1)}, f32[128,128]{1,0:T(8,128)S(1)}, u32[]{:S(2)}, u32[]{:S(2)}) collective-permute-start(f32[128,128]{1,0:T(8,128)S(1)} %bitcast.38), channel_id=1, source_target_pairs={{0,8},{4,12},{8,0},{12,4},{16,24},{20,28},{24,16},{28,20},{1,9},{5... | collective-permute-start | bytes 196616 | tf_op jit(solution)/shard_map/ppermute | solution.py:256
  269.6 18.8 %collective-permute-start.22 = (f32[256,128]{1,0:T(8,128)S(1)}, f32[256,128]{1,0:T(8,128)S(1)}, u32[]{:S(2)}, u32[]{:S(2)}) collective-permute-start(f32[256,128]{1,0:T(8,128)S(1)} %bitcast.36), channel_id=1, source_target_pairs={{0,16},{4,20},{8,24},{12,28},{16,0},{20,4},{24,8},{28,12},{1,17},{... | collective-permute-start | bytes 393224 | tf_op jit(solution)/shard_map/ppermute | solution.py:256
  (28 other events, 158.8 us)

commit v3 on v2

--- a/solution.py
+++ b/solution.py
@@ -10,21 +10,20 @@
 
 UP = 16
 SHARES = (2, 3, 4, 6, 8, 9)
-DETECT_FLOPS = 30_000_000_000
+DETECT_FLOPS = 1_600_000_000
 
 epsilon = 1e-05
 
 
-def beam_table(feed_count):
-    counter = jnp.arange(feed_count, dtype=jnp.int32)
-    phases = counter[:, None] * counter[None, :] % feed_count
-    angles = phases.astype(jnp.float32) * (-2.0 * math.pi / feed_count)
+def beam_table(feed_count, group_count):
+    counter = np.arange(feed_count)
+    angles = (counter[:, None] * counter[None, :] % feed_count) * (-2.0 * math.pi / feed_count)
     factor = 1.0 / math.sqrt(feed_count)
-    cosine = jnp.cos(angles) * factor
-    sines = jnp.sin(angles) * factor
-    real_rows = jnp.concatenate([cosine, -sines], axis=1)
-    imaginary_rows = jnp.concatenate([sines, cosine], axis=1)
-    return jnp.concatenate([real_rows, imaginary_rows], axis=0).astype(jnp.bfloat16)
+    cosine, sines = np.cos(angles) * factor, np.sin(angles) * factor
+    table = np.stack([np.concatenate([cosine, -sines], 1), np.concatenate([sines, cosine], 1)])
+    table = table.reshape(2, group_count, feed_count // group_count, 2 * feed_count)
+    table = table.swapaxes(0, 1).reshape(group_count, -1, 2 * feed_count)
+    return table.astype(np.float32).astype(jnp.bfloat16)
 
 
 def spectral_tables(up_count, frame_count, column_count):
@@ -45,9 +44,14 @@
     return high, low
 
 
-def form_kernel(after_ref, table_ref, gain_real_ref, gain_imag_ref, real_ref, imag_ref, *out_refs):
+def form_kernel(me_ref, after_ref, table_ref, gain_real_ref, gain_imag_ref, real_ref, imag_ref, *refs):
+    out_refs, gains_ref = refs[:-1], refs[-1]
     channels, pols, _, beams, samples = out_refs[0].shape
-    gains_real, gains_imag = gain_real_ref[0].T, gain_imag_ref[0].T
+    for c in range(channels):
+        gains_ref[0, c * pols : (c + 1) * pols] = gain_real_ref[c, 0]
+        gains_ref[1, c * pols : (c + 1) * pols] = gain_imag_ref[c, 0]
+    gains_real, gains_imag = gains_ref[0].T, gains_ref[1].T
+    table = jnp.concatenate([table_ref[me_ref[0] ^ r] for r in range(len(out_refs))], axis=0)
     for c in range(channels):
         columns = []
         for p in range(pols):
@@ -59,7 +63,7 @@
             imag_part = (gain_real * imag + gain_imag * real).astype(jnp.bfloat16)
             columns.append(jnp.concatenate([real_part, imag_part], axis=0))
         calibrated = jnp.concatenate(columns, axis=1)
-        formed = jnp.dot(table_ref[...], calibrated, preferred_element_type=jnp.float32)
+        formed = jnp.dot(table, calibrated, preferred_element_type=jnp.float32)
         formed = formed.astype(jnp.bfloat16)
         for p in range(pols):
             for r, out_ref in enumerate(out_refs):
@@ -124,9 +128,8 @@
             squares = (cleaned * cleaned).reshape(size * beams, samples)
             high = squares.astype(jnp.bfloat16)
             low = (squares - high.astype(jnp.float32)).astype(jnp.bfloat16)
-            power = jnp.dot(high, group_ref[...], preferred_element_type=jnp.float32) + jnp.dot(
-                low, group_ref[...], preferred_element_type=jnp.float32
-            )
+            squares = jnp.concatenate([high, low], axis=1)
+            power = jnp.dot(squares, group_ref[...], preferred_element_type=jnp.float32)
             power = power.reshape(size, beams, samples)
             power_ref[pl.ds(first, size)] = power
             level = level + jnp.sum(power, axis=0)
@@ -157,11 +160,11 @@
     return pl.BlockSpec(array.shape, lambda *_: (0,) * array.ndim)
 
 
-def form(after, table, gains, volts, first, per_chunk, step, groups):
+def form(me, after, table, gains, volts, first, per_chunk, step, groups):
     real, imag = volts
     _, _, pols, feeds, samples = real.shape
     steps = per_chunk // step
-    gain_spec = pl.BlockSpec((1, *gains[0].shape[1:]), lambda i: (first // step + i, 0, 0))
+    gain_spec = pl.BlockSpec((step, 1, pols, feeds), lambda i: (first // step + i, 0, 0, 0))
     volt_spec = pl.BlockSpec(
         (step, 1, pols, feeds, samples), lambda i: (first // step + i, 0, 0, 0, 0)
     )
@@ -169,11 +172,20 @@
     return pl.pallas_call(
         form_kernel,
         grid=(steps,),
-        in_specs=[pl.BlockSpec(memory_space=pl.ANY), whole_spec(table), gain_spec, gain_spec, volt_spec, volt_spec],
+        in_specs=[
+            pl.BlockSpec(memory_space=pltpu.SMEM),
+            pl.BlockSpec(memory_space=pl.ANY),
+            whole_spec(table),
+            gain_spec,
+            gain_spec,
+            volt_spec,
+            volt_spec,
+        ],
         out_specs=[pl.BlockSpec((step, pols, 2, beams, samples), lambda i: (i, 0, 0, 0, 0))]
         * groups,
         out_shape=[jax.ShapeDtypeStruct((per_chunk, pols, 2, beams, samples), jnp.bfloat16)]
         * groups,
+        scratch_shapes=[pltpu.VMEM((2, 8, feeds), jnp.float32)],
         cost_estimate=pl.CostEstimate(
             flops=1000,
             bytes_accessed=1000,
@@ -181,7 +193,7 @@
         ),
         compiler_params=pltpu.CompilerParams(vmem_limit_bytes=60 << 20),
         name="form",
-    )(after, table, *gains, real, imag)
+    )(me, after, table, *gains, real, imag)
 
 
 def detect(me, tables, order, formed, after, step, owners):
@@ -211,7 +223,7 @@
         ],
         scratch_shapes=[pltpu.VMEM((pols, columns, beams, 2 * samples), jnp.bfloat16)],
         cost_estimate=pl.CostEstimate(
-            flops=DETECT_FLOPS,
+            flops=per_chunk * DETECT_FLOPS,
             bytes_accessed=1000,
             transcendentals=0,
         ),
@@ -226,7 +238,7 @@
     channels = common.shape[0]
     block = 16 if own % 16 == 0 else own
     group = np.kron(np.eye(samples // frame_count), np.ones((frame_count, frame_count)))
-    group = jnp.asarray(group / frame_count, jnp.bfloat16)
+    group = jnp.asarray(np.concatenate([group, group]) / frame_count, jnp.bfloat16)
     return pl.pallas_call(
         flag_kernel,
         grid=(own // block,),
@@ -267,14 +279,9 @@
     firsts = [sum(sizes[:chunk]) for chunk in range(chunks)]
     step = math.gcd(*sizes, 2)
 
-    def rows_of(gain):
-        rows = gain.reshape(local // step, step * pols, feeds)
-        return jnp.pad(rows, ((0, 0), (0, -rows.shape[1] % 8), (0, 0)))
-
-    gains = (rows_of(gain_real), rows_of(gain_imag))
+    gains = (gain_real, gain_imag)
     mine = lax.axis_index("grp")
-    table = beam_table(feeds).reshape(2, groups, feeds // groups, 2 * feeds)
-    table = jnp.stack([table[:, mine ^ r] for r in range(groups)]).reshape(2 * feeds, 2 * feeds)
+    table = jnp.asarray(beam_table(feeds, groups))
     me = mine.astype(jnp.int32).reshape(1)
     tables = [jnp.asarray(one) for one in spectral_tables(UP, frame_count, groups)]
     slots = beam_owner.shape[1]
@@ -288,7 +295,7 @@
     for chunk in range(chunks + 1):
         if chunk < chunks:
             formed = form(
-                after, table, gains, volts, firsts[chunk], sizes[chunk], step, groups
+                me, after, table, gains, volts, firsts[chunk], sizes[chunk], step, groups
             )
             turned.append([swap(one, "grp", r) if r else one for r, one in enumerate(formed)])
             after = formed[0]
@@ -306,11 +313,11 @@
     common = common / float(feeds * groups)
     piece = local // groups
     common_piece = lax.dynamic_slice_in_dim(common, mine * piece, piece).reshape(-1)
-    for bit in range(owners.bit_length() - 1):
-        other = swap(common, "chan", 1 << bit)
-        low = (lax.axis_index("chan") >> bit) % 2 == 0
-        common = jnp.where(low, jnp.stack([common, other]), jnp.stack([other, common]))
-        common = common.reshape(-1, samples)
+    near = lax.axis_index("chan")
+    others = [swap(common, "chan", r) if r else common for r in range(owners)]
+    common = jnp.zeros((owners, local, samples), jnp.float32)
+    for r, other in enumerate(others):
+        common = lax.dynamic_update_index_in_dim(common, other, near ^ r, 0)
     flagged = soft_flag(owned, common.reshape(channels, 1, samples), mask, frame_count)
     return (flagged, common_piece)
 

time: 305 us -> 292 us (0.957)
  waiting for transfers between devices: 123 us -> 110 us
  starting transfers between devices: 52.5 us -> 59.5 us
  other arithmetic: 4.5 us -> 0.78 us
  local copies, waits for them, and re-layouts: 12.4 us -> 9.19 us
    all_to_all x6, waiting for transfers between devices: 22.7 us -> 8.15 us  [body(): lax.all_to_all(stokes, 'chan', split_axis=0, concat_axis=0, tiled=True)]
    ppermute x23 -> x27, starting transfers between devices: 22.2 us -> 29.1 us  [swap(): lax.ppermute(one, axis, [(i, i ^ apart) for i in range(lax.axis_size(axis...]
    ppermute x23 -> x27, waiting for transfers between devices: 100 us -> 102 us  [swap(): lax.ppermute(one, axis, [(i, i ^ apart) for i in range(lax.axis_size(axis...]
    unnamed x46 -> x48, local copies, waits for them, and re-layouts: 6.6 us -> 6.88 us
  transfers between devices with their start and end apart: 29 -> 33, of which waited for: 12 -> 16; matrix products, arithmetic and copies ran while one was open for 1% -> 1% of each run, Pallas kernels for 31% -> 32%
where the time goes in v3:
time: 292 us; the launch traced here: 291 us
  Pallas kernels  110 us (38%)
  waiting for transfers between devices  110 us (38%)
  starting transfers between devices  59.5 us (20%)
  local copies, waits for them, and re-layouts  9.19 us (3%)
    ppermute x27, waiting for transfers between devices, swap(): lax.ppermute(one, axis, [(i, i ^ apart) for i in range(lax.axis_size(axis...  102 us
    pallas_call x6, Pallas kernels, detect(): pl.pallas_call(detect_kernel, grid=(steps,), in_specs=[pl.BlockSpec(memor...  51.7 us
    pallas_call x6, Pallas kernels, form(): pl.pallas_call(form_kernel, grid=(steps,), in_specs=[pl.BlockSpec(memory_...  45.5 us
    all_to_all x6, starting transfers between devices, body(): lax.all_to_all(stokes, 'chan', split_axis=0, concat_axis=0, tiled=True)  30.4 us
    ppermute x27, starting transfers between devices, swap(): lax.ppermute(one, axis, [(i, i ^ apart) for i in range(lax.axis_size(axis...  29.1 us
    pallas_call x1, Pallas kernels, soft_flag(): pl.pallas_call(flag_kernel, grid=(own // block,), in_specs=[whole_spec(gr...  13 us
    all_to_all x6, waiting for transfers between devices, body(): lax.all_to_all(stokes, 'chan', split_axis=0, concat_axis=0, tiled=True)  8.15 us
    unnamed x48, local copies, waits for them, and re-layouts  6.88 us
  transfers between devices with their start and end apart: 33, of which 16 were waited for; matrix products, arithmetic and copies ran while one was open for 1% of the time, Pallas kernels for 32%

profile of v3, /device:TPU:0, one launch (start us, length us, event | category | flops | bytes accessed | tf_op | source)
XLA Modules:
  0.0 290.8 jit_solution(6235848716024360603)
XLA Ops:
  7.8 5.1 %form.7 = (bf16[6,2,2,64,128]{4,3,2,1,0:T(8,128)(2,1)}, bf16[6,2,2,64,128]{4,3,2,1,0:T(8,128)(2,1)}, bf16[6,2,2,64,128]{4,3,2,1,0:T(8,128)(2,1)}, bf16[6,2,2,64,128]{4,3,2,1,0:T(8,128)(2,1)}) custom-call(s32[1]{0:T(128)} %bitcast.me_ref.after_ref.before_ref, bf16[4,2,2,64,128]{4,3,2,1,0:T(8,128)(2,1)} %get-tuple-element.38.after_ref.refs_0_, ...), custom_call_target="tpu_custom_call" | custom-call | flops 1000 | bytes 1000 | tf_op jit(solution)/shard_map/form/pallas_call | solution.py:172
  15.7 4.5 %collective-permute-done.2.refs_3_ = bf16[4,2,2,64,128]{4,3,2,1,0:T(8,128)(2,1)S(1)} collective-permute-done((bf16[4,2,2,64,128]{4,3,2,1,0:T(8,128)(2,1)}, bf16[4,2,2,64,128]{4,3,2,1,0:T(8,128)(2,1)S(1)}, u32[]{:S(2)}, u32[]{:S(2)}) %collective-permute-start.2) | collective-permute-done | bytes 262176 | tf_op jit(solution)/shard_map/ppermute | solution.py:268
  25.4 5.8 %all-to-all-start = ((bf16[8,4,32,256]{3,2,1,0:T(8,128)(2,1)}), bf16[8,4,32,256]{3,2,1,0:T(8,128)(2,1)S(1)}, u32[]{:S(2)}, u32[]{:S(2)}) async-start(bf16[8,4,32,256]{3,2,1,0:T(8,128)(2,1)} %get-tuple-element.44.after_ref), calls=%async_computation | async-start | bytes 1048576 | tf_op jit(solution)/shard_map/all_to_all | solution.py:307
  31.2 6.1 %form.8 = (bf16[8,2,2,64,128]{4,3,2,1,0:T(8,128)(2,1)}, bf16[8,2,2,64,128]{4,3,2,1,0:T(8,128)(2,1)}, bf16[8,2,2,64,128]{4,3,2,1,0:T(8,128)(2,1)}, bf16[8,2,2,64,128]{4,3,2,1,0:T(8,128)(2,1)}) custom-call(s32[1]{0:T(128)} %bitcast.me_ref.after_ref.before_ref, bf16[8,4,32,256]{3,2,1,0:T(8,128)(2,1)} %get-tuple-element.44.after_ref, ...), custom_call_target="tpu_custom_call" | custom-call | flops 1000 | bytes 1000 | tf_op jit(solution)/shard_map/form/pallas_call | solution.py:172
  40.3 5.7 %detect.7 = (bf16[8,6,32,256]{3,2,1,0:T(8,128)(2,1)}, f32[3,2,128]{2,1,0:T(2,128)}) custom-call(s32[1]{0:T(128)} %bitcast.me_ref.after_ref.before_ref, bf16[8,2,2,64,128]{4,3,2,1,0:T(8,128)(2,1)} %get-tuple-element.45.after_ref.refs_0_, s32[1]{0:T(128)} %bitcast.me_ref.after_ref.before_ref, bf16[256,256]{1,0:T(8,128)(2,1)} %constant.62.clone.high_ref, ...), custom_call_target="tpu_custom_call" | custom-call | flops 9600000000 | bytes 1000 | tf_op jit(solution)/shard_map/detect/pallas_call | solution.py:205
  46.5 5.4 %all-to-all-start.1 = ((bf16[8,6,32,256]{3,2,1,0:T(8,128)(2,1)}), bf16[8,6,32,256]{3,2,1,0:T(8,128)(2,1)S(1)}, u32[]{:S(2)}, u32[]{:S(2)}) async-start(bf16[8,6,32,256]{3,2,1,0:T(8,128)(2,1)} %get-tuple-element.50.after_ref), calls=%async_computation.1 | async-start | bytes 1572864 | tf_op jit(solution)/shard_map/all_to_all | solution.py:307
  51.9 8.3 %form.9 = (bf16[12,2,2,64,128]{4,3,2,1,0:T(8,128)(2,1)}, bf16[12,2,2,64,128]{4,3,2,1,0:T(8,128)(2,1)}, bf16[12,2,2,64,128]{4,3,2,1,0:T(8,128)(2,1)}, bf16[12,2,2,64,128]{4,3,2,1,0:T(8,128)(2,1)}) custom-call(s32[1]{0:T(128)} %bitcast.me_ref.after_ref.before_ref, bf16[8,6,32,256]{3,2,1,0:T(8,128)(2,1)} %get-tuple-element.50.after_ref, ...), custom_call_target="tpu_custom_call" | custom-call | flops 1000 | bytes 1000 | tf_op jit(solution)/shard_map/form/pallas_call | solution.py:172
  62.7 6.9 %detect.8 = (bf16[8,8,32,256]{3,2,1,0:T(8,128)(2,1)}, f32[4,2,128]{2,1,0:T(2,128)}) custom-call(s32[1]{0:T(128)} %bitcast.me_ref.after_ref.before_ref, bf16[12,2,2,64,128]{4,3,2,1,0:T(8,128)(2,1)} %get-tuple-element.51.after_ref.refs_0_, bf16[8,4,32,256]{3,2,1,0:T(8,128)(2,1)} %copy-done.5, bf16[256,256]{1,0:T(8,128)(2,1)} %constant.62.clone.high_ref, ...), custom_call_target="tpu_custom_call" | custom-call | flops 12800000000 | bytes 1000 | tf_op jit(solution)/shard_map/detect/pallas_call | solution.py:205
  76.2 10.5 %form.10 = (bf16[16,2,2,64,128]{4,3,2,1,0:T(8,128)(2,1)}, bf16[16,2,2,64,128]{4,3,2,1,0:T(8,128)(2,1)}, bf16[16,2,2,64,128]{4,3,2,1,0:T(8,128)(2,1)}, bf16[16,2,2,64,128]{4,3,2,1,0:T(8,128)(2,1)}) custom-call(s32[1]{0:T(128)} %bitcast.me_ref.after_ref.before_ref, bf16[8,8,32,256]{3,2,1,0:T(8,128)(2,1)} %get-tuple-element.56.after_ref, ...), custom_call_target="tpu_custom_call" | custom-call | flops 1000 | bytes 1000 | tf_op jit(solution)/shard_map/form/pallas_call | solution.py:172
  88.6 8.3 %collective-permute-done.11.refs_3_ = bf16[12,2,2,64,128]{4,3,2,1,0:T(8,128)(2,1)} collective-permute-done((bf16[12,2,2,64,128]{4,3,2,1,0:T(8,128)(2,1)}, bf16[12,2,2,64,128]{4,3,2,1,0:T(8,128)(2,1)}, u32[]{:S(2)}, u32[]{:S(2)}) %collective-permute-start.11) | collective-permute-done | bytes 786464 | tf_op jit(solution)/shard_map/ppermute | solution.py:268
  97.0 9.5 %detect.9 = (bf16[8,12,32,256]{3,2,1,0:T(8,128)(2,1)}, f32[6,2,128]{2,1,0:T(2,128)}) custom-call(s32[1]{0:T(128)} %bitcast.me_ref.after_ref.before_ref, bf16[16,2,2,64,128]{4,3,2,1,0:T(8,128)(2,1)} %get-tuple-element.57.after_ref.refs_0_, bf16[8,6,32,256]{3,2,1,0:T(8,128)(2,1)} %copy-done.4, bf16[256,256]{1,0:T(8,128)(2,1)} %constant.62.clone.high_ref, ...), custom_call_target="tpu_custom_call" | custom-call | flops 19200000000 | bytes 1000 | tf_op jit(solution)/shard_map/detect/pallas_call | solution.py:205
  107.4 6.0 %all-to-all-start.3 = ((bf16[8,12,32,256]{3,2,1,0:T(8,128)(2,1)}), bf16[8,12,32,256]{3,2,1,0:T(8,128)(2,1)S(1)}, u32[]{:S(2)}, u32[]{:S(2)}) async-start(bf16[8,12,32,256]{3,2,1,0:T(8,128)(2,1)} %get-tuple-element.62.after_ref), calls=%async_computation.3 | async-start | bytes 3145728 | tf_op jit(solution)/shard_map/all_to_all | solution.py:307
  113.4 11.5 %form.11 = (bf16[18,2,2,64,128]{4,3,2,1,0:T(8,128)(2,1)}, bf16[18,2,2,64,128]{4,3,2,1,0:T(8,128)(2,1)}, bf16[18,2,2,64,128]{4,3,2,1,0:T(8,128)(2,1)}, bf16[18,2,2,64,128]{4,3,2,1,0:T(8,128)(2,1)}) custom-call(s32[1]{0:T(128)} %bitcast.me_ref.after_ref.before_ref, bf16[8,12,32,256]{3,2,1,0:T(8,128)(2,1)} %get-tuple-element.62.after_ref, ...), custom_call_target="tpu_custom_call" | custom-call | flops 1000 | bytes 1000 | tf_op jit(solution)/shard_map/form/pallas_call | solution.py:172
  127.1 14.8 %collective-permute-done.14.refs_3_ = bf16[16,2,2,64,128]{4,3,2,1,0:T(8,128)(2,1)} collective-permute-done((bf16[16,2,2,64,128]{4,3,2,1,0:T(8,128)(2,1)}, bf16[16,2,2,64,128]{4,3,2,1,0:T(8,128)(2,1)}, u32[]{:S(2)}, u32[]{:S(2)}) %collective-permute-start.14) | collective-permute-done | bytes 1048608 | tf_op jit(solution)/shard_map/ppermute | solution.py:268
  141.9 12.0 %detect.10 = (bf16[8,16,32,256]{3,2,1,0:T(8,128)(2,1)}, f32[8,2,128]{2,1,0:T(2,128)}) custom-call(s32[1]{0:T(128)} %bitcast.me_ref.after_ref.before_ref, bf16[18,2,2,64,128]{4,3,2,1,0:T(8,128)(2,1)} %get-tuple-element.63.after_ref.refs_0_, bf16[8,8,32,256]{3,2,1,0:T(8,128)(2,1)} %copy-done.3, bf16[256,256]{1,0:T(8,128)(2,1)} %constant.62.clone.high_ref, ...), custom_call_target="tpu_custom_call" | custom-call | flops 25600000000 | bytes 1000 | tf_op jit(solution)/shard_map/detect/pallas_call | solution.py:205
  155.0 6.0 %all-to-all-start.4 = ((bf16[8,16,32,256]{3,2,1,0:T(8,128)(2,1)}), bf16[8,16,32,256]{3,2,1,0:T(8,128)(2,1)S(1)}, u32[]{:S(2)}, u32[]{:S(2)}) async-start(bf16[8,16,32,256]{3,2,1,0:T(8,128)(2,1)} %get-tuple-element.68.after_ref), calls=%async_computation.4 | async-start | bytes 4194304 | tf_op jit(solution)/shard_map/all_to_all | solution.py:307
  161.0 7.0 %collective-permute-done.16.refs_2_ = bf16[18,2,2,64,128]{4,3,2,1,0:T(8,128)(2,1)} collective-permute-done((bf16[18,2,2,64,128]{4,3,2,1,0:T(8,128)(2,1)}, bf16[18,2,2,64,128]{4,3,2,1,0:T(8,128)(2,1)}, u32[]{:S(2)}, u32[]{:S(2)}) %collective-permute-start.16) | collective-permute-done | bytes 1179680 | tf_op jit(solution)/shard_map/ppermute | solution.py:268
  168.1 24.4 %collective-permute-done.17.refs_3_ = bf16[18,2,2,64,128]{4,3,2,1,0:T(8,128)(2,1)} collective-permute-done((bf16[18,2,2,64,128]{4,3,2,1,0:T(8,128)(2,1)}, bf16[18,2,2,64,128]{4,3,2,1,0:T(8,128)(2,1)}, u32[]{:S(2)}, u32[]{:S(2)}) %collective-permute-start.17) | collective-permute-done | bytes 1179680 | tf_op jit(solution)/shard_map/ppermute | solution.py:268
  192.5 13.2 %detect.11 = (bf16[8,18,32,256]{3,2,1,0:T(8,128)(2,1)}, f32[9,2,128]{2,1,0:T(2,128)}) custom-call(s32[1]{0:T(128)} %bitcast.me_ref.after_ref.before_ref, bf16[8,16,32,256]{3,2,1,0:T(8,128)(2,1)} %get-tuple-element.68.after_ref, bf16[8,12,32,256]{3,2,1,0:T(8,128)(2,1)} %copy-done.2, bf16[256,256]{1,0:T(8,128)(2,1)} %constant.62.clone.high_ref, ...), custom_call_target="tpu_custom_call" | custom-call | flops 28800000000 | bytes 1000 | tf_op jit(solution)/shard_map/detect/pallas_call | solution.py:205
  205.7 4.7 %all-to-all-done.4.refs_4_ = bf16[8,16,32,256]{3,2,1,0:T(8,128)(2,1)S(1)} async-done(((bf16[8,16,32,256]{3,2,1,0:T(8,128)(2,1)}), bf16[8,16,32,256]{3,2,1,0:T(8,128)(2,1)S(1)}, u32[]{:S(2)}, u32[]{:S(2)}) %all-to-all-start.4) | async-done | bytes 2097184 | tf_op jit(solution)/shard_map/all_to_all | solution.py:307
  221.3 4.8 %collective-permute-start.26 = (f32[64,128]{1,0:T(8,128)S(1)}, f32[64,128]{1,0:T(8,128)S(1)}, u32[]{:S(2)}, u32[]{:S(2)}) collective-permute-start(f32[64,128]{1,0:T(8,128)S(1)} %get-tuple-element.75), channel_id=1, source_target_pairs={{0,28},{4,24},{8,20},{12,16},{16,12},{20,8},{24,4},{28,0},{1,29},{... | collective-permute-start | bytes 98312 | tf_op jit(solution)/shard_map/ppermute | solution.py:268
  237.2 21.3 %collective-permute-done.21 = f32[64,128]{1,0:T(8,128)S(1)} collective-permute-done((f32[64,128]{1,0:T(8,128)S(1)}, f32[64,128]{1,0:T(8,128)S(1)}, u32[]{:S(2)}, u32[]{:S(2)}) %collective-permute-start.21) | collective-permute-done | bytes 32800 | tf_op jit(solution)/shard_map/ppermute | solution.py:268
  263.3 11.8 %collective-permute-done.23 = f32[64,128]{1,0:T(8,128)S(1)} collective-permute-done((f32[64,128]{1,0:T(8,128)S(1)}, f32[64,128]{1,0:T(8,128)S(1)}, u32[]{:S(2)}, u32[]{:S(2)}) %collective-permute-start.23) | collective-permute-done | bytes 32800 | tf_op jit(solution)/shard_map/ppermute | solution.py:268
  277.8 13.0 %flag.1 = bf16[2,32,65536]{2,1,0:T(8,128)(2,1)} custom-call(bf16[256,128]{1,0:T(8,128)(2,1)} %constant.64.clone.group_ref, f32[512,1,128]{2,1,0:T(1,128)} %bitcast.26, f32[512,1,128]{2,1,0:T(1,128)} %copy.13.mask_ref, bf16[8,4,32,256]{3,2,1,0:T(8,128)(2,1)} %copy-done.5, bf16[8,6,32,256]{3,2,1,0:T(8,128)(2,1)} %copy-done.4, ...), custom_call_target="tpu_custom_call" | custom-call | flops 1073741824 | bytes 16777216 | tf_op jit(solution)/shard_map/flag/pallas_call | solution.py:242
  (124 shorter events, 63.2 us)
Async XLA Ops:
  12.8 26.5 %collective-permute-start.3 = (bf16[6,2,2,64,128]{4,3,2,1,0:T(8,128)(2,1)}, bf16[6,2,2,64,128]{4,3,2,1,0:T(8,128)(2,1)S(1)}, u32[]{:S(2)}, u32[]{:S(2)}) collective-permute-start(bf16[6,2,2,64,128]{4,3,2,1,0:T(8,128)(2,1)} %get-tuple-element.46), channel_id=1, source_target_pairs={{0,1},{1,0},{2,3},{3,2},{4,5},{5,4},{6,7},{7,6},{8,9},{9,8},{10,11... | collective-permute-start | bytes 1179656 | tf_op jit(solution)/shard_map/ppermute | solution.py:268
  13.0 26.3 %collective-permute-start.4 = (bf16[6,2,2,64,128]{4,3,2,1,0:T(8,128)(2,1)}, bf16[6,2,2,64,128]{4,3,2,1,0:T(8,128)(2,1)S(1)}, u32[]{:S(2)}, u32[]{:S(2)}) collective-permute-start(bf16[6,2,2,64,128]{4,3,2,1,0:T(8,128)(2,1)} %get-tuple-element.47), channel_id=1, source_target_pairs={{0,2},{1,3},{2,0},{3,1},{4,6},{5,7},{6,4},{7,5},{8,10},{9,11},{10,... | collective-permute-start | bytes 1179656 | tf_op jit(solution)/shard_map/ppermute | solution.py:268
  15.7 23.6 %collective-permute-start.5 = (bf16[6,2,2,64,128]{4,3,2,1,0:T(8,128)(2,1)}, bf16[6,2,2,64,128]{4,3,2,1,0:T(8,128)(2,1)S(1)}, u32[]{:S(2)}, u32[]{:S(2)}) collective-permute-start(bf16[6,2,2,64,128]{4,3,2,1,0:T(8,128)(2,1)} %get-tuple-element.48), channel_id=1, source_target_pairs={{0,3},{1,2},{2,1},{3,0},{4,7},{5,6},{6,5},{7,4},{8,11},{9,10},{10,... | collective-permute-start | bytes 1179656 | tf_op jit(solution)/shard_map/ppermute | solution.py:268
  37.3 24.5 %collective-permute-start.6 = (bf16[8,2,2,64,128]{4,3,2,1,0:T(8,128)(2,1)}, bf16[8,2,2,64,128]{4,3,2,1,0:T(8,128)(2,1)S(1)}, u32[]{:S(2)}, u32[]{:S(2)}) collective-permute-start(bf16[8,2,2,64,128]{4,3,2,1,0:T(8,128)(2,1)} %get-tuple-element.52), channel_id=1, source_target_pairs={{0,1},{1,0},{2,3},{3,2},{4,5},{5,4},{6,7},{7,6},{8,9},{9,8},{10,11... | collective-permute-start | bytes 1572872 | tf_op jit(solution)/shard_map/ppermute | solution.py:268
  37.8 24.4 %collective-permute-start.7 = (bf16[8,2,2,64,128]{4,3,2,1,0:T(8,128)(2,1)}, bf16[8,2,2,64,128]{4,3,2,1,0:T(8,128)(2,1)}, u32[]{:S(2)}, u32[]{:S(2)}) collective-permute-start(bf16[8,2,2,64,128]{4,3,2,1,0:T(8,128)(2,1)} %get-tuple-element.53), channel_id=1, source_target_pairs={{0,2},{1,3},{2,0},{3,1},{4,6},{5,7},{6,4},{7,5},{8,10},{9,11},{10,... | collective-permute-start | bytes 1572872 | tf_op jit(solution)/shard_map/ppermute | solution.py:268
  39.3 23.1 %collective-permute-start.8 = (bf16[8,2,2,64,128]{4,3,2,1,0:T(8,128)(2,1)}, bf16[8,2,2,64,128]{4,3,2,1,0:T(8,128)(2,1)}, u32[]{:S(2)}, u32[]{:S(2)}) collective-permute-start(bf16[8,2,2,64,128]{4,3,2,1,0:T(8,128)(2,1)} %get-tuple-element.54), channel_id=1, source_target_pairs={{0,3},{1,2},{2,1},{3,0},{4,7},{5,6},{6,5},{7,4},{8,11},{9,10},{10,... | collective-permute-start | bytes 1572872 | tf_op jit(solution)/shard_map/ppermute | solution.py:268
  46.5 26.0 %all-to-all-start.1 = ((bf16[8,6,32,256]{3,2,1,0:T(8,128)(2,1)}), bf16[8,6,32,256]{3,2,1,0:T(8,128)(2,1)S(1)}, u32[]{:S(2)}, u32[]{:S(2)}) async-start(bf16[8,6,32,256]{3,2,1,0:T(8,128)(2,1)} %get-tuple-element.50.after_ref), calls=%async_computation.1 | async-start | bytes 1572864 | tf_op jit(solution)/shard_map/all_to_all | solution.py:307
  60.2 28.1 %collective-permute-start.9 = (bf16[12,2,2,64,128]{4,3,2,1,0:T(8,128)(2,1)}, bf16[12,2,2,64,128]{4,3,2,1,0:T(8,128)(2,1)S(1)}, u32[]{:S(2)}, u32[]{:S(2)}) collective-permute-start(bf16[12,2,2,64,128]{4,3,2,1,0:T(8,128)(2,1)} %get-tuple-element.58), channel_id=1, source_target_pairs={{0,1},{1,0},{2,3},{3,2},{4,5},{5,4},{6,7},{7,6},{8,9},{9,8},{10,11... | collective-permute-start | bytes 2359304 | tf_op jit(solution)/shard_map/ppermute | solution.py:268
  60.3 28.3 %collective-permute-start.10 = (bf16[12,2,2,64,128]{4,3,2,1,0:T(8,128)(2,1)}, bf16[12,2,2,64,128]{4,3,2,1,0:T(8,128)(2,1)S(1)}, u32[]{:S(2)}, u32[]{:S(2)}) collective-permute-start(bf16[12,2,2,64,128]{4,3,2,1,0:T(8,128)(2,1)} %get-tuple-element.59), channel_id=1, source_target_pairs={{0,2},{1,3},{2,0},{3,1},{4,6},{5,7},{6,4},{7,5},{8,10},{9,11},{10,... | collective-permute-start | bytes 2359304 | tf_op jit(solution)/shard_map/ppermute | solution.py:268
  61.9 35.1 %collective-permute-start.11 = (bf16[12,2,2,64,128]{4,3,2,1,0:T(8,128)(2,1)}, bf16[12,2,2,64,128]{4,3,2,1,0:T(8,128)(2,1)}, u32[]{:S(2)}, u32[]{:S(2)}) collective-permute-start(bf16[12,2,2,64,128]{4,3,2,1,0:T(8,128)(2,1)} %get-tuple-element.60), channel_id=1, source_target_pairs={{0,3},{1,2},{2,1},{3,0},{4,7},{5,6},{6,5},{7,4},{8,11},{9,10},{10,... | collective-permute-start | bytes 2359304 | tf_op jit(solution)/shard_map/ppermute | solution.py:268
  72.6 33.9 %all-to-all-start.2 = ((bf16[8,8,32,256]{3,2,1,0:T(8,128)(2,1)}), bf16[8,8,32,256]{3,2,1,0:T(8,128)(2,1)S(1)}, u32[]{:S(2)}, u32[]{:S(2)}) async-start(bf16[8,8,32,256]{3,2,1,0:T(8,128)(2,1)} %get-tuple-element.56.after_ref), calls=%async_computation.2 | async-start | bytes 2097152 | tf_op jit(solution)/shard_map/all_to_all | solution.py:307
  86.7 40.4 %collective-permute-start.12 = (bf16[16,2,2,64,128]{4,3,2,1,0:T(8,128)(2,1)}, bf16[16,2,2,64,128]{4,3,2,1,0:T(8,128)(2,1)}, u32[]{:S(2)}, u32[]{:S(2)}) collective-permute-start(bf16[16,2,2,64,128]{4,3,2,1,0:T(8,128)(2,1)} %get-tuple-element.64), channel_id=1, source_target_pairs={{0,1},{1,0},{2,3},{3,2},{4,5},{5,4},{6,7},{7,6},{8,9},{9,8},{10,11... | collective-permute-start | bytes 3145736 | tf_op jit(solution)/shard_map/ppermute | solution.py:268
  86.8 40.3 %collective-permute-start.13 = (bf16[16,2,2,64,128]{4,3,2,1,0:T(8,128)(2,1)}, bf16[16,2,2,64,128]{4,3,2,1,0:T(8,128)(2,1)}, u32[]{:S(2)}, u32[]{:S(2)}) collective-permute-start(bf16[16,2,2,64,128]{4,3,2,1,0:T(8,128)(2,1)} %get-tuple-element.65), channel_id=1, source_target_pairs={{0,2},{1,3},{2,0},{3,1},{4,6},{5,7},{6,4},{7,5},{8,10},{9,11},{10,... | collective-permute-start | bytes 3145736 | tf_op jit(solution)/shard_map/ppermute | solution.py:268
  88.4 53.5 %collective-permute-start.14 = (bf16[16,2,2,64,128]{4,3,2,1,0:T(8,128)(2,1)}, bf16[16,2,2,64,128]{4,3,2,1,0:T(8,128)(2,1)}, u32[]{:S(2)}, u32[]{:S(2)}) collective-permute-start(bf16[16,2,2,64,128]{4,3,2,1,0:T(8,128)(2,1)} %get-tuple-element.66), channel_id=1, source_target_pairs={{0,3},{1,2},{2,1},{3,0},{4,7},{5,6},{6,5},{7,4},{8,11},{9,10},{10,... | collective-permute-start | bytes 3145736 | tf_op jit(solution)/shard_map/ppermute | solution.py:268
  107.4 46.4 %all-to-all-start.3 = ((bf16[8,12,32,256]{3,2,1,0:T(8,128)(2,1)}), bf16[8,12,32,256]{3,2,1,0:T(8,128)(2,1)S(1)}, u32[]{:S(2)}, u32[]{:S(2)}) async-start(bf16[8,12,32,256]{3,2,1,0:T(8,128)(2,1)} %get-tuple-element.62.after_ref), calls=%async_computation.3 | async-start | bytes 3145728 | tf_op jit(solution)/shard_map/all_to_all | solution.py:307
  125.0 36.1 %collective-permute-start.15 = (bf16[18,2,2,64,128]{4,3,2,1,0:T(8,128)(2,1)}, bf16[18,2,2,64,128]{4,3,2,1,0:T(8,128)(2,1)}, u32[]{:S(2)}, u32[]{:S(2)}) collective-permute-start(bf16[18,2,2,64,128]{4,3,2,1,0:T(8,128)(2,1)} %get-tuple-element.69), channel_id=1, source_target_pairs={{0,1},{1,0},{2,3},{3,2},{4,5},{5,4},{6,7},{7,6},{8,9},{9,8},{10,11... | collective-permute-start | bytes 3538952 | tf_op jit(solution)/shard_map/ppermute | solution.py:268
  125.6 42.5 %collective-permute-start.16 = (bf16[18,2,2,64,128]{4,3,2,1,0:T(8,128)(2,1)}, bf16[18,2,2,64,128]{4,3,2,1,0:T(8,128)(2,1)}, u32[]{:S(2)}, u32[]{:S(2)}) collective-permute-start(bf16[18,2,2,64,128]{4,3,2,1,0:T(8,128)(2,1)} %get-tuple-element.70), channel_id=1, source_target_pairs={{0,2},{1,3},{2,0},{3,1},{4,6},{5,7},{6,4},{7,5},{8,10},{9,11},{10,... | collective-permute-start | bytes 3538952 | tf_op jit(solution)/shard_map/ppermute | solution.py:268
  127.1 65.4 %collective-permute-start.17 = (bf16[18,2,2,64,128]{4,3,2,1,0:T(8,128)(2,1)}, bf16[18,2,2,64,128]{4,3,2,1,0:T(8,128)(2,1)}, u32[]{:S(2)}, u32[]{:S(2)}) collective-permute-start(bf16[18,2,2,64,128]{4,3,2,1,0:T(8,128)(2,1)} %get-tuple-element.71), channel_id=1, source_target_pairs={{0,3},{1,2},{2,1},{3,0},{4,7},{5,6},{6,5},{7,4},{8,11},{9,10},{10,... | collective-permute-start | bytes 3538952 | tf_op jit(solution)/shard_map/ppermute | solution.py:268
  155.0 55.3 %all-to-all-start.4 = ((bf16[8,16,32,256]{3,2,1,0:T(8,128)(2,1)}), bf16[8,16,32,256]{3,2,1,0:T(8,128)(2,1)S(1)}, u32[]{:S(2)}, u32[]{:S(2)}) async-start(bf16[8,16,32,256]{3,2,1,0:T(8,128)(2,1)} %get-tuple-element.68.after_ref), calls=%async_computation.4 | async-start | bytes 4194304 | tf_op jit(solution)/shard_map/all_to_all | solution.py:307
  211.7 64.6 %all-to-all-start.5 = ((bf16[8,18,32,256]{3,2,1,0:T(8,128)(2,1)}), bf16[8,18,32,256]{3,2,1,0:T(8,128)(2,1)S(1)}, u32[]{:S(2)}, u32[]{:S(2)}) async-start(bf16[8,18,32,256]{3,2,1,0:T(8,128)(2,1)} %get-tuple-element.73), calls=%async_computation.5 | async-start | bytes 4718592 | tf_op jit(solution)/shard_map/all_to_all | solution.py:307
  221.3 55.0 %collective-permute-start.26 = (f32[64,128]{1,0:T(8,128)S(1)}, f32[64,128]{1,0:T(8,128)S(1)}, u32[]{:S(2)}, u32[]{:S(2)}) collective-permute-start(f32[64,128]{1,0:T(8,128)S(1)} %get-tuple-element.75), channel_id=1, source_target_pairs={{0,28},{4,24},{8,20},{12,16},{16,12},{20,8},{24,4},{28,0},{1,29},{... | collective-permute-start | bytes 98312 | tf_op jit(solution)/shard_map/ppermute | solution.py:268
  226.1 50.2 %collective-permute-start.25 = (f32[64,128]{1,0:T(8,128)S(1)}, f32[64,128]{1,0:T(8,128)S(1)}, u32[]{:S(2)}, u32[]{:S(2)}) collective-permute-start(f32[64,128]{1,0:T(8,128)S(1)} %get-tuple-element.75), channel_id=1, source_target_pairs={{0,24},{4,28},{8,16},{12,20},{16,8},{20,12},{24,0},{28,4},{1,25},{... | collective-permute-start | bytes 98312 | tf_op jit(solution)/shard_map/ppermute | solution.py:268
  226.6 49.7 %collective-permute-start.24 = (f32[64,128]{1,0:T(8,128)S(1)}, f32[64,128]{1,0:T(8,128)S(1)}, u32[]{:S(2)}, u32[]{:S(2)}) collective-permute-start(f32[64,128]{1,0:T(8,128)S(1)} %get-tuple-element.75), channel_id=1, source_target_pairs={{0,20},{4,16},{8,28},{12,24},{16,4},{20,0},{24,12},{28,8},{1,21},{... | collective-permute-start | bytes 98312 | tf_op jit(solution)/shard_map/ppermute | solution.py:268
  227.2 48.0 %collective-permute-start.23 = (f32[64,128]{1,0:T(8,128)S(1)}, f32[64,128]{1,0:T(8,128)S(1)}, u32[]{:S(2)}, u32[]{:S(2)}) collective-permute-start(f32[64,128]{1,0:T(8,128)S(1)} %get-tuple-element.75), channel_id=1, source_target_pairs={{0,16},{4,20},{8,24},{12,28},{16,0},{20,4},{24,8},{28,12},{1,17},{... | collective-permute-start | bytes 98312 | tf_op jit(solution)/shard_map/ppermute | solution.py:268
  (33 other events, 201.7 us)

commit v4 on v3

--- a/solution.py
+++ b/solution.py
@@ -1,3 +1,4 @@
+import functools
 import math
 
 import jax
@@ -9,8 +10,10 @@
 from jax.sharding import PartitionSpec as P
 
 UP = 16
-SHARES = (2, 3, 4, 6, 8, 9)
-DETECT_FLOPS = 1_600_000_000
+QUAD = 4
+SHARES = (2, 4, 5, 6, 6, 5, 4)
+BEHIND = 2
+DETECT_FLOPS = 3_000_000_000
 
 epsilon = 1e-05
 
@@ -72,10 +75,11 @@
                     out_ref[c, p, a] = formed[row : row + beams, p * samples : (p + 1) * samples]
 
 
-def detect_kernel(me_ref, after_ref, before_ref, high_ref, low_ref, order_ref, *refs):
-    formed_refs, (out_ref, sum_ref, rows_ref) = refs[:-3], refs[-3:]
-    owners, channels, own, _ = out_ref.shape
-    columns = len(formed_refs)
+def detect_kernel(rows_count, me_ref, *refs):
+    high_ref, low_ref, order_ref, *refs = refs[2:]
+    columns = rows_count
+    formed_refs, out_refs, (sum_ref, rows_ref) = refs[:columns], refs[columns:-2], refs[-2:]
+    quad, channels, own, _ = out_refs[0].shape
     _, pols, _, beams, samples = formed_refs[0].shape
     for c in range(channels):
         for r, formed_ref in enumerate(formed_refs):
@@ -109,51 +113,59 @@
         ordered = jnp.dot(
             order_ref[...], jnp.concatenate(stokes, axis=0), preferred_element_type=jnp.float32
         )
-        for d in range(owners):
-            out_ref[d, c] = ordered[d * own : (d + 1) * own].astype(jnp.bfloat16)
-
-
-def flag_kernel(group_ref, common_ref, mask_ref, *refs):
-    chunk_refs, out_ref, power_ref = refs[:-2], refs[-2], refs[-1]
-    sources, _, beams, width = chunk_refs[0].shape
+        ordered = ordered.astype(jnp.bfloat16)
+        for r in range(ordered.shape[0] // own):
+            block = ordered[r * own : (r + 1) * own]
+            out_refs[r // quad][r % quad, c] = block
+
+
+def flag_kernel(layout, me_ref, group_ref, common_ref, mask_ref, *refs):
+    block_refs, out_ref, power_ref = refs[:-2], refs[-2], refs[-1]
+    beams, width = block_refs[0].shape[3:]
     samples = width // 2
-    sizes = [chunk_ref.shape[1] for chunk_ref in chunk_refs]
-    local = sum(sizes)
-
-    def measure(s, level):
-        first = s * local
-        for size, chunk_ref in zip(sizes, chunk_refs):
-            common = common_ref[pl.ds(first, size)]
-            cleaned = chunk_ref[s, :, :, :samples].astype(jnp.float32) - common
-            squares = (cleaned * cleaned).reshape(size * beams, samples)
-            high = squares.astype(jnp.bfloat16)
-            low = (squares - high.astype(jnp.float32)).astype(jnp.bfloat16)
-            squares = jnp.concatenate([high, low], axis=1)
-            power = jnp.dot(squares, group_ref[...], preferred_element_type=jnp.float32)
-            power = power.reshape(size, beams, samples)
-            power_ref[pl.ds(first, size)] = power
-            level = level + jnp.sum(power, axis=0)
-            first = first + size
-        return level
-
-    level = lax.fori_loop(0, sources, measure, jnp.zeros((beams, samples), jnp.float32))
-    level = jnp.sum(level, axis=1, keepdims=True) / float(sources * local * samples) + epsilon
+    local = layout[-1][0] + layout[-1][1]
+    channels = common_ref.shape[0]
+    near = me_ref[1]
+
+    def blocks(work, carry):
+        for (first, size), block_ref in zip(layout, block_refs):
+            fours = block_ref.shape[1]
+
+            def step(j, carry):
+                q, i = j // fours, j % fours
+                source = (near // QUAD * QUAD ^ i * QUAD) + q
+                return work(carry, block_ref.at[q, i], source * local + first, size)
+
+            carry = lax.fori_loop(0, QUAD * fours, step, carry)
+        return carry
+
+    def measure(level, block_ref, channel, size):
+        common = common_ref[pl.ds(channel, size)]
+        cleaned = block_ref[:, :, :samples].astype(jnp.float32) - common
+        squares = (cleaned * cleaned).reshape(size * beams, samples)
+        high = squares.astype(jnp.bfloat16)
+        low = (squares - high.astype(jnp.float32)).astype(jnp.bfloat16)
+        squares = jnp.concatenate([high, low], axis=1)
+        power = jnp.dot(squares, group_ref[...], preferred_element_type=jnp.float32)
+        power = power.reshape(size, beams, samples)
+        power_ref[pl.ds(channel, size)] = power
+        return level + jnp.sum(power, axis=0)
+
+    level = blocks(measure, jnp.zeros((beams, samples), jnp.float32))
+    level = jnp.sum(level, axis=1, keepdims=True) / float(channels * samples) + epsilon
     scale = jnp.broadcast_to(0.5 / level, (beams, samples))
 
-    def flag(s, carry):
-        channel = s * local
-        for size, chunk_ref in zip(sizes, chunk_refs):
-            for c in range(size):
-                row = chunk_ref[s, c].astype(jnp.float32)
-                cleaned = row[:, :samples] - common_ref[channel]
-                weight = mask_ref[channel] / (1.0 + power_ref[channel] * scale)
-                where = pl.ds(pl.multiple_of(channel * samples, samples), samples)
-                out_ref[0, :, where] = (cleaned * weight).astype(jnp.bfloat16)
-                out_ref[1, :, where] = (row[:, samples:] * weight).astype(jnp.bfloat16)
-                channel = channel + 1
+    def flag(carry, block_ref, channel, size):
+        for c in range(size):
+            row = block_ref[c].astype(jnp.float32)
+            cleaned = row[:, :samples] - common_ref[channel + c]
+            weight = mask_ref[channel + c] / (1.0 + power_ref[channel + c] * scale)
+            where = pl.ds(pl.multiple_of((channel + c) * samples, samples), samples)
+            out_ref[0, :, where] = (cleaned * weight).astype(jnp.bfloat16)
+            out_ref[1, :, where] = (row[:, samples:] * weight).astype(jnp.bfloat16)
         return carry
 
-    lax.fori_loop(0, sources, flag, 0)
+    blocks(flag, 0)
 
 
 def whole_spec(array):
@@ -201,24 +213,30 @@
     per_chunk, pols, _, beams, samples = formed[0].shape
     steps = per_chunk // step
     own = columns * beams // owners
+    counts = [QUAD] * (owners // QUAD)
     block_spec = pl.BlockSpec((step, pols, 2, beams, samples), lambda i: (i, 0, 0, 0, 0))
     return pl.pallas_call(
-        detect_kernel,
+        functools.partial(detect_kernel, columns),
         grid=(steps,),
         in_specs=[
             pl.BlockSpec(memory_space=pltpu.SMEM),
-            pl.BlockSpec(memory_space=pl.ANY),
-            pl.BlockSpec(memory_space=pl.ANY),
+            *[pl.BlockSpec(memory_space=pl.ANY)] * len(after),
             *[whole_spec(table) for table in tables],
             whole_spec(order),
             *[block_spec] * columns,
         ],
         out_specs=[
-            pl.BlockSpec((owners, step, own, 2 * samples), lambda i: (0, i, 0, 0)),
+            *[
+                pl.BlockSpec((count, step, own, 2 * samples), lambda i: (0, i, 0, 0))
+                for count in counts
+            ],
             pl.BlockSpec((1, step, samples), lambda i: (i, 0, 0)),
         ],
         out_shape=[
-            jax.ShapeDtypeStruct((owners, per_chunk, own, 2 * samples), jnp.bfloat16),
+            *[
+                jax.ShapeDtypeStruct((count, per_chunk, own, 2 * samples), jnp.bfloat16)
+                for count in counts
+            ],
             jax.ShapeDtypeStruct((steps, step, samples), jnp.float32),
         ],
         scratch_shapes=[pltpu.VMEM((pols, columns, beams, 2 * samples), jnp.bfloat16)],
@@ -232,28 +250,31 @@
     )(me, *after, *tables, order, *formed)
 
 
-def soft_flag(owned, common, mask, frame_count):
-    sources, _, own, width = owned[0].shape
+def soft_flag(me, owned, common, mask, frame_count):
+    own, width = owned[0].shape[3:]
+    sizes = [one.shape[2] for one in owned]
+    layout = [(sum(sizes[:i]), size) for i, size in enumerate(sizes)]
     samples = width // 2
     channels = common.shape[0]
-    block = 16 if own % 16 == 0 else own
+    rows = 16 if own % 16 == 0 else own
     group = np.kron(np.eye(samples // frame_count), np.ones((frame_count, frame_count)))
     group = jnp.asarray(np.concatenate([group, group]) / frame_count, jnp.bfloat16)
     return pl.pallas_call(
-        flag_kernel,
-        grid=(own // block,),
+        functools.partial(flag_kernel, layout),
+        grid=(own // rows,),
         in_specs=[
+            pl.BlockSpec(memory_space=pltpu.SMEM),
             whole_spec(group),
             whole_spec(common),
             whole_spec(mask),
             *[
-                pl.BlockSpec((sources, one.shape[1], block, width), lambda i: (0, 0, i, 0))
+                pl.BlockSpec((*one.shape[:3], rows, width), lambda i: (0, 0, 0, i, 0))
                 for one in owned
             ],
         ],
-        out_specs=pl.BlockSpec((2, block, channels * samples), lambda i: (0, i, 0)),
+        out_specs=pl.BlockSpec((2, rows, channels * samples), lambda i: (0, i, 0)),
         out_shape=jax.ShapeDtypeStruct((2, own, channels * samples), jnp.bfloat16),
-        scratch_shapes=[pltpu.VMEM((channels, block, samples), jnp.float32)],
+        scratch_shapes=[pltpu.VMEM((channels, rows, samples), jnp.float32)],
         cost_estimate=pl.CostEstimate(
             flops=channels * own * samples * samples * 4,
             bytes_accessed=channels * own * samples * 8,
@@ -261,7 +282,7 @@
         ),
         compiler_params=pltpu.CompilerParams(vmem_limit_bytes=60 << 20),
         name="flag",
-    )(group, common, mask, *owned)
+    )(me, group, common, mask, *owned)
 
 
 def swap(one, axis, apart):
@@ -282,43 +303,67 @@
     gains = (gain_real, gain_imag)
     mine = lax.axis_index("grp")
     table = jnp.asarray(beam_table(feeds, groups))
-    me = mine.astype(jnp.int32).reshape(1)
+    near = lax.axis_index("chan")
+    me = jnp.stack([mine, near]).astype(jnp.int32)
+    fours = [list(range(i, i + QUAD)) for i in range(0, owners, QUAD)]
     tables = [jnp.asarray(one) for one in spectral_tables(UP, frame_count, groups)]
     slots = beam_owner.shape[1]
-    order = (beam_owner[0][:, None] == jnp.arange(slots, dtype=jnp.int32)[None, :]).astype(
-        jnp.bfloat16
-    )
+    wanted = beam_owner[0].reshape(owners, slots // owners)
+    first_four = near // QUAD * QUAD
+    wanted = wanted[first_four ^ jnp.arange(owners, dtype=jnp.int32)].reshape(slots)
+    order = (wanted[:, None] == jnp.arange(slots, dtype=jnp.int32)[None, :]).astype(jnp.bfloat16)
     mask = jnp.repeat(channel_mask.astype(jnp.float32), frame_count).reshape(channels, 1, samples)
     volts = (voltage_real, voltage_imag)
     turned, owned, sums = [], [], []
     after = me
-    for chunk in range(chunks + 1):
+    for chunk in range(chunks + 2):
         if chunk < chunks:
             formed = form(
                 me, after, table, gains, volts, firsts[chunk], sizes[chunk], step, groups
             )
             turned.append([swap(one, "grp", r) if r else one for r, one in enumerate(formed)])
             after = formed[0]
-        if chunk > 0:
-            before = owned[-2:-1] or [me]
-            stokes, part = detect(
-                me, tables, order, turned[chunk - 1], [after, before[0]], step, owners
+        if 0 < chunk <= chunks:
+            before = owned[-BEHIND] if len(owned) >= BEHIND else me
+            *quads, part = detect(
+                me, tables, order, turned[chunk - 1], [after, before], step, owners
             )
-            owned.append(lax.all_to_all(stokes, "chan", split_axis=0, concat_axis=0, tiled=True))
+            quads = [swap(one, "chan", QUAD * i) if i else one for i, one in enumerate(quads)]
+            after = part
+        if chunk > 1:
+            if chunk <= chunks:
+                waiting, part = lax.optimization_barrier((waiting, part))
+            owned.append(
+                lax.all_to_all(
+                    jnp.stack(waiting, axis=1),
+                    "chan",
+                    split_axis=0,
+                    concat_axis=0,
+                    axis_index_groups=fours,
+                    tiled=True,
+                )
+            )
+        if 0 < chunk <= chunks:
+            waiting = quads
             sums.append(part.reshape(sizes[chunk - 1], samples))
-            after = stokes
-    common = jnp.concatenate(sums, axis=0)
-    for bit in range(groups.bit_length() - 1):
-        common = common + swap(common, "grp", 1 << bit)
+    common = jnp.concatenate(sums, axis=0).reshape(groups, local // groups, samples)
+    mine_of = [common[mine ^ r] for r in range(groups)]
+    common = mine_of[0]
+    for r in range(1, groups):
+        common = common + swap(mine_of[r], "grp", r)
     common = common / float(feeds * groups)
-    piece = local // groups
-    common_piece = lax.dynamic_slice_in_dim(common, mine * piece, piece).reshape(-1)
-    near = lax.axis_index("chan")
-    others = [swap(common, "chan", r) if r else common for r in range(owners)]
-    common = jnp.zeros((owners, local, samples), jnp.float32)
-    for r, other in enumerate(others):
-        common = lax.dynamic_update_index_in_dim(common, other, near ^ r, 0)
-    flagged = soft_flag(owned, common.reshape(channels, 1, samples), mask, frame_count)
+    common_piece = common.reshape(-1)
+    shared = common[None]
+    for bit in range(owners.bit_length() - 1):
+        other = swap(shared, "chan", 1 << bit)
+        low = (near >> bit) % 2 == 0
+        shared = jnp.where(low, jnp.stack([shared, other]), jnp.stack([other, shared]))
+        shared = shared.reshape(-1, local // groups, samples)
+    common = jnp.zeros((owners, groups, local // groups, samples), jnp.float32)
+    for r in range(groups):
+        other = swap(shared, "grp", r) if r else shared
+        common = lax.dynamic_update_index_in_dim(common, other, mine ^ r, 1)
+    flagged = soft_flag(me, owned, common.reshape(channels, 1, samples), mask, frame_count)
     return (flagged, common_piece)
 
 

time: 292 us -> 341 us (1.17)
  Pallas kernels: 110 us -> 130 us
  other arithmetic: 0.78 us -> 13.3 us
  waiting for transfers between devices: 110 us -> 121 us
  starting transfers between devices: 59.5 us -> 65.9 us
    all_to_all x6 -> x7, waiting for transfers between devices: 8.15 us -> 36 us  [body(): lax.all_to_all(jnp.stack(waiting, axis=1), 'chan', split_axis=0, concat_a...]
    pallas_call x7 -> x8, Pallas kernels: 64.7 us -> 82.6 us  [the longest x7 54.5 us: detect(): pl.pallas_call(functools.partial(detect_kernel, columns), grid=(steps,),...]
    ppermute x27 -> x37, waiting for transfers between devices: 102 us -> 84.6 us  [swap(): lax.ppermute(one, axis, [(i, i ^ apart) for i in range(lax.axis_size(axis...]
    another operation x0 -> x8, other arithmetic: none -> 11.8 us  [the longest x7 11.2 us: body(): jnp.stack(waiting, axis=1)]
    ppermute x27 -> x37, starting transfers between devices: 29.1 us -> 37.6 us  [swap(): lax.ppermute(one, axis, [(i, i ^ apart) for i in range(lax.axis_size(axis...]
    pallas_call x6 -> x7, Pallas kernels: 45.5 us -> 47.7 us  [form(): pl.pallas_call(form_kernel, grid=(steps,), in_specs=[pl.BlockSpec(memory_...]
    all_to_all x6 -> x7, starting transfers between devices: 30.4 us -> 28.4 us  [body(): lax.all_to_all(jnp.stack(waiting, axis=1), 'chan', split_axis=0, concat_a...]
    unnamed x48 -> x69, local copies, waits for them, and re-layouts: 6.88 us -> 5.42 us
  transfers between devices with their start and end apart: 33 -> 44, of which waited for: 16 -> 17; matrix products, arithmetic and copies ran while one was open for 1% -> 5% of each run, Pallas kernels for 32% -> 29%
where the time goes in v4:
time: 341 us; the launch traced here: 339 us
  Pallas kernels  130 us (38%)
  waiting for transfers between devices  121 us (35%)
  starting transfers between devices  65.9 us (19%)
  other arithmetic  13.3 us (4%)
  local copies, waits for them, and re-layouts  7.88 us (2%)
    ppermute x37, waiting for transfers between devices, swap(): lax.ppermute(one, axis, [(i, i ^ apart) for i in range(lax.axis_size(axis...  84.6 us
    pallas_call x7, Pallas kernels, detect(): pl.pallas_call(functools.partial(detect_kernel, columns), grid=(steps,),...  54.5 us
    pallas_call x7, Pallas kernels, form(): pl.pallas_call(form_kernel, grid=(steps,), in_specs=[pl.BlockSpec(memory_...  47.7 us
    ppermute x37, starting transfers between devices, swap(): lax.ppermute(one, axis, [(i, i ^ apart) for i in range(lax.axis_size(axis...  37.6 us
    all_to_all x7, waiting for transfers between devices, body(): lax.all_to_all(jnp.stack(waiting, axis=1), 'chan', split_axis=0, concat_a...  36 us
    all_to_all x7, starting transfers between devices, body(): lax.all_to_all(jnp.stack(waiting, axis=1), 'chan', split_axis=0, concat_a...  28.4 us
    pallas_call x1, Pallas kernels, soft_flag(): pl.pallas_call(functools.partial(flag_kernel, layout), grid=(own // rows,...  28 us
    another operation x7, other arithmetic, body(): jnp.stack(waiting, axis=1)  11.2 us
  transfers between devices with their start and end apart: 44, of which 17 were waited for; matrix products, arithmetic and copies ran while one was open for 5% of the time, Pallas kernels for 29%

profile of v4, /device:TPU:0, one launch (start us, length us, event | category | flops | bytes accessed | tf_op | source)
XLA Modules:
  0.0 339.2 jit_solution(13178414345017407137)
XLA Ops:
  8.4 6.2 %form.8 = (bf16[8,2,2,64,128]{4,3,2,1,0:T(8,128)(2,1)}, bf16[8,2,2,64,128]{4,3,2,1,0:T(8,128)(2,1)}, bf16[8,2,2,64,128]{4,3,2,1,0:T(8,128)(2,1)}, bf16[8,2,2,64,128]{4,3,2,1,0:T(8,128)(2,1)}) custom-call(s32[2]{0:T(128)} %pad_add_fusion.me_ref.after_ref.refs_1_, bf16[4,2,2,64,128]{4,3,2,1,0:T(8,128)(2,1)} %get-tuple-element.69.after_ref.refs_5_, ...), custom_call_target="tpu_custom_call" | custom-call | flops 1000 | bytes 1000 | tf_op jit(solution)/shard_map/form/pallas_call | solution.py:184
  21.6 4.5 %detect.7 = (bf16[4,4,32,256]{3,2,1,0:T(8,128)(2,1)}, bf16[4,4,32,256]{3,2,1,0:T(8,128)(2,1)}, f32[2,2,128]{2,1,0:T(2,128)}) custom-call(s32[2]{0:T(128)} %pad_add_fusion.me_ref.after_ref.refs_1_, bf16[8,2,2,64,128]{4,3,2,1,0:T(8,128)(2,1)} %get-tuple-element.70.refs_0_.refs_5_, s32[2]{0:T(128)} %pad_add_fusion.me_ref.after_ref.refs_1_, ...), custom_call_target="tpu_custom_call" | custom-call | flops 12000000000 | bytes 1000 | tf_op jit(solution)/shard_map/detect/pallas_call | solution.py:218
  28.8 7.3 %form.9 = (bf16[10,2,2,64,128]{4,3,2,1,0:T(8,128)(2,1)}, bf16[10,2,2,64,128]{4,3,2,1,0:T(8,128)(2,1)}, bf16[10,2,2,64,128]{4,3,2,1,0:T(8,128)(2,1)}, bf16[10,2,2,64,128]{4,3,2,1,0:T(8,128)(2,1)}) custom-call(s32[2]{0:T(128)} %pad_add_fusion.me_ref.after_ref.refs_1_, f32[2,2,128]{2,1,0:T(2,128)} %get-tuple-element.74.after_ref, ...), custom_call_target="tpu_custom_call" | custom-call | flops 1000 | bytes 1000 | tf_op jit(solution)/shard_map/form/pallas_call | solution.py:184
  38.0 5.3 %collective-permute-done.6.refs_8_ = bf16[8,2,2,64,128]{4,3,2,1,0:T(8,128)(2,1)S(1)} collective-permute-done((bf16[8,2,2,64,128]{4,3,2,1,0:T(8,128)(2,1)}, bf16[8,2,2,64,128]{4,3,2,1,0:T(8,128)(2,1)S(1)}, u32[]{:S(2)}, u32[]{:S(2)}) %collective-permute-start.6) | collective-permute-done | bytes 524320 | tf_op jit(solution)/shard_map/ppermute | solution.py:289
  44.1 7.0 %detect.8 = (bf16[4,8,32,256]{3,2,1,0:T(8,128)(2,1)}, bf16[4,8,32,256]{3,2,1,0:T(8,128)(2,1)}, f32[4,2,128]{2,1,0:T(2,128)}) custom-call(s32[2]{0:T(128)} %pad_add_fusion.me_ref.after_ref.refs_1_, bf16[10,2,2,64,128]{4,3,2,1,0:T(8,128)(2,1)} %get-tuple-element.77.refs_0_.refs_5_, s32[2]{0:T(128)} %pad_add_fusion.me_ref.after_ref.refs_1_, ...), custom_call_target="tpu_custom_call" | custom-call | flops 24000000000 | bytes 1000 | tf_op jit(solution)/shard_map/detect/pallas_call | solution.py:218
  51.2 8.4 %form.10 = (bf16[12,2,2,64,128]{4,3,2,1,0:T(8,128)(2,1)}, bf16[12,2,2,64,128]{4,3,2,1,0:T(8,128)(2,1)}, bf16[12,2,2,64,128]{4,3,2,1,0:T(8,128)(2,1)}, bf16[12,2,2,64,128]{4,3,2,1,0:T(8,128)(2,1)}) custom-call(s32[2]{0:T(128)} %pad_add_fusion.me_ref.after_ref.refs_1_, f32[4,2,128]{2,1,0:T(2,128)} %get-tuple-element.82.after_ref, ...), custom_call_target="tpu_custom_call" | custom-call | flops 1000 | bytes 1000 | tf_op jit(solution)/shard_map/form/pallas_call | solution.py:184
  71.4 8.3 %detect.9 = (bf16[4,10,32,256]{3,2,1,0:T(8,128)(2,1)}, bf16[4,10,32,256]{3,2,1,0:T(8,128)(2,1)}, f32[5,2,128]{2,1,0:T(2,128)}) custom-call(s32[2]{0:T(128)} %pad_add_fusion.me_ref.after_ref.refs_1_, bf16[12,2,2,64,128]{4,3,2,1,0:T(8,128)(2,1)} %get-tuple-element.85.refs_0_.refs_5_, s32[2]{0:T(128)} %pad_add_fusion.me_ref.after_ref.refs_1_, ...), custom_call_target="tpu_custom_call" | custom-call | flops 30000001024 | bytes 1000 | tf_op jit(solution)/shard_map/detect/pallas_call | solution.py:218
  82.5 8.4 %form.11 = (bf16[12,2,2,64,128]{4,3,2,1,0:T(8,128)(2,1)}, bf16[12,2,2,64,128]{4,3,2,1,0:T(8,128)(2,1)}, bf16[12,2,2,64,128]{4,3,2,1,0:T(8,128)(2,1)}, bf16[12,2,2,64,128]{4,3,2,1,0:T(8,128)(2,1)}) custom-call(s32[2]{0:T(128)} %pad_add_fusion.me_ref.after_ref.refs_1_, f32[5,2,128]{2,1,0:T(2,128)} %get-tuple-element.90.after_ref, ...), custom_call_target="tpu_custom_call" | custom-call | flops 1000 | bytes 1000 | tf_op jit(solution)/shard_map/form/pallas_call | solution.py:184
  90.8 14.5 %collective-permute-done.7 = bf16[4,8,32,256]{3,2,1,0:T(8,128)(2,1)S(1)} collective-permute-done((bf16[4,8,32,256]{3,2,1,0:T(8,128)(2,1)}, bf16[4,8,32,256]{3,2,1,0:T(8,128)(2,1)S(1)}, u32[]{:S(2)}, u32[]{:S(2)}) %collective-permute-start.7) | collective-permute-done | bytes 524320 | tf_op jit(solution)/shard_map/ppermute | solution.py:289
  111.9 9.6 %detect.10 = (bf16[4,12,32,256]{3,2,1,0:T(8,128)(2,1)}, bf16[4,12,32,256]{3,2,1,0:T(8,128)(2,1)}, f32[6,2,128]{2,1,0:T(2,128)}) custom-call(s32[2]{0:T(128)} %pad_add_fusion.me_ref.after_ref.refs_1_, bf16[12,2,2,64,128]{4,3,2,1,0:T(8,128)(2,1)} %get-tuple-element.93.refs_0_.refs_5_, bf16[4,2,4,32,256]{4,3,2,1,0:T(8,128)(2,1)} %copy-done.6, ...), custom_call_target="tpu_custom_call" | custom-call | flops 35999997952 | bytes 1000 | tf_op jit(solution)/shard_map/detect/pallas_call | solution.py:218
  124.8 7.4 %form.12 = (bf16[10,2,2,64,128]{4,3,2,1,0:T(8,128)(2,1)}, bf16[10,2,2,64,128]{4,3,2,1,0:T(8,128)(2,1)}, bf16[10,2,2,64,128]{4,3,2,1,0:T(8,128)(2,1)}, bf16[10,2,2,64,128]{4,3,2,1,0:T(8,128)(2,1)}) custom-call(s32[2]{0:T(128)} %pad_add_fusion.me_ref.after_ref.refs_1_, f32[6,2,128]{2,1,0:T(2,128)} %get-tuple-element.100.after_ref, ...), custom_call_target="tpu_custom_call" | custom-call | flops 1000 | bytes 1000 | tf_op jit(solution)/shard_map/form/pallas_call | solution.py:184
  143.2 9.6 %detect.11 = (bf16[4,12,32,256]{3,2,1,0:T(8,128)(2,1)}, bf16[4,12,32,256]{3,2,1,0:T(8,128)(2,1)}, f32[6,2,128]{2,1,0:T(2,128)}) custom-call(s32[2]{0:T(128)} %pad_add_fusion.me_ref.after_ref.refs_1_, bf16[10,2,2,64,128]{4,3,2,1,0:T(8,128)(2,1)} %get-tuple-element.103.refs_0_.refs_5_, bf16[4,2,8,32,256]{4,3,2,1,0:T(8,128)(2,1)} %copy-done.4, ...), custom_call_target="tpu_custom_call" | custom-call | flops 35999997952 | bytes 1000 | tf_op jit(solution)/shard_map/detect/pallas_call | solution.py:218
  152.8 6.3 %form.13 = (bf16[8,2,2,64,128]{4,3,2,1,0:T(8,128)(2,1)}, bf16[8,2,2,64,128]{4,3,2,1,0:T(8,128)(2,1)}, bf16[8,2,2,64,128]{4,3,2,1,0:T(8,128)(2,1)}, bf16[8,2,2,64,128]{4,3,2,1,0:T(8,128)(2,1)}) custom-call(s32[2]{0:T(128)} %pad_add_fusion.me_ref.after_ref.refs_1_, f32[6,2,128]{2,1,0:T(2,128)} %get-tuple-element.110.after_ref, ...), custom_call_target="tpu_custom_call" | custom-call | flops 1000 | bytes 1000 | tf_op jit(solution)/shard_map/form/pallas_call | solution.py:184
  161.2 10.6 %all-to-all-done.2.refs_1_.refs_2_ = bf16[4,2,10,32,256]{4,3,2,1,0:T(8,128)(2,1)S(1)} async-done(((bf16[4,2,10,32,256]{4,3,2,1,0:T(8,128)(2,1)}), bf16[4,2,10,32,256]{4,3,2,1,0:T(8,128)(2,1)S(1)}, u32[]{:S(2)}, u32[]{:S(2)}) %all-to-all-start.2) | async-done | bytes 1310752 | tf_op jit(solution)/shard_map/all_to_all | solution.py:337
  178.0 8.4 %detect.12 = (bf16[4,10,32,256]{3,2,1,0:T(8,128)(2,1)}, bf16[4,10,32,256]{3,2,1,0:T(8,128)(2,1)}, f32[5,2,128]{2,1,0:T(2,128)}) custom-call(s32[2]{0:T(128)} %pad_add_fusion.me_ref.after_ref.refs_1_, bf16[8,2,2,64,128]{4,3,2,1,0:T(8,128)(2,1)} %get-tuple-element.113.refs_0_.refs_5_, bf16[4,2,10,32,256]{4,3,2,1,0:T(8,128)(2,1)} %copy-done.2, ...), custom_call_target="tpu_custom_call" | custom-call | flops 30000001024 | bytes 1000 | tf_op jit(solution)/shard_map/detect/pallas_call | solution.py:218
  186.4 11.2 %collective-permute-done.19 = bf16[4,12,32,256]{3,2,1,0:T(8,128)(2,1)} collective-permute-done((bf16[4,12,32,256]{3,2,1,0:T(8,128)(2,1)}, bf16[4,12,32,256]{3,2,1,0:T(8,128)(2,1)}, u32[]{:S(2)}, u32[]{:S(2)}) %collective-permute-start.19) | collective-permute-done | bytes 786464 | tf_op jit(solution)/shard_map/ppermute | solution.py:289
  200.0 11.0 %all-to-all-done.3.refs_1_.refs_3_ = bf16[4,2,12,32,256]{4,3,2,1,0:T(8,128)(2,1)S(1)} async-done(((bf16[4,2,12,32,256]{4,3,2,1,0:T(8,128)(2,1)}), bf16[4,2,12,32,256]{4,3,2,1,0:T(8,128)(2,1)S(1)}, u32[]{:S(2)}, u32[]{:S(2)}) %all-to-all-start.3) | async-done | bytes 1572896 | tf_op jit(solution)/shard_map/all_to_all | solution.py:337
  215.8 7.1 %detect.13 = (bf16[4,8,32,256]{3,2,1,0:T(8,128)(2,1)}, bf16[4,8,32,256]{3,2,1,0:T(8,128)(2,1)}, f32[4,2,128]{2,1,0:T(2,128)}) custom-call(s32[2]{0:T(128)} %pad_add_fusion.me_ref.after_ref.refs_1_, f32[5,2,128]{2,1,0:T(2,128)} %get-tuple-element.120.refs_0_, bf16[4,2,12,32,256]{4,3,2,1,0:T(8,128)(2,1)} %copy-done, bf16[256,256]{1,0:T(8,128)(2,1)} %constant.74.clone.refs_2_, ...), custom_call_target="tpu_custom_call" | custom-call | flops 24000000000 | bytes 1000 | tf_op jit(solution)/shard_map/detect/pallas_call | solution.py:218
  222.9 5.2 %collective-permute-done.23 = bf16[4,10,32,256]{3,2,1,0:T(8,128)(2,1)} collective-permute-done((bf16[4,10,32,256]{3,2,1,0:T(8,128)(2,1)}, bf16[4,10,32,256]{3,2,1,0:T(8,128)(2,1)}, u32[]{:S(2)}, u32[]{:S(2)}) %collective-permute-start.23) | collective-permute-done | bytes 655392 | tf_op jit(solution)/shard_map/ppermute | solution.py:289
  230.4 14.3 %all-to-all-done.4.refs_4_ = bf16[4,2,12,32,256]{4,3,2,1,0:T(8,128)(2,1)S(1)} async-done(((bf16[4,2,12,32,256]{4,3,2,1,0:T(8,128)(2,1)}), bf16[4,2,12,32,256]{4,3,2,1,0:T(8,128)(2,1)S(1)}, u32[]{:S(2)}, u32[]{:S(2)}) %all-to-all-start.4) | async-done | bytes 1572896 | tf_op jit(solution)/shard_map/all_to_all | solution.py:337
  253.3 21.0 %collective-permute-done.36 = bf16[4,8,32,256]{3,2,1,0:T(8,128)(2,1)} collective-permute-done((bf16[4,8,32,256]{3,2,1,0:T(8,128)(2,1)}, bf16[4,8,32,256]{3,2,1,0:T(8,128)(2,1)}, u32[]{:S(2)}, u32[]{:S(2)}) %collective-permute-start.36) | collective-permute-done | bytes 524320 | tf_op jit(solution)/shard_map/ppermute | solution.py:289
  276.5 6.2 %all-to-all-start.6 = ((bf16[4,2,8,32,256]{4,3,2,1,0:T(8,128)(2,1)}), bf16[4,2,8,32,256]{4,3,2,1,0:T(8,128)(2,1)S(1)}, u32[]{:S(2)}, u32[]{:S(2)}) async-start(bf16[4,2,8,32,256]{4,3,2,1,0:T(8,128)(2,1)} %pad_maximum_fusion.5), calls=%async_computation.6 | async-start | bytes 2097152 | tf_op jit(solution)/shard_map/all_to_all | solution.py:337
  285.0 10.5 %collective-permute-done.30 = f32[1,16,128]{2,1,0:T(8,128)S(1)} collective-permute-done((f32[1,16,128]{2,1,0:T(8,128)S(1)}, f32[1,16,128]{2,1,0:T(8,128)S(1)}, u32[]{:S(2)}, u32[]{:S(2)}) %collective-permute-start.30) | collective-permute-done | bytes 8224 | tf_op jit(solution)/shard_map/ppermute | solution.py:289
  311.0 28.0 %flag.1 = bf16[2,32,65536]{2,1,0:T(8,128)(2,1)} custom-call(s32[2]{0:T(128)} %pad_add_fusion.me_ref.after_ref.refs_1_, bf16[256,128]{1,0:T(8,128)(2,1)} %constant.76.clone.group_ref, f32[512,1,128]{2,1,0:T(1,128)} %bitcast.59, f32[512,1,128]{2,1,0:T(1,128)} %copy.17.mask_ref, bf16[4,2,4,32,256]{4,3,2,1,0:T(8,128)(2,1)} %copy-done.6, ...), custom_call_target="tpu_custom_call" | custom-call | flops 1073741824 | bytes 16777216 | tf_op jit(solution)/shard_map/flag/pallas_call | solution.py:262
  (184 shorter events, 101.8 us)
Async XLA Ops:
  26.1 33.4 %collective-permute-start.3 = (bf16[4,4,32,256]{3,2,1,0:T(8,128)(2,1)}, bf16[4,4,32,256]{3,2,1,0:T(8,128)(2,1)S(1)}, u32[]{:S(2)}, u32[]{:S(2)}) collective-permute-start(bf16[4,4,32,256]{3,2,1,0:T(8,128)(2,1)} %get-tuple-element.76), channel_id=1, source_target_pairs={{0,16},{4,20},{8,24},{12,28},{16,0},{20,4},{24,8},{28,12},{1,17},{... | collective-permute-start | bytes 786440 | tf_op jit(solution)/shard_map/ppermute | solution.py:289
  36.5 32.0 %collective-permute-start.9 = (bf16[10,2,2,64,128]{4,3,2,1,0:T(8,128)(2,1)}, bf16[10,2,2,64,128]{4,3,2,1,0:T(8,128)(2,1)S(1)}, u32[]{:S(2)}, u32[]{:S(2)}) collective-permute-start(bf16[10,2,2,64,128]{4,3,2,1,0:T(8,128)(2,1)} %get-tuple-element.87), channel_id=1, source_target_pairs={{0,2},{1,3},{2,0},{3,1},{4,6},{5,7},{6,4},{7,5},{8,10},{9,11},{10,... | collective-permute-start | bytes 1966088 | tf_op jit(solution)/shard_map/ppermute | solution.py:289
  38.0 33.5 %collective-permute-start.10 = (bf16[10,2,2,64,128]{4,3,2,1,0:T(8,128)(2,1)}, bf16[10,2,2,64,128]{4,3,2,1,0:T(8,128)(2,1)}, u32[]{:S(2)}, u32[]{:S(2)}) collective-permute-start(bf16[10,2,2,64,128]{4,3,2,1,0:T(8,128)(2,1)} %get-tuple-element.88), channel_id=1, source_target_pairs={{0,3},{1,2},{2,1},{3,0},{4,7},{5,6},{6,5},{7,4},{8,11},{9,10},{10,... | collective-permute-start | bytes 1966088 | tf_op jit(solution)/shard_map/ppermute | solution.py:289
  60.4 47.9 %all-to-all-start = ((bf16[4,2,4,32,256]{4,3,2,1,0:T(8,128)(2,1)}), bf16[4,2,4,32,256]{4,3,2,1,0:T(8,128)(2,1)S(1)}, u32[]{:S(2)}, u32[]{:S(2)}) async-start(bf16[4,2,4,32,256]{4,3,2,1,0:T(8,128)(2,1)} %pad_maximum_fusion.6), calls=%async_computation | async-start | bytes 1048576 | tf_op jit(solution)/shard_map/all_to_all | solution.py:337
  64.2 41.2 %collective-permute-start.7 = (bf16[4,8,32,256]{3,2,1,0:T(8,128)(2,1)}, bf16[4,8,32,256]{3,2,1,0:T(8,128)(2,1)S(1)}, u32[]{:S(2)}, u32[]{:S(2)}) collective-permute-start(bf16[4,8,32,256]{3,2,1,0:T(8,128)(2,1)} %get-tuple-element.84), channel_id=1, source_target_pairs={{0,16},{4,20},{8,24},{12,28},{16,0},{20,4},{24,8},{28,12},{1,17},{... | collective-permute-start | bytes 1572872 | tf_op jit(solution)/shard_map/ppermute | solution.py:289
  66.8 39.6 %collective-permute-start.12 = (bf16[12,2,2,64,128]{4,3,2,1,0:T(8,128)(2,1)}, bf16[12,2,2,64,128]{4,3,2,1,0:T(8,128)(2,1)}, u32[]{:S(2)}, u32[]{:S(2)}) collective-permute-start(bf16[12,2,2,64,128]{4,3,2,1,0:T(8,128)(2,1)} %get-tuple-element.96), channel_id=1, source_target_pairs={{0,1},{1,0},{2,3},{3,2},{4,5},{5,4},{6,7},{7,6},{8,9},{9,8},{10,11... | collective-permute-start | bytes 2359304 | tf_op jit(solution)/shard_map/ppermute | solution.py:289
  67.0 40.9 %collective-permute-start.13 = (bf16[12,2,2,64,128]{4,3,2,1,0:T(8,128)(2,1)}, bf16[12,2,2,64,128]{4,3,2,1,0:T(8,128)(2,1)}, u32[]{:S(2)}, u32[]{:S(2)}) collective-permute-start(bf16[12,2,2,64,128]{4,3,2,1,0:T(8,128)(2,1)} %get-tuple-element.97), channel_id=1, source_target_pairs={{0,2},{1,3},{2,0},{3,1},{4,6},{5,7},{6,4},{7,5},{8,10},{9,11},{10,... | collective-permute-start | bytes 2359304 | tf_op jit(solution)/shard_map/ppermute | solution.py:289
  68.5 43.4 %collective-permute-start.14 = (bf16[12,2,2,64,128]{4,3,2,1,0:T(8,128)(2,1)S(1)}, bf16[12,2,2,64,128]{4,3,2,1,0:T(8,128)(2,1)}, u32[]{:S(2)}, u32[]{:S(2)}) collective-permute-start(bf16[12,2,2,64,128]{4,3,2,1,0:T(8,128)(2,1)S(1)} %copy-done.25), channel_id=1, source_target_pairs={{0,3},{1,2},{2,1},{3,0},{4,7},{5,6},{6,5},{7,4},{8,11},{9,10},{10,... | collective-permute-start | bytes 2359304 | tf_op jit(solution)/shard_map/ppermute | solution.py:289
  79.8 52.4 %collective-permute-start.11 = (bf16[4,10,32,256]{3,2,1,0:T(8,128)(2,1)}, bf16[4,10,32,256]{3,2,1,0:T(8,128)(2,1)S(1)}, u32[]{:S(2)}, u32[]{:S(2)}) collective-permute-start(bf16[4,10,32,256]{3,2,1,0:T(8,128)(2,1)} %get-tuple-element.92), channel_id=1, source_target_pairs={{0,16},{4,20},{8,24},{12,28},{16,0},{20,4},{24,8},{28,12},{1,17},{... | collective-permute-start | bytes 1966088 | tf_op jit(solution)/shard_map/ppermute | solution.py:289
  107.9 35.3 %collective-permute-start.18 = (bf16[12,2,2,64,128]{4,3,2,1,0:T(8,128)(2,1)}, bf16[12,2,2,64,128]{4,3,2,1,0:T(8,128)(2,1)}, u32[]{:S(2)}, u32[]{:S(2)}) collective-permute-start(bf16[12,2,2,64,128]{4,3,2,1,0:T(8,128)(2,1)} %get-tuple-element.108), channel_id=1, source_target_pairs={{0,3},{1,2},{2,1},{3,0},{4,7},{5,6},{6,5},{7,4},{8,11},{9,10},{10,... | collective-permute-start | bytes 2359304 | tf_op jit(solution)/shard_map/ppermute | solution.py:289
  121.4 38.2 %collective-permute-start.15 = (bf16[4,12,32,256]{3,2,1,0:T(8,128)(2,1)}, bf16[4,12,32,256]{3,2,1,0:T(8,128)(2,1)S(1)}, u32[]{:S(2)}, u32[]{:S(2)}) collective-permute-start(bf16[4,12,32,256]{3,2,1,0:T(8,128)(2,1)} %get-tuple-element.102), channel_id=1, source_target_pairs={{0,16},{4,20},{8,24},{12,28},{16,0},{20,4},{24,8},{28,12},{1,17},{... | collective-permute-start | bytes 2359304 | tf_op jit(solution)/shard_map/ppermute | solution.py:289
  132.1 44.3 %collective-permute-start.20 = (bf16[10,2,2,64,128]{4,3,2,1,0:T(8,128)(2,1)}, bf16[10,2,2,64,128]{4,3,2,1,0:T(8,128)(2,1)}, u32[]{:S(2)}, u32[]{:S(2)}) collective-permute-start(bf16[10,2,2,64,128]{4,3,2,1,0:T(8,128)(2,1)} %get-tuple-element.116), channel_id=1, source_target_pairs={{0,1},{1,0},{2,3},{3,2},{4,5},{5,4},{6,7},{7,6},{8,9},{9,8},{10,11... | collective-permute-start | bytes 1966088 | tf_op jit(solution)/shard_map/ppermute | solution.py:289
  133.4 44.6 %collective-permute-start.21 = (bf16[10,2,2,64,128]{4,3,2,1,0:T(8,128)(2,1)}, bf16[10,2,2,64,128]{4,3,2,1,0:T(8,128)(2,1)}, u32[]{:S(2)}, u32[]{:S(2)}) collective-permute-start(bf16[10,2,2,64,128]{4,3,2,1,0:T(8,128)(2,1)} %get-tuple-element.117), channel_id=1, source_target_pairs={{0,2},{1,3},{2,0},{3,1},{4,6},{5,7},{6,4},{7,5},{8,10},{9,11},{10,... | collective-permute-start | bytes 1966088 | tf_op jit(solution)/shard_map/ppermute | solution.py:289
  134.9 43.1 %collective-permute-start.22 = (bf16[10,2,2,64,128]{4,3,2,1,0:T(8,128)(2,1)}, bf16[10,2,2,64,128]{4,3,2,1,0:T(8,128)(2,1)}, u32[]{:S(2)}, u32[]{:S(2)}) collective-permute-start(bf16[10,2,2,64,128]{4,3,2,1,0:T(8,128)(2,1)} %get-tuple-element.118), channel_id=1, source_target_pairs={{0,3},{1,2},{2,1},{3,0},{4,7},{5,6},{6,5},{7,4},{8,11},{9,10},{10,... | collective-permute-start | bytes 1966088 | tf_op jit(solution)/shard_map/ppermute | solution.py:289
  135.3 36.6 %all-to-all-start.2 = ((bf16[4,2,10,32,256]{4,3,2,1,0:T(8,128)(2,1)}), bf16[4,2,10,32,256]{4,3,2,1,0:T(8,128)(2,1)S(1)}, u32[]{:S(2)}, u32[]{:S(2)}) async-start(bf16[4,2,10,32,256]{4,3,2,1,0:T(8,128)(2,1)} %pad_maximum_fusion.2), calls=%async_computation.2 | async-start | bytes 2621440 | tf_op jit(solution)/shard_map/all_to_all | solution.py:337
  159.7 37.9 %collective-permute-start.19 = (bf16[4,12,32,256]{3,2,1,0:T(8,128)(2,1)}, bf16[4,12,32,256]{3,2,1,0:T(8,128)(2,1)}, u32[]{:S(2)}, u32[]{:S(2)}) collective-permute-start(bf16[4,12,32,256]{3,2,1,0:T(8,128)(2,1)} %get-tuple-element.112), channel_id=1, source_target_pairs={{0,16},{4,20},{8,24},{12,28},{16,0},{20,4},{24,8},{28,12},{1,17},{... | collective-permute-start | bytes 2359304 | tf_op jit(solution)/shard_map/ppermute | solution.py:289
  159.7 56.1 %collective-permute-start.24 = (bf16[8,2,2,64,128]{4,3,2,1,0:T(8,128)(2,1)}, bf16[8,2,2,64,128]{4,3,2,1,0:T(8,128)(2,1)}, u32[]{:S(2)}, u32[]{:S(2)}) collective-permute-start(bf16[8,2,2,64,128]{4,3,2,1,0:T(8,128)(2,1)} %get-tuple-element.125), channel_id=1, source_target_pairs={{0,1},{1,0},{2,3},{3,2},{4,5},{5,4},{6,7},{7,6},{8,9},{9,8},{10,11... | collective-permute-start | bytes 1572872 | tf_op jit(solution)/shard_map/ppermute | solution.py:289
  172.9 38.1 %all-to-all-start.3 = ((bf16[4,2,12,32,256]{4,3,2,1,0:T(8,128)(2,1)}), bf16[4,2,12,32,256]{4,3,2,1,0:T(8,128)(2,1)S(1)}, u32[]{:S(2)}, u32[]{:S(2)}) async-start(bf16[4,2,12,32,256]{4,3,2,1,0:T(8,128)(2,1)} %pad_maximum_fusion), calls=%async_computation.3 | async-start | bytes 3145728 | tf_op jit(solution)/shard_map/all_to_all | solution.py:337
  176.5 39.3 %collective-permute-start.25 = (bf16[8,2,2,64,128]{4,3,2,1,0:T(8,128)(2,1)}, bf16[8,2,2,64,128]{4,3,2,1,0:T(8,128)(2,1)}, u32[]{:S(2)}, u32[]{:S(2)}) collective-permute-start(bf16[8,2,2,64,128]{4,3,2,1,0:T(8,128)(2,1)} %get-tuple-element.126), channel_id=1, source_target_pairs={{0,2},{1,3},{2,0},{3,1},{4,6},{5,7},{6,4},{7,5},{8,10},{9,11},{10,... | collective-permute-start | bytes 1572872 | tf_op jit(solution)/shard_map/ppermute | solution.py:289
  178.0 37.8 %collective-permute-start.26 = (bf16[8,2,2,64,128]{4,3,2,1,0:T(8,128)(2,1)}, bf16[8,2,2,64,128]{4,3,2,1,0:T(8,128)(2,1)}, u32[]{:S(2)}, u32[]{:S(2)}) collective-permute-start(bf16[8,2,2,64,128]{4,3,2,1,0:T(8,128)(2,1)} %get-tuple-element.127), channel_id=1, source_target_pairs={{0,3},{1,2},{2,1},{3,0},{4,7},{5,6},{6,5},{7,4},{8,11},{9,10},{10,... | collective-permute-start | bytes 1572872 | tf_op jit(solution)/shard_map/ppermute | solution.py:289
  212.2 32.5 %all-to-all-start.4 = ((bf16[4,2,12,32,256]{4,3,2,1,0:T(8,128)(2,1)}), bf16[4,2,12,32,256]{4,3,2,1,0:T(8,128)(2,1)S(1)}, u32[]{:S(2)}, u32[]{:S(2)}) async-start(bf16[4,2,12,32,256]{4,3,2,1,0:T(8,128)(2,1)} %pad_maximum_fusion.1), calls=%async_computation.4 | async-start | bytes 3145728 | tf_op jit(solution)/shard_map/all_to_all | solution.py:337
  244.7 31.7 %all-to-all-start.5 = ((bf16[4,2,10,32,256]{4,3,2,1,0:T(8,128)(2,1)}), bf16[4,2,10,32,256]{4,3,2,1,0:T(8,128)(2,1)S(1)}, u32[]{:S(2)}, u32[]{:S(2)}) async-start(bf16[4,2,10,32,256]{4,3,2,1,0:T(8,128)(2,1)} %pad_maximum_fusion.3), calls=%async_computation.5 | async-start | bytes 2621440 | tf_op jit(solution)/shard_map/all_to_all | solution.py:337
  251.1 31.6 %collective-permute-start.27 = (f32[16,128]{1,0:T(8,128)S(1)}, f32[16,128]{1,0:T(8,128)S(1)}, u32[]{:S(2)}, u32[]{:S(2)}) collective-permute-start(f32[16,128]{1,0:T(8,128)S(1)} %get-tuple-element.136), channel_id=1, source_target_pairs={{0,1},{1,0},{2,3},{3,2},{4,5},{5,4},{6,7},{7,6},{8,9},{9,8},{10,11... | collective-permute-start | bytes 24584 | tf_op jit(solution)/shard_map/ppermute | solution.py:289
  276.5 33.5 %all-to-all-start.6 = ((bf16[4,2,8,32,256]{4,3,2,1,0:T(8,128)(2,1)}), bf16[4,2,8,32,256]{4,3,2,1,0:T(8,128)(2,1)S(1)}, u32[]{:S(2)}, u32[]{:S(2)}) async-start(bf16[4,2,8,32,256]{4,3,2,1,0:T(8,128)(2,1)} %pad_maximum_fusion.5), calls=%async_computation.6 | async-start | bytes 2097152 | tf_op jit(solution)/shard_map/all_to_all | solution.py:337
  (54 other events, 816.8 us)

commit v5 on v4

--- a/solution.py
+++ b/solution.py
@@ -10,10 +10,9 @@
 from jax.sharding import PartitionSpec as P
 
 UP = 16
-QUAD = 4
-SHARES = (2, 4, 5, 6, 6, 5, 4)
-BEHIND = 2
-DETECT_FLOPS = 3_000_000_000
+SHARES = (2, 4, 5, 6, 7, 8)
+DIRECT = (False,) * 6
+DETECT_FLOPS = 1_600_000_000
 
 epsilon = 1e-05
 
@@ -75,11 +74,9 @@
                     out_ref[c, p, a] = formed[row : row + beams, p * samples : (p + 1) * samples]
 
 
-def detect_kernel(rows_count, me_ref, *refs):
-    high_ref, low_ref, order_ref, *refs = refs[2:]
-    columns = rows_count
+def detect_kernel(columns, me_ref, after_ref, before_ref, high_ref, low_ref, order_ref, *refs):
     formed_refs, out_refs, (sum_ref, rows_ref) = refs[:columns], refs[columns:-2], refs[-2:]
-    quad, channels, own, _ = out_refs[0].shape
+    owners, channels, own, _ = out_refs[0].shape
     _, pols, _, beams, samples = formed_refs[0].shape
     for c in range(channels):
         for r, formed_ref in enumerate(formed_refs):
@@ -113,30 +110,36 @@
         ordered = jnp.dot(
             order_ref[...], jnp.concatenate(stokes, axis=0), preferred_element_type=jnp.float32
         )
-        ordered = ordered.astype(jnp.bfloat16)
-        for r in range(ordered.shape[0] // own):
-            block = ordered[r * own : (r + 1) * own]
-            out_refs[r // quad][r % quad, c] = block
+        for d in range(owners * len(out_refs)):
+            block = ordered[d * own : (d + 1) * own].astype(jnp.bfloat16)
+            out_refs[d // owners][d % owners, c] = block
 
 
 def flag_kernel(layout, me_ref, group_ref, common_ref, mask_ref, *refs):
-    block_refs, out_ref, power_ref = refs[:-2], refs[-2], refs[-1]
-    beams, width = block_refs[0].shape[3:]
+    chunk_refs, out_ref, power_ref = refs[:-2], refs[-2], refs[-1]
+    beams, width = chunk_refs[0].shape[2:]
     samples = width // 2
+    channels = common_ref.shape[0]
     local = layout[-1][0] + layout[-1][1]
-    channels = common_ref.shape[0]
-    near = me_ref[1]
+    sources = channels // local
 
     def blocks(work, carry):
-        for (first, size), block_ref in zip(layout, block_refs):
-            fours = block_ref.shape[1]
-
-            def step(j, carry):
-                q, i = j // fours, j % fours
-                source = (near // QUAD * QUAD ^ i * QUAD) + q
-                return work(carry, block_ref.at[q, i], source * local + first, size)
-
-            carry = lax.fori_loop(0, QUAD * fours, step, carry)
+        refs = iter(chunk_refs)
+        whole, single = [], []
+        for first, size, count in layout:
+            if count == 1:
+                whole.append((first, size, next(refs)))
+            else:
+                single.extend((first, size, r, next(refs)) for r in range(count))
+
+        def step(s, carry):
+            for first, size, ref in whole:
+                carry = work(carry, ref.at[s], s * local + first, size)
+            return carry
+
+        carry = lax.fori_loop(0, sources, step, carry)
+        for first, size, r, ref in single:
+            carry = work(carry, ref.at[0], (me_ref[1] ^ r) * local + first, size)
         return carry
 
     def measure(level, block_ref, channel, size):
@@ -208,19 +211,20 @@
     )(me, after, table, *gains, real, imag)
 
 
-def detect(me, tables, order, formed, after, step, owners):
+def detect(me, tables, order, formed, after, step, owners, direct):
     columns = len(formed)
     per_chunk, pols, _, beams, samples = formed[0].shape
     steps = per_chunk // step
     own = columns * beams // owners
-    counts = [QUAD] * (owners // QUAD)
+    counts = [1] * owners if direct else [owners]
     block_spec = pl.BlockSpec((step, pols, 2, beams, samples), lambda i: (i, 0, 0, 0, 0))
     return pl.pallas_call(
         functools.partial(detect_kernel, columns),
         grid=(steps,),
         in_specs=[
             pl.BlockSpec(memory_space=pltpu.SMEM),
-            *[pl.BlockSpec(memory_space=pl.ANY)] * len(after),
+            pl.BlockSpec(memory_space=pl.ANY),
+            pl.BlockSpec(memory_space=pl.ANY),
             *[whole_spec(table) for table in tables],
             whole_spec(order),
             *[block_spec] * columns,
@@ -251,30 +255,31 @@
 
 
 def soft_flag(me, owned, common, mask, frame_count):
-    own, width = owned[0].shape[3:]
-    sizes = [one.shape[2] for one in owned]
-    layout = [(sum(sizes[:i]), size) for i, size in enumerate(sizes)]
+    own, width = owned[0][0].shape[2:]
+    sizes = [one[0].shape[1] for one in owned]
+    layout = [(sum(sizes[:i]), sizes[i], len(one)) for i, one in enumerate(owned)]
+    owned = [block for one in owned for block in one]
     samples = width // 2
     channels = common.shape[0]
-    rows = 16 if own % 16 == 0 else own
+    block = 16 if own % 16 == 0 else own
     group = np.kron(np.eye(samples // frame_count), np.ones((frame_count, frame_count)))
     group = jnp.asarray(np.concatenate([group, group]) / frame_count, jnp.bfloat16)
     return pl.pallas_call(
         functools.partial(flag_kernel, layout),
-        grid=(own // rows,),
+        grid=(own // block,),
         in_specs=[
             pl.BlockSpec(memory_space=pltpu.SMEM),
             whole_spec(group),
             whole_spec(common),
             whole_spec(mask),
             *[
-                pl.BlockSpec((*one.shape[:3], rows, width), lambda i: (0, 0, 0, i, 0))
+                pl.BlockSpec((*one.shape[:2], block, width), lambda i: (0, 0, i, 0))
                 for one in owned
             ],
         ],
-        out_specs=pl.BlockSpec((2, rows, channels * samples), lambda i: (0, i, 0)),
+        out_specs=pl.BlockSpec((2, block, channels * samples), lambda i: (0, i, 0)),
         out_shape=jax.ShapeDtypeStruct((2, own, channels * samples), jnp.bfloat16),
-        scratch_shapes=[pltpu.VMEM((channels, rows, samples), jnp.float32)],
+        scratch_shapes=[pltpu.VMEM((channels, block, samples), jnp.float32)],
         cost_estimate=pl.CostEstimate(
             flops=channels * own * samples * samples * 4,
             bytes_accessed=channels * own * samples * 8,
@@ -305,47 +310,43 @@
     table = jnp.asarray(beam_table(feeds, groups))
     near = lax.axis_index("chan")
     me = jnp.stack([mine, near]).astype(jnp.int32)
-    fours = [list(range(i, i + QUAD)) for i in range(0, owners, QUAD)]
     tables = [jnp.asarray(one) for one in spectral_tables(UP, frame_count, groups)]
     slots = beam_owner.shape[1]
     wanted = beam_owner[0].reshape(owners, slots // owners)
-    first_four = near // QUAD * QUAD
-    wanted = wanted[first_four ^ jnp.arange(owners, dtype=jnp.int32)].reshape(slots)
-    order = (wanted[:, None] == jnp.arange(slots, dtype=jnp.int32)[None, :]).astype(jnp.bfloat16)
+    orders = [
+        (one.reshape(slots, 1) == jnp.arange(slots, dtype=jnp.int32)).astype(jnp.bfloat16)
+        for one in (wanted, wanted[near ^ jnp.arange(owners, dtype=jnp.int32)])
+    ]
     mask = jnp.repeat(channel_mask.astype(jnp.float32), frame_count).reshape(channels, 1, samples)
     volts = (voltage_real, voltage_imag)
     turned, owned, sums = [], [], []
     after = me
-    for chunk in range(chunks + 2):
+    for chunk in range(chunks + 1):
         if chunk < chunks:
             formed = form(
                 me, after, table, gains, volts, firsts[chunk], sizes[chunk], step, groups
             )
             turned.append([swap(one, "grp", r) if r else one for r, one in enumerate(formed)])
             after = formed[0]
-        if 0 < chunk <= chunks:
-            before = owned[-BEHIND] if len(owned) >= BEHIND else me
-            *quads, part = detect(
-                me, tables, order, turned[chunk - 1], [after, before], step, owners
+        if chunk > 0:
+            direct = chunks == len(DIRECT) and DIRECT[chunk - 1]
+            before = owned[-2][-1] if len(owned) > 1 else me
+            *sent, part = detect(
+                me,
+                tables,
+                orders[direct],
+                turned[chunk - 1],
+                [after, before],
+                step,
+                owners,
+                direct,
             )
-            quads = [swap(one, "chan", QUAD * i) if i else one for i, one in enumerate(quads)]
+            if direct:
+                owned.append([swap(one, "chan", r) if r else one for r, one in enumerate(sent)])
+            else:
+                owned.append([lax.all_to_all(*sent, "chan", split_axis=0, concat_axis=0, tiled=True)])
+            sums.append(part.reshape(sizes[chunk - 1], samples))
             after = part
-        if chunk > 1:
-            if chunk <= chunks:
-                waiting, part = lax.optimization_barrier((waiting, part))
-            owned.append(
-                lax.all_to_all(
-                    jnp.stack(waiting, axis=1),
-                    "chan",
-                    split_axis=0,
-                    concat_axis=0,
-                    axis_index_groups=fours,
-                    tiled=True,
-                )
-            )
-        if 0 < chunk <= chunks:
-            waiting = quads
-            sums.append(part.reshape(sizes[chunk - 1], samples))
     common = jnp.concatenate(sums, axis=0).reshape(groups, local // groups, samples)
     mine_of = [common[mine ^ r] for r in range(groups)]
     common = mine_of[0]

time: 341 us -> 285 us (0.84)
  Pallas kernels: 130 us -> 111 us
  starting transfers between devices: 65.9 us -> 51.1 us
  other arithmetic: 13.3 us -> 1.36 us
  waiting for transfers between devices: 121 us -> 111 us
    all_to_all x7 -> x6, waiting for transfers between devices: 36 us -> 19.6 us  [body(): lax.all_to_all(*sent, 'chan', split_axis=0, concat_axis=0, tiled=True)]
    pallas_call x1, Pallas kernels: 28 us -> 13.3 us  [soft_flag(): pl.pallas_call(functools.partial(flag_kernel, layout), grid=(own // block...]
    ppermute x37 -> x27, starting transfers between devices: 37.6 us -> 24.8 us  [swap(): lax.ppermute(one, axis, [(i, i ^ apart) for i in range(lax.axis_size(axis...]
    another operation x7 -> x0, other arithmetic: 11.2 us -> none  [body(): jnp.stack(waiting, axis=1)]
    ppermute x37 -> x27, waiting for transfers between devices: 84.6 us -> 91.9 us  [swap(): lax.ppermute(one, axis, [(i, i ^ apart) for i in range(lax.axis_size(axis...]
    pallas_call x7 -> x6, Pallas kernels: 54.5 us -> 52.1 us  [detect(): pl.pallas_call(functools.partial(detect_kernel, columns), grid=(steps,),...]
    all_to_all x7 -> x6, starting transfers between devices: 28.4 us -> 26.3 us  [body(): lax.all_to_all(*sent, 'chan', split_axis=0, concat_axis=0, tiled=True)]
    pallas_call x7 -> x6, Pallas kernels: 47.7 us -> 45.7 us  [form(): pl.pallas_call(form_kernel, grid=(steps,), in_specs=[pl.BlockSpec(memory_...]
  transfers between devices with their start and end apart: 44 -> 33, of which waited for: 17 -> 18; matrix products, arithmetic and copies ran while one was open for 5% -> 1% of each run, Pallas kernels for 29% -> 33%
where the time goes in v5:
time: 285 us; the launch traced here: 283 us
  Pallas kernels  111 us (39%)
  waiting for transfers between devices  111 us (39%)
  starting transfers between devices  51.1 us (18%)
  local copies, waits for them, and re-layouts  7 us (2%)
    ppermute x27, waiting for transfers between devices, swap(): lax.ppermute(one, axis, [(i, i ^ apart) for i in range(lax.axis_size(axis...  91.9 us
    pallas_call x6, Pallas kernels, detect(): pl.pallas_call(functools.partial(detect_kernel, columns), grid=(steps,),...  52.1 us
    pallas_call x6, Pallas kernels, form(): pl.pallas_call(form_kernel, grid=(steps,), in_specs=[pl.BlockSpec(memory_...  45.7 us
    all_to_all x6, starting transfers between devices, body(): lax.all_to_all(*sent, 'chan', split_axis=0, concat_axis=0, tiled=True)  26.3 us
    ppermute x27, starting transfers between devices, swap(): lax.ppermute(one, axis, [(i, i ^ apart) for i in range(lax.axis_size(axis...  24.8 us
    all_to_all x6, waiting for transfers between devices, body(): lax.all_to_all(*sent, 'chan', split_axis=0, concat_axis=0, tiled=True)  19.6 us
    pallas_call x1, Pallas kernels, soft_flag(): pl.pallas_call(functools.partial(flag_kernel, layout), grid=(own // block...  13.3 us
  transfers between devices with their start and end apart: 33, of which 18 were waited for; matrix products, arithmetic and copies ran while one was open for 1% of the time, Pallas kernels for 33%

profile of v5, /device:TPU:0, one launch (start us, length us, event | category | flops | bytes accessed | tf_op | source)
XLA Modules:
  0.0 283.1 jit_solution(17214304134284800781)
XLA Ops:
  8.4 6.1 %form.7 = (bf16[8,2,2,64,128]{4,3,2,1,0:T(8,128)(2,1)}, bf16[8,2,2,64,128]{4,3,2,1,0:T(8,128)(2,1)}, bf16[8,2,2,64,128]{4,3,2,1,0:T(8,128)(2,1)}, bf16[8,2,2,64,128]{4,3,2,1,0:T(8,128)(2,1)}) custom-call(s32[2]{0:T(128)} %pad_add_fusion.me_ref.after_ref.before_ref, bf16[4,2,2,64,128]{4,3,2,1,0:T(8,128)(2,1)} %get-tuple-element.38.after_ref.refs_0_, ...), custom_call_target="tpu_custom_call" | custom-call | flops 1000 | bytes 1000 | tf_op jit(solution)/shard_map/form/pallas_call | solution.py:187
  21.5 4.5 %detect.6 = (bf16[8,4,32,256]{3,2,1,0:T(8,128)(2,1)}, f32[2,2,128]{2,1,0:T(2,128)}) custom-call(s32[2]{0:T(128)} %pad_add_fusion.me_ref.after_ref.before_ref, bf16[8,2,2,64,128]{4,3,2,1,0:T(8,128)(2,1)} %get-tuple-element.39.after_ref.refs_0_, s32[2]{0:T(128)} %pad_add_fusion.me_ref.after_ref.before_ref, bf16[256,256]{1,0:T(8,128)(2,1)} %constant.60.clone.high_ref, ...), custom_call_target="tpu_custom_call" | custom-call | flops 6400000000 | bytes 1000 | tf_op jit(solution)/shard_map/detect/pallas_call | solution.py:221
  26.0 5.8 %all-to-all-start = ((bf16[8,4,32,256]{3,2,1,0:T(8,128)(2,1)}), bf16[8,4,32,256]{3,2,1,0:T(8,128)(2,1)S(1)}, u32[]{:S(2)}, u32[]{:S(2)}) async-start(bf16[8,4,32,256]{3,2,1,0:T(8,128)(2,1)} %get-tuple-element.50), calls=%async_computation | async-start | bytes 1048576 | tf_op jit(solution)/shard_map/all_to_all | solution.py:347
  31.8 7.3 %form.8 = (bf16[10,2,2,64,128]{4,3,2,1,0:T(8,128)(2,1)}, bf16[10,2,2,64,128]{4,3,2,1,0:T(8,128)(2,1)}, bf16[10,2,2,64,128]{4,3,2,1,0:T(8,128)(2,1)}, bf16[10,2,2,64,128]{4,3,2,1,0:T(8,128)(2,1)}) custom-call(s32[2]{0:T(128)} %pad_add_fusion.me_ref.after_ref.before_ref, f32[2,2,128]{2,1,0:T(2,128)} %get-tuple-element.43.after_ref, ...), custom_call_target="tpu_custom_call" | custom-call | flops 1000 | bytes 1000 | tf_op jit(solution)/shard_map/form/pallas_call | solution.py:187
  44.1 7.0 %detect.7 = (bf16[8,8,32,256]{3,2,1,0:T(8,128)(2,1)}, f32[4,2,128]{2,1,0:T(2,128)}) custom-call(s32[2]{0:T(128)} %pad_add_fusion.me_ref.after_ref.before_ref, bf16[10,2,2,64,128]{4,3,2,1,0:T(8,128)(2,1)} %get-tuple-element.44.after_ref.refs_0_, s32[2]{0:T(128)} %pad_add_fusion.me_ref.after_ref.before_ref, bf16[256,256]{1,0:T(8,128)(2,1)} %constant.60.clone.high_ref, ...), custom_call_target="tpu_custom_call" | custom-call | flops 12800000000 | bytes 1000 | tf_op jit(solution)/shard_map/detect/pallas_call | solution.py:221
  51.1 5.8 %all-to-all-start.1 = ((bf16[8,8,32,256]{3,2,1,0:T(8,128)(2,1)}), bf16[8,8,32,256]{3,2,1,0:T(8,128)(2,1)S(1)}, u32[]{:S(2)}, u32[]{:S(2)}) async-start(bf16[8,8,32,256]{3,2,1,0:T(8,128)(2,1)} %get-tuple-element.56), calls=%async_computation.1 | async-start | bytes 2097152 | tf_op jit(solution)/shard_map/all_to_all | solution.py:347
  56.9 8.3 %form.9 = (bf16[12,2,2,64,128]{4,3,2,1,0:T(8,128)(2,1)}, bf16[12,2,2,64,128]{4,3,2,1,0:T(8,128)(2,1)}, bf16[12,2,2,64,128]{4,3,2,1,0:T(8,128)(2,1)}, bf16[12,2,2,64,128]{4,3,2,1,0:T(8,128)(2,1)}) custom-call(s32[2]{0:T(128)} %pad_add_fusion.me_ref.after_ref.before_ref, f32[4,2,128]{2,1,0:T(2,128)} %get-tuple-element.48.after_ref, ...), custom_call_target="tpu_custom_call" | custom-call | flops 1000 | bytes 1000 | tf_op jit(solution)/shard_map/form/pallas_call | solution.py:187
  71.4 8.3 %detect.8 = (bf16[8,10,32,256]{3,2,1,0:T(8,128)(2,1)}, f32[5,2,128]{2,1,0:T(2,128)}) custom-call(s32[2]{0:T(128)} %pad_add_fusion.me_ref.after_ref.before_ref, bf16[12,2,2,64,128]{4,3,2,1,0:T(8,128)(2,1)} %get-tuple-element.49.after_ref.refs_0_, bf16[8,4,32,256]{3,2,1,0:T(8,128)(2,1)} %copy-done.5, bf16[256,256]{1,0:T(8,128)(2,1)} %constant.60.clone.high_ref, ...), custom_call_target="tpu_custom_call" | custom-call | flops 16000000000 | bytes 1000 | tf_op jit(solution)/shard_map/detect/pallas_call | solution.py:221
  79.7 4.2 %all-to-all-done.1.before_ref.refs_1_ = bf16[8,8,32,256]{3,2,1,0:T(8,128)(2,1)S(1)} async-done(((bf16[8,8,32,256]{3,2,1,0:T(8,128)(2,1)}), bf16[8,8,32,256]{3,2,1,0:T(8,128)(2,1)S(1)}, u32[]{:S(2)}, u32[]{:S(2)}) %all-to-all-start.1) | async-done | bytes 1048608 | tf_op jit(solution)/shard_map/all_to_all | solution.py:347
  87.5 9.4 %form.10 = (bf16[14,2,2,64,128]{4,3,2,1,0:T(8,128)(2,1)}, bf16[14,2,2,64,128]{4,3,2,1,0:T(8,128)(2,1)}, bf16[14,2,2,64,128]{4,3,2,1,0:T(8,128)(2,1)}, bf16[14,2,2,64,128]{4,3,2,1,0:T(8,128)(2,1)}) custom-call(s32[2]{0:T(128)} %pad_add_fusion.me_ref.after_ref.before_ref, f32[5,2,128]{2,1,0:T(2,128)} %get-tuple-element.54.after_ref, ...), custom_call_target="tpu_custom_call" | custom-call | flops 1000 | bytes 1000 | tf_op jit(solution)/shard_map/form/pallas_call | solution.py:187
  98.9 6.2 %collective-permute-done.11.refs_3_ = bf16[12,2,2,64,128]{4,3,2,1,0:T(8,128)(2,1)} collective-permute-done((bf16[12,2,2,64,128]{4,3,2,1,0:T(8,128)(2,1)}, bf16[12,2,2,64,128]{4,3,2,1,0:T(8,128)(2,1)}, u32[]{:S(2)}, u32[]{:S(2)}) %collective-permute-start.11) | collective-permute-done | bytes 786464 | tf_op jit(solution)/shard_map/ppermute | solution.py:294
  105.1 9.5 %detect.9 = (bf16[8,12,32,256]{3,2,1,0:T(8,128)(2,1)}, f32[6,2,128]{2,1,0:T(2,128)}) custom-call(s32[2]{0:T(128)} %pad_add_fusion.me_ref.after_ref.before_ref, bf16[14,2,2,64,128]{4,3,2,1,0:T(8,128)(2,1)} %get-tuple-element.55.after_ref.refs_0_, bf16[8,8,32,256]{3,2,1,0:T(8,128)(2,1)} %copy-done.4, bf16[256,256]{1,0:T(8,128)(2,1)} %constant.60.clone.high_ref, ...), custom_call_target="tpu_custom_call" | custom-call | flops 19200000000 | bytes 1000 | tf_op jit(solution)/shard_map/detect/pallas_call | solution.py:221
  114.6 4.5 %all-to-all-done.2.before_ref.refs_2_ = bf16[8,10,32,256]{3,2,1,0:T(8,128)(2,1)S(1)} async-done(((bf16[8,10,32,256]{3,2,1,0:T(8,128)(2,1)}), bf16[8,10,32,256]{3,2,1,0:T(8,128)(2,1)S(1)}, u32[]{:S(2)}, u32[]{:S(2)}) %all-to-all-start.2) | async-done | bytes 1310752 | tf_op jit(solution)/shard_map/all_to_all | solution.py:347
  122.8 10.5 %form.11 = (bf16[16,2,2,64,128]{4,3,2,1,0:T(8,128)(2,1)}, bf16[16,2,2,64,128]{4,3,2,1,0:T(8,128)(2,1)}, bf16[16,2,2,64,128]{4,3,2,1,0:T(8,128)(2,1)}, bf16[16,2,2,64,128]{4,3,2,1,0:T(8,128)(2,1)}) custom-call(s32[2]{0:T(128)} %pad_add_fusion.me_ref.after_ref.before_ref, f32[6,2,128]{2,1,0:T(2,128)} %get-tuple-element.60.after_ref, ...), custom_call_target="tpu_custom_call" | custom-call | flops 1000 | bytes 1000 | tf_op jit(solution)/shard_map/form/pallas_call | solution.py:187
  135.2 9.2 %collective-permute-done.14.refs_3_ = bf16[14,2,2,64,128]{4,3,2,1,0:T(8,128)(2,1)} collective-permute-done((bf16[14,2,2,64,128]{4,3,2,1,0:T(8,128)(2,1)}, bf16[14,2,2,64,128]{4,3,2,1,0:T(8,128)(2,1)}, u32[]{:S(2)}, u32[]{:S(2)}) %collective-permute-start.14) | collective-permute-done | bytes 917536 | tf_op jit(solution)/shard_map/ppermute | solution.py:294
  144.4 10.8 %detect.10 = (bf16[8,14,32,256]{3,2,1,0:T(8,128)(2,1)}, f32[7,2,128]{2,1,0:T(2,128)}) custom-call(s32[2]{0:T(128)} %pad_add_fusion.me_ref.after_ref.before_ref, bf16[16,2,2,64,128]{4,3,2,1,0:T(8,128)(2,1)} %get-tuple-element.61.after_ref.refs_0_, bf16[8,10,32,256]{3,2,1,0:T(8,128)(2,1)} %copy-done.3, bf16[256,256]{1,0:T(8,128)(2,1)} %constant.60.clone.high_ref, ...), custom_call_target="tpu_custom_call" | custom-call | flops 22400000000 | bytes 1000 | tf_op jit(solution)/shard_map/detect/pallas_call | solution.py:221
  155.2 4.7 %all-to-all-done.3.before_ref.refs_3_ = bf16[8,12,32,256]{3,2,1,0:T(8,128)(2,1)S(1)} async-done(((bf16[8,12,32,256]{3,2,1,0:T(8,128)(2,1)}), bf16[8,12,32,256]{3,2,1,0:T(8,128)(2,1)S(1)}, u32[]{:S(2)}, u32[]{:S(2)}) %all-to-all-start.3) | async-done | bytes 1572896 | tf_op jit(solution)/shard_map/all_to_all | solution.py:347
  167.4 21.9 %collective-permute-done.17.refs_3_ = bf16[16,2,2,64,128]{4,3,2,1,0:T(8,128)(2,1)} collective-permute-done((bf16[16,2,2,64,128]{4,3,2,1,0:T(8,128)(2,1)}, bf16[16,2,2,64,128]{4,3,2,1,0:T(8,128)(2,1)}, u32[]{:S(2)}, u32[]{:S(2)}) %collective-permute-start.17) | collective-permute-done | bytes 1048608 | tf_op jit(solution)/shard_map/ppermute | solution.py:294
  189.4 12.0 %detect.11 = (bf16[8,16,32,256]{3,2,1,0:T(8,128)(2,1)}, f32[8,2,128]{2,1,0:T(2,128)}) custom-call(s32[2]{0:T(128)} %pad_add_fusion.me_ref.after_ref.before_ref, f32[7,2,128]{2,1,0:T(2,128)} %get-tuple-element.66.after_ref, bf16[8,12,32,256]{3,2,1,0:T(8,128)(2,1)} %copy-done.2, bf16[256,256]{1,0:T(8,128)(2,1)} %constant.60.clone.high_ref, ...), custom_call_target="tpu_custom_call" | custom-call | flops 25600000000 | bytes 1000 | tf_op jit(solution)/shard_map/detect/pallas_call | solution.py:221
  201.4 6.2 %all-to-all-done.4.refs_4_ = bf16[8,14,32,256]{3,2,1,0:T(8,128)(2,1)S(1)} async-done(((bf16[8,14,32,256]{3,2,1,0:T(8,128)(2,1)}), bf16[8,14,32,256]{3,2,1,0:T(8,128)(2,1)S(1)}, u32[]{:S(2)}, u32[]{:S(2)}) %all-to-all-start.4) | async-done | bytes 1835040 | tf_op jit(solution)/shard_map/all_to_all | solution.py:347
  220.7 9.1 %collective-permute-done.21 = f32[1,16,128]{2,1,0:T(8,128)S(1)} collective-permute-done((f32[1,16,128]{2,1,0:T(8,128)S(1)}, f32[1,16,128]{2,1,0:T(8,128)S(1)}, u32[]{:S(2)}, u32[]{:S(2)}) %collective-permute-start.21) | collective-permute-done | bytes 8224 | tf_op jit(solution)/shard_map/ppermute | solution.py:294
  231.6 16.5 %collective-permute-done.22 = f32[2,16,128]{2,1,0:T(8,128)S(1)} collective-permute-done((f32[2,16,128]{2,1,0:T(8,128)S(1)}, f32[2,16,128]{2,1,0:T(8,128)S(1)}, u32[]{:S(2)}, u32[]{:S(2)}) %collective-permute-start.22) | collective-permute-done | bytes 16416 | tf_op jit(solution)/shard_map/ppermute | solution.py:294
  252.4 9.8 %collective-permute-done.23 = f32[4,16,128]{2,1,0:T(8,128)S(1)} collective-permute-done((f32[4,16,128]{2,1,0:T(8,128)S(1)}, f32[4,16,128]{2,1,0:T(8,128)S(1)}, u32[]{:S(2)}, u32[]{:S(2)}) %collective-permute-start.23) | collective-permute-done | bytes 32800 | tf_op jit(solution)/shard_map/ppermute | solution.py:294
  269.7 13.3 %flag.1 = bf16[2,32,65536]{2,1,0:T(8,128)(2,1)} custom-call(s32[2]{0:T(128)} %pad_add_fusion.me_ref.after_ref.before_ref, bf16[256,128]{1,0:T(8,128)(2,1)} %constant.62.clone.group_ref, f32[512,1,128]{2,1,0:T(1,128)} %bitcast.44, f32[512,1,128]{2,1,0:T(1,128)} %copy.17.mask_ref, bf16[8,4,32,256]{3,2,1,0:T(8,128)(2,1)} %copy-done.5, ...), custom_call_target="tpu_custom_call" | custom-call | flops 1073741824 | bytes 16777216 | tf_op jit(solution)/shard_map/flag/pallas_call | solution.py:267
  (125 shorter events, 70.9 us)
Async XLA Ops:
  8.3 12.6 %collective-permute-start.2 = (bf16[4,2,2,64,128]{4,3,2,1,0:T(8,128)(2,1)}, bf16[4,2,2,64,128]{4,3,2,1,0:T(8,128)(2,1)S(1)}, u32[]{:S(2)}, u32[]{:S(2)}) collective-permute-start(bf16[4,2,2,64,128]{4,3,2,1,0:T(8,128)(2,1)} %get-tuple-element.42), channel_id=1, source_target_pairs={{0,3},{1,2},{2,1},{3,0},{4,7},{5,6},{6,5},{7,4},{8,11},{9,10},{10,... | collective-permute-start | bytes 786440 | tf_op jit(solution)/shard_map/ppermute | solution.py:294
  14.5 26.6 %collective-permute-start.3 = (bf16[8,2,2,64,128]{4,3,2,1,0:T(8,128)(2,1)}, bf16[8,2,2,64,128]{4,3,2,1,0:T(8,128)(2,1)S(1)}, u32[]{:S(2)}, u32[]{:S(2)}) collective-permute-start(bf16[8,2,2,64,128]{4,3,2,1,0:T(8,128)(2,1)} %get-tuple-element.45), channel_id=1, source_target_pairs={{0,1},{1,0},{2,3},{3,2},{4,5},{5,4},{6,7},{7,6},{8,9},{9,8},{10,11... | collective-permute-start | bytes 1572872 | tf_op jit(solution)/shard_map/ppermute | solution.py:294
  14.7 26.4 %collective-permute-start.4 = (bf16[8,2,2,64,128]{4,3,2,1,0:T(8,128)(2,1)}, bf16[8,2,2,64,128]{4,3,2,1,0:T(8,128)(2,1)S(1)}, u32[]{:S(2)}, u32[]{:S(2)}) collective-permute-start(bf16[8,2,2,64,128]{4,3,2,1,0:T(8,128)(2,1)} %get-tuple-element.46), channel_id=1, source_target_pairs={{0,2},{1,3},{2,0},{3,1},{4,6},{5,7},{6,4},{7,5},{8,10},{9,11},{10,... | collective-permute-start | bytes 1572872 | tf_op jit(solution)/shard_map/ppermute | solution.py:294
  17.4 25.9 %collective-permute-start.5 = (bf16[8,2,2,64,128]{4,3,2,1,0:T(8,128)(2,1)}, bf16[8,2,2,64,128]{4,3,2,1,0:T(8,128)(2,1)S(1)}, u32[]{:S(2)}, u32[]{:S(2)}) collective-permute-start(bf16[8,2,2,64,128]{4,3,2,1,0:T(8,128)(2,1)} %get-tuple-element.47), channel_id=1, source_target_pairs={{0,3},{1,2},{2,1},{3,0},{4,7},{5,6},{6,5},{7,4},{8,11},{9,10},{10,... | collective-permute-start | bytes 1572872 | tf_op jit(solution)/shard_map/ppermute | solution.py:294
  26.0 25.1 %all-to-all-start = ((bf16[8,4,32,256]{3,2,1,0:T(8,128)(2,1)}), bf16[8,4,32,256]{3,2,1,0:T(8,128)(2,1)S(1)}, u32[]{:S(2)}, u32[]{:S(2)}) async-start(bf16[8,4,32,256]{3,2,1,0:T(8,128)(2,1)} %get-tuple-element.50), calls=%async_computation | async-start | bytes 1048576 | tf_op jit(solution)/shard_map/all_to_all | solution.py:347
  39.1 28.5 %collective-permute-start.6 = (bf16[10,2,2,64,128]{4,3,2,1,0:T(8,128)(2,1)}, bf16[10,2,2,64,128]{4,3,2,1,0:T(8,128)(2,1)S(1)}, u32[]{:S(2)}, u32[]{:S(2)}) collective-permute-start(bf16[10,2,2,64,128]{4,3,2,1,0:T(8,128)(2,1)} %get-tuple-element.51), channel_id=1, source_target_pairs={{0,1},{1,0},{2,3},{3,2},{4,5},{5,4},{6,7},{7,6},{8,9},{9,8},{10,11... | collective-permute-start | bytes 1966088 | tf_op jit(solution)/shard_map/ppermute | solution.py:294
  39.5 28.0 %collective-permute-start.7 = (bf16[10,2,2,64,128]{4,3,2,1,0:T(8,128)(2,1)}, bf16[10,2,2,64,128]{4,3,2,1,0:T(8,128)(2,1)}, u32[]{:S(2)}, u32[]{:S(2)}) collective-permute-start(bf16[10,2,2,64,128]{4,3,2,1,0:T(8,128)(2,1)} %get-tuple-element.52), channel_id=1, source_target_pairs={{0,2},{1,3},{2,0},{3,1},{4,6},{5,7},{6,4},{7,5},{8,10},{9,11},{10,... | collective-permute-start | bytes 1966088 | tf_op jit(solution)/shard_map/ppermute | solution.py:294
  41.1 30.4 %collective-permute-start.8 = (bf16[10,2,2,64,128]{4,3,2,1,0:T(8,128)(2,1)}, bf16[10,2,2,64,128]{4,3,2,1,0:T(8,128)(2,1)}, u32[]{:S(2)}, u32[]{:S(2)}) collective-permute-start(bf16[10,2,2,64,128]{4,3,2,1,0:T(8,128)(2,1)} %get-tuple-element.53), channel_id=1, source_target_pairs={{0,3},{1,2},{2,1},{3,0},{4,7},{5,6},{6,5},{7,4},{8,11},{9,10},{10,... | collective-permute-start | bytes 1966088 | tf_op jit(solution)/shard_map/ppermute | solution.py:294
  51.1 32.7 %all-to-all-start.1 = ((bf16[8,8,32,256]{3,2,1,0:T(8,128)(2,1)}), bf16[8,8,32,256]{3,2,1,0:T(8,128)(2,1)S(1)}, u32[]{:S(2)}, u32[]{:S(2)}) async-start(bf16[8,8,32,256]{3,2,1,0:T(8,128)(2,1)} %get-tuple-element.56), calls=%async_computation.1 | async-start | bytes 2097152 | tf_op jit(solution)/shard_map/all_to_all | solution.py:347
  65.3 33.3 %collective-permute-start.9 = (bf16[12,2,2,64,128]{4,3,2,1,0:T(8,128)(2,1)}, bf16[12,2,2,64,128]{4,3,2,1,0:T(8,128)(2,1)S(1)}, u32[]{:S(2)}, u32[]{:S(2)}) collective-permute-start(bf16[12,2,2,64,128]{4,3,2,1,0:T(8,128)(2,1)} %get-tuple-element.57), channel_id=1, source_target_pairs={{0,1},{1,0},{2,3},{3,2},{4,5},{5,4},{6,7},{7,6},{8,9},{9,8},{10,11... | collective-permute-start | bytes 2359304 | tf_op jit(solution)/shard_map/ppermute | solution.py:294
  66.0 32.8 %collective-permute-start.10 = (bf16[12,2,2,64,128]{4,3,2,1,0:T(8,128)(2,1)}, bf16[12,2,2,64,128]{4,3,2,1,0:T(8,128)(2,1)}, u32[]{:S(2)}, u32[]{:S(2)}) collective-permute-start(bf16[12,2,2,64,128]{4,3,2,1,0:T(8,128)(2,1)} %get-tuple-element.58), channel_id=1, source_target_pairs={{0,2},{1,3},{2,0},{3,1},{4,6},{5,7},{6,4},{7,5},{8,10},{9,11},{10,... | collective-permute-start | bytes 2359304 | tf_op jit(solution)/shard_map/ppermute | solution.py:294
  67.6 37.5 %collective-permute-start.11 = (bf16[12,2,2,64,128]{4,3,2,1,0:T(8,128)(2,1)}, bf16[12,2,2,64,128]{4,3,2,1,0:T(8,128)(2,1)}, u32[]{:S(2)}, u32[]{:S(2)}) collective-permute-start(bf16[12,2,2,64,128]{4,3,2,1,0:T(8,128)(2,1)} %get-tuple-element.59), channel_id=1, source_target_pairs={{0,3},{1,2},{2,1},{3,0},{4,7},{5,6},{6,5},{7,4},{8,11},{9,10},{10,... | collective-permute-start | bytes 2359304 | tf_op jit(solution)/shard_map/ppermute | solution.py:294
  83.9 35.3 %all-to-all-start.2 = ((bf16[8,10,32,256]{3,2,1,0:T(8,128)(2,1)}), bf16[8,10,32,256]{3,2,1,0:T(8,128)(2,1)S(1)}, u32[]{:S(2)}, u32[]{:S(2)}) async-start(bf16[8,10,32,256]{3,2,1,0:T(8,128)(2,1)} %get-tuple-element.62), calls=%async_computation.2 | async-start | bytes 2621440 | tf_op jit(solution)/shard_map/all_to_all | solution.py:347
  96.9 38.0 %collective-permute-start.12 = (bf16[14,2,2,64,128]{4,3,2,1,0:T(8,128)(2,1)}, bf16[14,2,2,64,128]{4,3,2,1,0:T(8,128)(2,1)}, u32[]{:S(2)}, u32[]{:S(2)}) collective-permute-start(bf16[14,2,2,64,128]{4,3,2,1,0:T(8,128)(2,1)} %get-tuple-element.63), channel_id=1, source_target_pairs={{0,1},{1,0},{2,3},{3,2},{4,5},{5,4},{6,7},{7,6},{8,9},{9,8},{10,11... | collective-permute-start | bytes 2752520 | tf_op jit(solution)/shard_map/ppermute | solution.py:294
  97.0 38.2 %collective-permute-start.13 = (bf16[14,2,2,64,128]{4,3,2,1,0:T(8,128)(2,1)}, bf16[14,2,2,64,128]{4,3,2,1,0:T(8,128)(2,1)}, u32[]{:S(2)}, u32[]{:S(2)}) collective-permute-start(bf16[14,2,2,64,128]{4,3,2,1,0:T(8,128)(2,1)} %get-tuple-element.64), channel_id=1, source_target_pairs={{0,2},{1,3},{2,0},{3,1},{4,6},{5,7},{6,4},{7,5},{8,10},{9,11},{10,... | collective-permute-start | bytes 2752520 | tf_op jit(solution)/shard_map/ppermute | solution.py:294
  98.6 45.8 %collective-permute-start.14 = (bf16[14,2,2,64,128]{4,3,2,1,0:T(8,128)(2,1)}, bf16[14,2,2,64,128]{4,3,2,1,0:T(8,128)(2,1)}, u32[]{:S(2)}, u32[]{:S(2)}) collective-permute-start(bf16[14,2,2,64,128]{4,3,2,1,0:T(8,128)(2,1)} %get-tuple-element.65), channel_id=1, source_target_pairs={{0,3},{1,2},{2,1},{3,0},{4,7},{5,6},{6,5},{7,4},{8,11},{9,10},{10,... | collective-permute-start | bytes 2752520 | tf_op jit(solution)/shard_map/ppermute | solution.py:294
  119.1 40.8 %all-to-all-start.3 = ((bf16[8,12,32,256]{3,2,1,0:T(8,128)(2,1)}), bf16[8,12,32,256]{3,2,1,0:T(8,128)(2,1)S(1)}, u32[]{:S(2)}, u32[]{:S(2)}) async-start(bf16[8,12,32,256]{3,2,1,0:T(8,128)(2,1)} %get-tuple-element.67), calls=%async_computation.3 | async-start | bytes 3145728 | tf_op jit(solution)/shard_map/all_to_all | solution.py:347
  133.3 31.6 %collective-permute-start.15 = (bf16[16,2,2,64,128]{4,3,2,1,0:T(8,128)(2,1)}, bf16[16,2,2,64,128]{4,3,2,1,0:T(8,128)(2,1)}, u32[]{:S(2)}, u32[]{:S(2)}) collective-permute-start(bf16[16,2,2,64,128]{4,3,2,1,0:T(8,128)(2,1)} %get-tuple-element.68), channel_id=1, source_target_pairs={{0,1},{1,0},{2,3},{3,2},{4,5},{5,4},{6,7},{7,6},{8,9},{9,8},{10,11... | collective-permute-start | bytes 3145736 | tf_op jit(solution)/shard_map/ppermute | solution.py:294
  133.4 34.1 %collective-permute-start.16 = (bf16[16,2,2,64,128]{4,3,2,1,0:T(8,128)(2,1)}, bf16[16,2,2,64,128]{4,3,2,1,0:T(8,128)(2,1)}, u32[]{:S(2)}, u32[]{:S(2)}) collective-permute-start(bf16[16,2,2,64,128]{4,3,2,1,0:T(8,128)(2,1)} %get-tuple-element.69), channel_id=1, source_target_pairs={{0,2},{1,3},{2,0},{3,1},{4,6},{5,7},{6,4},{7,5},{8,10},{9,11},{10,... | collective-permute-start | bytes 3145736 | tf_op jit(solution)/shard_map/ppermute | solution.py:294
  135.0 54.4 %collective-permute-start.17 = (bf16[16,2,2,64,128]{4,3,2,1,0:T(8,128)(2,1)}, bf16[16,2,2,64,128]{4,3,2,1,0:T(8,128)(2,1)}, u32[]{:S(2)}, u32[]{:S(2)}) collective-permute-start(bf16[16,2,2,64,128]{4,3,2,1,0:T(8,128)(2,1)} %get-tuple-element.70), channel_id=1, source_target_pairs={{0,3},{1,2},{2,1},{3,0},{4,7},{5,6},{6,5},{7,4},{8,11},{9,10},{10,... | collective-permute-start | bytes 3145736 | tf_op jit(solution)/shard_map/ppermute | solution.py:294
  161.1 46.5 %all-to-all-start.4 = ((bf16[8,14,32,256]{3,2,1,0:T(8,128)(2,1)}), bf16[8,14,32,256]{3,2,1,0:T(8,128)(2,1)S(1)}, u32[]{:S(2)}, u32[]{:S(2)}) async-start(bf16[8,14,32,256]{3,2,1,0:T(8,128)(2,1)} %get-tuple-element.72), calls=%async_computation.4 | async-start | bytes 3670016 | tf_op jit(solution)/shard_map/all_to_all | solution.py:347
  208.9 59.4 %all-to-all-start.5 = ((bf16[8,16,32,256]{3,2,1,0:T(8,128)(2,1)}), bf16[8,16,32,256]{3,2,1,0:T(8,128)(2,1)S(1)}, u32[]{:S(2)}, u32[]{:S(2)}) async-start(bf16[8,16,32,256]{3,2,1,0:T(8,128)(2,1)} %get-tuple-element.73), calls=%async_computation.5 | async-start | bytes 4194304 | tf_op jit(solution)/shard_map/all_to_all | solution.py:347
  229.9 18.2 %collective-permute-start.22 = (f32[2,16,128]{2,1,0:T(8,128)S(1)}, f32[2,16,128]{2,1,0:T(8,128)S(1)}, u32[]{:S(2)}, u32[]{:S(2)}) collective-permute-start(f32[2,16,128]{2,1,0:T(8,128)S(1)} %maximum_select_fusion.3), channel_id=1, source_target_pairs={{0,8},{4,12},{8,0},{12,4},{16,24},{20,28},{24,16},{28,20},{1,9},{5... | collective-permute-start | bytes 49160 | tf_op jit(solution)/shard_map/ppermute | solution.py:294
  248.1 14.2 %collective-permute-start.23 = (f32[4,16,128]{2,1,0:T(8,128)S(1)}, f32[4,16,128]{2,1,0:T(8,128)S(1)}, u32[]{:S(2)}, u32[]{:S(2)}) collective-permute-start(f32[4,16,128]{2,1,0:T(8,128)S(1)} %bitcast.51), channel_id=1, source_target_pairs={{0,16},{4,20},{8,24},{12,28},{16,0},{20,4},{24,8},{28,12},{1,17},{... | collective-permute-start | bytes 98312 | tf_op jit(solution)/shard_map/ppermute | solution.py:294
  (33 other events, 241.7 us)

commit v6 on v5

--- a/solution.py
+++ b/solution.py
@@ -11,7 +11,7 @@
 
 UP = 16
 SHARES = (2, 4, 5, 6, 7, 8)
-DIRECT = (False,) * 6
+DIRECT = (False, False, False, False, False, False)
 DETECT_FLOPS = 1_600_000_000
 
 epsilon = 1e-05
@@ -74,7 +74,8 @@
                     out_ref[c, p, a] = formed[row : row + beams, p * samples : (p + 1) * samples]
 
 
-def detect_kernel(columns, me_ref, after_ref, before_ref, high_ref, low_ref, order_ref, *refs):
+def detect_kernel(columns, ignored, me_ref, *refs):
+    high_ref, low_ref, order_ref, *refs = refs[ignored:]
     formed_refs, out_refs, (sum_ref, rows_ref) = refs[:columns], refs[columns:-2], refs[-2:]
     owners, channels, own, _ = out_refs[0].shape
     _, pols, _, beams, samples = formed_refs[0].shape
@@ -219,12 +220,11 @@
     counts = [1] * owners if direct else [owners]
     block_spec = pl.BlockSpec((step, pols, 2, beams, samples), lambda i: (i, 0, 0, 0, 0))
     return pl.pallas_call(
-        functools.partial(detect_kernel, columns),
+        functools.partial(detect_kernel, columns, len(after)),
         grid=(steps,),
         in_specs=[
             pl.BlockSpec(memory_space=pltpu.SMEM),
-            pl.BlockSpec(memory_space=pl.ANY),
-            pl.BlockSpec(memory_space=pl.ANY),
+            *[pl.BlockSpec(memory_space=pl.ANY)] * len(after),
             *[whole_spec(table) for table in tables],
             whole_spec(order),
             *[block_spec] * columns,
@@ -330,36 +330,36 @@
             after = formed[0]
         if chunk > 0:
             direct = chunks == len(DIRECT) and DIRECT[chunk - 1]
-            before = owned[-2][-1] if len(owned) > 1 else me
+            before = owned[-2] if len(owned) > 1 else []
             *sent, part = detect(
                 me,
                 tables,
                 orders[direct],
                 turned[chunk - 1],
-                [after, before],
+                [after, *before],
                 step,
                 owners,
                 direct,
             )
+            sums.append(part.reshape(sizes[chunk - 1], samples))
+            after = part
+            if chunk == chunks:
+                common = jnp.concatenate(sums, axis=0).reshape(groups, local // groups, samples)
+                parts = [common[mine ^ r] for r in range(groups)]
+                common = parts[0]
+                for r in range(1, groups):
+                    common = common + swap(parts[r], "grp", r)
+                common = common / float(feeds * groups)
+                common_piece = common.reshape(-1)
+                common, *sent = lax.optimization_barrier((common, *sent))
             if direct:
                 owned.append([swap(one, "chan", r) if r else one for r, one in enumerate(sent)])
             else:
                 owned.append([lax.all_to_all(*sent, "chan", split_axis=0, concat_axis=0, tiled=True)])
-            sums.append(part.reshape(sizes[chunk - 1], samples))
-            after = part
-    common = jnp.concatenate(sums, axis=0).reshape(groups, local // groups, samples)
-    mine_of = [common[mine ^ r] for r in range(groups)]
-    common = mine_of[0]
-    for r in range(1, groups):
-        common = common + swap(mine_of[r], "grp", r)
-    common = common / float(feeds * groups)
-    common_piece = common.reshape(-1)
-    shared = common[None]
-    for bit in range(owners.bit_length() - 1):
-        other = swap(shared, "chan", 1 << bit)
-        low = (near >> bit) % 2 == 0
-        shared = jnp.where(low, jnp.stack([shared, other]), jnp.stack([other, shared]))
-        shared = shared.reshape(-1, local // groups, samples)
+    shared = jnp.zeros((owners, local // groups, samples), jnp.float32)
+    for r in range(owners):
+        other = swap(common, "chan", r) if r else common
+        shared = lax.dynamic_update_index_in_dim(shared, other, near ^ r, 0)
     common = jnp.zeros((owners, groups, local // groups, samples), jnp.float32)
     for r in range(groups):
         other = swap(shared, "grp", r) if r else shared

time: 285 us -> 287 us (level)
  starting transfers between devices: 51.1 us -> 60.6 us
  waiting for transfers between devices: 111 us -> 103 us
    ppermute x27 -> x31, starting transfers between devices: 24.8 us -> 32.2 us  [swap(): lax.ppermute(one, axis, [(i, i ^ apart) for i in range(lax.axis_size(axis...]
    all_to_all x6, waiting for transfers between devices: 19.6 us -> 13.4 us  [body(): lax.all_to_all(*sent, 'chan', split_axis=0, concat_axis=0, tiled=True)]
    ppermute x27 -> x31, waiting for transfers between devices: 91.9 us -> 89.6 us  [swap(): lax.ppermute(one, axis, [(i, i ^ apart) for i in range(lax.axis_size(axis...]
  transfers between devices with their start and end apart: 33 -> 37, of which waited for: 18 -> 19; matrix products, arithmetic and copies ran while one was open for 1% -> 1% of each run, Pallas kernels for 33% -> 33%
where the time goes in v6:
time: 287 us; the launch traced here: 285 us
  Pallas kernels  111 us (39%)
  waiting for transfers between devices  103 us (36%)
  starting transfers between devices  60.6 us (21%)
  local copies, waits for them, and re-layouts  7.79 us (3%)
    ppermute x31, waiting for transfers between devices, swap(): lax.ppermute(one, axis, [(i, i ^ apart) for i in range(lax.axis_size(axis...  89.6 us
    pallas_call x6, Pallas kernels, detect(): pl.pallas_call(functools.partial(detect_kernel, columns, len(after)), gri...  52.1 us
    pallas_call x6, Pallas kernels, form(): pl.pallas_call(form_kernel, grid=(steps,), in_specs=[pl.BlockSpec(memory_...  45.7 us
    ppermute x31, starting transfers between devices, swap(): lax.ppermute(one, axis, [(i, i ^ apart) for i in range(lax.axis_size(axis...  32.2 us
    all_to_all x6, starting transfers between devices, body(): lax.all_to_all(*sent, 'chan', split_axis=0, concat_axis=0, tiled=True)  28.5 us
    all_to_all x6, waiting for transfers between devices, body(): lax.all_to_all(*sent, 'chan', split_axis=0, concat_axis=0, tiled=True)  13.4 us
    pallas_call x1, Pallas kernels, soft_flag(): pl.pallas_call(functools.partial(flag_kernel, layout), grid=(own // block...  13.3 us
  transfers between devices with their start and end apart: 37, of which 19 were waited for; matrix products, arithmetic and copies ran while one was open for 1% of the time, Pallas kernels for 33%

profile of v6, /device:TPU:0, one launch (start us, length us, event | category | flops | bytes accessed | tf_op | source)
XLA Modules:
  0.0 285.0 jit_solution(10896924750591203489)
XLA Ops:
  8.4 6.1 %form.7 = (bf16[8,2,2,64,128]{4,3,2,1,0:T(8,128)(2,1)}, bf16[8,2,2,64,128]{4,3,2,1,0:T(8,128)(2,1)}, bf16[8,2,2,64,128]{4,3,2,1,0:T(8,128)(2,1)}, bf16[8,2,2,64,128]{4,3,2,1,0:T(8,128)(2,1)}) custom-call(s32[2]{0:T(128)} %pad_add_fusion.me_ref.after_ref, bf16[4,2,2,64,128]{4,3,2,1,0:T(8,128)(2,1)} %get-tuple-element.40.after_ref.refs_4_, ...), custom_call_target="tpu_custom_call" | custom-call | flops 1000 | bytes 1000 | tf_op jit(solution)/shard_map/form/pallas_call | solution.py:188
  21.6 4.5 %detect.6 = (bf16[8,4,32,256]{3,2,1,0:T(8,128)(2,1)}, f32[2,2,128]{2,1,0:T(2,128)}) custom-call(s32[2]{0:T(128)} %pad_add_fusion.me_ref.after_ref, bf16[8,2,2,64,128]{4,3,2,1,0:T(8,128)(2,1)} %get-tuple-element.41.refs_0_.refs_4_, bf16[256,256]{1,0:T(8,128)(2,1)} %constant.69.clone.refs_1_.refs_2_, bf16[256,256]{1,0:T(8,128)(2,1)} %constant.70.clone.refs_2_.refs_3_, ...), custom_call_target="tpu_custom_call" | custom-call | flops 6400000000 | bytes 1000 | tf_op jit(solution)/shard_map/detect/pallas_call | solution.py:222
  26.1 5.8 %all-to-all-start = ((bf16[8,4,32,256]{3,2,1,0:T(8,128)(2,1)}), bf16[8,4,32,256]{3,2,1,0:T(8,128)(2,1)S(1)}, u32[]{:S(2)}, u32[]{:S(2)}) async-start(bf16[8,4,32,256]{3,2,1,0:T(8,128)(2,1)} %get-tuple-element.52), calls=%async_computation | async-start | bytes 1048576 | tf_op jit(solution)/shard_map/all_to_all | solution.py:358
  31.9 7.3 %form.8 = (bf16[10,2,2,64,128]{4,3,2,1,0:T(8,128)(2,1)}, bf16[10,2,2,64,128]{4,3,2,1,0:T(8,128)(2,1)}, bf16[10,2,2,64,128]{4,3,2,1,0:T(8,128)(2,1)}, bf16[10,2,2,64,128]{4,3,2,1,0:T(8,128)(2,1)}) custom-call(s32[2]{0:T(128)} %pad_add_fusion.me_ref.after_ref, f32[2,2,128]{2,1,0:T(2,128)} %get-tuple-element.45.after_ref, ...), custom_call_target="tpu_custom_call" | custom-call | flops 1000 | bytes 1000 | tf_op jit(solution)/shard_map/form/pallas_call | solution.py:188
  44.2 7.0 %detect.7 = (bf16[8,8,32,256]{3,2,1,0:T(8,128)(2,1)}, f32[4,2,128]{2,1,0:T(2,128)}) custom-call(s32[2]{0:T(128)} %pad_add_fusion.me_ref.after_ref, bf16[10,2,2,64,128]{4,3,2,1,0:T(8,128)(2,1)} %get-tuple-element.46.refs_0_.refs_5_, bf16[256,256]{1,0:T(8,128)(2,1)} %constant.69.clone.refs_1_.refs_2_, bf16[256,256]{1,0:T(8,128)(2,1)} %constant.70.clone.refs_2_.refs_3_, ...), custom_call_target="tpu_custom_call" | custom-call | flops 12800000000 | bytes 1000 | tf_op jit(solution)/shard_map/detect/pallas_call | solution.py:222
  51.2 5.8 %all-to-all-start.1 = ((bf16[8,8,32,256]{3,2,1,0:T(8,128)(2,1)}), bf16[8,8,32,256]{3,2,1,0:T(8,128)(2,1)S(1)}, u32[]{:S(2)}, u32[]{:S(2)}) async-start(bf16[8,8,32,256]{3,2,1,0:T(8,128)(2,1)} %get-tuple-element.58), calls=%async_computation.1 | async-start | bytes 2097152 | tf_op jit(solution)/shard_map/all_to_all | solution.py:358
  57.0 8.3 %form.9 = (bf16[12,2,2,64,128]{4,3,2,1,0:T(8,128)(2,1)}, bf16[12,2,2,64,128]{4,3,2,1,0:T(8,128)(2,1)}, bf16[12,2,2,64,128]{4,3,2,1,0:T(8,128)(2,1)}, bf16[12,2,2,64,128]{4,3,2,1,0:T(8,128)(2,1)}) custom-call(s32[2]{0:T(128)} %pad_add_fusion.me_ref.after_ref, f32[4,2,128]{2,1,0:T(2,128)} %get-tuple-element.50.after_ref, ...), custom_call_target="tpu_custom_call" | custom-call | flops 1000 | bytes 1000 | tf_op jit(solution)/shard_map/form/pallas_call | solution.py:188
  71.5 8.3 %detect.8 = (bf16[8,10,32,256]{3,2,1,0:T(8,128)(2,1)}, f32[5,2,128]{2,1,0:T(2,128)}) custom-call(s32[2]{0:T(128)} %pad_add_fusion.me_ref.after_ref, bf16[12,2,2,64,128]{4,3,2,1,0:T(8,128)(2,1)} %get-tuple-element.51.refs_0_.refs_5_, bf16[8,4,32,256]{3,2,1,0:T(8,128)(2,1)} %copy-done.5, bf16[256,256]{1,0:T(8,128)(2,1)} %constant.69.clone.refs_1_.refs_2_, ...), custom_call_target="tpu_custom_call" | custom-call | flops 16000000000 | bytes 1000 | tf_op jit(solution)/shard_map/detect/pallas_call | solution.py:222
  87.6 9.4 %form.10 = (bf16[14,2,2,64,128]{4,3,2,1,0:T(8,128)(2,1)}, bf16[14,2,2,64,128]{4,3,2,1,0:T(8,128)(2,1)}, bf16[14,2,2,64,128]{4,3,2,1,0:T(8,128)(2,1)}, bf16[14,2,2,64,128]{4,3,2,1,0:T(8,128)(2,1)}) custom-call(s32[2]{0:T(128)} %pad_add_fusion.me_ref.after_ref, f32[5,2,128]{2,1,0:T(2,128)} %get-tuple-element.56.after_ref, ...), custom_call_target="tpu_custom_call" | custom-call | flops 1000 | bytes 1000 | tf_op jit(solution)/shard_map/form/pallas_call | solution.py:188
  99.0 6.2 %collective-permute-done.11.refs_8_ = bf16[12,2,2,64,128]{4,3,2,1,0:T(8,128)(2,1)} collective-permute-done((bf16[12,2,2,64,128]{4,3,2,1,0:T(8,128)(2,1)}, bf16[12,2,2,64,128]{4,3,2,1,0:T(8,128)(2,1)}, u32[]{:S(2)}, u32[]{:S(2)}) %collective-permute-start.11) | collective-permute-done | bytes 786464 | tf_op jit(solution)/shard_map/ppermute | solution.py:294
  105.2 9.5 %detect.9 = (bf16[8,12,32,256]{3,2,1,0:T(8,128)(2,1)}, f32[6,2,128]{2,1,0:T(2,128)}) custom-call(s32[2]{0:T(128)} %pad_add_fusion.me_ref.after_ref, bf16[14,2,2,64,128]{4,3,2,1,0:T(8,128)(2,1)} %get-tuple-element.57.refs_0_.refs_5_, bf16[8,8,32,256]{3,2,1,0:T(8,128)(2,1)} %copy-done.4, bf16[256,256]{1,0:T(8,128)(2,1)} %constant.69.clone.refs_1_.refs_2_, ...), custom_call_target="tpu_custom_call" | custom-call | flops 19200000000 | bytes 1000 | tf_op jit(solution)/shard_map/detect/pallas_call | solution.py:222
  114.7 4.5 %all-to-all-done.2.refs_1_.refs_2_ = bf16[8,10,32,256]{3,2,1,0:T(8,128)(2,1)S(1)} async-done(((bf16[8,10,32,256]{3,2,1,0:T(8,128)(2,1)}), bf16[8,10,32,256]{3,2,1,0:T(8,128)(2,1)S(1)}, u32[]{:S(2)}, u32[]{:S(2)}) %all-to-all-start.2) | async-done | bytes 1310752 | tf_op jit(solution)/shard_map/all_to_all | solution.py:358
  122.8 10.5 %form.11 = (bf16[16,2,2,64,128]{4,3,2,1,0:T(8,128)(2,1)}, bf16[16,2,2,64,128]{4,3,2,1,0:T(8,128)(2,1)}, bf16[16,2,2,64,128]{4,3,2,1,0:T(8,128)(2,1)}, bf16[16,2,2,64,128]{4,3,2,1,0:T(8,128)(2,1)}) custom-call(s32[2]{0:T(128)} %pad_add_fusion.me_ref.after_ref, f32[6,2,128]{2,1,0:T(2,128)} %get-tuple-element.62.after_ref, ...), custom_call_target="tpu_custom_call" | custom-call | flops 1000 | bytes 1000 | tf_op jit(solution)/shard_map/form/pallas_call | solution.py:188
  135.3 9.2 %collective-permute-done.14.refs_8_ = bf16[14,2,2,64,128]{4,3,2,1,0:T(8,128)(2,1)} collective-permute-done((bf16[14,2,2,64,128]{4,3,2,1,0:T(8,128)(2,1)}, bf16[14,2,2,64,128]{4,3,2,1,0:T(8,128)(2,1)}, u32[]{:S(2)}, u32[]{:S(2)}) %collective-permute-start.14) | collective-permute-done | bytes 917536 | tf_op jit(solution)/shard_map/ppermute | solution.py:294
  144.5 10.8 %detect.10 = (bf16[8,14,32,256]{3,2,1,0:T(8,128)(2,1)}, f32[7,2,128]{2,1,0:T(2,128)}) custom-call(s32[2]{0:T(128)} %pad_add_fusion.me_ref.after_ref, bf16[16,2,2,64,128]{4,3,2,1,0:T(8,128)(2,1)} %get-tuple-element.63.refs_0_.refs_5_, bf16[8,10,32,256]{3,2,1,0:T(8,128)(2,1)} %copy-done.3, bf16[256,256]{1,0:T(8,128)(2,1)} %constant.69.clone.refs_1_.refs_2_, ...), custom_call_target="tpu_custom_call" | custom-call | flops 22400000000 | bytes 1000 | tf_op jit(solution)/shard_map/detect/pallas_call | solution.py:222
  155.3 4.7 %all-to-all-done.3.refs_1_.refs_3_ = bf16[8,12,32,256]{3,2,1,0:T(8,128)(2,1)S(1)} async-done(((bf16[8,12,32,256]{3,2,1,0:T(8,128)(2,1)}), bf16[8,12,32,256]{3,2,1,0:T(8,128)(2,1)S(1)}, u32[]{:S(2)}, u32[]{:S(2)}) %all-to-all-start.3) | async-done | bytes 1572896 | tf_op jit(solution)/shard_map/all_to_all | solution.py:358
  167.5 21.9 %collective-permute-done.17.refs_8_ = bf16[16,2,2,64,128]{4,3,2,1,0:T(8,128)(2,1)} collective-permute-done((bf16[16,2,2,64,128]{4,3,2,1,0:T(8,128)(2,1)}, bf16[16,2,2,64,128]{4,3,2,1,0:T(8,128)(2,1)}, u32[]{:S(2)}, u32[]{:S(2)}) %collective-permute-start.17) | collective-permute-done | bytes 1048608 | tf_op jit(solution)/shard_map/ppermute | solution.py:294
  189.5 12.0 %detect.11 = (bf16[8,16,32,256]{3,2,1,0:T(8,128)(2,1)}, f32[8,2,128]{2,1,0:T(2,128)}) custom-call(s32[2]{0:T(128)} %pad_add_fusion.me_ref.after_ref, f32[7,2,128]{2,1,0:T(2,128)} %get-tuple-element.68.refs_0_, bf16[8,12,32,256]{3,2,1,0:T(8,128)(2,1)} %copy-done.2, bf16[256,256]{1,0:T(8,128)(2,1)} %constant.69.clone.refs_1_.refs_2_, ...), custom_call_target="tpu_custom_call" | custom-call | flops 25600000000 | bytes 1000 | tf_op jit(solution)/shard_map/detect/pallas_call | solution.py:222
  209.3 5.8 %all-to-all-start.5 = ((bf16[8,16,32,256]{3,2,1,0:T(8,128)(2,1)}), bf16[8,16,32,256]{3,2,1,0:T(8,128)(2,1)S(1)}, u32[]{:S(2)}, u32[]{:S(2)}) async-start(bf16[8,16,32,256]{3,2,1,0:T(8,128)(2,1)} %get-tuple-element.77), calls=%async_computation.5 | async-start | bytes 4194304 | tf_op jit(solution)/shard_map/all_to_all | solution.py:358
  216.2 4.7 %collective-permute-start.27 = (f32[16,128]{1,0:T(8,128)S(1)}, f32[16,128]{1,0:T(8,128)S(1)}, u32[]{:S(2)}, u32[]{:S(2)}) collective-permute-start(f32[16,128]{1,0:T(8,128)S(1)} %fusion.3), channel_id=1, source_target_pairs={{0,28},{4,24},{8,20},{12,16},{16,12},{20,8},{24,4},{28,0},{1,29},{... | collective-permute-start | bytes 24584 | tf_op jit(solution)/shard_map/ppermute | solution.py:294
  225.9 5.9 %collective-permute-done.21 = f32[16,128]{1,0:T(8,128)S(1)} collective-permute-done((f32[16,128]{1,0:T(8,128)S(1)}, f32[16,128]{1,0:T(8,128)S(1)}, u32[]{:S(2)}, u32[]{:S(2)}) %collective-permute-start.21) | collective-permute-done | bytes 8224 | tf_op jit(solution)/shard_map/ppermute | solution.py:294
  233.5 16.3 %collective-permute-done.22 = f32[16,128]{1,0:T(8,128)S(1)} collective-permute-done((f32[16,128]{1,0:T(8,128)S(1)}, f32[16,128]{1,0:T(8,128)S(1)}, u32[]{:S(2)}, u32[]{:S(2)}) %collective-permute-start.22) | collective-permute-done | bytes 8224 | tf_op jit(solution)/shard_map/ppermute | solution.py:294
  254.9 9.4 %collective-permute-done.24 = f32[16,128]{1,0:T(8,128)S(1)} collective-permute-done((f32[16,128]{1,0:T(8,128)S(1)}, f32[16,128]{1,0:T(8,128)S(1)}, u32[]{:S(2)}, u32[]{:S(2)}) %collective-permute-start.24) | collective-permute-done | bytes 8224 | tf_op jit(solution)/shard_map/ppermute | solution.py:294
  271.6 13.3 %flag.1 = bf16[2,32,65536]{2,1,0:T(8,128)(2,1)} custom-call(s32[2]{0:T(128)} %pad_add_fusion.me_ref.after_ref, bf16[256,128]{1,0:T(8,128)(2,1)} %constant.71.clone.group_ref, f32[512,1,128]{2,1,0:T(1,128)} %bitcast.55, f32[512,1,128]{2,1,0:T(1,128)} %copy.19.mask_ref, bf16[8,4,32,256]{3,2,1,0:T(8,128)(2,1)} %copy-done.5, bf16[8,8,32,256]{3,2,1,0:T(8,128)(2,1)} %copy-done.4, ...), custom_call_target="tpu_custom_call" | custom-call | flops 1073741824 | bytes 16777216 | tf_op jit(solution)/shard_map/flag/pallas_call | solution.py:267
  (136 shorter events, 76.5 us)
Async XLA Ops:
  14.6 26.6 %collective-permute-start.3 = (bf16[8,2,2,64,128]{4,3,2,1,0:T(8,128)(2,1)}, bf16[8,2,2,64,128]{4,3,2,1,0:T(8,128)(2,1)S(1)}, u32[]{:S(2)}, u32[]{:S(2)}) collective-permute-start(bf16[8,2,2,64,128]{4,3,2,1,0:T(8,128)(2,1)} %get-tuple-element.47), channel_id=1, source_target_pairs={{0,1},{1,0},{2,3},{3,2},{4,5},{5,4},{6,7},{7,6},{8,9},{9,8},{10,11... | collective-permute-start | bytes 1572872 | tf_op jit(solution)/shard_map/ppermute | solution.py:294
  14.7 26.4 %collective-permute-start.4 = (bf16[8,2,2,64,128]{4,3,2,1,0:T(8,128)(2,1)}, bf16[8,2,2,64,128]{4,3,2,1,0:T(8,128)(2,1)S(1)}, u32[]{:S(2)}, u32[]{:S(2)}) collective-permute-start(bf16[8,2,2,64,128]{4,3,2,1,0:T(8,128)(2,1)} %get-tuple-element.48), channel_id=1, source_target_pairs={{0,2},{1,3},{2,0},{3,1},{4,6},{5,7},{6,4},{7,5},{8,10},{9,11},{10,... | collective-permute-start | bytes 1572872 | tf_op jit(solution)/shard_map/ppermute | solution.py:294
  17.4 25.9 %collective-permute-start.5 = (bf16[8,2,2,64,128]{4,3,2,1,0:T(8,128)(2,1)}, bf16[8,2,2,64,128]{4,3,2,1,0:T(8,128)(2,1)S(1)}, u32[]{:S(2)}, u32[]{:S(2)}) collective-permute-start(bf16[8,2,2,64,128]{4,3,2,1,0:T(8,128)(2,1)} %get-tuple-element.49), channel_id=1, source_target_pairs={{0,3},{1,2},{2,1},{3,0},{4,7},{5,6},{6,5},{7,4},{8,11},{9,10},{10,... | collective-permute-start | bytes 1572872 | tf_op jit(solution)/shard_map/ppermute | solution.py:294
  39.2 28.4 %collective-permute-start.6 = (bf16[10,2,2,64,128]{4,3,2,1,0:T(8,128)(2,1)}, bf16[10,2,2,64,128]{4,3,2,1,0:T(8,128)(2,1)S(1)}, u32[]{:S(2)}, u32[]{:S(2)}) collective-permute-start(bf16[10,2,2,64,128]{4,3,2,1,0:T(8,128)(2,1)} %get-tuple-element.53), channel_id=1, source_target_pairs={{0,1},{1,0},{2,3},{3,2},{4,5},{5,4},{6,7},{7,6},{8,9},{9,8},{10,11... | collective-permute-start | bytes 1966088 | tf_op jit(solution)/shard_map/ppermute | solution.py:294
  39.6 28.0 %collective-permute-start.7 = (bf16[10,2,2,64,128]{4,3,2,1,0:T(8,128)(2,1)}, bf16[10,2,2,64,128]{4,3,2,1,0:T(8,128)(2,1)}, u32[]{:S(2)}, u32[]{:S(2)}) collective-permute-start(bf16[10,2,2,64,128]{4,3,2,1,0:T(8,128)(2,1)} %get-tuple-element.54), channel_id=1, source_target_pairs={{0,2},{1,3},{2,0},{3,1},{4,6},{5,7},{6,4},{7,5},{8,10},{9,11},{10,... | collective-permute-start | bytes 1966088 | tf_op jit(solution)/shard_map/ppermute | solution.py:294
  41.1 30.3 %collective-permute-start.8 = (bf16[10,2,2,64,128]{4,3,2,1,0:T(8,128)(2,1)}, bf16[10,2,2,64,128]{4,3,2,1,0:T(8,128)(2,1)}, u32[]{:S(2)}, u32[]{:S(2)}) collective-permute-start(bf16[10,2,2,64,128]{4,3,2,1,0:T(8,128)(2,1)} %get-tuple-element.55), channel_id=1, source_target_pairs={{0,3},{1,2},{2,1},{3,0},{4,7},{5,6},{6,5},{7,4},{8,11},{9,10},{10,... | collective-permute-start | bytes 1966088 | tf_op jit(solution)/shard_map/ppermute | solution.py:294
  51.2 32.7 %all-to-all-start.1 = ((bf16[8,8,32,256]{3,2,1,0:T(8,128)(2,1)}), bf16[8,8,32,256]{3,2,1,0:T(8,128)(2,1)S(1)}, u32[]{:S(2)}, u32[]{:S(2)}) async-start(bf16[8,8,32,256]{3,2,1,0:T(8,128)(2,1)} %get-tuple-element.58), calls=%async_computation.1 | async-start | bytes 2097152 | tf_op jit(solution)/shard_map/all_to_all | solution.py:358
  65.4 33.3 %collective-permute-start.9 = (bf16[12,2,2,64,128]{4,3,2,1,0:T(8,128)(2,1)}, bf16[12,2,2,64,128]{4,3,2,1,0:T(8,128)(2,1)S(1)}, u32[]{:S(2)}, u32[]{:S(2)}) collective-permute-start(bf16[12,2,2,64,128]{4,3,2,1,0:T(8,128)(2,1)} %get-tuple-element.59), channel_id=1, source_target_pairs={{0,1},{1,0},{2,3},{3,2},{4,5},{5,4},{6,7},{7,6},{8,9},{9,8},{10,11... | collective-permute-start | bytes 2359304 | tf_op jit(solution)/shard_map/ppermute | solution.py:294
  66.1 32.8 %collective-permute-start.10 = (bf16[12,2,2,64,128]{4,3,2,1,0:T(8,128)(2,1)}, bf16[12,2,2,64,128]{4,3,2,1,0:T(8,128)(2,1)}, u32[]{:S(2)}, u32[]{:S(2)}) collective-permute-start(bf16[12,2,2,64,128]{4,3,2,1,0:T(8,128)(2,1)} %get-tuple-element.60), channel_id=1, source_target_pairs={{0,2},{1,3},{2,0},{3,1},{4,6},{5,7},{6,4},{7,5},{8,10},{9,11},{10,... | collective-permute-start | bytes 2359304 | tf_op jit(solution)/shard_map/ppermute | solution.py:294
  67.6 37.6 %collective-permute-start.11 = (bf16[12,2,2,64,128]{4,3,2,1,0:T(8,128)(2,1)}, bf16[12,2,2,64,128]{4,3,2,1,0:T(8,128)(2,1)}, u32[]{:S(2)}, u32[]{:S(2)}) collective-permute-start(bf16[12,2,2,64,128]{4,3,2,1,0:T(8,128)(2,1)} %get-tuple-element.61), channel_id=1, source_target_pairs={{0,3},{1,2},{2,1},{3,0},{4,7},{5,6},{6,5},{7,4},{8,11},{9,10},{10,... | collective-permute-start | bytes 2359304 | tf_op jit(solution)/shard_map/ppermute | solution.py:294
  83.9 35.3 %all-to-all-start.2 = ((bf16[8,10,32,256]{3,2,1,0:T(8,128)(2,1)}), bf16[8,10,32,256]{3,2,1,0:T(8,128)(2,1)S(1)}, u32[]{:S(2)}, u32[]{:S(2)}) async-start(bf16[8,10,32,256]{3,2,1,0:T(8,128)(2,1)} %get-tuple-element.64), calls=%async_computation.2 | async-start | bytes 2621440 | tf_op jit(solution)/shard_map/all_to_all | solution.py:358
  97.0 38.0 %collective-permute-start.12 = (bf16[14,2,2,64,128]{4,3,2,1,0:T(8,128)(2,1)}, bf16[14,2,2,64,128]{4,3,2,1,0:T(8,128)(2,1)}, u32[]{:S(2)}, u32[]{:S(2)}) collective-permute-start(bf16[14,2,2,64,128]{4,3,2,1,0:T(8,128)(2,1)} %get-tuple-element.65), channel_id=1, source_target_pairs={{0,1},{1,0},{2,3},{3,2},{4,5},{5,4},{6,7},{7,6},{8,9},{9,8},{10,11... | collective-permute-start | bytes 2752520 | tf_op jit(solution)/shard_map/ppermute | solution.py:294
  97.1 38.2 %collective-permute-start.13 = (bf16[14,2,2,64,128]{4,3,2,1,0:T(8,128)(2,1)}, bf16[14,2,2,64,128]{4,3,2,1,0:T(8,128)(2,1)}, u32[]{:S(2)}, u32[]{:S(2)}) collective-permute-start(bf16[14,2,2,64,128]{4,3,2,1,0:T(8,128)(2,1)} %get-tuple-element.66), channel_id=1, source_target_pairs={{0,2},{1,3},{2,0},{3,1},{4,6},{5,7},{6,4},{7,5},{8,10},{9,11},{10,... | collective-permute-start | bytes 2752520 | tf_op jit(solution)/shard_map/ppermute | solution.py:294
  98.7 45.8 %collective-permute-start.14 = (bf16[14,2,2,64,128]{4,3,2,1,0:T(8,128)(2,1)}, bf16[14,2,2,64,128]{4,3,2,1,0:T(8,128)(2,1)}, u32[]{:S(2)}, u32[]{:S(2)}) collective-permute-start(bf16[14,2,2,64,128]{4,3,2,1,0:T(8,128)(2,1)} %get-tuple-element.67), channel_id=1, source_target_pairs={{0,3},{1,2},{2,1},{3,0},{4,7},{5,6},{6,5},{7,4},{8,11},{9,10},{10,... | collective-permute-start | bytes 2752520 | tf_op jit(solution)/shard_map/ppermute | solution.py:294
  119.2 40.8 %all-to-all-start.3 = ((bf16[8,12,32,256]{3,2,1,0:T(8,128)(2,1)}), bf16[8,12,32,256]{3,2,1,0:T(8,128)(2,1)S(1)}, u32[]{:S(2)}, u32[]{:S(2)}) async-start(bf16[8,12,32,256]{3,2,1,0:T(8,128)(2,1)} %get-tuple-element.69), calls=%async_computation.3 | async-start | bytes 3145728 | tf_op jit(solution)/shard_map/all_to_all | solution.py:358
  133.4 31.8 %collective-permute-start.15 = (bf16[16,2,2,64,128]{4,3,2,1,0:T(8,128)(2,1)}, bf16[16,2,2,64,128]{4,3,2,1,0:T(8,128)(2,1)}, u32[]{:S(2)}, u32[]{:S(2)}) collective-permute-start(bf16[16,2,2,64,128]{4,3,2,1,0:T(8,128)(2,1)} %get-tuple-element.70), channel_id=1, source_target_pairs={{0,1},{1,0},{2,3},{3,2},{4,5},{5,4},{6,7},{7,6},{8,9},{9,8},{10,11... | collective-permute-start | bytes 3145736 | tf_op jit(solution)/shard_map/ppermute | solution.py:294
  133.4 34.1 %collective-permute-start.16 = (bf16[16,2,2,64,128]{4,3,2,1,0:T(8,128)(2,1)}, bf16[16,2,2,64,128]{4,3,2,1,0:T(8,128)(2,1)}, u32[]{:S(2)}, u32[]{:S(2)}) collective-permute-start(bf16[16,2,2,64,128]{4,3,2,1,0:T(8,128)(2,1)} %get-tuple-element.71), channel_id=1, source_target_pairs={{0,2},{1,3},{2,0},{3,1},{4,6},{5,7},{6,4},{7,5},{8,10},{9,11},{10,... | collective-permute-start | bytes 3145736 | tf_op jit(solution)/shard_map/ppermute | solution.py:294
  135.0 54.4 %collective-permute-start.17 = (bf16[16,2,2,64,128]{4,3,2,1,0:T(8,128)(2,1)}, bf16[16,2,2,64,128]{4,3,2,1,0:T(8,128)(2,1)}, u32[]{:S(2)}, u32[]{:S(2)}) collective-permute-start(bf16[16,2,2,64,128]{4,3,2,1,0:T(8,128)(2,1)} %get-tuple-element.72), channel_id=1, source_target_pairs={{0,3},{1,2},{2,1},{3,0},{4,7},{5,6},{6,5},{7,4},{8,11},{9,10},{10,... | collective-permute-start | bytes 3145736 | tf_op jit(solution)/shard_map/ppermute | solution.py:294
  161.2 46.8 %all-to-all-start.4 = ((bf16[8,14,32,256]{3,2,1,0:T(8,128)(2,1)}), bf16[8,14,32,256]{3,2,1,0:T(8,128)(2,1)S(1)}, u32[]{:S(2)}, u32[]{:S(2)}) async-start(bf16[8,14,32,256]{3,2,1,0:T(8,128)(2,1)} %get-tuple-element.76), calls=%async_computation.4 | async-start | bytes 3670016 | tf_op jit(solution)/shard_map/all_to_all | solution.py:358
  209.3 60.9 %all-to-all-start.5 = ((bf16[8,16,32,256]{3,2,1,0:T(8,128)(2,1)}), bf16[8,16,32,256]{3,2,1,0:T(8,128)(2,1)S(1)}, u32[]{:S(2)}, u32[]{:S(2)}) async-start(bf16[8,16,32,256]{3,2,1,0:T(8,128)(2,1)} %get-tuple-element.77), calls=%async_computation.5 | async-start | bytes 4194304 | tf_op jit(solution)/shard_map/all_to_all | solution.py:358
  216.2 48.8 %collective-permute-start.27 = (f32[16,128]{1,0:T(8,128)S(1)}, f32[16,128]{1,0:T(8,128)S(1)}, u32[]{:S(2)}, u32[]{:S(2)}) collective-permute-start(f32[16,128]{1,0:T(8,128)S(1)} %fusion.3), channel_id=1, source_target_pairs={{0,28},{4,24},{8,20},{12,16},{16,12},{20,8},{24,4},{28,0},{1,29},{... | collective-permute-start | bytes 24584 | tf_op jit(solution)/shard_map/ppermute | solution.py:294
  221.0 44.1 %collective-permute-start.26 = (f32[16,128]{1,0:T(8,128)S(1)}, f32[16,128]{1,0:T(8,128)S(1)}, u32[]{:S(2)}, u32[]{:S(2)}) collective-permute-start(f32[16,128]{1,0:T(8,128)S(1)} %fusion.3), channel_id=1, source_target_pairs={{0,24},{4,28},{8,16},{12,20},{16,8},{20,12},{24,0},{28,4},{1,25},{... | collective-permute-start | bytes 24584 | tf_op jit(solution)/shard_map/ppermute | solution.py:294
  221.5 43.5 %collective-permute-start.25 = (f32[16,128]{1,0:T(8,128)S(1)}, f32[16,128]{1,0:T(8,128)S(1)}, u32[]{:S(2)}, u32[]{:S(2)}) collective-permute-start(f32[16,128]{1,0:T(8,128)S(1)} %fusion.3), channel_id=1, source_target_pairs={{0,20},{4,16},{8,28},{12,24},{16,4},{20,0},{24,12},{28,8},{1,21},{... | collective-permute-start | bytes 24584 | tf_op jit(solution)/shard_map/ppermute | solution.py:294
  222.1 42.2 %collective-permute-start.24 = (f32[16,128]{1,0:T(8,128)S(1)}, f32[16,128]{1,0:T(8,128)S(1)}, u32[]{:S(2)}, u32[]{:S(2)}) collective-permute-start(f32[16,128]{1,0:T(8,128)S(1)} %fusion.3), channel_id=1, source_target_pairs={{0,16},{4,20},{8,24},{12,28},{16,0},{20,4},{24,8},{28,12},{1,17},{... | collective-permute-start | bytes 24584 | tf_op jit(solution)/shard_map/ppermute | solution.py:294
  (36 other events, 362.8 us)

commit v7 on v6

--- a/solution.py
+++ b/solution.py
@@ -11,7 +11,7 @@
 
 UP = 16
 SHARES = (2, 4, 5, 6, 7, 8)
-DIRECT = (False, False, False, False, False, False)
+DIRECT = (False, True, False, True, False, False)
 DETECT_FLOPS = 1_600_000_000
 
 epsilon = 1e-05

time: 287 us -> 376 us (1.31)
  waiting for transfers between devices: 103 us -> 177 us
  starting transfers between devices: 60.6 us -> 72.3 us
    ppermute x31 -> x45, waiting for transfers between devices: 89.6 us -> 177 us  [swap(): lax.ppermute(one, axis, [(i, i ^ apart) for i in range(lax.axis_size(axis...]
    ppermute x31 -> x45, starting transfers between devices: 32.2 us -> 50.8 us  [swap(): lax.ppermute(one, axis, [(i, i ^ apart) for i in range(lax.axis_size(axis...]
    all_to_all x6 -> x4, waiting for transfers between devices: 13.4 us -> 0.01 us  [body(): lax.all_to_all(*sent, 'chan', split_axis=0, concat_axis=0, tiled=True)]
    all_to_all x6 -> x4, starting transfers between devices: 28.5 us -> 21.5 us  [body(): lax.all_to_all(*sent, 'chan', split_axis=0, concat_axis=0, tiled=True)]
  transfers between devices with their start and end apart: 37 -> 49, of which waited for: 19 -> 18; matrix products, arithmetic and copies ran while one was open for 1% -> 2% of each run, Pallas kernels for 33% -> 25%
where the time goes in v7:
time: 376 us; the launch traced here: 375 us
  waiting for transfers between devices  177 us (47%)
  Pallas kernels  111 us (30%)
  starting transfers between devices  72.3 us (19%)
  local copies, waits for them, and re-layouts  10.4 us (3%)
    ppermute x45, waiting for transfers between devices, swap(): lax.ppermute(one, axis, [(i, i ^ apart) for i in range(lax.axis_size(axis...  177 us
    pallas_call x6, Pallas kernels, detect(): pl.pallas_call(functools.partial(detect_kernel, columns, len(after)), gri...  52 us
    ppermute x45, starting transfers between devices, swap(): lax.ppermute(one, axis, [(i, i ^ apart) for i in range(lax.axis_size(axis...  50.8 us
    pallas_call x6, Pallas kernels, form(): pl.pallas_call(form_kernel, grid=(steps,), in_specs=[pl.BlockSpec(memory_...  45.7 us
    all_to_all x4, starting transfers between devices, body(): lax.all_to_all(*sent, 'chan', split_axis=0, concat_axis=0, tiled=True)  21.5 us
    pallas_call x1, Pallas kernels, soft_flag(): pl.pallas_call(functools.partial(flag_kernel, layout), grid=(own // block...  13.4 us
  transfers between devices with their start and end apart: 49, of which 18 were waited for; matrix products, arithmetic and copies ran while one was open for 2% of the time, Pallas kernels for 25%

profile of v7, /device:TPU:0, one launch (start us, length us, event | category | flops | bytes accessed | tf_op | source)
XLA Modules:
  0.0 375.1 jit_solution(8080470476515387603)
XLA Ops:
  8.4 6.2 %form.7 = (bf16[8,2,2,64,128]{4,3,2,1,0:T(8,128)(2,1)}, bf16[8,2,2,64,128]{4,3,2,1,0:T(8,128)(2,1)}, bf16[8,2,2,64,128]{4,3,2,1,0:T(8,128)(2,1)}, bf16[8,2,2,64,128]{4,3,2,1,0:T(8,128)(2,1)}) custom-call(s32[2]{0:T(128)} %pad_add_fusion.me_ref.after_ref, bf16[4,2,2,64,128]{4,3,2,1,0:T(8,128)(2,1)} %get-tuple-element.54.after_ref.refs_4_, ...), custom_call_target="tpu_custom_call" | custom-call | flops 1000 | bytes 1000 | tf_op jit(solution)/shard_map/form/pallas_call | solution.py:188
  26.1 5.8 %all-to-all-start = ((bf16[8,4,32,256]{3,2,1,0:T(8,128)(2,1)}), bf16[8,4,32,256]{3,2,1,0:T(8,128)(2,1)S(1)}, u32[]{:S(2)}, u32[]{:S(2)}) async-start(bf16[8,4,32,256]{3,2,1,0:T(8,128)(2,1)} %get-tuple-element.66), calls=%async_computation | async-start | bytes 1048576 | tf_op jit(solution)/shard_map/all_to_all | solution.py:358
  31.9 7.2 %form.8 = (bf16[10,2,2,64,128]{4,3,2,1,0:T(8,128)(2,1)}, bf16[10,2,2,64,128]{4,3,2,1,0:T(8,128)(2,1)}, bf16[10,2,2,64,128]{4,3,2,1,0:T(8,128)(2,1)}, bf16[10,2,2,64,128]{4,3,2,1,0:T(8,128)(2,1)}) custom-call(s32[2]{0:T(128)} %pad_add_fusion.me_ref.after_ref, f32[2,2,128]{2,1,0:T(2,128)} %get-tuple-element.59.after_ref, ...), custom_call_target="tpu_custom_call" | custom-call | flops 1000 | bytes 1000 | tf_op jit(solution)/shard_map/form/pallas_call | solution.py:188
  44.2 6.9 %detect.7 = (bf16[1,8,32,256]{3,2,1,0:T(8,128)(2,1)}, bf16[1,8,32,256]{3,2,1,0:T(8,128)(2,1)}, bf16[1,8,32,256]{3,2,1,0:T(8,128)(2,1)}, bf16[1,8,32,256]{3,2,1,0...) custom-call(s32[2]{0:T(128)} %pad_add_fusion.me_ref.after_ref, ...), custom_call_target="tpu_custom_call" | custom-call | flops 12800000000 | bytes 1000 | tf_op jit(solution)/shard_map/detect/pallas_call | solution.py:222
  54.2 8.3 %form.9 = (bf16[12,2,2,64,128]{4,3,2,1,0:T(8,128)(2,1)}, bf16[12,2,2,64,128]{4,3,2,1,0:T(8,128)(2,1)}, bf16[12,2,2,64,128]{4,3,2,1,0:T(8,128)(2,1)}, bf16[12,2,2,64,128]{4,3,2,1,0:T(8,128)(2,1)}) custom-call(s32[2]{0:T(128)} %pad_add_fusion.me_ref.after_ref, f32[4,2,128]{2,1,0:T(2,128)} %get-tuple-element.64.after_ref, ...), custom_call_target="tpu_custom_call" | custom-call | flops 1000 | bytes 1000 | tf_op jit(solution)/shard_map/form/pallas_call | solution.py:188
  64.8 6.7 %collective-permute-done.8.refs_8_ = bf16[10,2,2,64,128]{4,3,2,1,0:T(8,128)(2,1)} collective-permute-done((bf16[10,2,2,64,128]{4,3,2,1,0:T(8,128)(2,1)}, bf16[10,2,2,64,128]{4,3,2,1,0:T(8,128)(2,1)}, u32[]{:S(2)}, u32[]{:S(2)}) %collective-permute-start.8) | collective-permute-done | bytes 655392 | tf_op jit(solution)/shard_map/ppermute | solution.py:294
  74.2 8.2 %detect.8 = (bf16[8,10,32,256]{3,2,1,0:T(8,128)(2,1)}, f32[5,2,128]{2,1,0:T(2,128)}) custom-call(s32[2]{0:T(128)} %pad_add_fusion.me_ref.after_ref, bf16[12,2,2,64,128]{4,3,2,1,0:T(8,128)(2,1)} %get-tuple-element.65.refs_0_.refs_12_, bf16[8,4,32,256]{3,2,1,0:T(8,128)(2,1)} %copy-done.3, bf16[256,256]{1,0:T(8,128)(2,1)} %constant.71.clone.refs_1_.refs_2_.refs_9_, ...), custom_call_target="tpu_custom_call" | custom-call | flops 16000000000 | bytes 1000 | tf_op jit(solution)/shard_map/detect/pallas_call | solution.py:222
  82.5 6.0 %all-to-all-start.1 = ((bf16[8,10,32,256]{3,2,1,0:T(8,128)(2,1)}), bf16[8,10,32,256]{3,2,1,0:T(8,128)(2,1)S(1)}, u32[]{:S(2)}, u32[]{:S(2)}) async-start(bf16[8,10,32,256]{3,2,1,0:T(8,128)(2,1)} %get-tuple-element.85), calls=%async_computation.1 | async-start | bytes 2621440 | tf_op jit(solution)/shard_map/all_to_all | solution.py:358
  93.0 36.7 %collective-permute-done.12.refs_5_ = bf16[1,8,32,256]{3,2,1,0:T(8,128)(2,1)S(1)} collective-permute-done((bf16[1,8,32,256]{3,2,1,0:T(8,128)(2,1)S(1)}, bf16[1,8,32,256]{3,2,1,0:T(8,128)(2,1)S(1)}, u32[]{:S(2)}, u32[]{:S(2)}) %collective-permute-start.12) | collective-permute-done | bytes 131104 | tf_op jit(solution)/shard_map/ppermute | solution.py:294
  134.3 9.5 %form.10 = (bf16[14,2,2,64,128]{4,3,2,1,0:T(8,128)(2,1)}, bf16[14,2,2,64,128]{4,3,2,1,0:T(8,128)(2,1)}, bf16[14,2,2,64,128]{4,3,2,1,0:T(8,128)(2,1)}, bf16[14,2,2,64,128]{4,3,2,1,0:T(8,128)(2,1)}) custom-call(s32[2]{0:T(128)} %pad_add_fusion.me_ref.after_ref, f32[5,2,128]{2,1,0:T(2,128)} %get-tuple-element.70.after_ref, ...), custom_call_target="tpu_custom_call" | custom-call | flops 1000 | bytes 1000 | tf_op jit(solution)/shard_map/form/pallas_call | solution.py:188
  145.8 9.5 %detect.9 = (bf16[1,12,32,256]{3,2,1,0:T(8,128)(2,1)}, bf16[1,12,32,256]{3,2,1,0:T(8,128)(2,1)}, bf16[1,12,32,256]{3,2,1,0:T(8,128)(2,1)}, bf16[1,12,32,256]{3,2...) custom-call(s32[2]{0:T(128)} %pad_add_fusion.me_ref.after_ref, ...), custom_call_target="tpu_custom_call" | custom-call | flops 19200000000 | bytes 1000 | tf_op jit(solution)/shard_map/detect/pallas_call | solution.py:222
  156.5 10.5 %form.11 = (bf16[16,2,2,64,128]{4,3,2,1,0:T(8,128)(2,1)}, bf16[16,2,2,64,128]{4,3,2,1,0:T(8,128)(2,1)}, bf16[16,2,2,64,128]{4,3,2,1,0:T(8,128)(2,1)}, bf16[16,2,2,64,128]{4,3,2,1,0:T(8,128)(2,1)}) custom-call(s32[2]{0:T(128)} %pad_add_fusion.me_ref.after_ref, f32[6,2,128]{2,1,0:T(2,128)} %get-tuple-element.83.after_ref, ...), custom_call_target="tpu_custom_call" | custom-call | flops 1000 | bytes 1000 | tf_op jit(solution)/shard_map/form/pallas_call | solution.py:188
  170.7 15.5 %collective-permute-done.21.refs_8_ = bf16[14,2,2,64,128]{4,3,2,1,0:T(8,128)(2,1)} collective-permute-done((bf16[14,2,2,64,128]{4,3,2,1,0:T(8,128)(2,1)}, bf16[14,2,2,64,128]{4,3,2,1,0:T(8,128)(2,1)}, u32[]{:S(2)}, u32[]{:S(2)}) %collective-permute-start.21) | collective-permute-done | bytes 917536 | tf_op jit(solution)/shard_map/ppermute | solution.py:294
  188.3 10.8 %detect.10 = (bf16[8,14,32,256]{3,2,1,0:T(8,128)(2,1)}, f32[7,2,128]{2,1,0:T(2,128)}) custom-call(s32[2]{0:T(128)} %pad_add_fusion.me_ref.after_ref, bf16[16,2,2,64,128]{4,3,2,1,0:T(8,128)(2,1)} %get-tuple-element.84.refs_0_.refs_12_, bf16[8,10,32,256]{3,2,1,0:T(8,128)(2,1)} %copy-done.2, bf16[256,256]{1,0:T(8,128)(2,1)} %constant.71.clone.refs_1_.refs_2_.refs_9_, ...), custom_call_target="tpu_custom_call" | custom-call | flops 22400000000 | bytes 1000 | tf_op jit(solution)/shard_map/detect/pallas_call | solution.py:222
  199.1 6.1 %all-to-all-start.2 = ((bf16[8,14,32,256]{3,2,1,0:T(8,128)(2,1)}), bf16[8,14,32,256]{3,2,1,0:T(8,128)(2,1)S(1)}, u32[]{:S(2)}, u32[]{:S(2)}) async-start(bf16[8,14,32,256]{3,2,1,0:T(8,128)(2,1)} %get-tuple-element.104), calls=%async_computation.2 | async-start | bytes 3670016 | tf_op jit(solution)/shard_map/all_to_all | solution.py:358
  209.7 52.2 %collective-permute-done.25.refs_5_.refs_14_ = bf16[1,12,32,256]{3,2,1,0:T(8,128)(2,1)S(1)} collective-permute-done((bf16[1,12,32,256]{3,2,1,0:T(8,128)(2,1)S(1)}, bf16[1,12,32,256]{3,2,1,0:T(8,128)(2,1)S(1)}, u32[]{:S(2)}, u32[]{:S(2)}) %collective-permute-start.25) | collective-permute-done | bytes 196640 | tf_op jit(solution)/shard_map/ppermute | solution.py:294
  262.8 10.1 %collective-permute-done.26.refs_6_.refs_15_ = bf16[1,12,32,256]{3,2,1,0:T(8,128)(2,1)S(1)} collective-permute-done((bf16[1,12,32,256]{3,2,1,0:T(8,128)(2,1)S(1)}, bf16[1,12,32,256]{3,2,1,0:T(8,128)(2,1)S(1)}, u32[]{:S(2)}, u32[]{:S(2)}) %collective-permute-start.26) | collective-permute-done | bytes 196640 | tf_op jit(solution)/shard_map/ppermute | solution.py:294
  273.0 8.4 %collective-permute-done.28.refs_8_.refs_17_ = bf16[1,12,32,256]{3,2,1,0:T(8,128)(2,1)S(1)} collective-permute-done((bf16[1,12,32,256]{3,2,1,0:T(8,128)(2,1)S(1)}, bf16[1,12,32,256]{3,2,1,0:T(8,128)(2,1)S(1)}, u32[]{:S(2)}, u32[]{:S(2)}) %collective-permute-start.28) | collective-permute-done | bytes 196640 | tf_op jit(solution)/shard_map/ppermute | solution.py:294
  282.1 12.0 %detect.11 = (bf16[8,16,32,256]{3,2,1,0:T(8,128)(2,1)}, f32[8,2,128]{2,1,0:T(2,128)}) custom-call(s32[2]{0:T(128)} %pad_add_fusion.me_ref.after_ref, f32[7,2,128]{2,1,0:T(2,128)} %get-tuple-element.89.refs_0_, bf16[1,12,32,256]{3,2,1,0:T(8,128)(2,1)} %get-tuple-element.90.refs_1_.refs_10_, bf16[1,12,32,256]{3,2,1,0:T(8,128)(2,1)} %copy-done.5, ...), custom_call_target="tpu_custom_call" | custom-call | flops 25600000000 | bytes 1000 | tf_op jit(solution)/shard_map/detect/pallas_call | solution.py:222
  306.5 4.7 %collective-permute-start.41 = (f32[16,128]{1,0:T(8,128)S(1)}, f32[16,128]{1,0:T(8,128)S(1)}, u32[]{:S(2)}, u32[]{:S(2)}) collective-permute-start(f32[16,128]{1,0:T(8,128)S(1)} %fusion.4), channel_id=1, source_target_pairs={{0,28},{4,24},{8,20},{12,16},{16,12},{20,8},{24,4},{28,0},{1,29},{... | collective-permute-start | bytes 24584 | tf_op jit(solution)/shard_map/ppermute | solution.py:294
  316.1 5.9 %collective-permute-done.35 = f32[16,128]{1,0:T(8,128)S(1)} collective-permute-done((f32[16,128]{1,0:T(8,128)S(1)}, f32[16,128]{1,0:T(8,128)S(1)}, u32[]{:S(2)}, u32[]{:S(2)}) %collective-permute-start.35) | collective-permute-done | bytes 8224 | tf_op jit(solution)/shard_map/ppermute | solution.py:294
  323.5 16.1 %collective-permute-done.36 = f32[16,128]{1,0:T(8,128)S(1)} collective-permute-done((f32[16,128]{1,0:T(8,128)S(1)}, f32[16,128]{1,0:T(8,128)S(1)}, u32[]{:S(2)}, u32[]{:S(2)}) %collective-permute-start.36) | collective-permute-done | bytes 8224 | tf_op jit(solution)/shard_map/ppermute | solution.py:294
  344.7 9.5 %collective-permute-done.38 = f32[16,128]{1,0:T(8,128)S(1)} collective-permute-done((f32[16,128]{1,0:T(8,128)S(1)}, f32[16,128]{1,0:T(8,128)S(1)}, u32[]{:S(2)}, u32[]{:S(2)}) %collective-permute-start.38) | collective-permute-done | bytes 8224 | tf_op jit(solution)/shard_map/ppermute | solution.py:294
  361.6 13.4 %flag.1 = bf16[2,32,65536]{2,1,0:T(8,128)(2,1)} custom-call(s32[2]{0:T(128)} %pad_add_fusion.me_ref.after_ref, bf16[256,128]{1,0:T(8,128)(2,1)} %constant.73.clone.group_ref, f32[512,1,128]{2,1,0:T(1,128)} %bitcast.57, f32[512,1,128]{2,1,0:T(1,128)} %copy.19.mask_ref, bf16[8,4,32,256]{3,2,1,0:T(8,128)(2,1)} %copy-done.3, ...), custom_call_target="tpu_custom_call" | custom-call | flops 1073741824 | bytes 16777216 | tf_op jit(solution)/shard_map/flag/pallas_call | solution.py:267
  (214 shorter events, 87.5 us)
Async XLA Ops:
  26.1 47.3 %all-to-all-start = ((bf16[8,4,32,256]{3,2,1,0:T(8,128)(2,1)}), bf16[8,4,32,256]{3,2,1,0:T(8,128)(2,1)S(1)}, u32[]{:S(2)}, u32[]{:S(2)}) async-start(bf16[8,4,32,256]{3,2,1,0:T(8,128)(2,1)} %get-tuple-element.66), calls=%async_computation | async-start | bytes 1048576 | tf_op jit(solution)/shard_map/all_to_all | solution.py:358
  41.1 30.4 %collective-permute-start.8 = (bf16[10,2,2,64,128]{4,3,2,1,0:T(8,128)(2,1)}, bf16[10,2,2,64,128]{4,3,2,1,0:T(8,128)(2,1)}, u32[]{:S(2)}, u32[]{:S(2)}) collective-permute-start(bf16[10,2,2,64,128]{4,3,2,1,0:T(8,128)(2,1)} %get-tuple-element.69), channel_id=1, source_target_pairs={{0,3},{1,2},{2,1},{3,0},{4,7},{5,6},{6,5},{7,4},{8,11},{9,10},{10,... | collective-permute-start | bytes 1966088 | tf_op jit(solution)/shard_map/ppermute | solution.py:294
  52.7 35.8 %collective-permute-start.10 = (bf16[1,8,32,256]{3,2,1,0:T(8,128)(2,1)}, bf16[1,8,32,256]{3,2,1,0:T(8,128)(2,1)S(1)}, u32[]{:S(2)}, u32[]{:S(2)}) collective-permute-start(bf16[1,8,32,256]{3,2,1,0:T(8,128)(2,1)} %get-tuple-element.74), channel_id=1, source_target_pairs={{0,8},{4,12},{8,0},{12,4},{16,24},{20,28},{24,16},{28,20},{1,9},{5... | collective-permute-start | bytes 393224 | tf_op jit(solution)/shard_map/ppermute | solution.py:294
  62.6 28.8 %collective-permute-start.11 = (bf16[1,8,32,256]{3,2,1,0:T(8,128)(2,1)S(1)}, bf16[1,8,32,256]{3,2,1,0:T(8,128)(2,1)S(1)}, u32[]{:S(2)}, u32[]{:S(2)}) collective-permute-start(bf16[1,8,32,256]{3,2,1,0:T(8,128)(2,1)S(1)} %copy-done.45), channel_id=1, source_target_pairs={{0,12},{4,8},{8,4},{12,0},{16,28},{20,24},{24,20},{28,16},{1,13},{... | collective-permute-start | bytes 393224 | tf_op jit(solution)/shard_map/ppermute | solution.py:294
  63.1 81.5 %collective-permute-start.16 = (bf16[12,2,2,64,128]{4,3,2,1,0:T(8,128)(2,1)}, bf16[12,2,2,64,128]{4,3,2,1,0:T(8,128)(2,1)S(1)}, u32[]{:S(2)}, u32[]{:S(2)}) collective-permute-start(bf16[12,2,2,64,128]{4,3,2,1,0:T(8,128)(2,1)} %get-tuple-element.80), channel_id=1, source_target_pairs={{0,1},{1,0},{2,3},{3,2},{4,5},{5,4},{6,7},{7,6},{8,9},{9,8},{10,11... | collective-permute-start | bytes 2359304 | tf_op jit(solution)/shard_map/ppermute | solution.py:294
  63.2 82.6 %collective-permute-start.17 = (bf16[12,2,2,64,128]{4,3,2,1,0:T(8,128)(2,1)}, bf16[12,2,2,64,128]{4,3,2,1,0:T(8,128)(2,1)}, u32[]{:S(2)}, u32[]{:S(2)}) collective-permute-start(bf16[12,2,2,64,128]{4,3,2,1,0:T(8,128)(2,1)} %get-tuple-element.81), channel_id=1, source_target_pairs={{0,2},{1,3},{2,0},{3,1},{4,6},{5,7},{6,4},{7,5},{8,10},{9,11},{10,... | collective-permute-start | bytes 2359304 | tf_op jit(solution)/shard_map/ppermute | solution.py:294
  71.5 74.4 %collective-permute-start.18 = (bf16[12,2,2,64,128]{4,3,2,1,0:T(8,128)(2,1)}, bf16[12,2,2,64,128]{4,3,2,1,0:T(8,128)(2,1)}, u32[]{:S(2)}, u32[]{:S(2)}) collective-permute-start(bf16[12,2,2,64,128]{4,3,2,1,0:T(8,128)(2,1)} %get-tuple-element.82), channel_id=1, source_target_pairs={{0,3},{1,2},{2,1},{3,0},{4,7},{5,6},{6,5},{7,4},{8,11},{9,10},{10,... | collective-permute-start | bytes 2359304 | tf_op jit(solution)/shard_map/ppermute | solution.py:294
  82.5 104.7 %all-to-all-start.1 = ((bf16[8,10,32,256]{3,2,1,0:T(8,128)(2,1)}), bf16[8,10,32,256]{3,2,1,0:T(8,128)(2,1)S(1)}, u32[]{:S(2)}, u32[]{:S(2)}) async-start(bf16[8,10,32,256]{3,2,1,0:T(8,128)(2,1)} %get-tuple-element.85), calls=%async_computation.1 | async-start | bytes 2621440 | tf_op jit(solution)/shard_map/all_to_all | solution.py:358
  88.5 41.2 %collective-permute-start.12 = (bf16[1,8,32,256]{3,2,1,0:T(8,128)(2,1)S(1)}, bf16[1,8,32,256]{3,2,1,0:T(8,128)(2,1)S(1)}, u32[]{:S(2)}, u32[]{:S(2)}) collective-permute-start(bf16[1,8,32,256]{3,2,1,0:T(8,128)(2,1)S(1)} %copy-done.44), channel_id=1, source_target_pairs={{0,16},{4,20},{8,24},{12,28},{16,0},{20,4},{24,8},{28,12},{1,17},{... | collective-permute-start | bytes 393224 | tf_op jit(solution)/shard_map/ppermute | solution.py:294
  91.4 42.9 %collective-permute-start.13 = (bf16[1,8,32,256]{3,2,1,0:T(8,128)(2,1)S(1)}, bf16[1,8,32,256]{3,2,1,0:T(8,128)(2,1)S(1)}, u32[]{:S(2)}, u32[]{:S(2)}) collective-permute-start(bf16[1,8,32,256]{3,2,1,0:T(8,128)(2,1)S(1)} %copy-done.43), channel_id=1, source_target_pairs={{0,20},{4,16},{8,28},{12,24},{16,4},{20,0},{24,12},{28,8},{1,21},{... | collective-permute-start | bytes 393224 | tf_op jit(solution)/shard_map/ppermute | solution.py:294
  144.6 41.6 %collective-permute-start.21 = (bf16[14,2,2,64,128]{4,3,2,1,0:T(8,128)(2,1)}, bf16[14,2,2,64,128]{4,3,2,1,0:T(8,128)(2,1)}, u32[]{:S(2)}, u32[]{:S(2)}) collective-permute-start(bf16[14,2,2,64,128]{4,3,2,1,0:T(8,128)(2,1)} %get-tuple-element.88), channel_id=1, source_target_pairs={{0,3},{1,2},{2,1},{3,0},{4,7},{5,6},{6,5},{7,4},{8,11},{9,10},{10,... | collective-permute-start | bytes 2752520 | tf_op jit(solution)/shard_map/ppermute | solution.py:294
  156.4 48.8 %collective-permute-start.23 = (bf16[1,12,32,256]{3,2,1,0:T(8,128)(2,1)}, bf16[1,12,32,256]{3,2,1,0:T(8,128)(2,1)S(1)}, u32[]{:S(2)}, u32[]{:S(2)}) collective-permute-start(bf16[1,12,32,256]{3,2,1,0:T(8,128)(2,1)} %get-tuple-element.92), channel_id=1, source_target_pairs={{0,8},{4,12},{8,0},{12,4},{16,24},{20,28},{24,16},{28,20},{1,9},{5... | collective-permute-start | bytes 589832 | tf_op jit(solution)/shard_map/ppermute | solution.py:294
  167.0 41.2 %collective-permute-start.24 = (bf16[1,12,32,256]{3,2,1,0:T(8,128)(2,1)S(1)}, bf16[1,12,32,256]{3,2,1,0:T(8,128)(2,1)S(1)}, u32[]{:S(2)}, u32[]{:S(2)}) collective-permute-start(bf16[1,12,32,256]{3,2,1,0:T(8,128)(2,1)S(1)} %copy-done.40), channel_id=1, source_target_pairs={{0,12},{4,8},{8,4},{12,0},{16,28},{20,24},{24,20},{28,16},{1,13},{... | collective-permute-start | bytes 589832 | tf_op jit(solution)/shard_map/ppermute | solution.py:294
  169.5 111.9 %collective-permute-start.29 = (bf16[16,2,2,64,128]{4,3,2,1,0:T(8,128)(2,1)}, bf16[16,2,2,64,128]{4,3,2,1,0:T(8,128)(2,1)}, u32[]{:S(2)}, u32[]{:S(2)}) collective-permute-start(bf16[16,2,2,64,128]{4,3,2,1,0:T(8,128)(2,1)} %get-tuple-element.98), channel_id=1, source_target_pairs={{0,1},{1,0},{2,3},{3,2},{4,5},{5,4},{6,7},{7,6},{8,9},{9,8},{10,11... | collective-permute-start | bytes 3145736 | tf_op jit(solution)/shard_map/ppermute | solution.py:294
  169.5 111.9 %collective-permute-start.30 = (bf16[16,2,2,64,128]{4,3,2,1,0:T(8,128)(2,1)}, bf16[16,2,2,64,128]{4,3,2,1,0:T(8,128)(2,1)}, u32[]{:S(2)}, u32[]{:S(2)}) collective-permute-start(bf16[16,2,2,64,128]{4,3,2,1,0:T(8,128)(2,1)} %get-tuple-element.99), channel_id=1, source_target_pairs={{0,2},{1,3},{2,0},{3,1},{4,6},{5,7},{6,4},{7,5},{8,10},{9,11},{10,... | collective-permute-start | bytes 3145736 | tf_op jit(solution)/shard_map/ppermute | solution.py:294
  186.2 95.2 %collective-permute-start.31 = (bf16[16,2,2,64,128]{4,3,2,1,0:T(8,128)(2,1)}, bf16[16,2,2,64,128]{4,3,2,1,0:T(8,128)(2,1)}, u32[]{:S(2)}, u32[]{:S(2)}) collective-permute-start(bf16[16,2,2,64,128]{4,3,2,1,0:T(8,128)(2,1)} %get-tuple-element.100), channel_id=1, source_target_pairs={{0,3},{1,2},{2,1},{3,0},{4,7},{5,6},{6,5},{7,4},{8,11},{9,10},{10,... | collective-permute-start | bytes 3145736 | tf_op jit(solution)/shard_map/ppermute | solution.py:294
  199.1 101.3 %all-to-all-start.2 = ((bf16[8,14,32,256]{3,2,1,0:T(8,128)(2,1)}), bf16[8,14,32,256]{3,2,1,0:T(8,128)(2,1)S(1)}, u32[]{:S(2)}, u32[]{:S(2)}) async-start(bf16[8,14,32,256]{3,2,1,0:T(8,128)(2,1)} %get-tuple-element.104), calls=%async_computation.2 | async-start | bytes 3670016 | tf_op jit(solution)/shard_map/all_to_all | solution.py:358
  205.2 56.7 %collective-permute-start.25 = (bf16[1,12,32,256]{3,2,1,0:T(8,128)(2,1)S(1)}, bf16[1,12,32,256]{3,2,1,0:T(8,128)(2,1)S(1)}, u32[]{:S(2)}, u32[]{:S(2)}) collective-permute-start(bf16[1,12,32,256]{3,2,1,0:T(8,128)(2,1)S(1)} %copy-done.39), channel_id=1, source_target_pairs={{0,16},{4,20},{8,24},{12,28},{16,0},{20,4},{24,8},{28,12},{1,17},{... | collective-permute-start | bytes 589832 | tf_op jit(solution)/shard_map/ppermute | solution.py:294
  208.2 64.7 %collective-permute-start.26 = (bf16[1,12,32,256]{3,2,1,0:T(8,128)(2,1)S(1)}, bf16[1,12,32,256]{3,2,1,0:T(8,128)(2,1)S(1)}, u32[]{:S(2)}, u32[]{:S(2)}) collective-permute-start(bf16[1,12,32,256]{3,2,1,0:T(8,128)(2,1)S(1)} %copy-done.38), channel_id=1, source_target_pairs={{0,20},{4,16},{8,28},{12,24},{16,4},{20,0},{24,12},{28,8},{1,21},{... | collective-permute-start | bytes 589832 | tf_op jit(solution)/shard_map/ppermute | solution.py:294
  301.7 58.5 %all-to-all-start.3 = ((bf16[8,16,32,256]{3,2,1,0:T(8,128)(2,1)}), bf16[8,16,32,256]{3,2,1,0:T(8,128)(2,1)S(1)}, u32[]{:S(2)}, u32[]{:S(2)}) async-start(bf16[8,16,32,256]{3,2,1,0:T(8,128)(2,1)} %get-tuple-element.105), calls=%async_computation.3 | async-start | bytes 4194304 | tf_op jit(solution)/shard_map/all_to_all | solution.py:358
  306.5 48.6 %collective-permute-start.41 = (f32[16,128]{1,0:T(8,128)S(1)}, f32[16,128]{1,0:T(8,128)S(1)}, u32[]{:S(2)}, u32[]{:S(2)}) collective-permute-start(f32[16,128]{1,0:T(8,128)S(1)} %fusion.4), channel_id=1, source_target_pairs={{0,28},{4,24},{8,20},{12,16},{16,12},{20,8},{24,4},{28,0},{1,29},{... | collective-permute-start | bytes 24584 | tf_op jit(solution)/shard_map/ppermute | solution.py:294
  311.2 43.8 %collective-permute-start.40 = (f32[16,128]{1,0:T(8,128)S(1)}, f32[16,128]{1,0:T(8,128)S(1)}, u32[]{:S(2)}, u32[]{:S(2)}) collective-permute-start(f32[16,128]{1,0:T(8,128)S(1)} %fusion.4), channel_id=1, source_target_pairs={{0,24},{4,28},{8,16},{12,20},{16,8},{20,12},{24,0},{28,4},{1,25},{... | collective-permute-start | bytes 24584 | tf_op jit(solution)/shard_map/ppermute | solution.py:294
  311.8 43.3 %collective-permute-start.39 = (f32[16,128]{1,0:T(8,128)S(1)}, f32[16,128]{1,0:T(8,128)S(1)}, u32[]{:S(2)}, u32[]{:S(2)}) collective-permute-start(f32[16,128]{1,0:T(8,128)S(1)} %fusion.4), channel_id=1, source_target_pairs={{0,20},{4,16},{8,28},{12,24},{16,4},{20,0},{24,12},{28,8},{1,21},{... | collective-permute-start | bytes 24584 | tf_op jit(solution)/shard_map/ppermute | solution.py:294
  312.3 41.9 %collective-permute-start.38 = (f32[16,128]{1,0:T(8,128)S(1)}, f32[16,128]{1,0:T(8,128)S(1)}, u32[]{:S(2)}, u32[]{:S(2)}) collective-permute-start(f32[16,128]{1,0:T(8,128)S(1)} %fusion.4), channel_id=1, source_target_pairs={{0,16},{4,20},{8,24},{12,28},{16,0},{20,4},{24,8},{28,12},{1,17},{... | collective-permute-start | bytes 24584 | tf_op jit(solution)/shard_map/ppermute | solution.py:294
  (71 other events, 1369.2 us)

commit v8 on v5

--- a/solution.py
+++ b/solution.py
@@ -10,9 +10,9 @@
 from jax.sharding import PartitionSpec as P
 
 UP = 16
-SHARES = (2, 4, 5, 6, 7, 8)
-DIRECT = (False,) * 6
-DETECT_FLOPS = 1_600_000_000
+SHARES = (2,3,4,5,5,6,7)
+DIRECT = (False,) * 7
+DETECT_FLOPS = 1750000000
 
 epsilon = 1e-05
 

time: 285 us -> 288 us (1.011)
  waiting for transfers between devices: 111 us -> 103 us
  starting transfers between devices: 51.1 us -> 56.9 us
  Pallas kernels: 111 us -> 115 us
    ppermute x27 -> x30, waiting for transfers between devices: 91.9 us -> 64.3 us  [swap(): lax.ppermute(one, axis, [(i, i ^ apart) for i in range(lax.axis_size(axis...]
    all_to_all x6 -> x7, waiting for transfers between devices: 19.6 us -> 38.7 us  [body(): lax.all_to_all(*sent, 'chan', split_axis=0, concat_axis=0, tiled=True)]
    all_to_all x6 -> x7, starting transfers between devices: 26.3 us -> 29.7 us  [body(): lax.all_to_all(*sent, 'chan', split_axis=0, concat_axis=0, tiled=True)]
    ppermute x27 -> x30, starting transfers between devices: 24.8 us -> 27.1 us  [swap(): lax.ppermute(one, axis, [(i, i ^ apart) for i in range(lax.axis_size(axis...]
    pallas_call x6 -> x7, Pallas kernels: 52.1 us -> 54.1 us  [detect(): pl.pallas_call(functools.partial(detect_kernel, columns), grid=(steps,),...]
    pallas_call x6 -> x7, Pallas kernels: 45.7 us -> 47.5 us  [form(): pl.pallas_call(form_kernel, grid=(steps,), in_specs=[pl.BlockSpec(memory_...]
    unnamed x48 -> x60, local copies, waits for them, and re-layouts: 5.4 us -> 6.85 us
  transfers between devices with their start and end apart: 33 -> 37, of which waited for: 18 -> 18; matrix products, arithmetic and copies ran while one was open for 1% -> 1% of each run, Pallas kernels for 33% -> 34%
where the time goes in v8:
time: 288 us; the launch traced here: 286 us
  Pallas kernels  115 us (40%)
  waiting for transfers between devices  103 us (36%)
  starting transfers between devices  56.9 us (20%)
  local copies, waits for them, and re-layouts  8.68 us (3%)
    ppermute x30, waiting for transfers between devices, swap(): lax.ppermute(one, axis, [(i, i ^ apart) for i in range(lax.axis_size(axis...  64.3 us
    pallas_call x7, Pallas kernels, detect(): pl.pallas_call(functools.partial(detect_kernel, columns), grid=(steps,),...  54.1 us
    pallas_call x7, Pallas kernels, form(): pl.pallas_call(form_kernel, grid=(steps,), in_specs=[pl.BlockSpec(memory_...  47.5 us
    all_to_all x7, waiting for transfers between devices, body(): lax.all_to_all(*sent, 'chan', split_axis=0, concat_axis=0, tiled=True)  38.7 us
    all_to_all x7, starting transfers between devices, body(): lax.all_to_all(*sent, 'chan', split_axis=0, concat_axis=0, tiled=True)  29.7 us
    ppermute x30, starting transfers between devices, swap(): lax.ppermute(one, axis, [(i, i ^ apart) for i in range(lax.axis_size(axis...  27.1 us
    pallas_call x1, Pallas kernels, soft_flag(): pl.pallas_call(functools.partial(flag_kernel, layout), grid=(own // block...  13.2 us
    unnamed x60, local copies, waits for them, and re-layouts  6.85 us
  transfers between devices with their start and end apart: 37, of which 18 were waited for; matrix products, arithmetic and copies ran while one was open for 1% of the time, Pallas kernels for 34%

profile of v8, /device:TPU:0, one launch (start us, length us, event | category | flops | bytes accessed | tf_op | source)
XLA Modules:
  0.0 286.1 jit_solution(14144615104331051945)
XLA Ops:
  8.4 5.1 %form.8 = (bf16[6,2,2,64,128]{4,3,2,1,0:T(8,128)(2,1)}, bf16[6,2,2,64,128]{4,3,2,1,0:T(8,128)(2,1)}, bf16[6,2,2,64,128]{4,3,2,1,0:T(8,128)(2,1)}, bf16[6,2,2,64,128]{4,3,2,1,0:T(8,128)(2,1)}) custom-call(s32[2]{0:T(128)} %pad_add_fusion.me_ref.after_ref.before_ref, bf16[4,2,2,64,128]{4,3,2,1,0:T(8,128)(2,1)} %get-tuple-element.44.after_ref.refs_0_, ...), custom_call_target="tpu_custom_call" | custom-call | flops 1000 | bytes 1000 | tf_op jit(solution)/shard_map/form/pallas_call | solution.py:187
  26.0 5.8 %all-to-all-start = ((bf16[8,4,32,256]{3,2,1,0:T(8,128)(2,1)}), bf16[8,4,32,256]{3,2,1,0:T(8,128)(2,1)S(1)}, u32[]{:S(2)}, u32[]{:S(2)}) async-start(bf16[8,4,32,256]{3,2,1,0:T(8,128)(2,1)} %get-tuple-element.56), calls=%async_computation | async-start | bytes 1048576 | tf_op jit(solution)/shard_map/all_to_all | solution.py:347
  31.8 6.2 %form.9 = (bf16[8,2,2,64,128]{4,3,2,1,0:T(8,128)(2,1)}, bf16[8,2,2,64,128]{4,3,2,1,0:T(8,128)(2,1)}, bf16[8,2,2,64,128]{4,3,2,1,0:T(8,128)(2,1)}, bf16[8,2,2,64,128]{4,3,2,1,0:T(8,128)(2,1)}) custom-call(s32[2]{0:T(128)} %pad_add_fusion.me_ref.after_ref.before_ref, f32[2,2,128]{2,1,0:T(2,128)} %get-tuple-element.49.after_ref, ...), custom_call_target="tpu_custom_call" | custom-call | flops 1000 | bytes 1000 | tf_op jit(solution)/shard_map/form/pallas_call | solution.py:187
  41.0 5.7 %detect.8 = (bf16[8,6,32,256]{3,2,1,0:T(8,128)(2,1)}, f32[3,2,128]{2,1,0:T(2,128)}) custom-call(s32[2]{0:T(128)} %pad_add_fusion.me_ref.after_ref.before_ref, bf16[8,2,2,64,128]{4,3,2,1,0:T(8,128)(2,1)} %get-tuple-element.50.after_ref.refs_0_, s32[2]{0:T(128)} %pad_add_fusion.me_ref.after_ref.before_ref, bf16[256,256]{1,0:T(8,128)(2,1)} %constant.60.clone.high_ref, ...), custom_call_target="tpu_custom_call" | custom-call | flops 10499999744 | bytes 1000 | tf_op jit(solution)/shard_map/detect/pallas_call | solution.py:221
  47.2 5.4 %all-to-all-start.1 = ((bf16[8,6,32,256]{3,2,1,0:T(8,128)(2,1)}), bf16[8,6,32,256]{3,2,1,0:T(8,128)(2,1)S(1)}, u32[]{:S(2)}, u32[]{:S(2)}) async-start(bf16[8,6,32,256]{3,2,1,0:T(8,128)(2,1)} %get-tuple-element.62), calls=%async_computation.1 | async-start | bytes 1572864 | tf_op jit(solution)/shard_map/all_to_all | solution.py:347
  52.6 7.3 %form.10 = (bf16[10,2,2,64,128]{4,3,2,1,0:T(8,128)(2,1)}, bf16[10,2,2,64,128]{4,3,2,1,0:T(8,128)(2,1)}, bf16[10,2,2,64,128]{4,3,2,1,0:T(8,128)(2,1)}, bf16[10,2,2,64,128]{4,3,2,1,0:T(8,128)(2,1)}) custom-call(s32[2]{0:T(128)} %pad_add_fusion.me_ref.after_ref.before_ref, f32[3,2,128]{2,1,0:T(2,128)} %get-tuple-element.54.after_ref, ...), custom_call_target="tpu_custom_call" | custom-call | flops 1000 | bytes 1000 | tf_op jit(solution)/shard_map/form/pallas_call | solution.py:187
  64.3 7.0 %detect.9 = (bf16[8,8,32,256]{3,2,1,0:T(8,128)(2,1)}, f32[4,2,128]{2,1,0:T(2,128)}) custom-call(s32[2]{0:T(128)} %pad_add_fusion.me_ref.after_ref.before_ref, bf16[10,2,2,64,128]{4,3,2,1,0:T(8,128)(2,1)} %get-tuple-element.55.after_ref.refs_0_, bf16[8,4,32,256]{3,2,1,0:T(8,128)(2,1)} %copy-done.6, bf16[256,256]{1,0:T(8,128)(2,1)} %constant.60.clone.high_ref, ...), custom_call_target="tpu_custom_call" | custom-call | flops 14000000000 | bytes 1000 | tf_op jit(solution)/shard_map/detect/pallas_call | solution.py:221
  77.3 7.2 %form.11 = (bf16[10,2,2,64,128]{4,3,2,1,0:T(8,128)(2,1)}, bf16[10,2,2,64,128]{4,3,2,1,0:T(8,128)(2,1)}, bf16[10,2,2,64,128]{4,3,2,1,0:T(8,128)(2,1)}, bf16[10,2,2,64,128]{4,3,2,1,0:T(8,128)(2,1)}) custom-call(s32[2]{0:T(128)} %pad_add_fusion.me_ref.after_ref.before_ref, f32[4,2,128]{2,1,0:T(2,128)} %get-tuple-element.60.after_ref, ...), custom_call_target="tpu_custom_call" | custom-call | flops 1000 | bytes 1000 | tf_op jit(solution)/shard_map/form/pallas_call | solution.py:187
  86.9 4.7 %collective-permute-done.11.refs_3_ = bf16[10,2,2,64,128]{4,3,2,1,0:T(8,128)(2,1)} collective-permute-done((bf16[10,2,2,64,128]{4,3,2,1,0:T(8,128)(2,1)}, bf16[10,2,2,64,128]{4,3,2,1,0:T(8,128)(2,1)}, u32[]{:S(2)}, u32[]{:S(2)}) %collective-permute-start.11) | collective-permute-done | bytes 655392 | tf_op jit(solution)/shard_map/ppermute | solution.py:294
  91.5 8.3 %detect.10 = (bf16[8,10,32,256]{3,2,1,0:T(8,128)(2,1)}, f32[5,2,128]{2,1,0:T(2,128)}) custom-call(s32[2]{0:T(128)} %pad_add_fusion.me_ref.after_ref.before_ref, bf16[10,2,2,64,128]{4,3,2,1,0:T(8,128)(2,1)} %get-tuple-element.61.after_ref.refs_0_, bf16[8,6,32,256]{3,2,1,0:T(8,128)(2,1)} %copy-done.5, bf16[256,256]{1,0:T(8,128)(2,1)} %constant.60.clone.high_ref, ...), custom_call_target="tpu_custom_call" | custom-call | flops 17500000256 | bytes 1000 | tf_op jit(solution)/shard_map/detect/pallas_call | solution.py:221
  99.8 4.5 %all-to-all-done.2.before_ref.refs_2_ = bf16[8,8,32,256]{3,2,1,0:T(8,128)(2,1)S(1)} async-done(((bf16[8,8,32,256]{3,2,1,0:T(8,128)(2,1)}), bf16[8,8,32,256]{3,2,1,0:T(8,128)(2,1)S(1)}, u32[]{:S(2)}, u32[]{:S(2)}) %all-to-all-start.2) | async-done | bytes 1048608 | tf_op jit(solution)/shard_map/all_to_all | solution.py:347
  107.9 8.3 %form.12 = (bf16[12,2,2,64,128]{4,3,2,1,0:T(8,128)(2,1)}, bf16[12,2,2,64,128]{4,3,2,1,0:T(8,128)(2,1)}, bf16[12,2,2,64,128]{4,3,2,1,0:T(8,128)(2,1)}, bf16[12,2,2,64,128]{4,3,2,1,0:T(8,128)(2,1)}) custom-call(s32[2]{0:T(128)} %pad_add_fusion.me_ref.after_ref.before_ref, f32[5,2,128]{2,1,0:T(2,128)} %get-tuple-element.66.after_ref, ...), custom_call_target="tpu_custom_call" | custom-call | flops 1000 | bytes 1000 | tf_op jit(solution)/shard_map/form/pallas_call | solution.py:187
  119.6 8.3 %detect.11 = (bf16[8,10,32,256]{3,2,1,0:T(8,128)(2,1)}, f32[5,2,128]{2,1,0:T(2,128)}) custom-call(s32[2]{0:T(128)} %pad_add_fusion.me_ref.after_ref.before_ref, bf16[12,2,2,64,128]{4,3,2,1,0:T(8,128)(2,1)} %get-tuple-element.67.after_ref.refs_0_, bf16[8,8,32,256]{3,2,1,0:T(8,128)(2,1)} %copy-done.4, bf16[256,256]{1,0:T(8,128)(2,1)} %constant.60.clone.high_ref, ...), custom_call_target="tpu_custom_call" | custom-call | flops 17500000256 | bytes 1000 | tf_op jit(solution)/shard_map/detect/pallas_call | solution.py:221
  127.9 11.7 %all-to-all-done.3.before_ref.refs_3_ = bf16[8,10,32,256]{3,2,1,0:T(8,128)(2,1)S(1)} async-done(((bf16[8,10,32,256]{3,2,1,0:T(8,128)(2,1)}), bf16[8,10,32,256]{3,2,1,0:T(8,128)(2,1)S(1)}, u32[]{:S(2)}, u32[]{:S(2)}) %all-to-all-start.3) | async-done | bytes 1310752 | tf_op jit(solution)/shard_map/all_to_all | solution.py:347
  143.3 9.4 %form.13 = (bf16[14,2,2,64,128]{4,3,2,1,0:T(8,128)(2,1)}, bf16[14,2,2,64,128]{4,3,2,1,0:T(8,128)(2,1)}, bf16[14,2,2,64,128]{4,3,2,1,0:T(8,128)(2,1)}, bf16[14,2,2,64,128]{4,3,2,1,0:T(8,128)(2,1)}) custom-call(s32[2]{0:T(128)} %pad_add_fusion.me_ref.after_ref.before_ref, f32[5,2,128]{2,1,0:T(2,128)} %get-tuple-element.72.after_ref, ...), custom_call_target="tpu_custom_call" | custom-call | flops 1000 | bytes 1000 | tf_op jit(solution)/shard_map/form/pallas_call | solution.py:187
  155.7 9.5 %detect.12 = (bf16[8,12,32,256]{3,2,1,0:T(8,128)(2,1)}, f32[6,2,128]{2,1,0:T(2,128)}) custom-call(s32[2]{0:T(128)} %pad_add_fusion.me_ref.after_ref.before_ref, bf16[14,2,2,64,128]{4,3,2,1,0:T(8,128)(2,1)} %get-tuple-element.73.after_ref.refs_0_, bf16[8,10,32,256]{3,2,1,0:T(8,128)(2,1)} %copy-done.2, bf16[256,256]{1,0:T(8,128)(2,1)} %constant.60.clone.high_ref, ...), custom_call_target="tpu_custom_call" | custom-call | flops 20999999488 | bytes 1000 | tf_op jit(solution)/shard_map/detect/pallas_call | solution.py:221
  165.2 9.6 %all-to-all-done.4.before_ref.refs_4_ = bf16[8,10,32,256]{3,2,1,0:T(8,128)(2,1)S(1)} async-done(((bf16[8,10,32,256]{3,2,1,0:T(8,128)(2,1)}), bf16[8,10,32,256]{3,2,1,0:T(8,128)(2,1)S(1)}, u32[]{:S(2)}, u32[]{:S(2)}) %all-to-all-start.4) | async-done | bytes 1310752 | tf_op jit(solution)/shard_map/all_to_all | solution.py:347
  179.5 15.9 %collective-permute-done.20.refs_3_ = bf16[14,2,2,64,128]{4,3,2,1,0:T(8,128)(2,1)} collective-permute-done((bf16[14,2,2,64,128]{4,3,2,1,0:T(8,128)(2,1)}, bf16[14,2,2,64,128]{4,3,2,1,0:T(8,128)(2,1)}, u32[]{:S(2)}, u32[]{:S(2)}) %collective-permute-start.20) | collective-permute-done | bytes 917536 | tf_op jit(solution)/shard_map/ppermute | solution.py:294
  195.4 10.8 %detect.13 = (bf16[8,14,32,256]{3,2,1,0:T(8,128)(2,1)}, f32[7,2,128]{2,1,0:T(2,128)}) custom-call(s32[2]{0:T(128)} %pad_add_fusion.me_ref.after_ref.before_ref, f32[6,2,128]{2,1,0:T(2,128)} %get-tuple-element.78.after_ref, bf16[8,10,32,256]{3,2,1,0:T(8,128)(2,1)} %copy-done.3, bf16[256,256]{1,0:T(8,128)(2,1)} %constant.60.clone.high_ref, ...), custom_call_target="tpu_custom_call" | custom-call | flops 24500000768 | bytes 1000 | tf_op jit(solution)/shard_map/detect/pallas_call | solution.py:221
  206.2 10.5 %all-to-all-done.5.refs_5_ = bf16[8,12,32,256]{3,2,1,0:T(8,128)(2,1)S(1)} async-done(((bf16[8,12,32,256]{3,2,1,0:T(8,128)(2,1)}), bf16[8,12,32,256]{3,2,1,0:T(8,128)(2,1)S(1)}, u32[]{:S(2)}, u32[]{:S(2)}) %all-to-all-start.5) | async-done | bytes 1572896 | tf_op jit(solution)/shard_map/all_to_all | solution.py:347
  230.3 6.4 %collective-permute-done.24 = f32[1,16,128]{2,1,0:T(8,128)S(1)} collective-permute-done((f32[1,16,128]{2,1,0:T(8,128)S(1)}, f32[1,16,128]{2,1,0:T(8,128)S(1)}, u32[]{:S(2)}, u32[]{:S(2)}) %collective-permute-start.24) | collective-permute-done | bytes 8224 | tf_op jit(solution)/shard_map/ppermute | solution.py:294
  238.5 14.4 %collective-permute-done.25 = f32[2,16,128]{2,1,0:T(8,128)S(1)} collective-permute-done((f32[2,16,128]{2,1,0:T(8,128)S(1)}, f32[2,16,128]{2,1,0:T(8,128)S(1)}, u32[]{:S(2)}, u32[]{:S(2)}) %collective-permute-start.25) | collective-permute-done | bytes 16416 | tf_op jit(solution)/shard_map/ppermute | solution.py:294
  257.2 8.4 %collective-permute-done.26 = f32[4,16,128]{2,1,0:T(8,128)S(1)} collective-permute-done((f32[4,16,128]{2,1,0:T(8,128)S(1)}, f32[4,16,128]{2,1,0:T(8,128)S(1)}, u32[]{:S(2)}, u32[]{:S(2)}) %collective-permute-start.26) | collective-permute-done | bytes 32800 | tf_op jit(solution)/shard_map/ppermute | solution.py:294
  272.7 13.2 %flag.1 = bf16[2,32,65536]{2,1,0:T(8,128)(2,1)} custom-call(s32[2]{0:T(128)} %pad_add_fusion.me_ref.after_ref.before_ref, bf16[256,128]{1,0:T(8,128)(2,1)} %constant.62.clone.group_ref, f32[512,1,128]{2,1,0:T(1,128)} %bitcast.43, f32[512,1,128]{2,1,0:T(1,128)} %copy.17.mask_ref, bf16[8,4,32,256]{3,2,1,0:T(8,128)(2,1)} %copy-done.6, ...), custom_call_target="tpu_custom_call" | custom-call | flops 1073741824 | bytes 16777216 | tf_op jit(solution)/shard_map/flag/pallas_call | solution.py:267
  (149 shorter events, 81.3 us)
Async XLA Ops:
  13.5 26.5 %collective-permute-start.3 = (bf16[6,2,2,64,128]{4,3,2,1,0:T(8,128)(2,1)}, bf16[6,2,2,64,128]{4,3,2,1,0:T(8,128)(2,1)S(1)}, u32[]{:S(2)}, u32[]{:S(2)}) collective-permute-start(bf16[6,2,2,64,128]{4,3,2,1,0:T(8,128)(2,1)} %get-tuple-element.51), channel_id=1, source_target_pairs={{0,1},{1,0},{2,3},{3,2},{4,5},{5,4},{6,7},{7,6},{8,9},{9,8},{10,11... | collective-permute-start | bytes 1179656 | tf_op jit(solution)/shard_map/ppermute | solution.py:294
  13.6 26.3 %collective-permute-start.4 = (bf16[6,2,2,64,128]{4,3,2,1,0:T(8,128)(2,1)}, bf16[6,2,2,64,128]{4,3,2,1,0:T(8,128)(2,1)S(1)}, u32[]{:S(2)}, u32[]{:S(2)}) collective-permute-start(bf16[6,2,2,64,128]{4,3,2,1,0:T(8,128)(2,1)} %get-tuple-element.52), channel_id=1, source_target_pairs={{0,2},{1,3},{2,0},{3,1},{4,6},{5,7},{6,4},{7,5},{8,10},{9,11},{10,... | collective-permute-start | bytes 1179656 | tf_op jit(solution)/shard_map/ppermute | solution.py:294
  16.3 23.7 %collective-permute-start.5 = (bf16[6,2,2,64,128]{4,3,2,1,0:T(8,128)(2,1)}, bf16[6,2,2,64,128]{4,3,2,1,0:T(8,128)(2,1)S(1)}, u32[]{:S(2)}, u32[]{:S(2)}) collective-permute-start(bf16[6,2,2,64,128]{4,3,2,1,0:T(8,128)(2,1)} %get-tuple-element.53), channel_id=1, source_target_pairs={{0,3},{1,2},{2,1},{3,0},{4,7},{5,6},{6,5},{7,4},{8,11},{9,10},{10,... | collective-permute-start | bytes 1179656 | tf_op jit(solution)/shard_map/ppermute | solution.py:294
  38.0 23.6 %collective-permute-start.6 = (bf16[8,2,2,64,128]{4,3,2,1,0:T(8,128)(2,1)}, bf16[8,2,2,64,128]{4,3,2,1,0:T(8,128)(2,1)S(1)}, u32[]{:S(2)}, u32[]{:S(2)}) collective-permute-start(bf16[8,2,2,64,128]{4,3,2,1,0:T(8,128)(2,1)} %get-tuple-element.57), channel_id=1, source_target_pairs={{0,1},{1,0},{2,3},{3,2},{4,5},{5,4},{6,7},{7,6},{8,9},{9,8},{10,11... | collective-permute-start | bytes 1572872 | tf_op jit(solution)/shard_map/ppermute | solution.py:294
  38.4 23.4 %collective-permute-start.7 = (bf16[8,2,2,64,128]{4,3,2,1,0:T(8,128)(2,1)}, bf16[8,2,2,64,128]{4,3,2,1,0:T(8,128)(2,1)S(1)}, u32[]{:S(2)}, u32[]{:S(2)}) collective-permute-start(bf16[8,2,2,64,128]{4,3,2,1,0:T(8,128)(2,1)} %get-tuple-element.58), channel_id=1, source_target_pairs={{0,2},{1,3},{2,0},{3,1},{4,6},{5,7},{6,4},{7,5},{8,10},{9,11},{10,... | collective-permute-start | bytes 1572872 | tf_op jit(solution)/shard_map/ppermute | solution.py:294
  40.0 23.5 %collective-permute-start.8 = (bf16[8,2,2,64,128]{4,3,2,1,0:T(8,128)(2,1)}, bf16[8,2,2,64,128]{4,3,2,1,0:T(8,128)(2,1)S(1)}, u32[]{:S(2)}, u32[]{:S(2)}) collective-permute-start(bf16[8,2,2,64,128]{4,3,2,1,0:T(8,128)(2,1)} %get-tuple-element.59), channel_id=1, source_target_pairs={{0,3},{1,2},{2,1},{3,0},{4,7},{5,6},{6,5},{7,4},{8,11},{9,10},{10,... | collective-permute-start | bytes 1572872 | tf_op jit(solution)/shard_map/ppermute | solution.py:294
  47.2 26.1 %all-to-all-start.1 = ((bf16[8,6,32,256]{3,2,1,0:T(8,128)(2,1)}), bf16[8,6,32,256]{3,2,1,0:T(8,128)(2,1)S(1)}, u32[]{:S(2)}, u32[]{:S(2)}) async-start(bf16[8,6,32,256]{3,2,1,0:T(8,128)(2,1)} %get-tuple-element.62), calls=%async_computation.1 | async-start | bytes 1572864 | tf_op jit(solution)/shard_map/all_to_all | solution.py:347
  59.9 27.0 %collective-permute-start.9 = (bf16[10,2,2,64,128]{4,3,2,1,0:T(8,128)(2,1)}, bf16[10,2,2,64,128]{4,3,2,1,0:T(8,128)(2,1)S(1)}, u32[]{:S(2)}, u32[]{:S(2)}) collective-permute-start(bf16[10,2,2,64,128]{4,3,2,1,0:T(8,128)(2,1)} %get-tuple-element.63), channel_id=1, source_target_pairs={{0,1},{1,0},{2,3},{3,2},{4,5},{5,4},{6,7},{7,6},{8,9},{9,8},{10,11... | collective-permute-start | bytes 1966088 | tf_op jit(solution)/shard_map/ppermute | solution.py:294
  60.1 26.7 %collective-permute-start.10 = (bf16[10,2,2,64,128]{4,3,2,1,0:T(8,128)(2,1)}, bf16[10,2,2,64,128]{4,3,2,1,0:T(8,128)(2,1)}, u32[]{:S(2)}, u32[]{:S(2)}) collective-permute-start(bf16[10,2,2,64,128]{4,3,2,1,0:T(8,128)(2,1)} %get-tuple-element.64), channel_id=1, source_target_pairs={{0,2},{1,3},{2,0},{3,1},{4,6},{5,7},{6,4},{7,5},{8,10},{9,11},{10,... | collective-permute-start | bytes 1966088 | tf_op jit(solution)/shard_map/ppermute | solution.py:294
  61.6 29.9 %collective-permute-start.11 = (bf16[10,2,2,64,128]{4,3,2,1,0:T(8,128)(2,1)}, bf16[10,2,2,64,128]{4,3,2,1,0:T(8,128)(2,1)}, u32[]{:S(2)}, u32[]{:S(2)}) collective-permute-start(bf16[10,2,2,64,128]{4,3,2,1,0:T(8,128)(2,1)} %get-tuple-element.65), channel_id=1, source_target_pairs={{0,3},{1,2},{2,1},{3,0},{4,7},{5,6},{6,5},{7,4},{8,11},{9,10},{10,... | collective-permute-start | bytes 1966088 | tf_op jit(solution)/shard_map/ppermute | solution.py:294
  73.4 31.0 %all-to-all-start.2 = ((bf16[8,8,32,256]{3,2,1,0:T(8,128)(2,1)}), bf16[8,8,32,256]{3,2,1,0:T(8,128)(2,1)S(1)}, u32[]{:S(2)}, u32[]{:S(2)}) async-start(bf16[8,8,32,256]{3,2,1,0:T(8,128)(2,1)} %get-tuple-element.68), calls=%async_computation.2 | async-start | bytes 2097152 | tf_op jit(solution)/shard_map/all_to_all | solution.py:347
  84.6 33.6 %collective-permute-start.12 = (bf16[10,2,2,64,128]{4,3,2,1,0:T(8,128)(2,1)}, bf16[10,2,2,64,128]{4,3,2,1,0:T(8,128)(2,1)}, u32[]{:S(2)}, u32[]{:S(2)}) collective-permute-start(bf16[10,2,2,64,128]{4,3,2,1,0:T(8,128)(2,1)} %get-tuple-element.69), channel_id=1, source_target_pairs={{0,1},{1,0},{2,3},{3,2},{4,5},{5,4},{6,7},{7,6},{8,9},{9,8},{10,11... | collective-permute-start | bytes 1966088 | tf_op jit(solution)/shard_map/ppermute | solution.py:294
  85.4 32.9 %collective-permute-start.13 = (bf16[10,2,2,64,128]{4,3,2,1,0:T(8,128)(2,1)}, bf16[10,2,2,64,128]{4,3,2,1,0:T(8,128)(2,1)}, u32[]{:S(2)}, u32[]{:S(2)}) collective-permute-start(bf16[10,2,2,64,128]{4,3,2,1,0:T(8,128)(2,1)} %get-tuple-element.70), channel_id=1, source_target_pairs={{0,2},{1,3},{2,0},{3,1},{4,6},{5,7},{6,4},{7,5},{8,10},{9,11},{10,... | collective-permute-start | bytes 1966088 | tf_op jit(solution)/shard_map/ppermute | solution.py:294
  86.9 32.8 %collective-permute-start.14 = (bf16[10,2,2,64,128]{4,3,2,1,0:T(8,128)(2,1)}, bf16[10,2,2,64,128]{4,3,2,1,0:T(8,128)(2,1)}, u32[]{:S(2)}, u32[]{:S(2)}) collective-permute-start(bf16[10,2,2,64,128]{4,3,2,1,0:T(8,128)(2,1)} %get-tuple-element.71), channel_id=1, source_target_pairs={{0,3},{1,2},{2,1},{3,0},{4,7},{5,6},{6,5},{7,4},{8,11},{9,10},{10,... | collective-permute-start | bytes 1966088 | tf_op jit(solution)/shard_map/ppermute | solution.py:294
  104.3 35.2 %all-to-all-start.3 = ((bf16[8,10,32,256]{3,2,1,0:T(8,128)(2,1)}), bf16[8,10,32,256]{3,2,1,0:T(8,128)(2,1)S(1)}, u32[]{:S(2)}, u32[]{:S(2)}) async-start(bf16[8,10,32,256]{3,2,1,0:T(8,128)(2,1)} %get-tuple-element.74), calls=%async_computation.3 | async-start | bytes 2621440 | tf_op jit(solution)/shard_map/all_to_all | solution.py:347
  116.3 38.5 %collective-permute-start.15 = (bf16[12,2,2,64,128]{4,3,2,1,0:T(8,128)(2,1)}, bf16[12,2,2,64,128]{4,3,2,1,0:T(8,128)(2,1)S(1)}, u32[]{:S(2)}, u32[]{:S(2)}) collective-permute-start(bf16[12,2,2,64,128]{4,3,2,1,0:T(8,128)(2,1)} %get-tuple-element.75), channel_id=1, source_target_pairs={{0,1},{1,0},{2,3},{3,2},{4,5},{5,4},{6,7},{7,6},{8,9},{9,8},{10,11... | collective-permute-start | bytes 2359304 | tf_op jit(solution)/shard_map/ppermute | solution.py:294
  116.3 38.5 %collective-permute-start.16 = (bf16[12,2,2,64,128]{4,3,2,1,0:T(8,128)(2,1)}, bf16[12,2,2,64,128]{4,3,2,1,0:T(8,128)(2,1)}, u32[]{:S(2)}, u32[]{:S(2)}) collective-permute-start(bf16[12,2,2,64,128]{4,3,2,1,0:T(8,128)(2,1)} %get-tuple-element.76), channel_id=1, source_target_pairs={{0,2},{1,3},{2,0},{3,1},{4,6},{5,7},{6,4},{7,5},{8,10},{9,11},{10,... | collective-permute-start | bytes 2359304 | tf_op jit(solution)/shard_map/ppermute | solution.py:294
  118.2 36.7 %collective-permute-start.17 = (bf16[12,2,2,64,128]{4,3,2,1,0:T(8,128)(2,1)}, bf16[12,2,2,64,128]{4,3,2,1,0:T(8,128)(2,1)}, u32[]{:S(2)}, u32[]{:S(2)}) collective-permute-start(bf16[12,2,2,64,128]{4,3,2,1,0:T(8,128)(2,1)} %get-tuple-element.77), channel_id=1, source_target_pairs={{0,3},{1,2},{2,1},{3,0},{4,7},{5,6},{6,5},{7,4},{8,11},{9,10},{10,... | collective-permute-start | bytes 2359304 | tf_op jit(solution)/shard_map/ppermute | solution.py:294
  139.6 35.2 %all-to-all-start.4 = ((bf16[8,10,32,256]{3,2,1,0:T(8,128)(2,1)}), bf16[8,10,32,256]{3,2,1,0:T(8,128)(2,1)S(1)}, u32[]{:S(2)}, u32[]{:S(2)}) async-start(bf16[8,10,32,256]{3,2,1,0:T(8,128)(2,1)} %get-tuple-element.79), calls=%async_computation.4 | async-start | bytes 2621440 | tf_op jit(solution)/shard_map/all_to_all | solution.py:347
  152.7 26.7 %collective-permute-start.18 = (bf16[14,2,2,64,128]{4,3,2,1,0:T(8,128)(2,1)}, bf16[14,2,2,64,128]{4,3,2,1,0:T(8,128)(2,1)S(1)}, u32[]{:S(2)}, u32[]{:S(2)}) collective-permute-start(bf16[14,2,2,64,128]{4,3,2,1,0:T(8,128)(2,1)} %get-tuple-element.80), channel_id=1, source_target_pairs={{0,1},{1,0},{2,3},{3,2},{4,5},{5,4},{6,7},{7,6},{8,9},{9,8},{10,11... | collective-permute-start | bytes 2752520 | tf_op jit(solution)/shard_map/ppermute | solution.py:294
  152.8 26.7 %collective-permute-start.19 = (bf16[14,2,2,64,128]{4,3,2,1,0:T(8,128)(2,1)}, bf16[14,2,2,64,128]{4,3,2,1,0:T(8,128)(2,1)}, u32[]{:S(2)}, u32[]{:S(2)}) collective-permute-start(bf16[14,2,2,64,128]{4,3,2,1,0:T(8,128)(2,1)} %get-tuple-element.81), channel_id=1, source_target_pairs={{0,2},{1,3},{2,0},{3,1},{4,6},{5,7},{6,4},{7,5},{8,10},{9,11},{10,... | collective-permute-start | bytes 2752520 | tf_op jit(solution)/shard_map/ppermute | solution.py:294
  154.8 40.6 %collective-permute-start.20 = (bf16[14,2,2,64,128]{4,3,2,1,0:T(8,128)(2,1)}, bf16[14,2,2,64,128]{4,3,2,1,0:T(8,128)(2,1)}, u32[]{:S(2)}, u32[]{:S(2)}) collective-permute-start(bf16[14,2,2,64,128]{4,3,2,1,0:T(8,128)(2,1)} %get-tuple-element.82), channel_id=1, source_target_pairs={{0,3},{1,2},{2,1},{3,0},{4,7},{5,6},{6,5},{7,4},{8,11},{9,10},{10,... | collective-permute-start | bytes 2752520 | tf_op jit(solution)/shard_map/ppermute | solution.py:294
  175.8 40.8 %all-to-all-start.5 = ((bf16[8,12,32,256]{3,2,1,0:T(8,128)(2,1)}), bf16[8,12,32,256]{3,2,1,0:T(8,128)(2,1)S(1)}, u32[]{:S(2)}, u32[]{:S(2)}) async-start(bf16[8,12,32,256]{3,2,1,0:T(8,128)(2,1)} %get-tuple-element.84), calls=%async_computation.5 | async-start | bytes 3145728 | tf_op jit(solution)/shard_map/all_to_all | solution.py:347
  217.8 53.6 %all-to-all-start.6 = ((bf16[8,14,32,256]{3,2,1,0:T(8,128)(2,1)}), bf16[8,14,32,256]{3,2,1,0:T(8,128)(2,1)S(1)}, u32[]{:S(2)}, u32[]{:S(2)}) async-start(bf16[8,14,32,256]{3,2,1,0:T(8,128)(2,1)} %get-tuple-element.85), calls=%async_computation.6 | async-start | bytes 3670016 | tf_op jit(solution)/shard_map/all_to_all | solution.py:347
  (43 other events, 318.4 us)

commit v9 on v5

--- a/solution.py
+++ b/solution.py
@@ -115,13 +115,26 @@
             out_refs[d // owners][d % owners, c] = block
 
 
-def flag_kernel(layout, me_ref, group_ref, common_ref, mask_ref, *refs):
-    chunk_refs, out_ref, power_ref = refs[:-2], refs[-2], refs[-1]
+def flag_kernel(layout, groups, me_ref, group_ref, mask_ref, *refs):
+    part_refs, chunk_refs = refs[:groups], refs[groups:-3]
+    out_ref, power_ref, common_ref = refs[-3:]
     beams, width = chunk_refs[0].shape[2:]
     samples = width // 2
     channels = common_ref.shape[0]
     local = layout[-1][0] + layout[-1][1]
     sources = channels // local
+
+    @pl.when(pl.program_id(0) == 0)
+    def _():
+        part = local // groups
+
+        def place(s, carry):
+            for r, part_ref in enumerate(part_refs):
+                first = s * local + (me_ref[0] ^ r) * part
+                common_ref[pl.ds(first, part)] = part_ref[s]
+            return carry
+
+        lax.fori_loop(0, sources, place, 0)
 
     def blocks(work, carry):
         refs = iter(chunk_refs)
@@ -162,7 +175,7 @@
         for c in range(size):
             row = block_ref[c].astype(jnp.float32)
             cleaned = row[:, :samples] - common_ref[channel + c]
-            weight = mask_ref[channel + c] / (1.0 + power_ref[channel + c] * scale)
+            weight = mask_ref[channel + c] * pl.reciprocal(1.0 + power_ref[channel + c] * scale)
             where = pl.ds(pl.multiple_of((channel + c) * samples, samples), samples)
             out_ref[0, :, where] = (cleaned * weight).astype(jnp.bfloat16)
             out_ref[1, :, where] = (row[:, samples:] * weight).astype(jnp.bfloat16)
@@ -254,24 +267,24 @@
     )(me, *after, *tables, order, *formed)
 
 
-def soft_flag(me, owned, common, mask, frame_count):
+def soft_flag(me, owned, parts, mask, frame_count):
     own, width = owned[0][0].shape[2:]
     sizes = [one[0].shape[1] for one in owned]
     layout = [(sum(sizes[:i]), sizes[i], len(one)) for i, one in enumerate(owned)]
     owned = [block for one in owned for block in one]
     samples = width // 2
-    channels = common.shape[0]
+    channels = mask.shape[0]
     block = 16 if own % 16 == 0 else own
     group = np.kron(np.eye(samples // frame_count), np.ones((frame_count, frame_count)))
     group = jnp.asarray(np.concatenate([group, group]) / frame_count, jnp.bfloat16)
     return pl.pallas_call(
-        functools.partial(flag_kernel, layout),
+        functools.partial(flag_kernel, layout, len(parts)),
         grid=(own // block,),
         in_specs=[
             pl.BlockSpec(memory_space=pltpu.SMEM),
             whole_spec(group),
-            whole_spec(common),
             whole_spec(mask),
+            *[whole_spec(part) for part in parts],
             *[
                 pl.BlockSpec((*one.shape[:2], block, width), lambda i: (0, 0, i, 0))
                 for one in owned
@@ -279,7 +292,10 @@
         ],
         out_specs=pl.BlockSpec((2, block, channels * samples), lambda i: (0, i, 0)),
         out_shape=jax.ShapeDtypeStruct((2, own, channels * samples), jnp.bfloat16),
-        scratch_shapes=[pltpu.VMEM((channels, block, samples), jnp.float32)],
+        scratch_shapes=[
+            pltpu.VMEM((channels, block, samples), jnp.float32),
+            pltpu.VMEM((channels, 1, samples), jnp.float32),
+        ],
         cost_estimate=pl.CostEstimate(
             flops=channels * own * samples * samples * 4,
             bytes_accessed=channels * own * samples * 8,
@@ -287,7 +303,7 @@
         ),
         compiler_params=pltpu.CompilerParams(vmem_limit_bytes=60 << 20),
         name="flag",
-    )(me, group, common, mask, *owned)
+    )(me, group, mask, *parts, *owned)
 
 
 def swap(one, axis, apart):
@@ -360,11 +376,9 @@
         low = (near >> bit) % 2 == 0
         shared = jnp.where(low, jnp.stack([shared, other]), jnp.stack([other, shared]))
         shared = shared.reshape(-1, local // groups, samples)
-    common = jnp.zeros((owners, groups, local // groups, samples), jnp.float32)
-    for r in range(groups):
-        other = swap(shared, "grp", r) if r else shared
-        common = lax.dynamic_update_index_in_dim(common, other, mine ^ r, 1)
-    flagged = soft_flag(me, owned, common.reshape(channels, 1, samples), mask, frame_count)
+    shared = shared[:, :, None]
+    shared = [swap(shared, "grp", r) if r else shared for r in range(groups)]
+    flagged = soft_flag(me, owned, shared, mask, frame_count)
     return (flagged, common_piece)
 
 

time: 285 us -> 285 us (level)
    unnamed x48 -> x54, local copies, waits for them, and re-layouts: 5.4 us -> 5.96 us
where the time goes in v9:
time: 285 us; the launch traced here: 284 us
  waiting for transfers between devices  112 us (39%)
  Pallas kernels  111 us (39%)
  starting transfers between devices  51.1 us (18%)
  local copies, waits for them, and re-layouts  7.51 us (3%)
    ppermute x27, waiting for transfers between devices, swap(): lax.ppermute(one, axis, [(i, i ^ apart) for i in range(lax.axis_size(axis...  92 us
    pallas_call x6, Pallas kernels, detect(): pl.pallas_call(functools.partial(detect_kernel, columns), grid=(steps,),...  52.1 us
    pallas_call x6, Pallas kernels, form(): pl.pallas_call(form_kernel, grid=(steps,), in_specs=[pl.BlockSpec(memory_...  45.6 us
    all_to_all x6, starting transfers between devices, body(): lax.all_to_all(*sent, 'chan', split_axis=0, concat_axis=0, tiled=True)  26.3 us
    ppermute x27, starting transfers between devices, swap(): lax.ppermute(one, axis, [(i, i ^ apart) for i in range(lax.axis_size(axis...  24.8 us
    all_to_all x6, waiting for transfers between devices, body(): lax.all_to_all(*sent, 'chan', split_axis=0, concat_axis=0, tiled=True)  19.6 us
    pallas_call x1, Pallas kernels, soft_flag(): pl.pallas_call(functools.partial(flag_kernel, layout, len(parts)), grid=(...  13.5 us
    unnamed x54, local copies, waits for them, and re-layouts  5.96 us
  transfers between devices with their start and end apart: 33, of which 18 were waited for; matrix products, arithmetic and copies ran while one was open for 1% of the time, Pallas kernels for 33%

profile of v9, /device:TPU:0, one launch (start us, length us, event | category | flops | bytes accessed | tf_op | source)
XLA Modules:
  0.0 284.0 jit_solution(7999615771372559437)
XLA Ops:
  8.5 6.1 %form.7 = (bf16[8,2,2,64,128]{4,3,2,1,0:T(8,128)(2,1)}, bf16[8,2,2,64,128]{4,3,2,1,0:T(8,128)(2,1)}, bf16[8,2,2,64,128]{4,3,2,1,0:T(8,128)(2,1)}, bf16[8,2,2,64,128]{4,3,2,1,0:T(8,128)(2,1)}) custom-call(s32[2]{0:T(128)} %pad_add_fusion.me_ref.after_ref.before_ref, bf16[4,2,2,64,128]{4,3,2,1,0:T(8,128)(2,1)} %get-tuple-element.38.after_ref.refs_0_, ...), custom_call_target="tpu_custom_call" | custom-call | flops 1000 | bytes 1000 | tf_op jit(solution)/shard_map/form/pallas_call | solution.py:200
  21.6 4.5 %detect.6 = (bf16[8,4,32,256]{3,2,1,0:T(8,128)(2,1)}, f32[2,2,128]{2,1,0:T(2,128)}) custom-call(s32[2]{0:T(128)} %pad_add_fusion.me_ref.after_ref.before_ref, bf16[8,2,2,64,128]{4,3,2,1,0:T(8,128)(2,1)} %get-tuple-element.39.after_ref.refs_0_, s32[2]{0:T(128)} %pad_add_fusion.me_ref.after_ref.before_ref, bf16[256,256]{1,0:T(8,128)(2,1)} %constant.48.clone.high_ref, ...), custom_call_target="tpu_custom_call" | custom-call | flops 6400000000 | bytes 1000 | tf_op jit(solution)/shard_map/detect/pallas_call | solution.py:234
  26.1 5.8 %all-to-all-start = ((bf16[8,4,32,256]{3,2,1,0:T(8,128)(2,1)}), bf16[8,4,32,256]{3,2,1,0:T(8,128)(2,1)S(1)}, u32[]{:S(2)}, u32[]{:S(2)}) async-start(bf16[8,4,32,256]{3,2,1,0:T(8,128)(2,1)} %get-tuple-element.50), calls=%async_computation | async-start | bytes 1048576 | tf_op jit(solution)/shard_map/all_to_all | solution.py:363
  31.9 7.3 %form.8 = (bf16[10,2,2,64,128]{4,3,2,1,0:T(8,128)(2,1)}, bf16[10,2,2,64,128]{4,3,2,1,0:T(8,128)(2,1)}, bf16[10,2,2,64,128]{4,3,2,1,0:T(8,128)(2,1)}, bf16[10,2,2,64,128]{4,3,2,1,0:T(8,128)(2,1)}) custom-call(s32[2]{0:T(128)} %pad_add_fusion.me_ref.after_ref.before_ref, f32[2,2,128]{2,1,0:T(2,128)} %get-tuple-element.43.after_ref, ...), custom_call_target="tpu_custom_call" | custom-call | flops 1000 | bytes 1000 | tf_op jit(solution)/shard_map/form/pallas_call | solution.py:200
  44.2 7.0 %detect.7 = (bf16[8,8,32,256]{3,2,1,0:T(8,128)(2,1)}, f32[4,2,128]{2,1,0:T(2,128)}) custom-call(s32[2]{0:T(128)} %pad_add_fusion.me_ref.after_ref.before_ref, bf16[10,2,2,64,128]{4,3,2,1,0:T(8,128)(2,1)} %get-tuple-element.44.after_ref.refs_0_, s32[2]{0:T(128)} %pad_add_fusion.me_ref.after_ref.before_ref, bf16[256,256]{1,0:T(8,128)(2,1)} %constant.48.clone.high_ref, ...), custom_call_target="tpu_custom_call" | custom-call | flops 12800000000 | bytes 1000 | tf_op jit(solution)/shard_map/detect/pallas_call | solution.py:234
  51.2 5.8 %all-to-all-start.1 = ((bf16[8,8,32,256]{3,2,1,0:T(8,128)(2,1)}), bf16[8,8,32,256]{3,2,1,0:T(8,128)(2,1)S(1)}, u32[]{:S(2)}, u32[]{:S(2)}) async-start(bf16[8,8,32,256]{3,2,1,0:T(8,128)(2,1)} %get-tuple-element.56), calls=%async_computation.1 | async-start | bytes 2097152 | tf_op jit(solution)/shard_map/all_to_all | solution.py:363
  57.0 8.3 %form.9 = (bf16[12,2,2,64,128]{4,3,2,1,0:T(8,128)(2,1)}, bf16[12,2,2,64,128]{4,3,2,1,0:T(8,128)(2,1)}, bf16[12,2,2,64,128]{4,3,2,1,0:T(8,128)(2,1)}, bf16[12,2,2,64,128]{4,3,2,1,0:T(8,128)(2,1)}) custom-call(s32[2]{0:T(128)} %pad_add_fusion.me_ref.after_ref.before_ref, f32[4,2,128]{2,1,0:T(2,128)} %get-tuple-element.48.after_ref, ...), custom_call_target="tpu_custom_call" | custom-call | flops 1000 | bytes 1000 | tf_op jit(solution)/shard_map/form/pallas_call | solution.py:200
  71.5 8.3 %detect.8 = (bf16[8,10,32,256]{3,2,1,0:T(8,128)(2,1)}, f32[5,2,128]{2,1,0:T(2,128)}) custom-call(s32[2]{0:T(128)} %pad_add_fusion.me_ref.after_ref.before_ref, bf16[12,2,2,64,128]{4,3,2,1,0:T(8,128)(2,1)} %get-tuple-element.49.after_ref.refs_0_, bf16[8,4,32,256]{3,2,1,0:T(8,128)(2,1)} %copy-done.5, bf16[256,256]{1,0:T(8,128)(2,1)} %constant.48.clone.high_ref, ...), custom_call_target="tpu_custom_call" | custom-call | flops 16000000000 | bytes 1000 | tf_op jit(solution)/shard_map/detect/pallas_call | solution.py:234
  79.8 4.2 %all-to-all-done.1.before_ref.refs_5_ = bf16[8,8,32,256]{3,2,1,0:T(8,128)(2,1)S(1)} async-done(((bf16[8,8,32,256]{3,2,1,0:T(8,128)(2,1)}), bf16[8,8,32,256]{3,2,1,0:T(8,128)(2,1)S(1)}, u32[]{:S(2)}, u32[]{:S(2)}) %all-to-all-start.1) | async-done | bytes 1048608 | tf_op jit(solution)/shard_map/all_to_all | solution.py:363
  87.6 9.4 %form.10 = (bf16[14,2,2,64,128]{4,3,2,1,0:T(8,128)(2,1)}, bf16[14,2,2,64,128]{4,3,2,1,0:T(8,128)(2,1)}, bf16[14,2,2,64,128]{4,3,2,1,0:T(8,128)(2,1)}, bf16[14,2,2,64,128]{4,3,2,1,0:T(8,128)(2,1)}) custom-call(s32[2]{0:T(128)} %pad_add_fusion.me_ref.after_ref.before_ref, f32[5,2,128]{2,1,0:T(2,128)} %get-tuple-element.54.after_ref, ...), custom_call_target="tpu_custom_call" | custom-call | flops 1000 | bytes 1000 | tf_op jit(solution)/shard_map/form/pallas_call | solution.py:200
  99.0 6.3 %collective-permute-done.11.refs_3_ = bf16[12,2,2,64,128]{4,3,2,1,0:T(8,128)(2,1)} collective-permute-done((bf16[12,2,2,64,128]{4,3,2,1,0:T(8,128)(2,1)}, bf16[12,2,2,64,128]{4,3,2,1,0:T(8,128)(2,1)}, u32[]{:S(2)}, u32[]{:S(2)}) %collective-permute-start.11) | collective-permute-done | bytes 786464 | tf_op jit(solution)/shard_map/ppermute | solution.py:310
  105.2 9.5 %detect.9 = (bf16[8,12,32,256]{3,2,1,0:T(8,128)(2,1)}, f32[6,2,128]{2,1,0:T(2,128)}) custom-call(s32[2]{0:T(128)} %pad_add_fusion.me_ref.after_ref.before_ref, bf16[14,2,2,64,128]{4,3,2,1,0:T(8,128)(2,1)} %get-tuple-element.55.after_ref.refs_0_, bf16[8,8,32,256]{3,2,1,0:T(8,128)(2,1)} %copy-done.4, bf16[256,256]{1,0:T(8,128)(2,1)} %constant.48.clone.high_ref, ...), custom_call_target="tpu_custom_call" | custom-call | flops 19200000000 | bytes 1000 | tf_op jit(solution)/shard_map/detect/pallas_call | solution.py:234
  114.7 4.5 %all-to-all-done.2.before_ref.refs_6_ = bf16[8,10,32,256]{3,2,1,0:T(8,128)(2,1)S(1)} async-done(((bf16[8,10,32,256]{3,2,1,0:T(8,128)(2,1)}), bf16[8,10,32,256]{3,2,1,0:T(8,128)(2,1)S(1)}, u32[]{:S(2)}, u32[]{:S(2)}) %all-to-all-start.2) | async-done | bytes 1310752 | tf_op jit(solution)/shard_map/all_to_all | solution.py:363
  122.9 10.5 %form.11 = (bf16[16,2,2,64,128]{4,3,2,1,0:T(8,128)(2,1)}, bf16[16,2,2,64,128]{4,3,2,1,0:T(8,128)(2,1)}, bf16[16,2,2,64,128]{4,3,2,1,0:T(8,128)(2,1)}, bf16[16,2,2,64,128]{4,3,2,1,0:T(8,128)(2,1)}) custom-call(s32[2]{0:T(128)} %pad_add_fusion.me_ref.after_ref.before_ref, f32[6,2,128]{2,1,0:T(2,128)} %get-tuple-element.60.after_ref, ...), custom_call_target="tpu_custom_call" | custom-call | flops 1000 | bytes 1000 | tf_op jit(solution)/shard_map/form/pallas_call | solution.py:200
  135.3 9.2 %collective-permute-done.14.refs_3_ = bf16[14,2,2,64,128]{4,3,2,1,0:T(8,128)(2,1)} collective-permute-done((bf16[14,2,2,64,128]{4,3,2,1,0:T(8,128)(2,1)}, bf16[14,2,2,64,128]{4,3,2,1,0:T(8,128)(2,1)}, u32[]{:S(2)}, u32[]{:S(2)}) %collective-permute-start.14) | collective-permute-done | bytes 917536 | tf_op jit(solution)/shard_map/ppermute | solution.py:310
  144.5 10.8 %detect.10 = (bf16[8,14,32,256]{3,2,1,0:T(8,128)(2,1)}, f32[7,2,128]{2,1,0:T(2,128)}) custom-call(s32[2]{0:T(128)} %pad_add_fusion.me_ref.after_ref.before_ref, bf16[16,2,2,64,128]{4,3,2,1,0:T(8,128)(2,1)} %get-tuple-element.61.after_ref.refs_0_, bf16[8,10,32,256]{3,2,1,0:T(8,128)(2,1)} %copy-done.3, bf16[256,256]{1,0:T(8,128)(2,1)} %constant.48.clone.high_ref, ...), custom_call_target="tpu_custom_call" | custom-call | flops 22400000000 | bytes 1000 | tf_op jit(solution)/shard_map/detect/pallas_call | solution.py:234
  155.3 4.7 %all-to-all-done.3.before_ref.refs_7_ = bf16[8,12,32,256]{3,2,1,0:T(8,128)(2,1)S(1)} async-done(((bf16[8,12,32,256]{3,2,1,0:T(8,128)(2,1)}), bf16[8,12,32,256]{3,2,1,0:T(8,128)(2,1)S(1)}, u32[]{:S(2)}, u32[]{:S(2)}) %all-to-all-start.3) | async-done | bytes 1572896 | tf_op jit(solution)/shard_map/all_to_all | solution.py:363
  167.5 21.9 %collective-permute-done.17.refs_3_ = bf16[16,2,2,64,128]{4,3,2,1,0:T(8,128)(2,1)} collective-permute-done((bf16[16,2,2,64,128]{4,3,2,1,0:T(8,128)(2,1)}, bf16[16,2,2,64,128]{4,3,2,1,0:T(8,128)(2,1)}, u32[]{:S(2)}, u32[]{:S(2)}) %collective-permute-start.17) | collective-permute-done | bytes 1048608 | tf_op jit(solution)/shard_map/ppermute | solution.py:310
  189.5 12.0 %detect.11 = (bf16[8,16,32,256]{3,2,1,0:T(8,128)(2,1)}, f32[8,2,128]{2,1,0:T(2,128)}) custom-call(s32[2]{0:T(128)} %pad_add_fusion.me_ref.after_ref.before_ref, f32[7,2,128]{2,1,0:T(2,128)} %get-tuple-element.66.after_ref, bf16[8,12,32,256]{3,2,1,0:T(8,128)(2,1)} %copy-done.2, bf16[256,256]{1,0:T(8,128)(2,1)} %constant.48.clone.high_ref, ...), custom_call_target="tpu_custom_call" | custom-call | flops 25600000000 | bytes 1000 | tf_op jit(solution)/shard_map/detect/pallas_call | solution.py:234
  201.5 6.2 %all-to-all-done.4.refs_8_ = bf16[8,14,32,256]{3,2,1,0:T(8,128)(2,1)S(1)} async-done(((bf16[8,14,32,256]{3,2,1,0:T(8,128)(2,1)}), bf16[8,14,32,256]{3,2,1,0:T(8,128)(2,1)S(1)}, u32[]{:S(2)}, u32[]{:S(2)}) %all-to-all-start.4) | async-done | bytes 1835040 | tf_op jit(solution)/shard_map/all_to_all | solution.py:363
  220.6 9.4 %collective-permute-done.21 = f32[1,16,128]{2,1,0:T(8,128)S(1)} collective-permute-done((f32[1,16,128]{2,1,0:T(8,128)S(1)}, f32[1,16,128]{2,1,0:T(8,128)S(1)}, u32[]{:S(2)}, u32[]{:S(2)}) %collective-permute-start.21) | collective-permute-done | bytes 8224 | tf_op jit(solution)/shard_map/ppermute | solution.py:310
  231.7 16.5 %collective-permute-done.22 = f32[2,16,128]{2,1,0:T(8,128)S(1)} collective-permute-done((f32[2,16,128]{2,1,0:T(8,128)S(1)}, f32[2,16,128]{2,1,0:T(8,128)S(1)}, u32[]{:S(2)}, u32[]{:S(2)}) %collective-permute-start.22) | collective-permute-done | bytes 16416 | tf_op jit(solution)/shard_map/ppermute | solution.py:310
  251.9 10.5 %collective-permute-done.23 = f32[4,16,128]{2,1,0:T(8,128)S(1)} collective-permute-done((f32[4,16,128]{2,1,0:T(8,128)S(1)}, f32[4,16,128]{2,1,0:T(8,128)S(1)}, u32[]{:S(2)}, u32[]{:S(2)}) %collective-permute-start.23) | collective-permute-done | bytes 32800 | tf_op jit(solution)/shard_map/ppermute | solution.py:310
  270.3 13.5 %flag.1 = bf16[2,32,65536]{2,1,0:T(8,128)(2,1)} custom-call(s32[2]{0:T(128)} %pad_add_fusion.me_ref.after_ref.before_ref, bf16[256,128]{1,0:T(8,128)(2,1)} %constant.50.clone.group_ref, f32[512,1,128]{2,1,0:T(1,128)} %copy.13.mask_ref, f32[8,16,1,128]{3,2,1,0:T(1,128)} %bitcast.35, f32[8,16,1,128]{3,2,1,0:T(1,128)} %copy-done.10, ...), custom_call_target="tpu_custom_call" | custom-call | flops 1073741824 | bytes 16777216 | tf_op jit(solution)/shard_map/flag/pallas_call | solution.py:280
  (126 shorter events, 70.7 us)
Async XLA Ops:
  8.4 12.6 %collective-permute-start.2 = (bf16[4,2,2,64,128]{4,3,2,1,0:T(8,128)(2,1)}, bf16[4,2,2,64,128]{4,3,2,1,0:T(8,128)(2,1)S(1)}, u32[]{:S(2)}, u32[]{:S(2)}) collective-permute-start(bf16[4,2,2,64,128]{4,3,2,1,0:T(8,128)(2,1)} %get-tuple-element.42), channel_id=1, source_target_pairs={{0,3},{1,2},{2,1},{3,0},{4,7},{5,6},{6,5},{7,4},{8,11},{9,10},{10,... | collective-permute-start | bytes 786440 | tf_op jit(solution)/shard_map/ppermute | solution.py:310
  14.6 26.6 %collective-permute-start.3 = (bf16[8,2,2,64,128]{4,3,2,1,0:T(8,128)(2,1)}, bf16[8,2,2,64,128]{4,3,2,1,0:T(8,128)(2,1)S(1)}, u32[]{:S(2)}, u32[]{:S(2)}) collective-permute-start(bf16[8,2,2,64,128]{4,3,2,1,0:T(8,128)(2,1)} %get-tuple-element.45), channel_id=1, source_target_pairs={{0,1},{1,0},{2,3},{3,2},{4,5},{5,4},{6,7},{7,6},{8,9},{9,8},{10,11... | collective-permute-start | bytes 1572872 | tf_op jit(solution)/shard_map/ppermute | solution.py:310
  14.8 26.4 %collective-permute-start.4 = (bf16[8,2,2,64,128]{4,3,2,1,0:T(8,128)(2,1)}, bf16[8,2,2,64,128]{4,3,2,1,0:T(8,128)(2,1)S(1)}, u32[]{:S(2)}, u32[]{:S(2)}) collective-permute-start(bf16[8,2,2,64,128]{4,3,2,1,0:T(8,128)(2,1)} %get-tuple-element.46), channel_id=1, source_target_pairs={{0,2},{1,3},{2,0},{3,1},{4,6},{5,7},{6,4},{7,5},{8,10},{9,11},{10,... | collective-permute-start | bytes 1572872 | tf_op jit(solution)/shard_map/ppermute | solution.py:310
  17.5 25.9 %collective-permute-start.5 = (bf16[8,2,2,64,128]{4,3,2,1,0:T(8,128)(2,1)}, bf16[8,2,2,64,128]{4,3,2,1,0:T(8,128)(2,1)S(1)}, u32[]{:S(2)}, u32[]{:S(2)}) collective-permute-start(bf16[8,2,2,64,128]{4,3,2,1,0:T(8,128)(2,1)} %get-tuple-element.47), channel_id=1, source_target_pairs={{0,3},{1,2},{2,1},{3,0},{4,7},{5,6},{6,5},{7,4},{8,11},{9,10},{10,... | collective-permute-start | bytes 1572872 | tf_op jit(solution)/shard_map/ppermute | solution.py:310
  26.1 25.1 %all-to-all-start = ((bf16[8,4,32,256]{3,2,1,0:T(8,128)(2,1)}), bf16[8,4,32,256]{3,2,1,0:T(8,128)(2,1)S(1)}, u32[]{:S(2)}, u32[]{:S(2)}) async-start(bf16[8,4,32,256]{3,2,1,0:T(8,128)(2,1)} %get-tuple-element.50), calls=%async_computation | async-start | bytes 1048576 | tf_op jit(solution)/shard_map/all_to_all | solution.py:363
  39.2 28.5 %collective-permute-start.6 = (bf16[10,2,2,64,128]{4,3,2,1,0:T(8,128)(2,1)}, bf16[10,2,2,64,128]{4,3,2,1,0:T(8,128)(2,1)S(1)}, u32[]{:S(2)}, u32[]{:S(2)}) collective-permute-start(bf16[10,2,2,64,128]{4,3,2,1,0:T(8,128)(2,1)} %get-tuple-element.51), channel_id=1, source_target_pairs={{0,1},{1,0},{2,3},{3,2},{4,5},{5,4},{6,7},{7,6},{8,9},{9,8},{10,11... | collective-permute-start | bytes 1966088 | tf_op jit(solution)/shard_map/ppermute | solution.py:310
  39.6 28.0 %collective-permute-start.7 = (bf16[10,2,2,64,128]{4,3,2,1,0:T(8,128)(2,1)}, bf16[10,2,2,64,128]{4,3,2,1,0:T(8,128)(2,1)}, u32[]{:S(2)}, u32[]{:S(2)}) collective-permute-start(bf16[10,2,2,64,128]{4,3,2,1,0:T(8,128)(2,1)} %get-tuple-element.52), channel_id=1, source_target_pairs={{0,2},{1,3},{2,0},{3,1},{4,6},{5,7},{6,4},{7,5},{8,10},{9,11},{10,... | collective-permute-start | bytes 1966088 | tf_op jit(solution)/shard_map/ppermute | solution.py:310
  41.2 30.4 %collective-permute-start.8 = (bf16[10,2,2,64,128]{4,3,2,1,0:T(8,128)(2,1)}, bf16[10,2,2,64,128]{4,3,2,1,0:T(8,128)(2,1)}, u32[]{:S(2)}, u32[]{:S(2)}) collective-permute-start(bf16[10,2,2,64,128]{4,3,2,1,0:T(8,128)(2,1)} %get-tuple-element.53), channel_id=1, source_target_pairs={{0,3},{1,2},{2,1},{3,0},{4,7},{5,6},{6,5},{7,4},{8,11},{9,10},{10,... | collective-permute-start | bytes 1966088 | tf_op jit(solution)/shard_map/ppermute | solution.py:310
  51.2 32.7 %all-to-all-start.1 = ((bf16[8,8,32,256]{3,2,1,0:T(8,128)(2,1)}), bf16[8,8,32,256]{3,2,1,0:T(8,128)(2,1)S(1)}, u32[]{:S(2)}, u32[]{:S(2)}) async-start(bf16[8,8,32,256]{3,2,1,0:T(8,128)(2,1)} %get-tuple-element.56), calls=%async_computation.1 | async-start | bytes 2097152 | tf_op jit(solution)/shard_map/all_to_all | solution.py:363
  65.4 33.3 %collective-permute-start.9 = (bf16[12,2,2,64,128]{4,3,2,1,0:T(8,128)(2,1)}, bf16[12,2,2,64,128]{4,3,2,1,0:T(8,128)(2,1)S(1)}, u32[]{:S(2)}, u32[]{:S(2)}) collective-permute-start(bf16[12,2,2,64,128]{4,3,2,1,0:T(8,128)(2,1)} %get-tuple-element.57), channel_id=1, source_target_pairs={{0,1},{1,0},{2,3},{3,2},{4,5},{5,4},{6,7},{7,6},{8,9},{9,8},{10,11... | collective-permute-start | bytes 2359304 | tf_op jit(solution)/shard_map/ppermute | solution.py:310
  66.1 32.8 %collective-permute-start.10 = (bf16[12,2,2,64,128]{4,3,2,1,0:T(8,128)(2,1)}, bf16[12,2,2,64,128]{4,3,2,1,0:T(8,128)(2,1)}, u32[]{:S(2)}, u32[]{:S(2)}) collective-permute-start(bf16[12,2,2,64,128]{4,3,2,1,0:T(8,128)(2,1)} %get-tuple-element.58), channel_id=1, source_target_pairs={{0,2},{1,3},{2,0},{3,1},{4,6},{5,7},{6,4},{7,5},{8,10},{9,11},{10,... | collective-permute-start | bytes 2359304 | tf_op jit(solution)/shard_map/ppermute | solution.py:310
  67.7 37.6 %collective-permute-start.11 = (bf16[12,2,2,64,128]{4,3,2,1,0:T(8,128)(2,1)}, bf16[12,2,2,64,128]{4,3,2,1,0:T(8,128)(2,1)}, u32[]{:S(2)}, u32[]{:S(2)}) collective-permute-start(bf16[12,2,2,64,128]{4,3,2,1,0:T(8,128)(2,1)} %get-tuple-element.59), channel_id=1, source_target_pairs={{0,3},{1,2},{2,1},{3,0},{4,7},{5,6},{6,5},{7,4},{8,11},{9,10},{10,... | collective-permute-start | bytes 2359304 | tf_op jit(solution)/shard_map/ppermute | solution.py:310
  83.9 35.3 %all-to-all-start.2 = ((bf16[8,10,32,256]{3,2,1,0:T(8,128)(2,1)}), bf16[8,10,32,256]{3,2,1,0:T(8,128)(2,1)S(1)}, u32[]{:S(2)}, u32[]{:S(2)}) async-start(bf16[8,10,32,256]{3,2,1,0:T(8,128)(2,1)} %get-tuple-element.62), calls=%async_computation.2 | async-start | bytes 2621440 | tf_op jit(solution)/shard_map/all_to_all | solution.py:363
  97.0 38.0 %collective-permute-start.12 = (bf16[14,2,2,64,128]{4,3,2,1,0:T(8,128)(2,1)}, bf16[14,2,2,64,128]{4,3,2,1,0:T(8,128)(2,1)}, u32[]{:S(2)}, u32[]{:S(2)}) collective-permute-start(bf16[14,2,2,64,128]{4,3,2,1,0:T(8,128)(2,1)} %get-tuple-element.63), channel_id=1, source_target_pairs={{0,1},{1,0},{2,3},{3,2},{4,5},{5,4},{6,7},{7,6},{8,9},{9,8},{10,11... | collective-permute-start | bytes 2752520 | tf_op jit(solution)/shard_map/ppermute | solution.py:310
  97.1 38.2 %collective-permute-start.13 = (bf16[14,2,2,64,128]{4,3,2,1,0:T(8,128)(2,1)}, bf16[14,2,2,64,128]{4,3,2,1,0:T(8,128)(2,1)}, u32[]{:S(2)}, u32[]{:S(2)}) collective-permute-start(bf16[14,2,2,64,128]{4,3,2,1,0:T(8,128)(2,1)} %get-tuple-element.64), channel_id=1, source_target_pairs={{0,2},{1,3},{2,0},{3,1},{4,6},{5,7},{6,4},{7,5},{8,10},{9,11},{10,... | collective-permute-start | bytes 2752520 | tf_op jit(solution)/shard_map/ppermute | solution.py:310
  98.7 45.9 %collective-permute-start.14 = (bf16[14,2,2,64,128]{4,3,2,1,0:T(8,128)(2,1)}, bf16[14,2,2,64,128]{4,3,2,1,0:T(8,128)(2,1)}, u32[]{:S(2)}, u32[]{:S(2)}) collective-permute-start(bf16[14,2,2,64,128]{4,3,2,1,0:T(8,128)(2,1)} %get-tuple-element.65), channel_id=1, source_target_pairs={{0,3},{1,2},{2,1},{3,0},{4,7},{5,6},{6,5},{7,4},{8,11},{9,10},{10,... | collective-permute-start | bytes 2752520 | tf_op jit(solution)/shard_map/ppermute | solution.py:310
  119.2 40.8 %all-to-all-start.3 = ((bf16[8,12,32,256]{3,2,1,0:T(8,128)(2,1)}), bf16[8,12,32,256]{3,2,1,0:T(8,128)(2,1)S(1)}, u32[]{:S(2)}, u32[]{:S(2)}) async-start(bf16[8,12,32,256]{3,2,1,0:T(8,128)(2,1)} %get-tuple-element.67), calls=%async_computation.3 | async-start | bytes 3145728 | tf_op jit(solution)/shard_map/all_to_all | solution.py:363
  133.4 31.7 %collective-permute-start.15 = (bf16[16,2,2,64,128]{4,3,2,1,0:T(8,128)(2,1)}, bf16[16,2,2,64,128]{4,3,2,1,0:T(8,128)(2,1)}, u32[]{:S(2)}, u32[]{:S(2)}) collective-permute-start(bf16[16,2,2,64,128]{4,3,2,1,0:T(8,128)(2,1)} %get-tuple-element.68), channel_id=1, source_target_pairs={{0,1},{1,0},{2,3},{3,2},{4,5},{5,4},{6,7},{7,6},{8,9},{9,8},{10,11... | collective-permute-start | bytes 3145736 | tf_op jit(solution)/shard_map/ppermute | solution.py:310
  133.4 34.1 %collective-permute-start.16 = (bf16[16,2,2,64,128]{4,3,2,1,0:T(8,128)(2,1)}, bf16[16,2,2,64,128]{4,3,2,1,0:T(8,128)(2,1)}, u32[]{:S(2)}, u32[]{:S(2)}) collective-permute-start(bf16[16,2,2,64,128]{4,3,2,1,0:T(8,128)(2,1)} %get-tuple-element.69), channel_id=1, source_target_pairs={{0,2},{1,3},{2,0},{3,1},{4,6},{5,7},{6,4},{7,5},{8,10},{9,11},{10,... | collective-permute-start | bytes 3145736 | tf_op jit(solution)/shard_map/ppermute | solution.py:310
  135.0 54.5 %collective-permute-start.17 = (bf16[16,2,2,64,128]{4,3,2,1,0:T(8,128)(2,1)}, bf16[16,2,2,64,128]{4,3,2,1,0:T(8,128)(2,1)}, u32[]{:S(2)}, u32[]{:S(2)}) collective-permute-start(bf16[16,2,2,64,128]{4,3,2,1,0:T(8,128)(2,1)} %get-tuple-element.70), channel_id=1, source_target_pairs={{0,3},{1,2},{2,1},{3,0},{4,7},{5,6},{6,5},{7,4},{8,11},{9,10},{10,... | collective-permute-start | bytes 3145736 | tf_op jit(solution)/shard_map/ppermute | solution.py:310
  161.2 46.5 %all-to-all-start.4 = ((bf16[8,14,32,256]{3,2,1,0:T(8,128)(2,1)}), bf16[8,14,32,256]{3,2,1,0:T(8,128)(2,1)S(1)}, u32[]{:S(2)}, u32[]{:S(2)}) async-start(bf16[8,14,32,256]{3,2,1,0:T(8,128)(2,1)} %get-tuple-element.72), calls=%async_computation.4 | async-start | bytes 3670016 | tf_op jit(solution)/shard_map/all_to_all | solution.py:363
  209.0 59.3 %all-to-all-start.5 = ((bf16[8,16,32,256]{3,2,1,0:T(8,128)(2,1)}), bf16[8,16,32,256]{3,2,1,0:T(8,128)(2,1)S(1)}, u32[]{:S(2)}, u32[]{:S(2)}) async-start(bf16[8,16,32,256]{3,2,1,0:T(8,128)(2,1)} %get-tuple-element.73), calls=%async_computation.5 | async-start | bytes 4194304 | tf_op jit(solution)/shard_map/all_to_all | solution.py:363
  230.0 18.2 %collective-permute-start.22 = (f32[2,16,128]{2,1,0:T(8,128)S(1)}, f32[2,16,128]{2,1,0:T(8,128)S(1)}, u32[]{:S(2)}, u32[]{:S(2)}) collective-permute-start(f32[2,16,128]{2,1,0:T(8,128)S(1)} %maximum_select_fusion.3), channel_id=1, source_target_pairs={{0,8},{4,12},{8,0},{12,4},{16,24},{20,28},{24,16},{28,20},{1,9},{5... | collective-permute-start | bytes 49160 | tf_op jit(solution)/shard_map/ppermute | solution.py:310
  248.2 14.2 %collective-permute-start.23 = (f32[4,16,128]{2,1,0:T(8,128)S(1)}, f32[4,16,128]{2,1,0:T(8,128)S(1)}, u32[]{:S(2)}, u32[]{:S(2)}) collective-permute-start(f32[4,16,128]{2,1,0:T(8,128)S(1)} %bitcast.38), channel_id=1, source_target_pairs={{0,16},{4,20},{8,24},{12,28},{16,0},{20,4},{24,8},{28,12},{1,17},{... | collective-permute-start | bytes 98312 | tf_op jit(solution)/shard_map/ppermute | solution.py:310
  (36 other events, 282.9 us)

commit v10 on v9

--- a/solution.py
+++ b/solution.py
@@ -357,18 +357,20 @@
                 owners,
                 direct,
             )
+            sums.append(part.reshape(sizes[chunk - 1], samples))
+            after = part
+            if chunk == chunks:
+                common = jnp.concatenate(sums, axis=0).reshape(groups, local // groups, samples)
+                parts = [common[mine ^ r] for r in range(groups)]
+                common = parts[0]
+                for r in range(1, groups):
+                    common = common + swap(parts[r], "grp", r)
+                common = common / float(feeds * groups)
+                common, *sent = lax.optimization_barrier((common, *sent))
             if direct:
                 owned.append([swap(one, "chan", r) if r else one for r, one in enumerate(sent)])
             else:
                 owned.append([lax.all_to_all(*sent, "chan", split_axis=0, concat_axis=0, tiled=True)])
-            sums.append(part.reshape(sizes[chunk - 1], samples))
-            after = part
-    common = jnp.concatenate(sums, axis=0).reshape(groups, local // groups, samples)
-    mine_of = [common[mine ^ r] for r in range(groups)]
-    common = mine_of[0]
-    for r in range(1, groups):
-        common = common + swap(mine_of[r], "grp", r)
-    common = common / float(feeds * groups)
     common_piece = common.reshape(-1)
     shared = common[None]
     for bit in range(owners.bit_length() - 1):

time: 285 us -> 286 us (level)
  waiting for transfers between devices: 112 us -> 109 us
    all_to_all x6, waiting for transfers between devices: 19.6 us -> 13.4 us  [body(): lax.all_to_all(*sent, 'chan', split_axis=0, concat_axis=0, tiled=True)]
    ppermute x27, waiting for transfers between devices: 92 us -> 95.7 us  [swap(): lax.ppermute(one, axis, [(i, i ^ apart) for i in range(lax.axis_size(axis...]
    unnamed x54 -> x52, local copies, waits for them, and re-layouts: 5.96 us -> 5.98 us
  transfers between devices with their start and end apart: 33 -> 33, of which waited for: 18 -> 17; matrix products, arithmetic and copies ran while one was open for 1% -> 1% of each run, Pallas kernels for 33% -> 33%
where the time goes in v10:
time: 286 us; the launch traced here: 285 us
  Pallas kernels  111 us (39%)
  waiting for transfers between devices  109 us (38%)
  starting transfers between devices  53.8 us (19%)
  local copies, waits for them, and re-layouts  8.23 us (3%)
    ppermute x27, waiting for transfers between devices, swap(): lax.ppermute(one, axis, [(i, i ^ apart) for i in range(lax.axis_size(axis...  95.7 us
    pallas_call x6, Pallas kernels, detect(): pl.pallas_call(functools.partial(detect_kernel, columns), grid=(steps,),...  52 us
    pallas_call x6, Pallas kernels, form(): pl.pallas_call(form_kernel, grid=(steps,), in_specs=[pl.BlockSpec(memory_...  45.7 us
    all_to_all x6, starting transfers between devices, body(): lax.all_to_all(*sent, 'chan', split_axis=0, concat_axis=0, tiled=True)  28.5 us
    ppermute x27, starting transfers between devices, swap(): lax.ppermute(one, axis, [(i, i ^ apart) for i in range(lax.axis_size(axis...  25.3 us
    all_to_all x6, waiting for transfers between devices, body(): lax.all_to_all(*sent, 'chan', split_axis=0, concat_axis=0, tiled=True)  13.4 us
    pallas_call x1, Pallas kernels, soft_flag(): pl.pallas_call(functools.partial(flag_kernel, layout, len(parts)), grid=(...  13.4 us
    unnamed x52, local copies, waits for them, and re-layouts  5.98 us
  transfers between devices with their start and end apart: 33, of which 17 were waited for; matrix products, arithmetic and copies ran while one was open for 1% of the time, Pallas kernels for 33%

profile of v10, /device:TPU:0, one launch (start us, length us, event | category | flops | bytes accessed | tf_op | source)
XLA Modules:
  0.0 284.8 jit_solution(16629787837102716964)
XLA Ops:
  8.4 6.1 %form.7 = (bf16[8,2,2,64,128]{4,3,2,1,0:T(8,128)(2,1)}, bf16[8,2,2,64,128]{4,3,2,1,0:T(8,128)(2,1)}, bf16[8,2,2,64,128]{4,3,2,1,0:T(8,128)(2,1)}, bf16[8,2,2,64,128]{4,3,2,1,0:T(8,128)(2,1)}) custom-call(s32[2]{0:T(128)} %pad_add_fusion.me_ref.after_ref.before_ref, bf16[4,2,2,64,128]{4,3,2,1,0:T(8,128)(2,1)} %get-tuple-element.40.after_ref.refs_0_, ...), custom_call_target="tpu_custom_call" | custom-call | flops 1000 | bytes 1000 | tf_op jit(solution)/shard_map/form/pallas_call | solution.py:200
  21.6 4.5 %detect.6 = (bf16[8,4,32,256]{3,2,1,0:T(8,128)(2,1)}, f32[2,2,128]{2,1,0:T(2,128)}) custom-call(s32[2]{0:T(128)} %pad_add_fusion.me_ref.after_ref.before_ref, bf16[8,2,2,64,128]{4,3,2,1,0:T(8,128)(2,1)} %get-tuple-element.41.after_ref.refs_0_, s32[2]{0:T(128)} %pad_add_fusion.me_ref.after_ref.before_ref, bf16[256,256]{1,0:T(8,128)(2,1)} %constant.48.clone.high_ref, ...), custom_call_target="tpu_custom_call" | custom-call | flops 6400000000 | bytes 1000 | tf_op jit(solution)/shard_map/detect/pallas_call | solution.py:234
  26.1 5.8 %all-to-all-start = ((bf16[8,4,32,256]{3,2,1,0:T(8,128)(2,1)}), bf16[8,4,32,256]{3,2,1,0:T(8,128)(2,1)S(1)}, u32[]{:S(2)}, u32[]{:S(2)}) async-start(bf16[8,4,32,256]{3,2,1,0:T(8,128)(2,1)} %get-tuple-element.52), calls=%async_computation | async-start | bytes 1048576 | tf_op jit(solution)/shard_map/all_to_all | solution.py:373
  31.9 7.3 %form.8 = (bf16[10,2,2,64,128]{4,3,2,1,0:T(8,128)(2,1)}, bf16[10,2,2,64,128]{4,3,2,1,0:T(8,128)(2,1)}, bf16[10,2,2,64,128]{4,3,2,1,0:T(8,128)(2,1)}, bf16[10,2,2,64,128]{4,3,2,1,0:T(8,128)(2,1)}) custom-call(s32[2]{0:T(128)} %pad_add_fusion.me_ref.after_ref.before_ref, f32[2,2,128]{2,1,0:T(2,128)} %get-tuple-element.45.after_ref, ...), custom_call_target="tpu_custom_call" | custom-call | flops 1000 | bytes 1000 | tf_op jit(solution)/shard_map/form/pallas_call | solution.py:200
  44.2 7.0 %detect.7 = (bf16[8,8,32,256]{3,2,1,0:T(8,128)(2,1)}, f32[4,2,128]{2,1,0:T(2,128)}) custom-call(s32[2]{0:T(128)} %pad_add_fusion.me_ref.after_ref.before_ref, bf16[10,2,2,64,128]{4,3,2,1,0:T(8,128)(2,1)} %get-tuple-element.46.after_ref.refs_0_, s32[2]{0:T(128)} %pad_add_fusion.me_ref.after_ref.before_ref, bf16[256,256]{1,0:T(8,128)(2,1)} %constant.48.clone.high_ref, ...), custom_call_target="tpu_custom_call" | custom-call | flops 12800000000 | bytes 1000 | tf_op jit(solution)/shard_map/detect/pallas_call | solution.py:234
  51.2 5.8 %all-to-all-start.1 = ((bf16[8,8,32,256]{3,2,1,0:T(8,128)(2,1)}), bf16[8,8,32,256]{3,2,1,0:T(8,128)(2,1)S(1)}, u32[]{:S(2)}, u32[]{:S(2)}) async-start(bf16[8,8,32,256]{3,2,1,0:T(8,128)(2,1)} %get-tuple-element.58), calls=%async_computation.1 | async-start | bytes 2097152 | tf_op jit(solution)/shard_map/all_to_all | solution.py:373
  57.0 8.3 %form.9 = (bf16[12,2,2,64,128]{4,3,2,1,0:T(8,128)(2,1)}, bf16[12,2,2,64,128]{4,3,2,1,0:T(8,128)(2,1)}, bf16[12,2,2,64,128]{4,3,2,1,0:T(8,128)(2,1)}, bf16[12,2,2,64,128]{4,3,2,1,0:T(8,128)(2,1)}) custom-call(s32[2]{0:T(128)} %pad_add_fusion.me_ref.after_ref.before_ref, f32[4,2,128]{2,1,0:T(2,128)} %get-tuple-element.50.after_ref, ...), custom_call_target="tpu_custom_call" | custom-call | flops 1000 | bytes 1000 | tf_op jit(solution)/shard_map/form/pallas_call | solution.py:200
  71.5 8.3 %detect.8 = (bf16[8,10,32,256]{3,2,1,0:T(8,128)(2,1)}, f32[5,2,128]{2,1,0:T(2,128)}) custom-call(s32[2]{0:T(128)} %pad_add_fusion.me_ref.after_ref.before_ref, bf16[12,2,2,64,128]{4,3,2,1,0:T(8,128)(2,1)} %get-tuple-element.51.after_ref.refs_0_, bf16[8,4,32,256]{3,2,1,0:T(8,128)(2,1)} %copy-done.5, bf16[256,256]{1,0:T(8,128)(2,1)} %constant.48.clone.high_ref, ...), custom_call_target="tpu_custom_call" | custom-call | flops 16000000000 | bytes 1000 | tf_op jit(solution)/shard_map/detect/pallas_call | solution.py:234
  79.8 4.2 %all-to-all-done.1.before_ref.refs_5_ = bf16[8,8,32,256]{3,2,1,0:T(8,128)(2,1)S(1)} async-done(((bf16[8,8,32,256]{3,2,1,0:T(8,128)(2,1)}), bf16[8,8,32,256]{3,2,1,0:T(8,128)(2,1)S(1)}, u32[]{:S(2)}, u32[]{:S(2)}) %all-to-all-start.1) | async-done | bytes 1048608 | tf_op jit(solution)/shard_map/all_to_all | solution.py:373
  87.6 9.4 %form.10 = (bf16[14,2,2,64,128]{4,3,2,1,0:T(8,128)(2,1)}, bf16[14,2,2,64,128]{4,3,2,1,0:T(8,128)(2,1)}, bf16[14,2,2,64,128]{4,3,2,1,0:T(8,128)(2,1)}, bf16[14,2,2,64,128]{4,3,2,1,0:T(8,128)(2,1)}) custom-call(s32[2]{0:T(128)} %pad_add_fusion.me_ref.after_ref.before_ref, f32[5,2,128]{2,1,0:T(2,128)} %get-tuple-element.56.after_ref, ...), custom_call_target="tpu_custom_call" | custom-call | flops 1000 | bytes 1000 | tf_op jit(solution)/shard_map/form/pallas_call | solution.py:200
  98.9 6.3 %collective-permute-done.11.refs_3_ = bf16[12,2,2,64,128]{4,3,2,1,0:T(8,128)(2,1)} collective-permute-done((bf16[12,2,2,64,128]{4,3,2,1,0:T(8,128)(2,1)}, bf16[12,2,2,64,128]{4,3,2,1,0:T(8,128)(2,1)}, u32[]{:S(2)}, u32[]{:S(2)}) %collective-permute-start.11) | collective-permute-done | bytes 786464 | tf_op jit(solution)/shard_map/ppermute | solution.py:310
  105.2 9.5 %detect.9 = (bf16[8,12,32,256]{3,2,1,0:T(8,128)(2,1)}, f32[6,2,128]{2,1,0:T(2,128)}) custom-call(s32[2]{0:T(128)} %pad_add_fusion.me_ref.after_ref.before_ref, bf16[14,2,2,64,128]{4,3,2,1,0:T(8,128)(2,1)} %get-tuple-element.57.after_ref.refs_0_, bf16[8,8,32,256]{3,2,1,0:T(8,128)(2,1)} %copy-done.4, bf16[256,256]{1,0:T(8,128)(2,1)} %constant.48.clone.high_ref, ...), custom_call_target="tpu_custom_call" | custom-call | flops 19200000000 | bytes 1000 | tf_op jit(solution)/shard_map/detect/pallas_call | solution.py:234
  114.7 4.5 %all-to-all-done.2.before_ref.refs_6_ = bf16[8,10,32,256]{3,2,1,0:T(8,128)(2,1)S(1)} async-done(((bf16[8,10,32,256]{3,2,1,0:T(8,128)(2,1)}), bf16[8,10,32,256]{3,2,1,0:T(8,128)(2,1)S(1)}, u32[]{:S(2)}, u32[]{:S(2)}) %all-to-all-start.2) | async-done | bytes 1310752 | tf_op jit(solution)/shard_map/all_to_all | solution.py:373
  122.9 10.5 %form.11 = (bf16[16,2,2,64,128]{4,3,2,1,0:T(8,128)(2,1)}, bf16[16,2,2,64,128]{4,3,2,1,0:T(8,128)(2,1)}, bf16[16,2,2,64,128]{4,3,2,1,0:T(8,128)(2,1)}, bf16[16,2,2,64,128]{4,3,2,1,0:T(8,128)(2,1)}) custom-call(s32[2]{0:T(128)} %pad_add_fusion.me_ref.after_ref.before_ref, f32[6,2,128]{2,1,0:T(2,128)} %get-tuple-element.62.after_ref, ...), custom_call_target="tpu_custom_call" | custom-call | flops 1000 | bytes 1000 | tf_op jit(solution)/shard_map/form/pallas_call | solution.py:200
  135.3 9.2 %collective-permute-done.14.refs_3_ = bf16[14,2,2,64,128]{4,3,2,1,0:T(8,128)(2,1)} collective-permute-done((bf16[14,2,2,64,128]{4,3,2,1,0:T(8,128)(2,1)}, bf16[14,2,2,64,128]{4,3,2,1,0:T(8,128)(2,1)}, u32[]{:S(2)}, u32[]{:S(2)}) %collective-permute-start.14) | collective-permute-done | bytes 917536 | tf_op jit(solution)/shard_map/ppermute | solution.py:310
  144.5 10.8 %detect.10 = (bf16[8,14,32,256]{3,2,1,0:T(8,128)(2,1)}, f32[7,2,128]{2,1,0:T(2,128)}) custom-call(s32[2]{0:T(128)} %pad_add_fusion.me_ref.after_ref.before_ref, bf16[16,2,2,64,128]{4,3,2,1,0:T(8,128)(2,1)} %get-tuple-element.63.after_ref.refs_0_, bf16[8,10,32,256]{3,2,1,0:T(8,128)(2,1)} %copy-done.3, bf16[256,256]{1,0:T(8,128)(2,1)} %constant.48.clone.high_ref, ...), custom_call_target="tpu_custom_call" | custom-call | flops 22400000000 | bytes 1000 | tf_op jit(solution)/shard_map/detect/pallas_call | solution.py:234
  155.3 4.8 %all-to-all-done.3.before_ref.refs_7_ = bf16[8,12,32,256]{3,2,1,0:T(8,128)(2,1)S(1)} async-done(((bf16[8,12,32,256]{3,2,1,0:T(8,128)(2,1)}), bf16[8,12,32,256]{3,2,1,0:T(8,128)(2,1)S(1)}, u32[]{:S(2)}, u32[]{:S(2)}) %all-to-all-start.3) | async-done | bytes 1572896 | tf_op jit(solution)/shard_map/all_to_all | solution.py:373
  167.5 21.9 %collective-permute-done.17.refs_3_ = bf16[16,2,2,64,128]{4,3,2,1,0:T(8,128)(2,1)} collective-permute-done((bf16[16,2,2,64,128]{4,3,2,1,0:T(8,128)(2,1)}, bf16[16,2,2,64,128]{4,3,2,1,0:T(8,128)(2,1)}, u32[]{:S(2)}, u32[]{:S(2)}) %collective-permute-start.17) | collective-permute-done | bytes 1048608 | tf_op jit(solution)/shard_map/ppermute | solution.py:310
  189.5 12.0 %detect.11 = (bf16[8,16,32,256]{3,2,1,0:T(8,128)(2,1)}, f32[8,2,128]{2,1,0:T(2,128)}) custom-call(s32[2]{0:T(128)} %pad_add_fusion.me_ref.after_ref.before_ref, f32[7,2,128]{2,1,0:T(2,128)} %get-tuple-element.68.after_ref, bf16[8,12,32,256]{3,2,1,0:T(8,128)(2,1)} %copy-done.2, bf16[256,256]{1,0:T(8,128)(2,1)} %constant.48.clone.high_ref, ...), custom_call_target="tpu_custom_call" | custom-call | flops 25600000000 | bytes 1000 | tf_op jit(solution)/shard_map/detect/pallas_call | solution.py:234
  209.3 5.8 %all-to-all-start.5 = ((bf16[8,16,32,256]{3,2,1,0:T(8,128)(2,1)}), bf16[8,16,32,256]{3,2,1,0:T(8,128)(2,1)S(1)}, u32[]{:S(2)}, u32[]{:S(2)}) async-start(bf16[8,16,32,256]{3,2,1,0:T(8,128)(2,1)} %get-tuple-element.77), calls=%async_computation.5 | async-start | bytes 4194304 | tf_op jit(solution)/shard_map/all_to_all | solution.py:373
  217.1 14.7 %collective-permute-done.21 = f32[1,16,128]{2,1,0:T(8,128)S(1)} collective-permute-done((f32[1,16,128]{2,1,0:T(8,128)S(1)}, f32[1,16,128]{2,1,0:T(8,128)S(1)}, u32[]{:S(2)}, u32[]{:S(2)}) %collective-permute-start.21) | collective-permute-done | bytes 8224 | tf_op jit(solution)/shard_map/ppermute | solution.py:310
  233.5 15.8 %collective-permute-done.22 = f32[2,16,128]{2,1,0:T(8,128)S(1)} collective-permute-done((f32[2,16,128]{2,1,0:T(8,128)S(1)}, f32[2,16,128]{2,1,0:T(8,128)S(1)}, u32[]{:S(2)}, u32[]{:S(2)}) %collective-permute-start.22) | collective-permute-done | bytes 16416 | tf_op jit(solution)/shard_map/ppermute | solution.py:310
  253.7 10.5 %collective-permute-done.23 = f32[4,16,128]{2,1,0:T(8,128)S(1)} collective-permute-done((f32[4,16,128]{2,1,0:T(8,128)S(1)}, f32[4,16,128]{2,1,0:T(8,128)S(1)}, u32[]{:S(2)}, u32[]{:S(2)}) %collective-permute-start.23) | collective-permute-done | bytes 32800 | tf_op jit(solution)/shard_map/ppermute | solution.py:310
  271.3 13.4 %flag.1 = bf16[2,32,65536]{2,1,0:T(8,128)(2,1)} custom-call(s32[2]{0:T(128)} %pad_add_fusion.me_ref.after_ref.before_ref, bf16[256,128]{1,0:T(8,128)(2,1)} %constant.50.clone.group_ref, f32[512,1,128]{2,1,0:T(1,128)} %copy.13.mask_ref, f32[8,16,1,128]{3,2,1,0:T(1,128)} %bitcast.35, f32[8,16,1,128]{3,2,1,0:T(1,128)} %copy-done.10, ...), custom_call_target="tpu_custom_call" | custom-call | flops 1073741824 | bytes 16777216 | tf_op jit(solution)/shard_map/flag/pallas_call | solution.py:280
  (124 shorter events, 67.4 us)
Async XLA Ops:
  14.6 26.5 %collective-permute-start.3 = (bf16[8,2,2,64,128]{4,3,2,1,0:T(8,128)(2,1)}, bf16[8,2,2,64,128]{4,3,2,1,0:T(8,128)(2,1)S(1)}, u32[]{:S(2)}, u32[]{:S(2)}) collective-permute-start(bf16[8,2,2,64,128]{4,3,2,1,0:T(8,128)(2,1)} %get-tuple-element.47), channel_id=1, source_target_pairs={{0,1},{1,0},{2,3},{3,2},{4,5},{5,4},{6,7},{7,6},{8,9},{9,8},{10,11... | collective-permute-start | bytes 1572872 | tf_op jit(solution)/shard_map/ppermute | solution.py:310
  14.7 26.4 %collective-permute-start.4 = (bf16[8,2,2,64,128]{4,3,2,1,0:T(8,128)(2,1)}, bf16[8,2,2,64,128]{4,3,2,1,0:T(8,128)(2,1)S(1)}, u32[]{:S(2)}, u32[]{:S(2)}) collective-permute-start(bf16[8,2,2,64,128]{4,3,2,1,0:T(8,128)(2,1)} %get-tuple-element.48), channel_id=1, source_target_pairs={{0,2},{1,3},{2,0},{3,1},{4,6},{5,7},{6,4},{7,5},{8,10},{9,11},{10,... | collective-permute-start | bytes 1572872 | tf_op jit(solution)/shard_map/ppermute | solution.py:310
  17.5 25.9 %collective-permute-start.5 = (bf16[8,2,2,64,128]{4,3,2,1,0:T(8,128)(2,1)}, bf16[8,2,2,64,128]{4,3,2,1,0:T(8,128)(2,1)S(1)}, u32[]{:S(2)}, u32[]{:S(2)}) collective-permute-start(bf16[8,2,2,64,128]{4,3,2,1,0:T(8,128)(2,1)} %get-tuple-element.49), channel_id=1, source_target_pairs={{0,3},{1,2},{2,1},{3,0},{4,7},{5,6},{6,5},{7,4},{8,11},{9,10},{10,... | collective-permute-start | bytes 1572872 | tf_op jit(solution)/shard_map/ppermute | solution.py:310
  26.1 25.1 %all-to-all-start = ((bf16[8,4,32,256]{3,2,1,0:T(8,128)(2,1)}), bf16[8,4,32,256]{3,2,1,0:T(8,128)(2,1)S(1)}, u32[]{:S(2)}, u32[]{:S(2)}) async-start(bf16[8,4,32,256]{3,2,1,0:T(8,128)(2,1)} %get-tuple-element.52), calls=%async_computation | async-start | bytes 1048576 | tf_op jit(solution)/shard_map/all_to_all | solution.py:373
  39.2 28.5 %collective-permute-start.6 = (bf16[10,2,2,64,128]{4,3,2,1,0:T(8,128)(2,1)}, bf16[10,2,2,64,128]{4,3,2,1,0:T(8,128)(2,1)S(1)}, u32[]{:S(2)}, u32[]{:S(2)}) collective-permute-start(bf16[10,2,2,64,128]{4,3,2,1,0:T(8,128)(2,1)} %get-tuple-element.53), channel_id=1, source_target_pairs={{0,1},{1,0},{2,3},{3,2},{4,5},{5,4},{6,7},{7,6},{8,9},{9,8},{10,11... | collective-permute-start | bytes 1966088 | tf_op jit(solution)/shard_map/ppermute | solution.py:310
  39.6 28.1 %collective-permute-start.7 = (bf16[10,2,2,64,128]{4,3,2,1,0:T(8,128)(2,1)}, bf16[10,2,2,64,128]{4,3,2,1,0:T(8,128)(2,1)}, u32[]{:S(2)}, u32[]{:S(2)}) collective-permute-start(bf16[10,2,2,64,128]{4,3,2,1,0:T(8,128)(2,1)} %get-tuple-element.54), channel_id=1, source_target_pairs={{0,2},{1,3},{2,0},{3,1},{4,6},{5,7},{6,4},{7,5},{8,10},{9,11},{10,... | collective-permute-start | bytes 1966088 | tf_op jit(solution)/shard_map/ppermute | solution.py:310
  41.1 30.4 %collective-permute-start.8 = (bf16[10,2,2,64,128]{4,3,2,1,0:T(8,128)(2,1)}, bf16[10,2,2,64,128]{4,3,2,1,0:T(8,128)(2,1)}, u32[]{:S(2)}, u32[]{:S(2)}) collective-permute-start(bf16[10,2,2,64,128]{4,3,2,1,0:T(8,128)(2,1)} %get-tuple-element.55), channel_id=1, source_target_pairs={{0,3},{1,2},{2,1},{3,0},{4,7},{5,6},{6,5},{7,4},{8,11},{9,10},{10,... | collective-permute-start | bytes 1966088 | tf_op jit(solution)/shard_map/ppermute | solution.py:310
  51.2 32.7 %all-to-all-start.1 = ((bf16[8,8,32,256]{3,2,1,0:T(8,128)(2,1)}), bf16[8,8,32,256]{3,2,1,0:T(8,128)(2,1)S(1)}, u32[]{:S(2)}, u32[]{:S(2)}) async-start(bf16[8,8,32,256]{3,2,1,0:T(8,128)(2,1)} %get-tuple-element.58), calls=%async_computation.1 | async-start | bytes 2097152 | tf_op jit(solution)/shard_map/all_to_all | solution.py:373
  65.4 33.3 %collective-permute-start.9 = (bf16[12,2,2,64,128]{4,3,2,1,0:T(8,128)(2,1)}, bf16[12,2,2,64,128]{4,3,2,1,0:T(8,128)(2,1)S(1)}, u32[]{:S(2)}, u32[]{:S(2)}) collective-permute-start(bf16[12,2,2,64,128]{4,3,2,1,0:T(8,128)(2,1)} %get-tuple-element.59), channel_id=1, source_target_pairs={{0,1},{1,0},{2,3},{3,2},{4,5},{5,4},{6,7},{7,6},{8,9},{9,8},{10,11... | collective-permute-start | bytes 2359304 | tf_op jit(solution)/shard_map/ppermute | solution.py:310
  66.1 32.8 %collective-permute-start.10 = (bf16[12,2,2,64,128]{4,3,2,1,0:T(8,128)(2,1)}, bf16[12,2,2,64,128]{4,3,2,1,0:T(8,128)(2,1)}, u32[]{:S(2)}, u32[]{:S(2)}) collective-permute-start(bf16[12,2,2,64,128]{4,3,2,1,0:T(8,128)(2,1)} %get-tuple-element.60), channel_id=1, source_target_pairs={{0,2},{1,3},{2,0},{3,1},{4,6},{5,7},{6,4},{7,5},{8,10},{9,11},{10,... | collective-permute-start | bytes 2359304 | tf_op jit(solution)/shard_map/ppermute | solution.py:310
  67.6 37.6 %collective-permute-start.11 = (bf16[12,2,2,64,128]{4,3,2,1,0:T(8,128)(2,1)}, bf16[12,2,2,64,128]{4,3,2,1,0:T(8,128)(2,1)}, u32[]{:S(2)}, u32[]{:S(2)}) collective-permute-start(bf16[12,2,2,64,128]{4,3,2,1,0:T(8,128)(2,1)} %get-tuple-element.61), channel_id=1, source_target_pairs={{0,3},{1,2},{2,1},{3,0},{4,7},{5,6},{6,5},{7,4},{8,11},{9,10},{10,... | collective-permute-start | bytes 2359304 | tf_op jit(solution)/shard_map/ppermute | solution.py:310
  83.9 35.3 %all-to-all-start.2 = ((bf16[8,10,32,256]{3,2,1,0:T(8,128)(2,1)}), bf16[8,10,32,256]{3,2,1,0:T(8,128)(2,1)S(1)}, u32[]{:S(2)}, u32[]{:S(2)}) async-start(bf16[8,10,32,256]{3,2,1,0:T(8,128)(2,1)} %get-tuple-element.64), calls=%async_computation.2 | async-start | bytes 2621440 | tf_op jit(solution)/shard_map/all_to_all | solution.py:373
  97.0 38.1 %collective-permute-start.12 = (bf16[14,2,2,64,128]{4,3,2,1,0:T(8,128)(2,1)}, bf16[14,2,2,64,128]{4,3,2,1,0:T(8,128)(2,1)}, u32[]{:S(2)}, u32[]{:S(2)}) collective-permute-start(bf16[14,2,2,64,128]{4,3,2,1,0:T(8,128)(2,1)} %get-tuple-element.65), channel_id=1, source_target_pairs={{0,1},{1,0},{2,3},{3,2},{4,5},{5,4},{6,7},{7,6},{8,9},{9,8},{10,11... | collective-permute-start | bytes 2752520 | tf_op jit(solution)/shard_map/ppermute | solution.py:310
  97.1 38.3 %collective-permute-start.13 = (bf16[14,2,2,64,128]{4,3,2,1,0:T(8,128)(2,1)}, bf16[14,2,2,64,128]{4,3,2,1,0:T(8,128)(2,1)}, u32[]{:S(2)}, u32[]{:S(2)}) collective-permute-start(bf16[14,2,2,64,128]{4,3,2,1,0:T(8,128)(2,1)} %get-tuple-element.66), channel_id=1, source_target_pairs={{0,2},{1,3},{2,0},{3,1},{4,6},{5,7},{6,4},{7,5},{8,10},{9,11},{10,... | collective-permute-start | bytes 2752520 | tf_op jit(solution)/shard_map/ppermute | solution.py:310
  98.7 45.9 %collective-permute-start.14 = (bf16[14,2,2,64,128]{4,3,2,1,0:T(8,128)(2,1)}, bf16[14,2,2,64,128]{4,3,2,1,0:T(8,128)(2,1)}, u32[]{:S(2)}, u32[]{:S(2)}) collective-permute-start(bf16[14,2,2,64,128]{4,3,2,1,0:T(8,128)(2,1)} %get-tuple-element.67), channel_id=1, source_target_pairs={{0,3},{1,2},{2,1},{3,0},{4,7},{5,6},{6,5},{7,4},{8,11},{9,10},{10,... | collective-permute-start | bytes 2752520 | tf_op jit(solution)/shard_map/ppermute | solution.py:310
  119.2 40.8 %all-to-all-start.3 = ((bf16[8,12,32,256]{3,2,1,0:T(8,128)(2,1)}), bf16[8,12,32,256]{3,2,1,0:T(8,128)(2,1)S(1)}, u32[]{:S(2)}, u32[]{:S(2)}) async-start(bf16[8,12,32,256]{3,2,1,0:T(8,128)(2,1)} %get-tuple-element.69), calls=%async_computation.3 | async-start | bytes 3145728 | tf_op jit(solution)/shard_map/all_to_all | solution.py:373
  133.4 31.8 %collective-permute-start.15 = (bf16[16,2,2,64,128]{4,3,2,1,0:T(8,128)(2,1)}, bf16[16,2,2,64,128]{4,3,2,1,0:T(8,128)(2,1)}, u32[]{:S(2)}, u32[]{:S(2)}) collective-permute-start(bf16[16,2,2,64,128]{4,3,2,1,0:T(8,128)(2,1)} %get-tuple-element.70), channel_id=1, source_target_pairs={{0,1},{1,0},{2,3},{3,2},{4,5},{5,4},{6,7},{7,6},{8,9},{9,8},{10,11... | collective-permute-start | bytes 3145736 | tf_op jit(solution)/shard_map/ppermute | solution.py:310
  133.5 34.0 %collective-permute-start.16 = (bf16[16,2,2,64,128]{4,3,2,1,0:T(8,128)(2,1)}, bf16[16,2,2,64,128]{4,3,2,1,0:T(8,128)(2,1)}, u32[]{:S(2)}, u32[]{:S(2)}) collective-permute-start(bf16[16,2,2,64,128]{4,3,2,1,0:T(8,128)(2,1)} %get-tuple-element.71), channel_id=1, source_target_pairs={{0,2},{1,3},{2,0},{3,1},{4,6},{5,7},{6,4},{7,5},{8,10},{9,11},{10,... | collective-permute-start | bytes 3145736 | tf_op jit(solution)/shard_map/ppermute | solution.py:310
  135.1 54.4 %collective-permute-start.17 = (bf16[16,2,2,64,128]{4,3,2,1,0:T(8,128)(2,1)}, bf16[16,2,2,64,128]{4,3,2,1,0:T(8,128)(2,1)}, u32[]{:S(2)}, u32[]{:S(2)}) collective-permute-start(bf16[16,2,2,64,128]{4,3,2,1,0:T(8,128)(2,1)} %get-tuple-element.72), channel_id=1, source_target_pairs={{0,3},{1,2},{2,1},{3,0},{4,7},{5,6},{6,5},{7,4},{8,11},{9,10},{10,... | collective-permute-start | bytes 3145736 | tf_op jit(solution)/shard_map/ppermute | solution.py:310
  161.2 46.8 %all-to-all-start.4 = ((bf16[8,14,32,256]{3,2,1,0:T(8,128)(2,1)}), bf16[8,14,32,256]{3,2,1,0:T(8,128)(2,1)S(1)}, u32[]{:S(2)}, u32[]{:S(2)}) async-start(bf16[8,14,32,256]{3,2,1,0:T(8,128)(2,1)} %get-tuple-element.76), calls=%async_computation.4 | async-start | bytes 3670016 | tf_op jit(solution)/shard_map/all_to_all | solution.py:373
  209.3 60.0 %all-to-all-start.5 = ((bf16[8,16,32,256]{3,2,1,0:T(8,128)(2,1)}), bf16[8,16,32,256]{3,2,1,0:T(8,128)(2,1)S(1)}, u32[]{:S(2)}, u32[]{:S(2)}) async-start(bf16[8,16,32,256]{3,2,1,0:T(8,128)(2,1)} %get-tuple-element.77), calls=%async_computation.5 | async-start | bytes 4194304 | tf_op jit(solution)/shard_map/all_to_all | solution.py:373
  215.1 16.7 %collective-permute-start.21 = (f32[1,16,128]{2,1,0:T(8,128)S(1)}, f32[1,16,128]{2,1,0:T(8,128)S(1)}, u32[]{:S(2)}, u32[]{:S(2)}) collective-permute-start(f32[1,16,128]{2,1,0:T(8,128)S(1)} %bitcast.40), channel_id=1, source_target_pairs={{0,4},{4,0},{8,12},{12,8},{16,20},{20,16},{24,28},{28,24},{1,5},{5... | collective-permute-start | bytes 24584 | tf_op jit(solution)/shard_map/ppermute | solution.py:310
  231.8 17.6 %collective-permute-start.22 = (f32[2,16,128]{2,1,0:T(8,128)S(1)}, f32[2,16,128]{2,1,0:T(8,128)S(1)}, u32[]{:S(2)}, u32[]{:S(2)}) collective-permute-start(f32[2,16,128]{2,1,0:T(8,128)S(1)} %maximum_select_fusion.3), channel_id=1, source_target_pairs={{0,8},{4,12},{8,0},{12,4},{16,24},{20,28},{24,16},{28,20},{1,9},{5... | collective-permute-start | bytes 49160 | tf_op jit(solution)/shard_map/ppermute | solution.py:310
  249.3 14.9 %collective-permute-start.23 = (f32[4,16,128]{2,1,0:T(8,128)S(1)}, f32[4,16,128]{2,1,0:T(8,128)S(1)}, u32[]{:S(2)}, u32[]{:S(2)}) collective-permute-start(f32[4,16,128]{2,1,0:T(8,128)S(1)} %bitcast.38), channel_id=1, source_target_pairs={{0,16},{4,20},{8,24},{12,28},{16,0},{20,4},{24,8},{28,12},{1,17},{... | collective-permute-start | bytes 98312 | tf_op jit(solution)/shard_map/ppermute | solution.py:310
  (35 other events, 352.9 us)
